TPU v7x, 512 devices: a whole 4x4x16 slice. The times are simulated.
512 devices in a mesh: dp: 32 (over x, z_lo, core), tensor: 16 (over z_hi, y).
Axes of the slice: x: 4, y: 4, z: 16 (z_hi: 4, z_lo: 4; z = z_hi * 4 + z_lo), core: 2. Of those that a mesh axis runs over, the one named last changes fastest.
Arguments:
- page_patches: bfloat16 [32768, 6144], P('dp', 'tensor'), may hold values from -720 to 720
- gain: bfloat16 [6144], P('tensor'), may hold values from 0.5 to 1.5
- q_weight: bfloat16 [6144, 4096], P('dp', 'tensor'), may hold values from -0.076546554 to 0.076546554
- k_weight: bfloat16 [6144, 4096], P('dp', 'tensor'), may hold values from -2.0412415 to 2.0412415
- v_weight: bfloat16 [6144, 4096], P('dp', 'tensor'), may hold values from -0.078125 to 0.078125
- pack_lengths: int32 [32, 32], replicated, may hold values from 1 to 32, 512 in all within a row
- line_order: int32 [32, 32], replicated, may hold values from 0 to 31, each once within a row
Outputs:
- context: bfloat16 [16384, 4096], P('dp', 'tensor')
Inputs may be any that keep to these rules, and one draw needn't show every extreme that they name: `pack_lengths`: every row sums to exactly 512 and holds the value 32. `line_order`: each row names every sequence 0 to 31 once.
All inputs are finite; a program needn't handle non-finite values.
Results may differ from a plain program's by a relative error of at most 0.0079.
Values may be sent and summed in bfloat16 or wider, within the bound.
No kernel may reach another device: no remote copies, remote signals or barrier semaphores. Data moves between devices by JAX's collectives and lax.ppermute only.
A program may use at most 64 MiB of HBM per device.

v0:
```python
import math

import jax
import jax.numpy as jnp
from jax import lax
from jax.sharding import PartitionSpec as P

HEAD_DIM = 128


norm_epsilon = 1e-06


def shards(page_patches, gain, q_weight, k_weight, v_weight, pack_lengths, line_order):
    groups = lax.axis_size("dp")
    page_index = lax.axis_index("dp")
    feature_cols = page_patches.shape[1]
    slot_rows = page_patches.shape[0] // groups
    seq_rows = slot_rows * groups // 2
    targets = jnp.arange(groups, dtype=jnp.int32)
    my_order = lax.dynamic_index_in_dim(line_order, page_index, 0, keepdims=False)
    slot_for = jnp.sum(
        jnp.where(my_order[None, :] == targets[:, None], targets[None, :], 0), axis=1
    )
    slots = page_patches.reshape(groups, slot_rows, feature_cols)
    outgoing = jnp.take(slots, slot_for, axis=0)
    incoming = lax.all_to_all(outgoing, "dp", split_axis=0, concat_axis=0, tiled=True)
    my_lengths = lax.dynamic_index_in_dim(pack_lengths, page_index, 0, keepdims=False)
    line_ends = jnp.cumsum(my_lengths)
    line_starts = line_ends - my_lengths
    places = jnp.arange(seq_rows, dtype=jnp.int32)
    segment = jnp.sum((line_ends[None, :] <= places[:, None]).astype(jnp.int32), axis=1)
    start_of_row = jnp.sum(
        jnp.where(segment[:, None] == targets[None, :], line_starts[None, :], 0), axis=1
    )
    source_rows = segment * slot_rows + places - start_of_row
    packed = jnp.take(incoming.reshape(groups * slot_rows, feature_cols), source_rows, axis=0)
    full_rows, full_gain = (
        lax.all_gather(packed, "tensor", axis=1, tiled=True),
        lax.all_gather(gain, "tensor", axis=0, tiled=True),
    )
    row_vals = full_rows.astype(jnp.float32)
    row_mean = jnp.mean(row_vals, axis=1, keepdims=True)
    row_var = jnp.mean(jnp.square(row_vals - row_mean), axis=1, keepdims=True)
    normed = (
        (row_vals - row_mean) * lax.rsqrt(row_var + norm_epsilon) * full_gain.astype(jnp.float32)
    ).astype(jnp.bfloat16)
    pieces = (
        lax.all_gather(q_weight, "dp", axis=0, tiled=True),
        lax.all_gather(k_weight, "dp", axis=0, tiled=True),
        lax.all_gather(v_weight, "dp", axis=0, tiled=True),
    )
    query_sum, key_sum, value_sum = tuple(
        (jnp.dot(normed, weight_rows, preferred_element_type=jnp.float32) for weight_rows in pieces)
    )
    local_heads = q_weight.shape[1] // HEAD_DIM
    query_heads = query_sum.astype(jnp.bfloat16).reshape(seq_rows, local_heads, HEAD_DIM)
    key_heads = key_sum.astype(jnp.bfloat16).reshape(seq_rows, local_heads, HEAD_DIM)
    value_heads = value_sum.astype(jnp.bfloat16).reshape(seq_rows, local_heads, HEAD_DIM)
    scores = jnp.einsum(
        "qhd,khd->hqk", query_heads, key_heads, preferred_element_type=jnp.float32
    ) * (1.0 / math.sqrt(HEAD_DIM))
    same_line = segment[:, None] == segment[None, :]
    scores = jnp.where(same_line[None, :, :], scores, -jnp.inf)
    row_max = jnp.max(scores, axis=2, keepdims=True)
    expo = jnp.exp(scores - row_max)
    attn_probs = (expo / jnp.sum(expo, axis=2, keepdims=True)).astype(jnp.bfloat16)
    context = jnp.einsum(
        "hqk,khd->qhd", attn_probs, value_heads, preferred_element_type=jnp.float32
    )
    return context.astype(jnp.bfloat16).reshape(seq_rows, local_heads * HEAD_DIM)


def solution(mesh):
    return jax.shard_map(
        shards,
        mesh=mesh,
        in_specs=(
            P("dp", "tensor"),
            P("tensor"),
            P("dp", "tensor"),
            P("dp", "tensor"),
            P("dp", "tensor"),
            P(),
            P(),
        ),
        out_specs=P("dp", "tensor"),
        check_vma=False,
    )
```

profile of v0, /device:TPU:1, one launch (start us, length us, event | category | flops | bytes accessed | tf_op | source)
XLA Modules:
  0.0 443.6 jit_solution(14901982915176972839)
XLA Ops:
  6.5 0.0 copy-start
  6.5 0.8 dynamic-slice_bitcast_fusion
  7.3 0.1 select_reduce_fusion.1
  7.5 0.2 copy-done
  7.7 0.7 gather_fusion
  8.4 1.0 broadcast_select_fusion
  9.4 0.0 copy-start.2
  9.4 10.6 %all-to-all-start = ((bf16[32,32,384]{2,1,0:T(8,128)(2,1)}), bf16[32,32,384]{2,1,0:T(8,128)(2,1)S(1)}, u32[]{:S(2)}, u32[]{:S(2)}) async-start(bf16[32,32,384]{2,1,0:T(8,128)(2,1)} %broadcast_select_fusion), calls=%async_computation | async-start | bytes 1572864 | tf_op jit(solution)/shard_map/all_to_all | solution.py:27
  20.0 0.0 all-gather.6.cloned.1.call-start
  20.1 0.7 fusion.17
  20.8 0.1 copy.23
  20.9 0.1 reduce-window.4
  20.9 0.1 reduce
  21.0 0.1 convert_reduce_fusion.1
  21.1 0.7 fusion.13
  21.8 0.1 select_reduce_fusion
  22.0 20.5 %all-to-all-done = bf16[32,32,384]{2,1,0:T(8,128)(2,1)S(1)} async-done(((bf16[32,32,384]{2,1,0:T(8,128)(2,1)}), bf16[32,32,384]{2,1,0:T(8,128)(2,1)S(1)}, u32[]{:S(2)}, u32[]{:S(2)}) %all-to-all-start) | async-done | bytes 786464 | tf_op jit(solution)/shard_map/all_to_all | solution.py:27
  42.5 1.9 gather_fusion.1
  44.4 0.9 broadcast_select_fusion.1
  45.3 0.0 all-gather.6.cloned.1.call-update
  45.3 0.0 all-gather.10.cloned.1.call-start
  45.4 0.7 all-gather.10.cloned.1.call-update
  46.1 0.0 all-gather.12.cloned.1.call-start
  46.1 0.7 all-gather.12.cloned.1.call-update
  46.8 0.0 all-gather.8.cloned.1.call-start
  46.9 0.5 all-gather.8.cloned.1.call-update
  47.4 0.0 copy-done.2
  47.4 49.9 %all-gather = bf16[16,1,384]{2,1,0:T(2,128)(2,1)S(1)} all-gather(bf16[1,1,384]{2,1,0:T(2,128)(2,1)S(1)} %reshape.150), channel_id=1, replica_groups=mesh['dp'=32,'tensor'=16] {'tensor'}, dimensions={0}, use_global_device_ids=true | all-gather | bytes 13056 | tf_op jit(solution)/shard_map/all_gather | solution.py:40
  97.4 0.2 broadcast_compare_fusion
  97.6 133.5 %all-gather.6.cloned.1.call-done = bf16[512,6144]{1,0:T(8,128)(2,1)} async-done(((bf16[512,384]{1,0:T(8,128)(2,1)}), bf16[512,6144]{1,0:T(8,128)(2,1)}) %all-gather.6.cloned.1.call-update) | async-done | bytes 6291472 | tf_op jit(solution)/shard_map/all_gather | solution.py:39
  231.1 0.0 copy-start.1
  231.1 3.8 convert_reduce_fusion
  234.9 0.7 copy-done.1
  235.7 1.8 fusion.3
  237.5 6.3 %fusion.5 = bf16[512,6144]{1,0:T(8,128)(2,1)} fusion(bf16[512,6144]{1,0:T(8,128)(2,1)S(1)} %copy-done.1, f32[6144]{0:T(1024)S(1)} %bitcast.40, f32[512]{0:T(512)S(1)} %add_rsqrt_fusion, f32[512]{0:T(512)S(1)} %broadcast_multiply_fusion), kind=kLoop, calls=%fused_computation.9 | loop fusion | flops 15728640 | bytes 12611584 | tf_op jit(solution)/shard_map/convert_element_type | solution.py:47
  243.7 50.1 %all-gather.10.cloned.1.call-done = bf16[6144,256]{1,0:T(8,128)(2,1)} async-done(((bf16[192,256]{1,0:T(8,128)(2,1)}), bf16[6144,256]{1,0:T(8,128)(2,1)}) %all-gather.10.cloned.1.call-update) | async-done | bytes 3145744 | tf_op jit(solution)/shard_map/all_gather | solution.py:49
  293.8 5.5 %convolution_convert_fusion.1 = bf16[512,256]{0,1:T(8,128)(2,1)S(1)} fusion(bf16[512,6144]{1,0:T(8,128)(2,1)} %fusion.5, bf16[6144,256]{1,0:T(8,128)(2,1)} %all-gather.10.cloned.1.call-done), kind=kOutput, calls=%fused_computation.15 | convolution fusion | flops 1610743808 | bytes 9699328 | tf_op jit(solution)/shard_map/dot_general | solution.py:54
  299.4 62.3 %all-gather.12.cloned.1.call-done = bf16[6144,256]{1,0:T(8,128)(2,1)} async-done(((bf16[192,256]{1,0:T(8,128)(2,1)}), bf16[6144,256]{1,0:T(8,128)(2,1)}) %all-gather.12.cloned.1.call-update) | async-done | bytes 3145744 | tf_op jit(solution)/shard_map/all_gather | solution.py:50
  361.7 5.5 %convolution_convert_fusion = bf16[512,256]{0,1:T(8,128)(2,1)S(1)} fusion(bf16[512,6144]{1,0:T(8,128)(2,1)} %fusion.5, bf16[6144,256]{1,0:T(8,128)(2,1)} %all-gather.12.cloned.1.call-done), kind=kOutput, calls=%fused_computation.14 | convolution fusion | flops 1610743808 | bytes 9699328 | tf_op jit(solution)/shard_map/dot_general | solution.py:54
  367.2 1.0 fusion.21
  368.2 61.2 %all-gather.8.cloned.1.call-done = bf16[6144,256]{1,0:T(8,128)(2,1)} async-done(((bf16[192,256]{1,0:T(8,128)(2,1)}), bf16[6144,256]{1,0:T(8,128)(2,1)}) %all-gather.8.cloned.1.call-update) | async-done | bytes 3145744 | tf_op jit(solution)/shard_map/all_gather | solution.py:51
  429.4 5.5 %convolution_convert_fusion.2 = bf16[512,256]{0,1:T(8,128)(2,1)S(1)} fusion(bf16[512,6144]{1,0:T(8,128)(2,1)} %fusion.5, bf16[6144,256]{1,0:T(8,128)(2,1)} %all-gather.8.cloned.1.call-done), kind=kOutput, calls=%fused_computation.16 | convolution fusion | flops 1610743808 | bytes 9699328 | tf_op jit(solution)/shard_map/dot_general | solution.py:54
  434.9 1.3 convolution_convert_fusion.3
  436.2 0.8 copy.27
  (11 shorter events, 0.1 us)
Async XLA Ops:
  6.5 1.1 copy-start
  9.4 38.0 %copy-start.2 = (bf16[384]{0:T(512)(128)(2,1)S(1)}, bf16[384]{0:T(512)(128)(2,1)}, u32[]{:S(2)}) copy-start(bf16[384]{0:T(512)(128)(2,1)} %param.8) | copy-start | bytes 2308
  9.4 33.0 %all-to-all-start = ((bf16[32,32,384]{2,1,0:T(8,128)(2,1)}), bf16[32,32,384]{2,1,0:T(8,128)(2,1)S(1)}, u32[]{:S(2)}, u32[]{:S(2)}) async-start(bf16[32,32,384]{2,1,0:T(8,128)(2,1)} %broadcast_select_fusion), calls=%async_computation | async-start | bytes 1572864 | tf_op jit(solution)/shard_map/all_to_all | solution.py:27
  20.0 211.1 %all-gather.6.cloned.1.call-start = ((), (), s32[]{:S(2)}) async-start(), calls=%async_computation.1 | async-start | bytes 6684672 | tf_op jit(solution)/shard_map/all_gather | solution.py:39
  45.3 248.5 %all-gather.10.cloned.1.call-start = ((), (), s32[]{:S(2)}) async-start(), calls=%async_computation.3 | async-start | bytes 3244032 | tf_op jit(solution)/shard_map/all_gather | solution.py:49
  46.1 315.6 %all-gather.12.cloned.1.call-start = ((), (), s32[]{:S(2)}) async-start(), calls=%async_computation.4 | async-start | bytes 3244032 | tf_op jit(solution)/shard_map/all_gather | solution.py:50
  46.8 382.6 %all-gather.8.cloned.1.call-start = ((), (), s32[]{:S(2)}) async-start(), calls=%async_computation.2 | async-start | bytes 3244032 | tf_op jit(solution)/shard_map/all_gather | solution.py:51
  231.1 4.6 %copy-start.1 = (bf16[512,6144]{1,0:T(8,128)(2,1)S(1)}, bf16[512,6144]{1,0:T(8,128)(2,1)}, u32[]{:S(2)}) copy-start(bf16[512,6144]{1,0:T(8,128)(2,1)} %all-gather.6.cloned.1.call-done) | copy-start | bytes 18874372
Sparse Core Ops, SparseCore 0:
  45.5 185.5 all-gather.5
  233.2 60.5 all-gather.9
  296.0 65.6 all-gather.11
  363.7 65.6 all-gather.7
where the time goes:
time: 444 us
  waiting for transfers between devices  329 us (74%)
  blocking collectives  49.9 us (11%)
  matrix products  18.8 us (4%)
  other arithmetic  15.3 us (3%)
  between operations  13.3 us (3%)
  starting transfers between devices  10.7 us (2%)
  local copies, waits for them, and re-layouts  6.03 us (1%)
    all_gather x1, waiting for transfers between devices, shards(): lax.all_gather(packed, 'tensor', axis=1, tiled=True)  133 us
    all_gather x1, waiting for transfers between devices, shards(): lax.all_gather(k_weight, 'dp', axis=0, tiled=True)  62.3 us
    all_gather x1, waiting for transfers between devices, shards(): lax.all_gather(v_weight, 'dp', axis=0, tiled=True)  61.2 us
    all_gather x1, waiting for transfers between devices, shards(): lax.all_gather(q_weight, 'dp', axis=0, tiled=True)  50.1 us
    all_gather x1, blocking collectives, shards(): lax.all_gather(gain, 'tensor', axis=0, tiled=True)  49.9 us
    all_to_all x1, waiting for transfers between devices, shards(): lax.all_to_all(outgoing, 'dp', split_axis=0, concat_axis=0, tiled=True)  20.5 us
    dot_general x3, matrix products, shards(): jnp.dot(normed, weight_rows, preferred_element_type=jnp.float32)  16.6 us
    all_to_all x1, starting transfers between devices, shards(): lax.all_to_all(outgoing, 'dp', split_axis=0, concat_axis=0, tiled=True)  10.6 us
  transfers between devices with their start and end apart: 5, of which 5 were waited for; matrix products, arithmetic and copies ran while one was open for 6% of the time, Pallas kernels for 0%

commit v1 on v0

v1 whole, which is shorter than its diff:
```python
import math

import jax
import jax.numpy as jnp
from jax import lax
from jax.experimental import pallas as pl
from jax.experimental.pallas import tpu as pltpu
from jax.sharding import PartitionSpec as P

HEAD_DIM = 128
NORM_EPSILON = 1e-06
Z_PARTS, Y_PARTS = 4, 4
GAIN_ROWS = 16
ROW_TILE = 16


def z_shift(step):
    return [
        (z * Y_PARTS + y, (z + step) % Z_PARTS * Y_PARTS + y)
        for z in range(Z_PARTS)
        for y in range(Y_PARTS)
    ]


def y_shift(step):
    return [
        (z * Y_PARTS + y, z * Y_PARTS + (y + step) % Y_PARTS)
        for z in range(Z_PARTS)
        for y in range(Y_PARTS)
    ]


def both_ways(block, shift, cut):
    up = lax.ppermute(block, "tensor", shift(1))
    down = lax.ppermute(block, "tensor", shift(-1))
    far_top = lax.ppermute(up[:cut], "tensor", shift(1))
    far_rest = lax.ppermute(down[cut:], "tensor", shift(-1))
    return up, down, far_top, far_rest


def attend_kernel(slots, count, rows, cut, *refs):
    places_ref, blocks = refs[0], refs[1 : 1 + count]
    weight_ref, seg_col_ref, seg_row_ref, out_ref, normed_ref = refs[1 + count :]
    features = normed_ref.shape[1]
    width = blocks[0].shape[1]

    def part(pieces, row):
        for ref_index, ref_row, first, last in pieces:
            if first <= row < last:
                return blocks[ref_index], ref_row - first
        return None

    gains = []
    for pieces in slots:
        ref, shift = part(pieces, rows)
        gains.append(ref[pl.ds(rows + shift, GAIN_ROWS), :][:1].astype(jnp.float32))
    columns = [pl.ds(pl.multiple_of(places_ref[j] * width, 128), width) for j in range(len(slots))]

    for first, last in ((0, cut), (cut, rows)):
        sources = [part(pieces, first) for pieces in slots]

        def step(i, carry):
            row = first + i * ROW_TILE
            def load(j):
                ref, shift = sources[j]
                at = pl.multiple_of(row + shift, ROW_TILE)
                return ref[pl.ds(at, ROW_TILE), :].astype(jnp.float32)

            total = load(0)
            for j in range(1, len(slots)):
                total = total + load(j)
            mean = jnp.sum(total, axis=1, keepdims=True) * (1.0 / features)
            square = jnp.square(load(0) - mean)
            for j in range(1, len(slots)):
                square = square + jnp.square(load(j) - mean)
            var = jnp.sum(square, axis=1, keepdims=True) * (1.0 / features)
            scale = lax.rsqrt(var + NORM_EPSILON)
            at = pl.multiple_of(row, ROW_TILE)
            for j in range(len(slots)):
                normed_ref[pl.ds(at, ROW_TILE), columns[j]] = (
                    (load(j) - mean) * scale * gains[j]
                ).astype(jnp.bfloat16)
            return carry

        lax.fori_loop(0, (last - first) // ROW_TILE, step, 0)

    local = out_ref.shape[1]
    sums = jnp.dot(normed_ref[...], weight_ref[...], preferred_element_type=jnp.float32)
    sums = sums.astype(jnp.bfloat16)
    query, key, value = sums[:, :local], sums[:, local : 2 * local], sums[:, 2 * local :]
    span, window = 128, 256
    for row in range(0, rows, span):
        low = min(max(row - (window - span) // 2, 0), rows - window)
        same = seg_col_ref[row : row + span, :1] == seg_row_ref[:1, low : low + window]
        for col in range(0, local, HEAD_DIM):
            head = slice(col, col + HEAD_DIM)
            scores = lax.dot_general(
                query[row : row + span, head],
                key[low : low + window, head],
                (((1,), (1,)), ((), ())),
                preferred_element_type=jnp.float32,
            ) * (1.0 / math.sqrt(HEAD_DIM))
            scores = jnp.where(same, scores, -jnp.inf)
            expo = jnp.exp(scores - jnp.max(scores, axis=1, keepdims=True))
            probs = (expo / jnp.sum(expo, axis=1, keepdims=True)).astype(jnp.bfloat16)
            out_ref[row : row + span, head] = jnp.dot(
                probs, value[low : low + window, head], preferred_element_type=jnp.float32
            ).astype(jnp.bfloat16)


def shards(page_patches, gain, q_weight, k_weight, v_weight, pack_lengths, line_order):
    groups = lax.axis_size("dp")
    page_index = lax.axis_index("dp")
    width = page_patches.shape[1]
    slot_rows = page_patches.shape[0] // groups
    rows = slot_rows * groups // 2
    local = q_weight.shape[1]
    weights = lax.all_gather(
        jnp.concatenate([q_weight, k_weight, v_weight], axis=1), "dp", axis=0, tiled=True
    )
    targets = jnp.arange(groups, dtype=jnp.int32)
    my_order = lax.dynamic_index_in_dim(line_order, page_index, 0, keepdims=False)
    slot_for = jnp.sum(
        jnp.where(my_order[None, :] == targets[:, None], targets[None, :], 0), axis=1
    )
    slots = page_patches.reshape(groups, slot_rows, width)
    outgoing = jnp.take(slots, slot_for, axis=0)
    incoming = lax.all_to_all(outgoing, "dp", split_axis=0, concat_axis=0, tiled=True)
    my_lengths = lax.dynamic_index_in_dim(pack_lengths, page_index, 0, keepdims=False)
    line_ends = jnp.cumsum(my_lengths)
    line_starts = line_ends - my_lengths
    row_ids = jnp.arange(rows, dtype=jnp.int32)
    segment = jnp.sum((line_ends[None, :] <= row_ids[:, None]).astype(jnp.int32), axis=1)
    start_of_row = jnp.sum(
        jnp.where(segment[:, None] == targets[None, :], line_starts[None, :], 0), axis=1
    )
    source_rows = segment * slot_rows + row_ids - start_of_row
    packed = jnp.take(incoming.reshape(groups * slot_rows, width), source_rows, axis=0)

    own = jnp.concatenate([packed, jnp.broadcast_to(gain[None, :], (GAIN_ROWS, width))], axis=0)
    all_rows = rows + GAIN_ROWS
    cut = rows // 2 + GAIN_ROWS
    z_up, z_down, z_far_top, z_far_rest = both_ways(own, z_shift, cut)
    pair = jnp.concatenate([z_up, z_down], axis=0)
    far = jnp.concatenate([z_far_top, z_far_rest], axis=0)
    blocks, slot_list, shifts = [], [], []

    def add(array):
        blocks.append(array)
        return len(blocks) - 1

    def slot(dz, dy, *pieces):
        slot_list.append(pieces)
        shifts.append((dz, dy))

    for array, dzs in ((own, (0,)), (pair, (-1, 1)), (far, (2,))):
        half = cut if len(dzs) == 1 else all_rows
        up, down, far_top, far_rest = both_ways(array, y_shift, half)
        for dy, source in ((0, array), (-1, up), (1, down)):
            ref = add(source)
            for k, dz in enumerate(dzs):
                slot(dz, dy, (ref, k * all_rows, 0, all_rows))
        top, rest = add(far_top), add(far_rest)
        if len(dzs) == 1:
            slot(dzs[0], 2, (top, 0, 0, cut), (rest, 0, cut, all_rows))
        else:
            slot(dzs[0], 2, (top, 0, 0, all_rows))
            slot(dzs[1], 2, (rest, 0, 0, all_rows))
    tensor = lax.axis_index("tensor")
    my_z, my_y = tensor // Y_PARTS, tensor % Y_PARTS
    step_z = jnp.array([dz for dz, _ in shifts], jnp.int32)
    step_y = jnp.array([dy for _, dy in shifts], jnp.int32)
    places = (my_z + step_z + Z_PARTS) % Z_PARTS * Y_PARTS + (my_y + step_y + Y_PARTS) % Y_PARTS

    def kernel(*refs):
        attend_kernel(slot_list, len(blocks), rows, cut, *refs)

    vmem = pl.BlockSpec(memory_space=pltpu.VMEM)
    return pl.pallas_call(
        kernel,
        out_shape=jax.ShapeDtypeStruct((rows, local), jnp.bfloat16),
        in_specs=[pl.BlockSpec(memory_space=pltpu.SMEM)] + [vmem] * (len(blocks) + 3),
        out_specs=vmem,
        scratch_shapes=[pltpu.VMEM((rows, width * len(slot_list)), jnp.bfloat16)],
        name="norm_project_attend",
    )(places, *blocks, weights, segment[:, None], segment[None, :])


def solution(mesh):
    return jax.shard_map(
        shards,
        mesh=mesh,
        in_specs=(
            P("dp", "tensor"),
            P("tensor"),
            P("dp", "tensor"),
            P("dp", "tensor"),
            P("dp", "tensor"),
            P(),
            P(),
        ),
        out_specs=P("dp", "tensor"),
        check_vma=False,
    )
```

time: 444 us -> 215 us (0.48)
  the two profiles are of different devices: /device:TPU:1 before, /device:TPU:56 now
where the time goes in v1:
time: 215 us; the launch traced here: 214 us
  waiting for transfers between devices  90 us (42%)
  starting transfers between devices  68.9 us (32%)
  Pallas kernels  23.5 us (11%)
  between operations  13.8 us (6%)
  local copies, waits for them, and re-layouts  13.2 us (6%)
  other arithmetic  4.82 us (2%)
    ppermute x4, waiting for transfers between devices, both_ways(): up = lax.ppermute(block, 'tensor', shift(1))  42.2 us
    pallas_call x1, Pallas kernels, shards(): pl.pallas_call(kernel, out_shape=jax.ShapeDtypeStruct((rows, local), jnp....  23.5 us
    all_to_all x1, waiting for transfers between devices, shards(): lax.all_to_all(outgoing, 'dp', split_axis=0, concat_axis=0, tiled=True)  20.7 us
    ppermute x4, starting transfers between devices, both_ways(): far_top = lax.ppermute(up[:cut], 'tensor', shift(1))  18.4 us
    ppermute x4, starting transfers between devices, both_ways(): up = lax.ppermute(block, 'tensor', shift(1))  18.2 us
    ppermute x4, starting transfers between devices, both_ways(): far_rest = lax.ppermute(down[cut:], 'tensor', shift(-1))  11.9 us
    ppermute x4, starting transfers between devices, both_ways(): down = lax.ppermute(block, 'tensor', shift(-1))  11.7 us
    ppermute x4, waiting for transfers between devices, both_ways(): far_rest = lax.ppermute(down[cut:], 'tensor', shift(-1))  10.9 us
  transfers between devices with their start and end apart: 18, of which 6 were waited for; matrix products, arithmetic and copies ran while one was open for 7% of the time, Pallas kernels for 0%

profile of v1, /device:TPU:56, one launch (start us, length us, event | category | flops | bytes accessed | tf_op | source)
XLA Modules:
  0.0 214.1 jit_solution(5926066940925124125)
XLA Ops:
  6.6 1.8 pad_maximum_fusion.1
  8.4 0.7 dynamic-slice_bitcast_fusion
  9.1 0.1 select_reduce_fusion.1
  9.2 0.7 gather_fusion
  10.0 1.0 broadcast_select_fusion
  11.0 8.6 %all-to-all-start = ((bf16[32,32,384]{2,1,0:T(8,128)(2,1)}), bf16[32,32,384]{2,1,0:T(8,128)(2,1)S(1)}, u32[]{:S(2)}, u32[]{:S(2)}) async-start(bf16[32,32,384]{2,1,0:T(8,128)(2,1)} %broadcast_select_fusion), calls=%async_computation | async-start | bytes 1572864 | tf_op jit(solution)/shard_map/all_to_all | solution.py:128
  19.6 0.7 fusion.6
  20.5 0.1 reduce
  20.6 0.1 convert_reduce_fusion
  20.7 0.7 fusion.5
  21.4 0.1 select_reduce_fusion
  21.5 20.7 %all-to-all-done = bf16[32,32,384]{2,1,0:T(8,128)(2,1)S(1)} async-done(((bf16[32,32,384]{2,1,0:T(8,128)(2,1)}), bf16[32,32,384]{2,1,0:T(8,128)(2,1)S(1)}, u32[]{:S(2)}, u32[]{:S(2)}) %all-to-all-start) | async-done | bytes 786464 | tf_op jit(solution)/shard_map/all_to_all | solution.py:128
  42.3 1.9 gather_fusion.1
  44.2 0.1 broadcast_select_fusion.1
  44.4 9.5 %collective-permute-start.4 = (bf16[528,384]{1,0:T(8,128)(2,1)S(1)}, bf16[528,384]{1,0:T(8,128)(2,1)S(1)}, u32[]{:S(2)}, u32[]{:S(2)}) collective-permute-start(bf16[528,384]{1,0:T(8,128)(2,1)S(1)} %pad_maximum_fusion.refs_1_), channel_id=1, source_target_pairs={{0,4},{1,5},{2,6},{3,7},{4,8},{5,9},{6,10},{7,11},{8,12},{9,13},{1... | collective-permute-start | bytes 1216520 | tf_op jit(solution)/shard_map/ppermute | solution.py:34
  53.9 3.3 %collective-permute-start.5 = (bf16[528,384]{1,0:T(8,128)(2,1)S(1)}, bf16[528,384]{1,0:T(8,128)(2,1)S(1)}, u32[]{:S(2)}, u32[]{:S(2)}) collective-permute-start(bf16[528,384]{1,0:T(8,128)(2,1)S(1)} %pad_maximum_fusion.refs_1_), channel_id=1, source_target_pairs={{0,12},{1,13},{2,14},{3,15},{4,0},{5,1},{6,2},{7,3},{8,4},{9,5},{1... | collective-permute-start | bytes 1216520 | tf_op jit(solution)/shard_map/ppermute | solution.py:35
  57.2 42.2 %collective-permute-done.4 = bf16[528,384]{1,0:T(8,128)(2,1)S(1)} collective-permute-done((bf16[528,384]{1,0:T(8,128)(2,1)S(1)}, bf16[528,384]{1,0:T(8,128)(2,1)S(1)}, u32[]{:S(2)}, u32[]{:S(2)}) %collective-permute-start.4) | collective-permute-done | bytes 405536 | tf_op jit(solution)/shard_map/ppermute | solution.py:34
  99.5 7.3 %collective-permute-done.5 = bf16[528,384]{1,0:T(8,128)(2,1)S(1)} collective-permute-done((bf16[528,384]{1,0:T(8,128)(2,1)S(1)}, bf16[528,384]{1,0:T(8,128)(2,1)S(1)}, u32[]{:S(2)}, u32[]{:S(2)}) %collective-permute-start.5) | collective-permute-done | bytes 405536 | tf_op jit(solution)/shard_map/ppermute | solution.py:35
  106.9 1.9 collective-permute-start.6
  108.8 3.9 %collective-permute-start.7 = (bf16[1056,384]{1,0:T(8,128)(2,1)S(1)}, bf16[1056,384]{1,0:T(8,128)(2,1)S(1)}, u32[]{:S(2)}, u32[]{:S(2)}) collective-permute-start(bf16[1056,384]{1,0:T(8,128)(2,1)S(1)} %constant_dynamic-update-slice_fusion.refs_6_), channel_id=1, source_target_pairs={{0,3},{1,0},{2,1},{3,2},{4,7},{5,4},{6,5},{7,6},{8,11},{9,8},{10,9... | collective-permute-start | bytes 2433032 | tf_op jit(solution)/shard_map/ppermute | solution.py:35
  112.8 6.4 %collective-permute-start.10 = (bf16[272,384]{1,0:T(8,128)(2,1)S(1)}, bf16[272,384]{1,0:T(8,128)(2,1)S(1)}, u32[]{:S(2)}, u32[]{:S(2)}) collective-permute-start(bf16[272,384]{1,0:T(8,128)(2,1)S(1)} %slice.40), channel_id=1, source_target_pairs={{0,4},{1,5},{2,6},{3,7},{4,8},{5,9},{6,10},{7,11},{8,12},{9,13},{1... | collective-permute-start | bytes 626696 | tf_op jit(solution)/shard_map/ppermute | solution.py:36
  119.2 2.3 %collective-permute-start.1 = (bf16[528,384]{1,0:T(8,128)(2,1)S(1)}, bf16[528,384]{1,0:T(8,128)(2,1)S(1)}, u32[]{:S(2)}, u32[]{:S(2)}) collective-permute-start(bf16[528,384]{1,0:T(8,128)(2,1)S(1)} %pad_maximum_fusion.refs_1_), channel_id=1, source_target_pairs={{0,3},{1,0},{2,1},{3,2},{4,7},{5,4},{6,5},{7,6},{8,11},{9,8},{10,9... | collective-permute-start | bytes 1216520 | tf_op jit(solution)/shard_map/ppermute | solution.py:35
  121.5 4.0 %collective-permute-start.11 = (bf16[256,384]{1,0:T(8,128)(2,1)S(1)}, bf16[256,384]{1,0:T(8,128)(2,1)S(1)}, u32[]{:S(2)}, u32[]{:S(2)}) collective-permute-start(bf16[256,384]{1,0:T(8,128)(2,1)S(1)} %slice.41), channel_id=1, source_target_pairs={{0,12},{1,13},{2,14},{3,15},{4,0},{5,1},{6,2},{7,3},{8,4},{9,5},{1... | collective-permute-start | bytes 589832 | tf_op jit(solution)/shard_map/ppermute | solution.py:37
  125.5 8.7 %collective-permute-done.10 = bf16[272,384]{1,0:T(8,128)(2,1)S(1)} collective-permute-done((bf16[272,384]{1,0:T(8,128)(2,1)S(1)}, bf16[272,384]{1,0:T(8,128)(2,1)S(1)}, u32[]{:S(2)}, u32[]{:S(2)}) %collective-permute-start.10) | collective-permute-done | bytes 208928 | tf_op jit(solution)/shard_map/ppermute | solution.py:36
  134.2 3.1 %collective-permute-start = (bf16[528,384]{1,0:T(8,128)(2,1)S(1)}, bf16[528,384]{1,0:T(8,128)(2,1)S(1)}, u32[]{:S(2)}, u32[]{:S(2)}) collective-permute-start(bf16[528,384]{1,0:T(8,128)(2,1)S(1)} %pad_maximum_fusion.refs_1_), channel_id=1, source_target_pairs={{0,1},{1,2},{2,3},{3,0},{4,5},{5,6},{6,7},{7,4},{8,9},{9,10},{10,1... | collective-permute-start | bytes 1216520 | tf_op jit(solution)/shard_map/ppermute | solution.py:34
  137.4 0.7 constant_dynamic-update-slice_fusion.3
  138.1 6.2 %collective-permute-done.11 = bf16[256,384]{1,0:T(8,128)(2,1)S(1)} collective-permute-done((bf16[256,384]{1,0:T(8,128)(2,1)S(1)}, bf16[256,384]{1,0:T(8,128)(2,1)S(1)}, u32[]{:S(2)}, u32[]{:S(2)}) %collective-permute-start.11) | collective-permute-done | bytes 196640 | tf_op jit(solution)/shard_map/ppermute | solution.py:37
  144.3 0.7 constant_dynamic-update-slice_fusion.2.refs_11_
  145.0 3.6 %collective-permute-start.12 = (bf16[528,384]{1,0:T(8,128)(2,1)}, bf16[528,384]{1,0:T(8,128)(2,1)}, u32[]{:S(2)}, u32[]{:S(2)}) collective-permute-start(bf16[528,384]{1,0:T(8,128)(2,1)} %constant_dynamic-update-slice_fusion.2.refs_11_), channel_id=1, source_target_pairs={{0,1},{1,2},{2,3},{3,0},{4,5},{5,6},{6,7},{7,4},{8,9},{9,10},{10,1... | collective-permute-start | bytes 1216520 | tf_op jit(solution)/shard_map/ppermute | solution.py:34
  148.6 2.2 %collective-permute-start.13 = (bf16[528,384]{1,0:T(8,128)(2,1)}, bf16[528,384]{1,0:T(8,128)(2,1)}, u32[]{:S(2)}, u32[]{:S(2)}) collective-permute-start(bf16[528,384]{1,0:T(8,128)(2,1)} %constant_dynamic-update-slice_fusion.2.refs_11_), channel_id=1, source_target_pairs={{0,3},{1,0},{2,1},{3,2},{4,7},{5,4},{6,5},{7,6},{8,11},{9,8},{10,9... | collective-permute-start | bytes 1216520 | tf_op jit(solution)/shard_map/ppermute | solution.py:35
  150.9 0.7 slice.37
  151.6 2.6 %collective-permute-start.3 = (bf16[256,384]{1,0:T(8,128)(2,1)}, bf16[256,384]{1,0:T(8,128)(2,1)}, u32[]{:S(2)}, u32[]{:S(2)}) collective-permute-start(bf16[256,384]{1,0:T(8,128)(2,1)} %slice.37), channel_id=1, source_target_pairs={{0,3},{1,0},{2,1},{3,2},{4,7},{5,4},{6,5},{7,6},{8,11},{9,8},{10,9... | collective-permute-start | bytes 589832 | tf_op jit(solution)/shard_map/ppermute | solution.py:37
  154.2 0.8 slice.38
  155.0 4.4 %collective-permute-start.8 = (bf16[528,384]{1,0:T(8,128)(2,1)}, bf16[528,384]{1,0:T(8,128)(2,1)}, u32[]{:S(2)}, u32[]{:S(2)}) collective-permute-start(bf16[528,384]{1,0:T(8,128)(2,1)} %slice.38), channel_id=1, source_target_pairs={{0,1},{1,2},{2,3},{3,0},{4,5},{5,6},{6,7},{7,4},{8,9},{9,10},{10,1... | collective-permute-start | bytes 1216520 | tf_op jit(solution)/shard_map/ppermute | solution.py:36
  159.4 0.8 slice.39
  160.2 0.7 copy-done.5
  161.0 1.9 collective-permute-start.9
  162.9 0.9 copy.14.refs_17_
  163.8 1.0 slice.36
  164.8 5.1 %collective-permute-start.2 = (bf16[272,384]{1,0:T(8,128)(2,1)S(1)}, bf16[272,384]{1,0:T(8,128)(2,1)S(1)}, u32[]{:S(2)}, u32[]{:S(2)}) collective-permute-start(bf16[272,384]{1,0:T(8,128)(2,1)S(1)} %slice.36), channel_id=1, source_target_pairs={{0,1},{1,2},{2,3},{3,0},{4,5},{5,6},{6,7},{7,4},{8,9},{9,10},{10,1... | collective-permute-start | bytes 626696 | tf_op jit(solution)/shard_map/ppermute | solution.py:36
  169.9 1.0 slice.42
  170.9 2.4 %collective-permute-start.14 = (bf16[272,384]{1,0:T(8,128)(2,1)S(1)}, bf16[272,384]{1,0:T(8,128)(2,1)}, u32[]{:S(2)}, u32[]{:S(2)}) collective-permute-start(bf16[272,384]{1,0:T(8,128)(2,1)S(1)} %slice.42), channel_id=1, source_target_pairs={{0,1},{1,2},{2,3},{3,0},{4,5},{5,6},{6,7},{7,4},{8,9},{9,10},{10,1... | collective-permute-start | bytes 626696 | tf_op jit(solution)/shard_map/ppermute | solution.py:36
  173.3 0.9 slice.43
  174.3 3.4 %collective-permute-start.15 = (bf16[256,384]{1,0:T(8,128)(2,1)S(1)}, bf16[256,384]{1,0:T(8,128)(2,1)S(1)}, u32[]{:S(2)}, u32[]{:S(2)}) collective-permute-start(bf16[256,384]{1,0:T(8,128)(2,1)S(1)} %slice.43), channel_id=1, source_target_pairs={{0,3},{1,0},{2,1},{3,2},{4,7},{5,4},{6,5},{7,6},{8,11},{9,8},{10,9... | collective-permute-start | bytes 589832 | tf_op jit(solution)/shard_map/ppermute | solution.py:37
  177.7 0.6 fusion.refs_0_
  178.3 4.7 %collective-permute-done.15.refs_15_ = bf16[256,384]{1,0:T(8,128)(2,1)S(1)} collective-permute-done((bf16[256,384]{1,0:T(8,128)(2,1)S(1)}, bf16[256,384]{1,0:T(8,128)(2,1)S(1)}, u32[]{:S(2)}, u32[]{:S(2)}) %collective-permute-start.15) | collective-permute-done | bytes 196640 | tf_op jit(solution)/shard_map/ppermute | solution.py:37
  183.0 0.7 copy-done.8
  183.8 23.5 %norm_project_attend.1 = bf16[512,256]{1,0:T(8,128)(2,1)} custom-call(s32[16]{0:T(128)} %fusion.refs_0_, bf16[528,384]{1,0:T(8,128)(2,1)} %copy-done.4, bf16[528,384]{1,0:T(8,128)(2,1)} %copy-done.5, bf16[528,384]{1,0:T(8,128)(2,1)} %copy-done.6, bf16[272,384]{1,0:T(8,128)(2,1)} %copy-done.7, bf16[256,384]{1,0:T(8,128)(2,1)} %collective-permute-done.3.refs_5_, ...), custom_call_target="tpu_custom_call" | custom-call | tf_op jit(solution)/shard_map/norm_project_attend/pallas_call | solution.py:179
  (52 shorter events, 0.5 us)
Async XLA Ops:
  6.5 2.7 %copy-start = (bf16[1024,384]{1,0:T(8,128)(2,1)S(1)}, bf16[1024,384]{1,0:T(8,128)(2,1)}, u32[]{:S(2)}) copy-start(bf16[1024,384]{1,0:T(8,128)(2,1)} %param.9) | copy-start | bytes 2359300
  6.5 171.2 %copy-start.11 = (s32[16]{0:T(128)S(1)}, s32[16]{0:T(128)}, u32[]{:S(2)}) copy-start(s32[16]{0:T(128)} %constant.94.clone) | copy-start | bytes 196
  6.5 171.2 %copy-start.12 = (s32[16]{0:T(128)S(1)}, s32[16]{0:T(128)}, u32[]{:S(2)}) copy-start(s32[16]{0:T(128)} %constant.93.clone) | copy-start | bytes 196
  6.5 37.8 %copy-start.10 = (bf16[384]{0:T(512)(128)(2,1)S(1)}, bf16[384]{0:T(512)(128)(2,1)}, u32[]{:S(2)}) copy-start(bf16[384]{0:T(512)(128)(2,1)} %param.10) | copy-start | bytes 2308
  6.5 177.2 %all-gather.2.cloned.1.call-start = ((), (), s32[]{:S(2)}) async-start(), calls=%async_computation.1 | async-start | bytes 9732096 | tf_op jit(solution)/shard_map/all_gather | solution.py:118
  11.0 31.3 %all-to-all-start = ((bf16[32,32,384]{2,1,0:T(8,128)(2,1)}), bf16[32,32,384]{2,1,0:T(8,128)(2,1)S(1)}, u32[]{:S(2)}, u32[]{:S(2)}) async-start(bf16[32,32,384]{2,1,0:T(8,128)(2,1)} %broadcast_select_fusion), calls=%async_computation | async-start | bytes 1572864 | tf_op jit(solution)/shard_map/all_to_all | solution.py:128
  20.7 163.0 %copy-start.9 = (s32[512]{0:T(512)}, s32[512]{0:T(512)S(1)}, u32[]{:S(2)}) copy-start(s32[512]{0:T(512)S(1)} %convert_reduce_fusion) | copy-start | bytes 6148
  44.4 110.6 %copy-start.4 = (bf16[528,384]{1,0:T(8,128)(2,1)}, bf16[528,384]{1,0:T(8,128)(2,1)S(1)}, u32[]{:S(2)}) copy-start(bf16[528,384]{1,0:T(8,128)(2,1)S(1)} %pad_maximum_fusion.refs_1_) | copy-start | bytes 1216516
  44.4 55.0 %collective-permute-start.4 = (bf16[528,384]{1,0:T(8,128)(2,1)S(1)}, bf16[528,384]{1,0:T(8,128)(2,1)S(1)}, u32[]{:S(2)}, u32[]{:S(2)}) collective-permute-start(bf16[528,384]{1,0:T(8,128)(2,1)S(1)} %pad_maximum_fusion.refs_1_), channel_id=1, source_target_pairs={{0,4},{1,5},{2,6},{3,7},{4,8},{5,9},{6,10},{7,11},{8,12},{9,13},{1... | collective-permute-start | bytes 1216520 | tf_op jit(solution)/shard_map/ppermute | solution.py:34
  53.9 52.9 %collective-permute-start.5 = (bf16[528,384]{1,0:T(8,128)(2,1)S(1)}, bf16[528,384]{1,0:T(8,128)(2,1)S(1)}, u32[]{:S(2)}, u32[]{:S(2)}) collective-permute-start(bf16[528,384]{1,0:T(8,128)(2,1)S(1)} %pad_maximum_fusion.refs_1_), channel_id=1, source_target_pairs={{0,12},{1,13},{2,14},{3,15},{4,0},{5,1},{6,2},{7,3},{8,4},{9,5},{1... | collective-permute-start | bytes 1216520 | tf_op jit(solution)/shard_map/ppermute | solution.py:35
  106.9 76.9 %copy-start.3 = (bf16[1056,384]{1,0:T(8,128)(2,1)}, bf16[1056,384]{1,0:T(8,128)(2,1)S(1)}, u32[]{:S(2)}) copy-start(bf16[1056,384]{1,0:T(8,128)(2,1)S(1)} %constant_dynamic-update-slice_fusion.refs_6_) | copy-start | bytes 2433028
  106.9 44.7 %collective-permute-start.6 = (bf16[1056,384]{1,0:T(8,128)(2,1)S(1)}, bf16[1056,384]{1,0:T(8,128)(2,1)S(1)}, u32[]{:S(2)}, u32[]{:S(2)}) collective-permute-start(bf16[1056,384]{1,0:T(8,128)(2,1)S(1)} %constant_dynamic-update-slice_fusion.refs_6_), channel_id=1, source_target_pairs={{0,1},{1,2},{2,3},{3,0},{4,5},{5,6},{6,7},{7,4},{8,9},{9,10},{10,1... | collective-permute-start | bytes 2433032 | tf_op jit(solution)/shard_map/ppermute | solution.py:34
  108.8 46.2 %collective-permute-start.7 = (bf16[1056,384]{1,0:T(8,128)(2,1)S(1)}, bf16[1056,384]{1,0:T(8,128)(2,1)S(1)}, u32[]{:S(2)}, u32[]{:S(2)}) collective-permute-start(bf16[1056,384]{1,0:T(8,128)(2,1)S(1)} %constant_dynamic-update-slice_fusion.refs_6_), channel_id=1, source_target_pairs={{0,3},{1,0},{2,1},{3,2},{4,7},{5,4},{6,5},{7,6},{8,11},{9,8},{10,9... | collective-permute-start | bytes 2433032 | tf_op jit(solution)/shard_map/ppermute | solution.py:35
  112.8 21.5 %collective-permute-start.10 = (bf16[272,384]{1,0:T(8,128)(2,1)S(1)}, bf16[272,384]{1,0:T(8,128)(2,1)S(1)}, u32[]{:S(2)}, u32[]{:S(2)}) collective-permute-start(bf16[272,384]{1,0:T(8,128)(2,1)S(1)} %slice.40), channel_id=1, source_target_pairs={{0,4},{1,5},{2,6},{3,7},{4,8},{5,9},{6,10},{7,11},{8,12},{9,13},{1... | collective-permute-start | bytes 626696 | tf_op jit(solution)/shard_map/ppermute | solution.py:36
  119.2 29.4 %collective-permute-start.1 = (bf16[528,384]{1,0:T(8,128)(2,1)S(1)}, bf16[528,384]{1,0:T(8,128)(2,1)S(1)}, u32[]{:S(2)}, u32[]{:S(2)}) collective-permute-start(bf16[528,384]{1,0:T(8,128)(2,1)S(1)} %pad_maximum_fusion.refs_1_), channel_id=1, source_target_pairs={{0,3},{1,0},{2,1},{3,2},{4,7},{5,4},{6,5},{7,6},{8,11},{9,8},{10,9... | collective-permute-start | bytes 1216520 | tf_op jit(solution)/shard_map/ppermute | solution.py:35
  121.5 22.8 %collective-permute-start.11 = (bf16[256,384]{1,0:T(8,128)(2,1)S(1)}, bf16[256,384]{1,0:T(8,128)(2,1)S(1)}, u32[]{:S(2)}, u32[]{:S(2)}) collective-permute-start(bf16[256,384]{1,0:T(8,128)(2,1)S(1)} %slice.41), channel_id=1, source_target_pairs={{0,12},{1,13},{2,14},{3,15},{4,0},{5,1},{6,2},{7,3},{8,4},{9,5},{1... | collective-permute-start | bytes 589832 | tf_op jit(solution)/shard_map/ppermute | solution.py:37
  134.2 26.0 %collective-permute-start = (bf16[528,384]{1,0:T(8,128)(2,1)S(1)}, bf16[528,384]{1,0:T(8,128)(2,1)S(1)}, u32[]{:S(2)}, u32[]{:S(2)}) collective-permute-start(bf16[528,384]{1,0:T(8,128)(2,1)S(1)} %pad_maximum_fusion.refs_1_), channel_id=1, source_target_pairs={{0,1},{1,2},{2,3},{3,0},{4,5},{5,6},{6,7},{7,4},{8,9},{9,10},{10,1... | collective-permute-start | bytes 1216520 | tf_op jit(solution)/shard_map/ppermute | solution.py:34
  145.0 19.8 %collective-permute-start.12 = (bf16[528,384]{1,0:T(8,128)(2,1)}, bf16[528,384]{1,0:T(8,128)(2,1)}, u32[]{:S(2)}, u32[]{:S(2)}) collective-permute-start(bf16[528,384]{1,0:T(8,128)(2,1)} %constant_dynamic-update-slice_fusion.2.refs_11_), channel_id=1, source_target_pairs={{0,1},{1,2},{2,3},{3,0},{4,5},{5,6},{6,7},{7,4},{8,9},{9,10},{10,1... | collective-permute-start | bytes 1216520 | tf_op jit(solution)/shard_map/ppermute | solution.py:34
  148.6 11.6 %copy-start.6 = (bf16[528,384]{1,0:T(8,128)(2,1)}, bf16[528,384]{1,0:T(8,128)(2,1)S(1)}, u32[]{:S(2)}) copy-start(bf16[528,384]{1,0:T(8,128)(2,1)S(1)} %collective-permute-done.1.refs_3_) | copy-start | bytes 1216516
  148.6 22.2 %collective-permute-start.13 = (bf16[528,384]{1,0:T(8,128)(2,1)}, bf16[528,384]{1,0:T(8,128)(2,1)}, u32[]{:S(2)}, u32[]{:S(2)}) collective-permute-start(bf16[528,384]{1,0:T(8,128)(2,1)} %constant_dynamic-update-slice_fusion.2.refs_11_), channel_id=1, source_target_pairs={{0,3},{1,0},{2,1},{3,2},{4,7},{5,4},{6,5},{7,6},{8,11},{9,8},{10,9... | collective-permute-start | bytes 1216520 | tf_op jit(solution)/shard_map/ppermute | solution.py:35
  151.6 32.2 %copy-start.1 = (bf16[1056,384]{1,0:T(8,128)(2,1)}, bf16[1056,384]{1,0:T(8,128)(2,1)S(1)}, u32[]{:S(2)}) copy-start(bf16[1056,384]{1,0:T(8,128)(2,1)S(1)} %collective-permute-done.6.refs_7_) | copy-start | bytes 2433028
  151.6 22.7 %collective-permute-start.3 = (bf16[256,384]{1,0:T(8,128)(2,1)}, bf16[256,384]{1,0:T(8,128)(2,1)}, u32[]{:S(2)}, u32[]{:S(2)}) collective-permute-start(bf16[256,384]{1,0:T(8,128)(2,1)} %slice.37), channel_id=1, source_target_pairs={{0,3},{1,0},{2,1},{3,2},{4,7},{5,4},{6,5},{7,6},{8,11},{9,8},{10,9... | collective-permute-start | bytes 589832 | tf_op jit(solution)/shard_map/ppermute | solution.py:37
  155.0 28.7 %copy-start.2 = (bf16[1056,384]{1,0:T(8,128)(2,1)}, bf16[1056,384]{1,0:T(8,128)(2,1)S(1)}, u32[]{:S(2)}) copy-start(bf16[1056,384]{1,0:T(8,128)(2,1)S(1)} %collective-permute-done.7.refs_8_) | copy-start | bytes 2433028
  155.0 28.7 %collective-permute-start.8 = (bf16[528,384]{1,0:T(8,128)(2,1)}, bf16[528,384]{1,0:T(8,128)(2,1)}, u32[]{:S(2)}, u32[]{:S(2)}) collective-permute-start(bf16[528,384]{1,0:T(8,128)(2,1)} %slice.38), channel_id=1, source_target_pairs={{0,1},{1,2},{2,3},{3,0},{4,5},{5,6},{6,7},{7,4},{8,9},{9,10},{10,1... | collective-permute-start | bytes 1216520 | tf_op jit(solution)/shard_map/ppermute | solution.py:36
  160.2 0.7 copy-start.5
  161.0 22.7 %collective-permute-start.9 = (bf16[528,384]{1,0:T(8,128)(2,1)}, bf16[528,384]{1,0:T(8,128)(2,1)}, u32[]{:S(2)}, u32[]{:S(2)}) collective-permute-start(bf16[528,384]{1,0:T(8,128)(2,1)} %slice.39), channel_id=1, source_target_pairs={{0,3},{1,0},{2,1},{3,2},{4,7},{5,4},{6,5},{7,6},{8,11},{9,8},{10,9... | collective-permute-start | bytes 1216520 | tf_op jit(solution)/shard_map/ppermute | solution.py:37
  164.8 13.6 %collective-permute-start.2 = (bf16[272,384]{1,0:T(8,128)(2,1)S(1)}, bf16[272,384]{1,0:T(8,128)(2,1)S(1)}, u32[]{:S(2)}, u32[]{:S(2)}) collective-permute-start(bf16[272,384]{1,0:T(8,128)(2,1)S(1)} %slice.36), channel_id=1, source_target_pairs={{0,1},{1,2},{2,3},{3,0},{4,5},{5,6},{6,7},{7,4},{8,9},{9,10},{10,1... | collective-permute-start | bytes 626696 | tf_op jit(solution)/shard_map/ppermute | solution.py:36
  170.9 12.2 %collective-permute-start.14 = (bf16[272,384]{1,0:T(8,128)(2,1)S(1)}, bf16[272,384]{1,0:T(8,128)(2,1)}, u32[]{:S(2)}, u32[]{:S(2)}) collective-permute-start(bf16[272,384]{1,0:T(8,128)(2,1)S(1)} %slice.42), channel_id=1, source_target_pairs={{0,1},{1,2},{2,3},{3,0},{4,5},{5,6},{6,7},{7,4},{8,9},{9,10},{10,1... | collective-permute-start | bytes 626696 | tf_op jit(solution)/shard_map/ppermute | solution.py:36
  174.3 8.8 %collective-permute-start.15 = (bf16[256,384]{1,0:T(8,128)(2,1)S(1)}, bf16[256,384]{1,0:T(8,128)(2,1)S(1)}, u32[]{:S(2)}, u32[]{:S(2)}) collective-permute-start(bf16[256,384]{1,0:T(8,128)(2,1)S(1)} %slice.43), channel_id=1, source_target_pairs={{0,3},{1,0},{2,1},{3,2},{4,7},{5,4},{6,5},{7,6},{8,11},{9,8},{10,9... | collective-permute-start | bytes 589832 | tf_op jit(solution)/shard_map/ppermute | solution.py:37
  178.3 5.5 %copy-start.7 = (bf16[272,384]{1,0:T(8,128)(2,1)}, bf16[272,384]{1,0:T(8,128)(2,1)S(1)}, u32[]{:S(2)}) copy-start(bf16[272,384]{1,0:T(8,128)(2,1)S(1)} %collective-permute-done.2.refs_4_) | copy-start | bytes 626692
  183.0 0.7 copy-start.8
Sparse Core Ops, SparseCore 0:
  9.5 135.3 all-gather.1

commit v2 on v1

--- a/solution.py
+++ b/solution.py
@@ -30,25 +30,41 @@
     ]
 
 
-def both_ways(block, shift, cut):
-    up = lax.ppermute(block, "tensor", shift(1))
-    down = lax.ppermute(block, "tensor", shift(-1))
-    far_top = lax.ppermute(up[:cut], "tensor", shift(1))
-    far_rest = lax.ppermute(down[cut:], "tensor", shift(-1))
-    return up, down, far_top, far_rest
-
-
-def attend_kernel(slots, count, rows, cut, *refs):
-    places_ref, blocks = refs[0], refs[1 : 1 + count]
-    weight_ref, seg_col_ref, seg_row_ref, out_ref, normed_ref = refs[1 + count :]
+def dp_move(x_step, z_step, core_step):
+    pairs = []
+    for x in range(4):
+        for z in range(4):
+            for core in range(2):
+                to = (x + x_step) % 4 * 8 + (z + z_step) % 4 * 2 + (core + core_step) % 2
+                pairs.append((x * 8 + z * 2 + core, to))
+    return pairs
+
+
+def attend_kernel(slots, count, rows, cut, strip, *refs):
+    places_ref, strips_ref, blocks = refs[0], refs[1], refs[2 : 2 + count]
+    held_ref, swapped_ref, seg_col_ref, seg_row_ref, out_ref = refs[2 + count : 7 + count]
+    normed_ref, weight_ref, weight_sem = refs[7 + count :]
     features = normed_ref.shape[1]
     width = blocks[0].shape[1]
+    copies = []
+    for source, ref in enumerate((held_ref, swapped_ref)):
+        for k in range(ref.shape[0] // strip):
+            at = pl.multiple_of(strips_ref[source * (ref.shape[0] // strip) + k] * strip, 16)
+            copies.append(
+                pltpu.make_async_copy(
+                    ref.at[pl.ds(k * strip, strip), :],
+                    weight_ref.at[pl.ds(at, strip), :],
+                    weight_sem,
+                )
+            )
+    for copy in copies:
+        copy.start()
+
 
     def part(pieces, row):
-        for ref_index, ref_row, first, last in pieces:
+        for ref, start, first, last in pieces:
             if first <= row < last:
-                return blocks[ref_index], ref_row - first
-        return None
+                return blocks[ref], start - first
 
     gains = []
     for pieces in slots:
@@ -60,11 +76,11 @@
         sources = [part(pieces, first) for pieces in slots]
 
         def step(i, carry):
-            row = first + i * ROW_TILE
+            at = pl.multiple_of(first + i * ROW_TILE, ROW_TILE)
+
             def load(j):
                 ref, shift = sources[j]
-                at = pl.multiple_of(row + shift, ROW_TILE)
-                return ref[pl.ds(at, ROW_TILE), :].astype(jnp.float32)
+                return ref[pl.ds(at + shift, ROW_TILE), :].astype(jnp.float32)
 
             total = load(0)
             for j in range(1, len(slots)):
@@ -75,7 +91,6 @@
                 square = square + jnp.square(load(j) - mean)
             var = jnp.sum(square, axis=1, keepdims=True) * (1.0 / features)
             scale = lax.rsqrt(var + NORM_EPSILON)
-            at = pl.multiple_of(row, ROW_TILE)
             for j in range(len(slots)):
                 normed_ref[pl.ds(at, ROW_TILE), columns[j]] = (
                     (load(j) - mean) * scale * gains[j]
@@ -83,7 +98,8 @@
             return carry
 
         lax.fori_loop(0, (last - first) // ROW_TILE, step, 0)
-
+    for copy in copies:
+        copy.wait()
     local = out_ref.shape[1]
     sums = jnp.dot(normed_ref[...], weight_ref[...], preferred_element_type=jnp.float32)
     sums = sums.astype(jnp.bfloat16)
@@ -115,9 +131,9 @@
     slot_rows = page_patches.shape[0] // groups
     rows = slot_rows * groups // 2
     local = q_weight.shape[1]
-    weights = lax.all_gather(
-        jnp.concatenate([q_weight, k_weight, v_weight], axis=1), "dp", axis=0, tiled=True
-    )
+    strip = q_weight.shape[0]
+    weight = jnp.concatenate([q_weight, k_weight, v_weight], axis=1)
+    column = [lax.ppermute(weight, "dp", dp_move(0, k, 0)) for k in (1, 2, 3)]
     targets = jnp.arange(groups, dtype=jnp.int32)
     my_order = lax.dynamic_index_in_dim(line_order, page_index, 0, keepdims=False)
     slot_for = jnp.sum(
@@ -126,6 +142,8 @@
     slots = page_patches.reshape(groups, slot_rows, width)
     outgoing = jnp.take(slots, slot_for, axis=0)
     incoming = lax.all_to_all(outgoing, "dp", split_axis=0, concat_axis=0, tiled=True)
+    incoming, *column = lax.optimization_barrier((incoming, *column))
+    column = jnp.concatenate([weight] + column, axis=0)
     my_lengths = lax.dynamic_index_in_dim(pack_lengths, page_index, 0, keepdims=False)
     line_ends = jnp.cumsum(my_lengths)
     line_starts = line_ends - my_lengths
@@ -140,50 +158,83 @@
     own = jnp.concatenate([packed, jnp.broadcast_to(gain[None, :], (GAIN_ROWS, width))], axis=0)
     all_rows = rows + GAIN_ROWS
     cut = rows // 2 + GAIN_ROWS
-    z_up, z_down, z_far_top, z_far_rest = both_ways(own, z_shift, cut)
+    z_up, z_down = (lax.ppermute(own, "tensor", z_shift(k)) for k in (1, -1))
+    x_up, x_down = (lax.ppermute(column, "dp", dp_move(k, 0, 0)) for k in (1, 3))
+    own_up = lax.ppermute(own, "tensor", y_shift(1))
+    own_up, own_again = lax.optimization_barrier((own_up, own))
+    own_down = lax.ppermute(own_again, "tensor", y_shift(-1))
+    z_up, z_down, own_up, own_down, x_up, x_down = lax.optimization_barrier(
+        (z_up, z_down, own_up, own_down, x_up, x_down)
+    )
+    z_far = [
+        lax.ppermute(z_up[:cut], "tensor", z_shift(1)),
+        lax.ppermute(z_down[cut:], "tensor", z_shift(-1)),
+    ]
     pair = jnp.concatenate([z_up, z_down], axis=0)
-    far = jnp.concatenate([z_far_top, z_far_rest], axis=0)
-    blocks, slot_list, shifts = [], [], []
-
-    def add(array):
-        blocks.append(array)
-        return len(blocks) - 1
-
-    def slot(dz, dy, *pieces):
-        slot_list.append(pieces)
-        shifts.append((dz, dy))
-
-    for array, dzs in ((own, (0,)), (pair, (-1, 1)), (far, (2,))):
-        half = cut if len(dzs) == 1 else all_rows
-        up, down, far_top, far_rest = both_ways(array, y_shift, half)
-        for dy, source in ((0, array), (-1, up), (1, down)):
-            ref = add(source)
-            for k, dz in enumerate(dzs):
-                slot(dz, dy, (ref, k * all_rows, 0, all_rows))
-        top, rest = add(far_top), add(far_rest)
-        if len(dzs) == 1:
-            slot(dzs[0], 2, (top, 0, 0, cut), (rest, 0, cut, all_rows))
-        else:
-            slot(dzs[0], 2, (top, 0, 0, all_rows))
-            slot(dzs[1], 2, (rest, 0, 0, all_rows))
+    pair_up, pair_down = (lax.ppermute(pair, "tensor", y_shift(k)) for k in (1, -1))
+    x_far = lax.ppermute(column, "dp", dp_move(2, 0, 0))
+    *z_far, pair_up, pair_down, x_far = lax.optimization_barrier(
+        (*z_far, pair_up, pair_down, x_far)
+    )
+    far = jnp.concatenate(z_far, axis=0)
+    far_y = [lax.ppermute(far, "tensor", y_shift(k)) for k in (1, -1, 2)]
+    far_up = jnp.concatenate([pair_up[:all_rows], own_up[:cut]], axis=0)
+    far_down = jnp.concatenate([pair_down[all_rows:], own_down[cut:]], axis=0)
+    far_up = lax.ppermute(far_up, "tensor", y_shift(1))
+    far_down = lax.ppermute(far_down, "tensor", y_shift(-1))
+    held = jnp.concatenate([column, x_up, x_far, x_down], axis=0)
+    swapped = lax.ppermute(held, "dp", dp_move(0, 0, 1))
+
+    blocks = [own, own_up, own_down, pair, pair_up, pair_down, far_up, far_down, far, *far_y]
+    whole = lambda ref, row: ((ref, row, 0, all_rows),)
+    slots_at = [
+        ((0, 0), whole(0, 0)),
+        ((0, -1), whole(1, 0)),
+        ((0, 1), whole(2, 0)),
+        ((0, 2), ((6, all_rows, 0, cut), (7, all_rows, cut, all_rows))),
+        ((-1, 0), whole(3, 0)),
+        ((1, 0), whole(3, all_rows)),
+        ((-1, -1), whole(4, 0)),
+        ((1, -1), whole(4, all_rows)),
+        ((-1, 1), whole(5, 0)),
+        ((1, 1), whole(5, all_rows)),
+        ((-1, 2), whole(6, 0)),
+        ((1, 2), whole(7, 0)),
+        ((2, 0), whole(8, 0)),
+        ((2, -1), whole(9, 0)),
+        ((2, 1), whole(10, 0)),
+        ((2, 2), whole(11, 0)),
+    ]
+    shifts, slots_at = zip(*slots_at)
     tensor = lax.axis_index("tensor")
     my_z, my_y = tensor // Y_PARTS, tensor % Y_PARTS
     step_z = jnp.array([dz for dz, _ in shifts], jnp.int32)
     step_y = jnp.array([dy for _, dy in shifts], jnp.int32)
     places = (my_z + step_z + Z_PARTS) % Z_PARTS * Y_PARTS + (my_y + step_y + Y_PARTS) % Y_PARTS
 
+    my_x, my_lo, my_core = page_index // 8, page_index // 2 % 4, page_index % 2
+    k = jnp.arange(groups, dtype=jnp.int32)
+    step_core, step_x, step_lo = k // 16, k // 4 % 4, k % 4
+    strips = (my_x - step_x + 4) % 4 * 8 + (my_lo - step_lo + 4) % 4 * 2 + (my_core + step_core) % 2
+
     def kernel(*refs):
-        attend_kernel(slot_list, len(blocks), rows, cut, *refs)
-
+        attend_kernel(slots_at, len(blocks), rows, cut, strip, *refs)
+
+    features = width * len(slots_at)
     vmem = pl.BlockSpec(memory_space=pltpu.VMEM)
+    smem, hbm = pl.BlockSpec(memory_space=pltpu.SMEM), pl.BlockSpec(memory_space=pl.ANY)
     return pl.pallas_call(
         kernel,
         out_shape=jax.ShapeDtypeStruct((rows, local), jnp.bfloat16),
-        in_specs=[pl.BlockSpec(memory_space=pltpu.SMEM)] + [vmem] * (len(blocks) + 3),
+        in_specs=[smem, smem] + [vmem] * len(blocks) + [hbm, hbm, vmem, vmem],
         out_specs=vmem,
-        scratch_shapes=[pltpu.VMEM((rows, width * len(slot_list)), jnp.bfloat16)],
+        scratch_shapes=[
+            pltpu.VMEM((rows, features), jnp.bfloat16),
+            pltpu.VMEM((features, 3 * local), jnp.bfloat16),
+            pltpu.SemaphoreType.DMA,
+        ],
         name="norm_project_attend",
-    )(places, *blocks, weights, segment[:, None], segment[None, :])
+    )(places, strips, *blocks, held, swapped, segment[:, None], segment[None, :])
 
 
 def solution(mesh):

time: 215 us -> 214 us (level)
  the two profiles are of different devices: /device:TPU:56 before, /device:TPU:1 now
where the time goes in v2:
time: 214 us; the launch traced here: 211 us
  waiting for transfers between devices  85.1 us (40%)
  starting transfers between devices  82.4 us (39%)
  Pallas kernels  20.9 us (10%)
  local copies, waits for them, and re-layouts  16.9 us (8%)
  other arithmetic  5.54 us (3%)
    ppermute x3, waiting for transfers between devices, shards(): column = [lax.ppermute(weight, 'dp', dp_move(0, k, 0)) for k in (1, 2, 3)]  33.8 us
    ppermute x2, waiting for transfers between devices, shards(): z_up, z_down = (lax.ppermute(own, 'tensor', z_shift(k)) for k in (1, -1))  24.8 us
    pallas_call x1, Pallas kernels, shards(): pl.pallas_call(kernel, out_shape=jax.ShapeDtypeStruct((rows, local), jnp....  20.9 us
    ppermute x3, waiting for transfers between devices, shards(): far_y = [lax.ppermute(far, 'tensor', y_shift(k)) for k in (1, -1, 2)]  17.6 us
    ppermute x2, starting transfers between devices, shards(): z_up, z_down = (lax.ppermute(own, 'tensor', z_shift(k)) for k in (1, -1))  11.7 us
    all_to_all x1, starting transfers between devices, shards(): lax.all_to_all(outgoing, 'dp', split_axis=0, concat_axis=0, tiled=True)  10.6 us
    ppermute x3, starting transfers between devices, shards(): far_y = [lax.ppermute(far, 'tensor', y_shift(k)) for k in (1, -1, 2)]  9.66 us
    ppermute x3, starting transfers between devices, shards(): column = [lax.ppermute(weight, 'dp', dp_move(0, k, 0)) for k in (1, 2, 3)]  9.48 us
  transfers between devices with their start and end apart: 21, of which 8 were waited for; matrix products, arithmetic and copies ran while one was open for 6% of the time, Pallas kernels for 0%

profile of v2, /device:TPU:1, one launch (start us, length us, event | category | flops | bytes accessed | tf_op | source)
XLA Modules:
  0.0 211.4 jit_solution(7977557484182182934)
XLA Ops:
  0.0 0.8 dynamic-slice_bitcast_fusion
  0.9 0.7 fusion.19
  1.9 0.7 fusion.18
  2.8 0.7 gather_fusion
  3.5 1.1 broadcast_select_fusion
  4.6 10.6 %all-to-all-start = ((bf16[32,32,384]{2,1,0:T(8,128)(2,1)}), bf16[32,32,384]{2,1,0:T(8,128)(2,1)S(1)}, u32[]{:S(2)}, u32[]{:S(2)}) async-start(bf16[32,32,384]{2,1,0:T(8,128)(2,1)} %broadcast_select_fusion), calls=%async_computation | async-start | bytes 1572864 | tf_op jit(solution)/shard_map/all_to_all | solution.py:144
  15.2 0.7 constant_dynamic-update-slice_fusion.15
  15.9 0.7 constant_dynamic-update-slice_fusion.14
  16.5 0.7 constant_dynamic-update-slice_fusion.13
  17.2 5.1 %collective-permute-start.2 = (bf16[192,768]{1,0:T(8,128)(2,1)S(1)}, bf16[192,768]{1,0:T(8,128)(2,1)S(1)}, u32[]{:S(2)}, u32[]{:S(2)}) collective-permute-start(bf16[192,768]{1,0:T(8,128)(2,1)S(1)} %get-tuple-element.40), channel_id=1, source_target_pairs={{0,96},{16,112},{32,0},{48,16},{64,32},{80,48},{96,64},{112,80},{1... | collective-permute-start | bytes 884744 | tf_op jit(solution)/shard_map/ppermute | solution.py:136
  22.3 1.9 collective-permute-start.1
  24.3 2.4 %collective-permute-start = (bf16[192,768]{1,0:T(8,128)(2,1)S(1)}, bf16[192,768]{1,0:T(8,128)(2,1)S(1)}, u32[]{:S(2)}, u32[]{:S(2)}) collective-permute-start(bf16[192,768]{1,0:T(8,128)(2,1)S(1)} %get-tuple-element.40), channel_id=1, source_target_pairs={{0,32},{16,48},{32,64},{48,80},{64,96},{80,112},{96,0},{112,16},{1... | collective-permute-start | bytes 884744 | tf_op jit(solution)/shard_map/ppermute | solution.py:136
  26.7 9.7 %collective-permute-done.2 = bf16[192,768]{1,0:T(8,128)(2,1)S(1)} collective-permute-done((bf16[192,768]{1,0:T(8,128)(2,1)S(1)}, bf16[192,768]{1,0:T(8,128)(2,1)S(1)}, u32[]{:S(2)}, u32[]{:S(2)}) %collective-permute-start.2) | collective-permute-done | bytes 294944 | tf_op jit(solution)/shard_map/ppermute | solution.py:136
  36.4 24.1 %collective-permute-done.1 = bf16[192,768]{1,0:T(8,128)(2,1)S(1)} collective-permute-done((bf16[192,768]{1,0:T(8,128)(2,1)S(1)}, bf16[192,768]{1,0:T(8,128)(2,1)S(1)}, u32[]{:S(2)}, u32[]{:S(2)}) %collective-permute-start.1) | collective-permute-done | bytes 294944 | tf_op jit(solution)/shard_map/ppermute | solution.py:136
  60.5 1.1 pad_maximum_fusion
  61.6 4.5 %collective-permute-start.8 = (bf16[768,768]{1,0:T(8,128)(2,1)}, bf16[768,768]{1,0:T(8,128)(2,1)}, u32[]{:S(2)}, u32[]{:S(2)}) collective-permute-start(bf16[768,768]{1,0:T(8,128)(2,1)} %pad_maximum_fusion), channel_id=1, source_target_pairs={{0,384},{16,400},{32,416},{48,432},{64,448},{80,464},{96,480},{112... | collective-permute-start | bytes 3538952 | tf_op jit(solution)/shard_map/ppermute | solution.py:162
  66.0 1.9 collective-permute-start.7
  68.0 1.9 gather_fusion.1
  70.2 2.7 %collective-permute-start.5 = (bf16[528,384]{1,0:T(8,128)(2,1)S(1)}, bf16[528,384]{1,0:T(8,128)(2,1)S(1)}, u32[]{:S(2)}, u32[]{:S(2)}) collective-permute-start(bf16[528,384]{1,0:T(8,128)(2,1)S(1)} %pad_maximum_fusion.3.refs_2_), channel_id=1, source_target_pairs={{0,1},{1,2},{2,3},{3,0},{4,5},{5,6},{6,7},{7,4},{8,9},{9,10},{10,1... | collective-permute-start | bytes 1216520 | tf_op jit(solution)/shard_map/ppermute | solution.py:163
  72.8 9.8 %collective-permute-start.4 = (bf16[528,384]{1,0:T(8,128)(2,1)S(1)}, bf16[528,384]{1,0:T(8,128)(2,1)S(1)}, u32[]{:S(2)}, u32[]{:S(2)}) collective-permute-start(bf16[528,384]{1,0:T(8,128)(2,1)S(1)} %pad_maximum_fusion.3.refs_2_), channel_id=1, source_target_pairs={{0,12},{1,13},{2,14},{3,15},{4,0},{5,1},{6,2},{7,3},{8,4},{9,5},{1... | collective-permute-start | bytes 1216520 | tf_op jit(solution)/shard_map/ppermute | solution.py:161
  82.6 1.9 collective-permute-start.3
  84.6 3.4 %collective-permute-start.6 = (bf16[528,384]{1,0:T(8,128)(2,1)S(1)}, bf16[528,384]{1,0:T(8,128)(2,1)S(1)}, u32[]{:S(2)}, u32[]{:S(2)}) collective-permute-start(bf16[528,384]{1,0:T(8,128)(2,1)S(1)} %pad_maximum_fusion.3.refs_2_), channel_id=1, source_target_pairs={{0,3},{1,0},{2,1},{3,2},{4,7},{5,4},{6,5},{7,6},{8,11},{9,8},{10,9... | collective-permute-start | bytes 1216520 | tf_op jit(solution)/shard_map/ppermute | solution.py:165
  87.9 24.8 %collective-permute-done.4 = bf16[528,384]{1,0:T(8,128)(2,1)S(1)} collective-permute-done((bf16[528,384]{1,0:T(8,128)(2,1)S(1)}, bf16[528,384]{1,0:T(8,128)(2,1)S(1)}, u32[]{:S(2)}, u32[]{:S(2)}) %collective-permute-start.4) | collective-permute-done | bytes 405536 | tf_op jit(solution)/shard_map/ppermute | solution.py:161
  112.7 3.6 %collective-permute-start.13 = (bf16[768,768]{1,0:T(8,128)(2,1)}, bf16[768,768]{1,0:T(8,128)(2,1)S(1)}, u32[]{:S(2)}, u32[]{:S(2)}) collective-permute-start(bf16[768,768]{1,0:T(8,128)(2,1)} %pad_maximum_fusion), channel_id=1, source_target_pairs={{0,256},{16,272},{32,288},{48,304},{64,320},{80,336},{96,352},{112... | collective-permute-start | bytes 3538952 | tf_op jit(solution)/shard_map/ppermute | solution.py:175
  116.5 3.3 %collective-permute-start.12 = (bf16[1056,384]{1,0:T(8,128)(2,1)S(1)}, bf16[1056,384]{1,0:T(8,128)(2,1)S(1)}, u32[]{:S(2)}, u32[]{:S(2)}) collective-permute-start(bf16[1056,384]{1,0:T(8,128)(2,1)S(1)} %constant_dynamic-update-slice_fusion.3.refs_5_), channel_id=1, source_target_pairs={{0,3},{1,0},{2,1},{3,2},{4,7},{5,4},{6,5},{7,6},{8,11},{9,8},{10,9... | collective-permute-start | bytes 2433032 | tf_op jit(solution)/shard_map/ppermute | solution.py:174
  119.9 1.9 collective-permute-start.11
  121.8 0.8 constant_dynamic-update-slice_fusion.12
  122.6 0.7 constant_dynamic-update-slice_fusion.11
  123.4 7.2 %collective-permute-start.10 = (bf16[256,384]{1,0:T(8,128)(2,1)S(1)}, bf16[256,384]{1,0:T(8,128)(2,1)S(1)}, u32[]{:S(2)}, u32[]{:S(2)}) collective-permute-start(bf16[256,384]{1,0:T(8,128)(2,1)S(1)} %slice.19), channel_id=1, source_target_pairs={{0,12},{1,13},{2,14},{3,15},{4,0},{5,1},{6,2},{7,3},{8,4},{9,5},{1... | collective-permute-start | bytes 589832 | tf_op jit(solution)/shard_map/ppermute | solution.py:171
  130.6 2.0 collective-permute-start.9
  132.6 0.7 constant_dynamic-update-slice_fusion.10
  133.3 2.4 %constant_dynamic-update-slice_fusion.9 = bf16[3072,768]{1,0:T(8,128)(2,1)} fusion(bf16[3072,768]{1,0:T(8,128)(2,1)} %constant_dynamic-update-slice_fusion.10, bf16[768,768]{1,0:T(8,128)(2,1)} %collective-permute-done.7), kind=kLoop, calls=%fused_computation.21 | loop fusion | bytes 2359296
  135.7 7.5 %collective-permute-done.13 = bf16[768,768]{1,0:T(8,128)(2,1)S(1)} collective-permute-done((bf16[768,768]{1,0:T(8,128)(2,1)}, bf16[768,768]{1,0:T(8,128)(2,1)S(1)}, u32[]{:S(2)}, u32[]{:S(2)}) %collective-permute-start.13) | collective-permute-done | bytes 1179680 | tf_op jit(solution)/shard_map/ppermute | solution.py:175
  143.2 1.5 collective-permute-done.9
  144.7 1.2 constant_dynamic-update-slice_fusion.8
  145.9 2.5 %constant_dynamic-update-slice_fusion.7.refs_14_ = bf16[3072,768]{1,0:T(8,128)(2,1)} fusion(bf16[3072,768]{1,0:T(8,128)(2,1)} %constant_dynamic-update-slice_fusion.8, bf16[768,768]{1,0:T(8,128)(2,1)} %collective-permute-done.8), kind=kLoop, calls=%fused_computation.19 | loop fusion | bytes 2359296 | tf_op jit(solution)/shard_map/concatenate | solution.py:185
  148.4 4.0 %collective-permute-start.19 = (bf16[3072,768]{1,0:T(8,128)(2,1)}, bf16[3072,768]{1,0:T(8,128)(2,1)}, u32[]{:S(2)}, u32[]{:S(2)}) collective-permute-start(bf16[3072,768]{1,0:T(8,128)(2,1)} %constant_dynamic-update-slice_fusion.7.refs_14_), channel_id=1, source_target_pairs={{0,16},{16,0},{32,48},{48,32},{64,80},{80,64},{96,112},{112,96},{1... | collective-permute-start | bytes 14155784 | tf_op jit(solution)/shard_map/ppermute | solution.py:186
  152.7 4.5 %collective-permute-start.18 = (bf16[528,384]{1,0:T(8,128)(2,1)S(1)}, bf16[528,384]{1,0:T(8,128)(2,1)S(1)}, u32[]{:S(2)}, u32[]{:S(2)}) collective-permute-start(bf16[528,384]{1,0:T(8,128)(2,1)S(1)} %constant_dynamic-update-slice_fusion.5.refs_10_), channel_id=1, source_target_pairs={{0,2},{1,3},{2,0},{3,1},{4,6},{5,7},{6,4},{7,5},{8,10},{9,11},{10,... | collective-permute-start | bytes 1216520 | tf_op jit(solution)/shard_map/ppermute | solution.py:180
  157.3 2.5 %collective-permute-start.14 = (bf16[800,384]{1,0:T(8,128)(2,1)S(1)}, bf16[800,384]{1,0:T(8,128)(2,1)S(1)}, u32[]{:S(2)}, u32[]{:S(2)}) collective-permute-start(bf16[800,384]{1,0:T(8,128)(2,1)S(1)} %pad_maximum_fusion.1), channel_id=1, source_target_pairs={{0,1},{1,2},{2,3},{3,0},{4,5},{5,6},{6,7},{7,4},{8,9},{9,10},{10,1... | collective-permute-start | bytes 1843208 | tf_op jit(solution)/shard_map/ppermute | solution.py:183
  159.8 0.9 pad_maximum_fusion.2
  160.7 4.0 %collective-permute-start.15 = (bf16[784,384]{1,0:T(8,128)(2,1)}, bf16[784,384]{1,0:T(8,128)(2,1)S(1)}, u32[]{:S(2)}, u32[]{:S(2)}) collective-permute-start(bf16[784,384]{1,0:T(8,128)(2,1)} %pad_maximum_fusion.2), channel_id=1, source_target_pairs={{0,3},{1,0},{2,1},{3,2},{4,7},{5,4},{6,5},{7,6},{8,11},{9,8},{10,9... | collective-permute-start | bytes 1806344 | tf_op jit(solution)/shard_map/ppermute | solution.py:184
  164.7 1.9 collective-permute-start.17
  166.7 0.5 collective-permute-done.18.refs_13_
  167.2 3.2 %collective-permute-start.16 = (bf16[528,384]{1,0:T(8,128)(2,1)S(1)}, bf16[528,384]{1,0:T(8,128)(2,1)}, u32[]{:S(2)}, u32[]{:S(2)}) collective-permute-start(bf16[528,384]{1,0:T(8,128)(2,1)S(1)} %constant_dynamic-update-slice_fusion.5.refs_10_), channel_id=1, source_target_pairs={{0,1},{1,2},{2,3},{3,0},{4,5},{5,6},{6,7},{7,4},{8,9},{9,10},{10,1... | collective-permute-start | bytes 1216520 | tf_op jit(solution)/shard_map/ppermute | solution.py:180
  170.5 0.9 copy.14.refs_16_
  172.4 16.7 %collective-permute-done.17.refs_12_ = bf16[528,384]{1,0:T(8,128)(2,1)} collective-permute-done((bf16[528,384]{1,0:T(8,128)(2,1)S(1)}, bf16[528,384]{1,0:T(8,128)(2,1)}, u32[]{:S(2)}, u32[]{:S(2)}) %collective-permute-start.17) | collective-permute-done | bytes 405536 | tf_op jit(solution)/shard_map/ppermute | solution.py:180
  189.5 0.8 copy-done.9
  190.5 20.9 %norm_project_attend.1 = bf16[512,256]{1,0:T(8,128)(2,1)} custom-call(s32[16]{0:T(128)} %fusion.refs_0_, s32[32]{0:T(128)} %fusion.3.refs_1_, bf16[528,384]{1,0:T(8,128)(2,1)} %copy-done.4, bf16[528,384]{1,0:T(8,128)(2,1)} %copy-done.5, bf16[528,384]{1,0:T(8,128)(2,1)} %copy-done.7, bf16[1056,384]{1,0:T(8,128)(2,1)} %copy-done.3, ...), custom_call_target="tpu_custom_call" | custom-call | tf_op jit(solution)/shard_map/norm_project_attend/pallas_call | solution.py:226
  (76 shorter events, 2.9 us)
Async XLA Ops:
  0.0 2.8 %copy-start = (bf16[1024,384]{1,0:T(8,128)(2,1)S(1)}, bf16[1024,384]{1,0:T(8,128)(2,1)}, u32[]{:S(2)}) copy-start(bf16[1024,384]{1,0:T(8,128)(2,1)} %param.9) | copy-start | bytes 2359300
  0.0 15.2 %copy-start.11 = (bf16[192,256]{1,0:T(8,128)(2,1)S(1)}, bf16[192,256]{1,0:T(8,128)(2,1)}, u32[]{:S(2)}) copy-start(bf16[192,256]{1,0:T(8,128)(2,1)} %param.11) | copy-start | bytes 294916
  0.0 15.9 %copy-start.12 = (bf16[192,256]{1,0:T(8,128)(2,1)S(1)}, bf16[192,256]{1,0:T(8,128)(2,1)}, u32[]{:S(2)}) copy-start(bf16[192,256]{1,0:T(8,128)(2,1)} %param.12) | copy-start | bytes 294916
  0.0 16.5 %copy-start.13 = (bf16[192,256]{1,0:T(8,128)(2,1)S(1)}, bf16[192,256]{1,0:T(8,128)(2,1)}, u32[]{:S(2)}) copy-start(bf16[192,256]{1,0:T(8,128)(2,1)} %param.13) | copy-start | bytes 294916
  2.7 167.8 %copy-start.14 = (s32[512]{0:T(512)}, s32[512]{0:T(512)S(1)}, u32[]{:S(2)}) copy-start(s32[512]{0:T(512)S(1)} %convert_reduce_fusion) | copy-start | bytes 6148
  4.6 65.5 %copy-start.15 = (bf16[384]{0:T(512)(128)(2,1)S(1)}, bf16[384]{0:T(512)(128)(2,1)}, u32[]{:S(2)}) copy-start(bf16[384]{0:T(512)(128)(2,1)} %param.10) | copy-start | bytes 2308
  4.6 55.9 %all-to-all-start = ((bf16[32,32,384]{2,1,0:T(8,128)(2,1)}), bf16[32,32,384]{2,1,0:T(8,128)(2,1)S(1)}, u32[]{:S(2)}, u32[]{:S(2)}) async-start(bf16[32,32,384]{2,1,0:T(8,128)(2,1)} %broadcast_select_fusion), calls=%async_computation | async-start | bytes 1572864 | tf_op jit(solution)/shard_map/all_to_all | solution.py:144
  17.2 19.2 %collective-permute-start.2 = (bf16[192,768]{1,0:T(8,128)(2,1)S(1)}, bf16[192,768]{1,0:T(8,128)(2,1)S(1)}, u32[]{:S(2)}, u32[]{:S(2)}) collective-permute-start(bf16[192,768]{1,0:T(8,128)(2,1)S(1)} %get-tuple-element.40), channel_id=1, source_target_pairs={{0,96},{16,112},{32,0},{48,16},{64,32},{80,48},{96,64},{112,80},{1... | collective-permute-start | bytes 884744 | tf_op jit(solution)/shard_map/ppermute | solution.py:136
  22.3 38.1 %collective-permute-start.1 = (bf16[192,768]{1,0:T(8,128)(2,1)S(1)}, bf16[192,768]{1,0:T(8,128)(2,1)S(1)}, u32[]{:S(2)}, u32[]{:S(2)}) collective-permute-start(bf16[192,768]{1,0:T(8,128)(2,1)S(1)} %get-tuple-element.40), channel_id=1, source_target_pairs={{0,64},{16,80},{32,96},{48,112},{64,0},{80,16},{96,32},{112,48},{1... | collective-permute-start | bytes 884744 | tf_op jit(solution)/shard_map/ppermute | solution.py:136
  24.3 36.2 %collective-permute-start = (bf16[192,768]{1,0:T(8,128)(2,1)S(1)}, bf16[192,768]{1,0:T(8,128)(2,1)S(1)}, u32[]{:S(2)}, u32[]{:S(2)}) collective-permute-start(bf16[192,768]{1,0:T(8,128)(2,1)S(1)} %get-tuple-element.40), channel_id=1, source_target_pairs={{0,32},{16,48},{32,64},{48,80},{64,96},{80,112},{96,0},{112,16},{1... | collective-permute-start | bytes 884744 | tf_op jit(solution)/shard_map/ppermute | solution.py:136
  61.6 54.8 %collective-permute-start.8 = (bf16[768,768]{1,0:T(8,128)(2,1)}, bf16[768,768]{1,0:T(8,128)(2,1)}, u32[]{:S(2)}, u32[]{:S(2)}) collective-permute-start(bf16[768,768]{1,0:T(8,128)(2,1)} %pad_maximum_fusion), channel_id=1, source_target_pairs={{0,384},{16,400},{32,416},{48,432},{64,448},{80,464},{96,480},{112... | collective-permute-start | bytes 3538952 | tf_op jit(solution)/shard_map/ppermute | solution.py:162
  66.0 50.3 %collective-permute-start.7 = (bf16[768,768]{1,0:T(8,128)(2,1)}, bf16[768,768]{1,0:T(8,128)(2,1)}, u32[]{:S(2)}, u32[]{:S(2)}) collective-permute-start(bf16[768,768]{1,0:T(8,128)(2,1)} %pad_maximum_fusion), channel_id=1, source_target_pairs={{0,128},{16,144},{32,160},{48,176},{64,192},{80,208},{96,224},{112... | collective-permute-start | bytes 3538952 | tf_op jit(solution)/shard_map/ppermute | solution.py:162
  70.2 46.3 %copy-start.4 = (bf16[528,384]{1,0:T(8,128)(2,1)}, bf16[528,384]{1,0:T(8,128)(2,1)S(1)}, u32[]{:S(2)}) copy-start(bf16[528,384]{1,0:T(8,128)(2,1)S(1)} %pad_maximum_fusion.3.refs_2_) | copy-start | bytes 1216516
  70.2 14.4 %collective-permute-start.5 = (bf16[528,384]{1,0:T(8,128)(2,1)S(1)}, bf16[528,384]{1,0:T(8,128)(2,1)S(1)}, u32[]{:S(2)}, u32[]{:S(2)}) collective-permute-start(bf16[528,384]{1,0:T(8,128)(2,1)S(1)} %pad_maximum_fusion.3.refs_2_), channel_id=1, source_target_pairs={{0,1},{1,2},{2,3},{3,0},{4,5},{5,6},{6,7},{7,4},{8,9},{9,10},{10,1... | collective-permute-start | bytes 1216520 | tf_op jit(solution)/shard_map/ppermute | solution.py:163
  72.8 39.8 %collective-permute-start.4 = (bf16[528,384]{1,0:T(8,128)(2,1)S(1)}, bf16[528,384]{1,0:T(8,128)(2,1)S(1)}, u32[]{:S(2)}, u32[]{:S(2)}) collective-permute-start(bf16[528,384]{1,0:T(8,128)(2,1)S(1)} %pad_maximum_fusion.3.refs_2_), channel_id=1, source_target_pairs={{0,12},{1,13},{2,14},{3,15},{4,0},{5,1},{6,2},{7,3},{8,4},{9,5},{1... | collective-permute-start | bytes 1216520 | tf_op jit(solution)/shard_map/ppermute | solution.py:161
  82.6 33.7 %collective-permute-start.3 = (bf16[528,384]{1,0:T(8,128)(2,1)S(1)}, bf16[528,384]{1,0:T(8,128)(2,1)S(1)}, u32[]{:S(2)}, u32[]{:S(2)}) collective-permute-start(bf16[528,384]{1,0:T(8,128)(2,1)S(1)} %pad_maximum_fusion.3.refs_2_), channel_id=1, source_target_pairs={{0,4},{1,5},{2,6},{3,7},{4,8},{5,9},{6,10},{7,11},{8,12},{9,13},{1... | collective-permute-start | bytes 1216520 | tf_op jit(solution)/shard_map/ppermute | solution.py:161
  84.6 68.0 %copy-start.5 = (bf16[528,384]{1,0:T(8,128)(2,1)}, bf16[528,384]{1,0:T(8,128)(2,1)S(1)}, u32[]{:S(2)}) copy-start(bf16[528,384]{1,0:T(8,128)(2,1)S(1)} %collective-permute-done.5.refs_3_) | copy-start | bytes 1216516
  84.6 31.8 %collective-permute-start.6 = (bf16[528,384]{1,0:T(8,128)(2,1)S(1)}, bf16[528,384]{1,0:T(8,128)(2,1)S(1)}, u32[]{:S(2)}, u32[]{:S(2)}) collective-permute-start(bf16[528,384]{1,0:T(8,128)(2,1)S(1)} %pad_maximum_fusion.3.refs_2_), channel_id=1, source_target_pairs={{0,3},{1,0},{2,1},{3,2},{4,7},{5,4},{6,5},{7,6},{8,11},{9,8},{10,9... | collective-permute-start | bytes 1216520 | tf_op jit(solution)/shard_map/ppermute | solution.py:165
  112.7 30.5 %collective-permute-start.13 = (bf16[768,768]{1,0:T(8,128)(2,1)}, bf16[768,768]{1,0:T(8,128)(2,1)S(1)}, u32[]{:S(2)}, u32[]{:S(2)}) collective-permute-start(bf16[768,768]{1,0:T(8,128)(2,1)} %pad_maximum_fusion), channel_id=1, source_target_pairs={{0,256},{16,272},{32,288},{48,304},{64,320},{80,336},{96,352},{112... | collective-permute-start | bytes 3538952 | tf_op jit(solution)/shard_map/ppermute | solution.py:175
  116.3 36.1 %copy-start.7 = (bf16[528,384]{1,0:T(8,128)(2,1)}, bf16[528,384]{1,0:T(8,128)(2,1)S(1)}, u32[]{:S(2)}) copy-start(bf16[528,384]{1,0:T(8,128)(2,1)S(1)} %collective-permute-done.6.refs_4_) | copy-start | bytes 1216516
  116.5 31.9 %copy-start.3 = (bf16[1056,384]{1,0:T(8,128)(2,1)}, bf16[1056,384]{1,0:T(8,128)(2,1)S(1)}, u32[]{:S(2)}) copy-start(bf16[1056,384]{1,0:T(8,128)(2,1)S(1)} %constant_dynamic-update-slice_fusion.3.refs_5_) | copy-start | bytes 2433028
  116.5 28.2 %collective-permute-start.12 = (bf16[1056,384]{1,0:T(8,128)(2,1)S(1)}, bf16[1056,384]{1,0:T(8,128)(2,1)S(1)}, u32[]{:S(2)}, u32[]{:S(2)}) collective-permute-start(bf16[1056,384]{1,0:T(8,128)(2,1)S(1)} %constant_dynamic-update-slice_fusion.3.refs_5_), channel_id=1, source_target_pairs={{0,3},{1,0},{2,1},{3,2},{4,7},{5,4},{6,5},{7,6},{8,11},{9,8},{10,9... | collective-permute-start | bytes 2433032 | tf_op jit(solution)/shard_map/ppermute | solution.py:174
  119.9 24.8 %collective-permute-start.11 = (bf16[1056,384]{1,0:T(8,128)(2,1)S(1)}, bf16[1056,384]{1,0:T(8,128)(2,1)S(1)}, u32[]{:S(2)}, u32[]{:S(2)}) collective-permute-start(bf16[1056,384]{1,0:T(8,128)(2,1)S(1)} %constant_dynamic-update-slice_fusion.3.refs_5_), channel_id=1, source_target_pairs={{0,1},{1,2},{2,3},{3,0},{4,5},{5,6},{6,7},{7,4},{8,9},{9,10},{10,1... | collective-permute-start | bytes 2433032 | tf_op jit(solution)/shard_map/ppermute | solution.py:174
  123.4 19.8 %collective-permute-start.10 = (bf16[256,384]{1,0:T(8,128)(2,1)S(1)}, bf16[256,384]{1,0:T(8,128)(2,1)S(1)}, u32[]{:S(2)}, u32[]{:S(2)}) collective-permute-start(bf16[256,384]{1,0:T(8,128)(2,1)S(1)} %slice.19), channel_id=1, source_target_pairs={{0,12},{1,13},{2,14},{3,15},{4,0},{5,1},{6,2},{7,3},{8,4},{9,5},{1... | collective-permute-start | bytes 589832 | tf_op jit(solution)/shard_map/ppermute | solution.py:171
  130.6 14.1 %collective-permute-start.9 = (bf16[272,384]{1,0:T(8,128)(2,1)S(1)}, bf16[272,384]{1,0:T(8,128)(2,1)S(1)}, u32[]{:S(2)}, u32[]{:S(2)}) collective-permute-start(bf16[272,384]{1,0:T(8,128)(2,1)S(1)} %slice.18), channel_id=1, source_target_pairs={{0,4},{1,5},{2,6},{3,7},{4,8},{5,9},{6,10},{7,11},{8,12},{9,13},{1... | collective-permute-start | bytes 626696 | tf_op jit(solution)/shard_map/ppermute | solution.py:170
  144.7 16.1 %copy-start.1 = (bf16[1056,384]{1,0:T(8,128)(2,1)}, bf16[1056,384]{1,0:T(8,128)(2,1)S(1)}, u32[]{:S(2)}) copy-start(bf16[1056,384]{1,0:T(8,128)(2,1)S(1)} %collective-permute-done.12.refs_7_) | copy-start | bytes 2433028
  144.7 16.1 %copy-start.2 = (bf16[1056,384]{1,0:T(8,128)(2,1)}, bf16[1056,384]{1,0:T(8,128)(2,1)S(1)}, u32[]{:S(2)}) copy-start(bf16[1056,384]{1,0:T(8,128)(2,1)S(1)} %collective-permute-done.11.refs_6_) | copy-start | bytes 2433028
  145.9 25.9 %copy-start.16 = (s32[16]{0:T(128)S(1)}, s32[16]{0:T(128)}, u32[]{:S(2)}) copy-start(s32[16]{0:T(128)} %constant.180.clone) | copy-start | bytes 196
  145.9 25.9 %copy-start.17 = (s32[16]{0:T(128)S(1)}, s32[16]{0:T(128)}, u32[]{:S(2)}) copy-start(s32[16]{0:T(128)} %constant.179.clone) | copy-start | bytes 196
  148.4 41.0 %collective-permute-start.19 = (bf16[3072,768]{1,0:T(8,128)(2,1)}, bf16[3072,768]{1,0:T(8,128)(2,1)}, u32[]{:S(2)}, u32[]{:S(2)}) collective-permute-start(bf16[3072,768]{1,0:T(8,128)(2,1)} %constant_dynamic-update-slice_fusion.7.refs_14_), channel_id=1, source_target_pairs={{0,16},{16,0},{32,48},{48,32},{64,80},{80,64},{96,112},{112,96},{1... | collective-permute-start | bytes 14155784 | tf_op jit(solution)/shard_map/ppermute | solution.py:186
  152.7 36.7 %copy-start.6 = (bf16[528,384]{1,0:T(8,128)(2,1)}, bf16[528,384]{1,0:T(8,128)(2,1)S(1)}, u32[]{:S(2)}) copy-start(bf16[528,384]{1,0:T(8,128)(2,1)S(1)} %constant_dynamic-update-slice_fusion.5.refs_10_) | copy-start | bytes 1216516
  152.7 14.4 %collective-permute-start.18 = (bf16[528,384]{1,0:T(8,128)(2,1)S(1)}, bf16[528,384]{1,0:T(8,128)(2,1)S(1)}, u32[]{:S(2)}, u32[]{:S(2)}) collective-permute-start(bf16[528,384]{1,0:T(8,128)(2,1)S(1)} %constant_dynamic-update-slice_fusion.5.refs_10_), channel_id=1, source_target_pairs={{0,2},{1,3},{2,0},{3,1},{4,6},{5,7},{6,4},{7,5},{8,10},{9,11},{10,... | collective-permute-start | bytes 1216520 | tf_op jit(solution)/shard_map/ppermute | solution.py:180
  157.3 32.1 %collective-permute-start.14 = (bf16[800,384]{1,0:T(8,128)(2,1)S(1)}, bf16[800,384]{1,0:T(8,128)(2,1)S(1)}, u32[]{:S(2)}, u32[]{:S(2)}) collective-permute-start(bf16[800,384]{1,0:T(8,128)(2,1)S(1)} %pad_maximum_fusion.1), channel_id=1, source_target_pairs={{0,1},{1,2},{2,3},{3,0},{4,5},{5,6},{6,7},{7,4},{8,9},{9,10},{10,1... | collective-permute-start | bytes 1843208 | tf_op jit(solution)/shard_map/ppermute | solution.py:183
  160.7 28.7 %collective-permute-start.15 = (bf16[784,384]{1,0:T(8,128)(2,1)}, bf16[784,384]{1,0:T(8,128)(2,1)S(1)}, u32[]{:S(2)}, u32[]{:S(2)}) collective-permute-start(bf16[784,384]{1,0:T(8,128)(2,1)} %pad_maximum_fusion.2), channel_id=1, source_target_pairs={{0,3},{1,0},{2,1},{3,2},{4,7},{5,4},{6,5},{7,6},{8,11},{9,8},{10,9... | collective-permute-start | bytes 1806344 | tf_op jit(solution)/shard_map/ppermute | solution.py:184
  164.7 24.3 %collective-permute-start.17 = (bf16[528,384]{1,0:T(8,128)(2,1)S(1)}, bf16[528,384]{1,0:T(8,128)(2,1)}, u32[]{:S(2)}, u32[]{:S(2)}) collective-permute-start(bf16[528,384]{1,0:T(8,128)(2,1)S(1)} %constant_dynamic-update-slice_fusion.5.refs_10_), channel_id=1, source_target_pairs={{0,3},{1,0},{2,1},{3,2},{4,7},{5,4},{6,5},{7,6},{8,11},{9,8},{10,9... | collective-permute-start | bytes 1216520 | tf_op jit(solution)/shard_map/ppermute | solution.py:180
  167.2 22.3 %copy-start.10 = (bf16[528,384]{1,0:T(8,128)(2,1)}, bf16[528,384]{1,0:T(8,128)(2,1)S(1)}, u32[]{:S(2)}) copy-start(bf16[528,384]{1,0:T(8,128)(2,1)S(1)} %collective-permute-done.18.refs_13_) | copy-start | bytes 1216516
  167.2 22.2 %collective-permute-start.16 = (bf16[528,384]{1,0:T(8,128)(2,1)S(1)}, bf16[528,384]{1,0:T(8,128)(2,1)}, u32[]{:S(2)}, u32[]{:S(2)}) collective-permute-start(bf16[528,384]{1,0:T(8,128)(2,1)S(1)} %constant_dynamic-update-slice_fusion.5.refs_10_), channel_id=1, source_target_pairs={{0,1},{1,2},{2,3},{3,0},{4,5},{5,6},{6,7},{7,4},{8,9},{9,10},{10,1... | collective-permute-start | bytes 1216520 | tf_op jit(solution)/shard_map/ppermute | solution.py:180
  189.4 0.9 copy-start.9
  189.4 1.1 copy-start.8

commit v3 on v0

v3 whole, which is shorter than its diff:
```python
import math

import jax
import jax.numpy as jnp
from jax import lax
from jax.experimental import pallas as pl
from jax.experimental.pallas import tpu as pltpu
from jax.sharding import PartitionSpec as P

HEAD_DIM = 128
NORM_EPSILON = 1e-06
Z_PARTS, Y_PARTS = 4, 4
GAIN_ROWS = 16
ROW_TILE = 16


def z_shift(step):
    return [
        (z * Y_PARTS + y, (z + step) % Z_PARTS * Y_PARTS + y)
        for z in range(Z_PARTS)
        for y in range(Y_PARTS)
    ]


def y_shift(step):
    return [
        (z * Y_PARTS + y, z * Y_PARTS + (y + step) % Y_PARTS)
        for z in range(Z_PARTS)
        for y in range(Y_PARTS)
    ]


def dp_groups(varying):
    groups = {}
    for x in range(4):
        for z in range(4):
            for core in range(2):
                key = tuple(v for name, v in (("x", x), ("z", z), ("c", core)) if name not in varying)
                groups.setdefault(key, []).append(x * 8 + z * 2 + core)
    return list(groups.values())


def load_weights(source_ref, weight_ref, sem, strip):
    copies = []
    for x in range(4):
        for z in range(4):
            for core in range(2):
                held, wanted = (x * 2 + core) * 4 + z, x * 8 + z * 2 + core
                copies.append(
                    pltpu.make_async_copy(
                        source_ref.at[pl.ds(held * strip, strip), :],
                        weight_ref.at[pl.ds(wanted * strip, strip), :],
                        sem,
                    )
                )
    for copy in copies:
        copy.start()
    return copies


def slot_columns(places_ref, count, width):
    return [pl.ds(pl.multiple_of(places_ref[j] * width, 128), width) for j in range(count)]


def normalize(sources, gains, columns, rows, normed_ref):
    features = normed_ref.shape[1]

    def step(i, carry):
        at = pl.multiple_of(i * ROW_TILE, ROW_TILE)

        def load(j):
            ref, start = sources[j]
            return ref[pl.ds(at + start, ROW_TILE), :].astype(jnp.float32)

        total = load(0)
        for j in range(1, len(sources)):
            total = total + load(j)
        mean = jnp.sum(total, axis=1, keepdims=True) * (1.0 / features)
        square = jnp.square(load(0) - mean)
        for j in range(1, len(sources)):
            square = square + jnp.square(load(j) - mean)
        var = jnp.sum(square, axis=1, keepdims=True) * (1.0 / features)
        scale = lax.rsqrt(var + NORM_EPSILON)
        for j in range(len(sources)):
            normed_ref[pl.ds(at, ROW_TILE), columns[j]] = (
                (load(j) - mean) * scale * gains[j]
            ).astype(jnp.bfloat16)
        return carry

    lax.fori_loop(0, rows // ROW_TILE, step, 0)


def first_half_kernel(slots, count, strip, *refs):
    places_ref, blocks = refs[0], refs[1 : 1 + count]
    source_ref, sums_ref, gain_ref, normed_ref, weight_ref, sem = refs[1 + count :]
    copies = load_weights(source_ref, weight_ref, sem, strip)
    columns = slot_columns(places_ref, len(slots), blocks[0].shape[1])
    gains = []
    for column, (ref, start) in zip(columns, slots):
        gain = blocks[ref][pl.ds(start - GAIN_ROWS, GAIN_ROWS), :][:1].astype(jnp.float32)
        gain_ref[:, column] = gain
        gains.append(gain)
    sources = [(blocks[ref], start) for ref, start in slots]
    normalize(sources, gains, columns, normed_ref.shape[0], normed_ref)
    for copy in copies:
        copy.wait()
    sums_ref[...] = jnp.dot(
        normed_ref[...], weight_ref[...], preferred_element_type=jnp.float32
    ).astype(jnp.bfloat16)


def second_half_kernel(slots, count, strip, *refs):
    places_ref, blocks = refs[0], refs[1 : 1 + count]
    source_ref, first_ref, gain_ref, seg_col_ref, seg_row_ref, out_ref = refs[1 + count : 7 + count]
    normed_ref, weight_ref, sums_ref, sem = refs[7 + count :]
    copies = load_weights(source_ref, weight_ref, sem, strip)
    columns = slot_columns(places_ref, len(slots), blocks[0].shape[1])
    gains = [gain_ref[:, column] for column in columns]
    sources = [(blocks[ref], start) for ref, start in slots]
    half = normed_ref.shape[0]
    normalize(sources, gains, columns, half, normed_ref)
    sums_ref[:half] = first_ref[...]
    for copy in copies:
        copy.wait()
    sums_ref[half:] = jnp.dot(
        normed_ref[...], weight_ref[...], preferred_element_type=jnp.float32
    ).astype(jnp.bfloat16)
    rows, local = out_ref.shape
    span, window = 128, 256
    for row in range(0, rows, span):
        low = min(max(row - (window - span) // 2, 0), rows - window)
        same = seg_col_ref[row : row + span, :1] == seg_row_ref[:1, low : low + window]
        for col in range(0, local, HEAD_DIM):
            query = sums_ref[row : row + span, col : col + HEAD_DIM]
            key = sums_ref[low : low + window, local + col : local + col + HEAD_DIM]
            value = sums_ref[low : low + window, 2 * local + col : 2 * local + col + HEAD_DIM]
            scores = lax.dot_general(
                query, key, (((1,), (1,)), ((), ())), preferred_element_type=jnp.float32
            ) * (1.0 / math.sqrt(HEAD_DIM))
            scores = jnp.where(same, scores, -jnp.inf)
            expo = jnp.exp(scores - jnp.max(scores, axis=1, keepdims=True))
            probs = (expo / jnp.sum(expo, axis=1, keepdims=True)).astype(jnp.bfloat16)
            out_ref[row : row + span, col : col + HEAD_DIM] = jnp.dot(
                probs, value, preferred_element_type=jnp.float32
            ).astype(jnp.bfloat16)


def along_y(block, last):
    return [lax.ppermute(block, "tensor", y_shift(step)) for step in (2, -1, 1)] + last


def shards(page_patches, gain, q_weight, k_weight, v_weight, pack_lengths, line_order):
    groups = lax.axis_size("dp")
    page_index = lax.axis_index("dp")
    width = page_patches.shape[1]
    slot_rows = page_patches.shape[0] // groups
    rows = slot_rows * groups // 2
    half = rows // 2
    local = q_weight.shape[1]
    strip = q_weight.shape[0]
    weight = jnp.concatenate([q_weight, k_weight, v_weight], axis=1)
    for varying in ("z", "xc"):
        weight = lax.all_gather(
            weight, "dp", axis=0, tiled=True, axis_index_groups=dp_groups(varying)
        )
    targets = jnp.arange(groups, dtype=jnp.int32)
    my_order = lax.dynamic_index_in_dim(line_order, page_index, 0, keepdims=False)
    slot_for = jnp.sum(
        jnp.where(my_order[None, :] == targets[:, None], targets[None, :], 0), axis=1
    )
    slots = page_patches.reshape(groups, slot_rows, width)
    outgoing = jnp.take(slots, slot_for, axis=0)
    incoming = lax.all_to_all(outgoing, "dp", split_axis=0, concat_axis=0, tiled=True)
    my_lengths = lax.dynamic_index_in_dim(pack_lengths, page_index, 0, keepdims=False)
    line_ends = jnp.cumsum(my_lengths)
    line_starts = line_ends - my_lengths
    row_ids = jnp.arange(rows, dtype=jnp.int32)
    segment = jnp.sum((line_ends[None, :] <= row_ids[:, None]).astype(jnp.int32), axis=1)
    start_of_row = jnp.sum(
        jnp.where(segment[:, None] == targets[None, :], line_starts[None, :], 0), axis=1
    )
    source_rows = segment * slot_rows + row_ids - start_of_row
    packed = jnp.take(incoming.reshape(groups * slot_rows, width), source_rows, axis=0)

    gain_rows = jnp.broadcast_to(gain[None, :], (GAIN_ROWS, width))
    own = jnp.concatenate([gain_rows, packed], axis=0)
    top, rest = own[: half + GAIN_ROWS], own[half + GAIN_ROWS :]

    up, down = z_shift(1), z_shift(-1)
    *own_y, top_down, top_up, rest = lax.optimization_barrier(
        (
            *along_y(own, []),
            lax.ppermute(top, "tensor", down),
            lax.ppermute(top, "tensor", up),
            rest,
        )
    )
    pair = jnp.concatenate([top_up, top_down], axis=0)
    *pair_y, rest_down, top_far, rest = lax.optimization_barrier(
        (
            *along_y(pair, []),
            lax.ppermute(rest, "tensor", down),
            lax.ppermute(top_up, "tensor", up),
            rest,
        )
    )
    *far_y, rest_far, rest_up = lax.optimization_barrier(
        (
            *along_y(top_far, []),
            lax.ppermute(rest_down, "tensor", down),
            lax.ppermute(rest, "tensor", up),
        )
    )
    trio = jnp.concatenate([rest_up, rest_down, rest_far], axis=0)
    trio_y = along_y(trio, [])

    shifts = [(dz, dy) for dy in (2, 1, -1, 0) for dz in (0, -1, 1, 2)]
    tensor = lax.axis_index("tensor")
    my_z, my_y = tensor // Y_PARTS, tensor % Y_PARTS
    step_z = jnp.array([dz for dz, _ in shifts], jnp.int32)
    step_y = jnp.array([dy for _, dy in shifts], jnp.int32)
    places = (my_z + step_z + Z_PARTS) % Z_PARTS * Y_PARTS + (my_y + step_y + Y_PARTS) % Y_PARTS

    first_blocks, first_slots, second_blocks, second_slots = [], [], [], []
    for k, arrays in enumerate(zip(own_y + [own], pair_y + [pair], far_y + [top_far])):
        first_blocks += arrays
        first_slots += [
            (3 * k, GAIN_ROWS),
            (3 * k + 1, GAIN_ROWS),
            (3 * k + 1, half + 2 * GAIN_ROWS),
            (3 * k + 2, GAIN_ROWS),
        ]
    for k, arrays in enumerate(zip(own_y + [own], trio_y + [trio])):
        second_blocks += arrays
        second_slots += [(2 * k, half + GAIN_ROWS)] + [(2 * k + 1, half * i) for i in range(3)]

    features = width * len(shifts)
    vmem = pl.BlockSpec(memory_space=pltpu.VMEM)
    smem, hbm = pl.BlockSpec(memory_space=pltpu.SMEM), pl.BlockSpec(memory_space=pl.ANY)
    normed = pltpu.VMEM((half, features), jnp.bfloat16)
    whole_weight = pltpu.VMEM((features, 3 * local), jnp.bfloat16)

    def first_kernel(*refs):
        first_half_kernel(first_slots, len(first_blocks), strip, *refs)

    def second_kernel(*refs):
        second_half_kernel(second_slots, len(second_blocks), strip, *refs)

    first_sums, all_gain = pl.pallas_call(
        first_kernel,
        out_shape=(
            jax.ShapeDtypeStruct((half, 3 * local), jnp.bfloat16),
            jax.ShapeDtypeStruct((1, features), jnp.float32),
        ),
        in_specs=[smem] + [vmem] * len(first_blocks) + [hbm],
        out_specs=(vmem, vmem),
        scratch_shapes=[normed, whole_weight, pltpu.SemaphoreType.DMA],
        name="norm_project",
    )(places, *first_blocks, weight)
    return pl.pallas_call(
        second_kernel,
        out_shape=jax.ShapeDtypeStruct((rows, local), jnp.bfloat16),
        in_specs=[smem] + [vmem] * len(second_blocks) + [hbm] + [vmem] * 4,
        out_specs=vmem,
        scratch_shapes=[
            normed,
            whole_weight,
            pltpu.VMEM((rows, 3 * local), jnp.bfloat16),
            pltpu.SemaphoreType.DMA,
        ],
        name="norm_project_attend",
    )(places, *second_blocks, weight, first_sums, all_gain, segment[:, None], segment[None, :])


def solution(mesh):
    return jax.shard_map(
        shards,
        mesh=mesh,
        in_specs=(
            P("dp", "tensor"),
            P("tensor"),
            P("dp", "tensor"),
            P("dp", "tensor"),
            P("dp", "tensor"),
            P(),
            P(),
        ),
        out_specs=P("dp", "tensor"),
        check_vma=False,
    )
```

time: 444 us -> 248 us (0.56)
  waiting for transfers between devices: 329 us -> 122 us
  starting transfers between devices: 10.7 us -> 74.4 us
  blocking collectives: 49.9 us -> 0 us
  Pallas kernels: 0 us -> 23.1 us
  matrix products: 18.8 us -> 0 us
  other arithmetic: 15.3 us -> 4.81 us
    all_gather x4 -> x2, waiting for transfers between devices: 307 us -> 46.8 us  [shards(): lax.all_gather(weight, 'dp', axis=0, tiled=True, axis_index_groups=dp_gro...]
    ppermute x0 -> x18, starting transfers between devices: none -> 68.5 us  [the longest x12 40.4 us: along_y(): lax.ppermute(block, 'tensor', y_shift(step))]
    ppermute x0 -> x18, waiting for transfers between devices: none -> 54.4 us  [the longest x1 16.1 us: shards(): lax.ppermute(rest, 'tensor', down)]
    all_gather x1 -> x0, blocking collectives: 49.9 us -> none  [shards(): lax.all_gather(gain, 'tensor', axis=0, tiled=True)]
    pallas_call x0 -> x2, Pallas kernels: none -> 23.1 us  [the longest x1 13.3 us: shards(): pl.pallas_call(second_kernel, out_shape=jax.ShapeDtypeStruct((rows, local...]
    dot_general x4 -> x0, matrix products: 17.9 us -> none  [the longest x3 16.6 us: shards(): jnp.dot(normed, weight_rows, preferred_element_type=jnp.float32)]
    convert_element_type x2 -> x0, other arithmetic: 6.29 us -> none  [the longest x1 6.27 us: shards(): normed = ((row_vals - row_mean) * lax.rsqrt(row_var + norm_epsilon) * ful...]
    reduce_sum x3 -> x1, other arithmetic: 5.7 us -> 0.09 us  [shards(): jnp.sum((line_ends[None, :] <= row_ids[:, None]).astype(jnp.int32), axis=1)]
  transfers between devices with their start and end apart: 5 -> 21, of which waited for: 5 -> 8; matrix products, arithmetic and copies ran while one was open for 6% -> 3% of each run, Pallas kernels for 0% -> 4%
where the time goes in v3:
time: 248 us; the launch traced here: 245 us
  waiting for transfers between devices  122 us (49%)
  starting transfers between devices  74.4 us (30%)
  Pallas kernels  23.1 us (9%)
  between operations  13.9 us (6%)
  local copies, waits for them, and re-layouts  6.54 us (3%)
  other arithmetic  4.81 us (2%)
    all_gather x2, waiting for transfers between devices, shards(): lax.all_gather(weight, 'dp', axis=0, tiled=True, axis_index_groups=dp_gro...  46.8 us
    ppermute x12, starting transfers between devices, along_y(): lax.ppermute(block, 'tensor', y_shift(step))  40.4 us
    all_to_all x1, waiting for transfers between devices, shards(): lax.all_to_all(outgoing, 'dp', split_axis=0, concat_axis=0, tiled=True)  20.6 us
    ppermute x1, waiting for transfers between devices, shards(): lax.ppermute(rest, 'tensor', down)  16.1 us
    pallas_call x1, Pallas kernels, shards(): pl.pallas_call(second_kernel, out_shape=jax.ShapeDtypeStruct((rows, local...  13.3 us
    ppermute x1, waiting for transfers between devices, shards(): lax.ppermute(top, 'tensor', down)  11.1 us
    ppermute x1, waiting for transfers between devices, shards(): lax.ppermute(top, 'tensor', up)  10.3 us
    pallas_call x1, Pallas kernels, shards(): pl.pallas_call(first_kernel, out_shape=(jax.ShapeDtypeStruct((half, 3 * l...  9.82 us
  transfers between devices with their start and end apart: 21, of which 8 were waited for; matrix products, arithmetic and copies ran while one was open for 3% of the time, Pallas kernels for 4%

profile of v3, /device:TPU:1, one launch (start us, length us, event | category | flops | bytes accessed | tf_op | source)
XLA Modules:
  0.0 244.7 jit_solution(12843553718405532199)
XLA Ops:
  6.6 1.8 pad_maximum_fusion.1
  8.4 0.0 all-gather.5.cloned.1.call-start
  8.4 46.8 %all-gather.3.cloned.1.call-done = bf16[768,768]{1,0:T(8,128)(2,1)} async-done(((bf16[192,768]{1,0:T(8,128)(2,1)}), bf16[768,768]{1,0:T(8,128)(2,1)}) %all-gather.3.cloned.1.call-update) | async-done | bytes 1179664 | tf_op jit(solution)/shard_map/all_gather | solution.py:163
  55.3 0.7 dynamic-slice_bitcast_fusion
  56.0 0.1 select_reduce_fusion.1
  56.2 0.7 gather_fusion
  56.9 1.0 broadcast_select_fusion
  57.9 5.9 %all-to-all-start = ((bf16[32,32,384]{2,1,0:T(8,128)(2,1)}), bf16[32,32,384]{2,1,0:T(8,128)(2,1)S(1)}, u32[]{:S(2)}, u32[]{:S(2)}) async-start(bf16[32,32,384]{2,1,0:T(8,128)(2,1)} %broadcast_select_fusion), calls=%async_computation | async-start | bytes 1572864 | tf_op jit(solution)/shard_map/all_to_all | solution.py:173
  63.8 0.7 fusion.7
  64.5 0.1 copy.13
  64.6 0.1 reduce-window.4
  64.6 0.1 reduce
  64.8 0.1 convert_reduce_fusion
  64.9 0.7 fusion.6
  65.6 0.1 select_reduce_fusion
  65.7 20.6 %all-to-all-done = bf16[32,32,384]{2,1,0:T(8,128)(2,1)S(1)} async-done(((bf16[32,32,384]{2,1,0:T(8,128)(2,1)}), bf16[32,32,384]{2,1,0:T(8,128)(2,1)S(1)}, u32[]{:S(2)}, u32[]{:S(2)}) %all-to-all-start) | async-done | bytes 786464 | tf_op jit(solution)/shard_map/all_to_all | solution.py:173
  86.3 1.9 gather_fusion.1
  88.3 0.1 broadcast_select_fusion.1
  88.5 3.1 %collective-permute-start.2 = (bf16[528,384]{1,0:T(8,128)(2,1)S(1)}, bf16[528,384]{1,0:T(8,128)(2,1)S(1)}, u32[]{:S(2)}, u32[]{:S(2)}) collective-permute-start(bf16[528,384]{1,0:T(8,128)(2,1)S(1)} %pad_maximum_fusion.refs_10_.refs_7_), channel_id=1, source_target_pairs={{0,1},{1,2},{2,3},{3,0},{4,5},{5,6},{6,7},{7,4},{8,9},{9,10},{10,1... | collective-permute-start | bytes 1216520 | tf_op jit(solution)/shard_map/ppermute | solution.py:149
  91.6 3.4 %collective-permute-start.1 = (bf16[528,384]{1,0:T(8,128)(2,1)S(1)}, bf16[528,384]{1,0:T(8,128)(2,1)S(1)}, u32[]{:S(2)}, u32[]{:S(2)}) collective-permute-start(bf16[528,384]{1,0:T(8,128)(2,1)S(1)} %pad_maximum_fusion.refs_10_.refs_7_), channel_id=1, source_target_pairs={{0,3},{1,0},{2,1},{3,2},{4,7},{5,4},{6,5},{7,6},{8,11},{9,8},{10,9... | collective-permute-start | bytes 1216520 | tf_op jit(solution)/shard_map/ppermute | solution.py:149
  95.0 3.4 %collective-permute-start = (bf16[528,384]{1,0:T(8,128)(2,1)S(1)}, bf16[528,384]{1,0:T(8,128)(2,1)S(1)}, u32[]{:S(2)}, u32[]{:S(2)}) collective-permute-start(bf16[528,384]{1,0:T(8,128)(2,1)S(1)} %pad_maximum_fusion.refs_10_.refs_7_), channel_id=1, source_target_pairs={{0,2},{1,3},{2,0},{3,1},{4,6},{5,7},{6,4},{7,5},{8,10},{9,11},{10,... | collective-permute-start | bytes 1216520 | tf_op jit(solution)/shard_map/ppermute | solution.py:149
  98.5 7.4 %collective-permute-start.4 = (bf16[272,384]{1,0:T(8,128)(2,1)S(1)}, bf16[272,384]{1,0:T(8,128)(2,1)S(1)}, u32[]{:S(2)}, u32[]{:S(2)}) collective-permute-start(bf16[272,384]{1,0:T(8,128)(2,1)S(1)} %fusion), channel_id=1, source_target_pairs={{0,4},{1,5},{2,6},{3,7},{4,8},{5,9},{6,10},{7,11},{8,12},{9,13},{1... | collective-permute-start | bytes 626696 | tf_op jit(solution)/shard_map/ppermute | solution.py:194
  105.9 2.4 collective-permute-start.3
  108.3 10.3 %collective-permute-done.4 = bf16[272,384]{1,0:T(8,128)(2,1)S(1)} collective-permute-done((bf16[272,384]{1,0:T(8,128)(2,1)S(1)}, bf16[272,384]{1,0:T(8,128)(2,1)S(1)}, u32[]{:S(2)}, u32[]{:S(2)}) %collective-permute-start.4) | collective-permute-done | bytes 208928 | tf_op jit(solution)/shard_map/ppermute | solution.py:194
  118.6 11.1 %collective-permute-done.3 = bf16[272,384]{1,0:T(8,128)(2,1)S(1)} collective-permute-done((bf16[272,384]{1,0:T(8,128)(2,1)S(1)}, bf16[272,384]{1,0:T(8,128)(2,1)S(1)}, u32[]{:S(2)}, u32[]{:S(2)}) %collective-permute-start.3) | collective-permute-done | bytes 208928 | tf_op jit(solution)/shard_map/ppermute | solution.py:193
  129.8 2.2 collective-permute-start.7
  132.0 4.3 %collective-permute-start.6 = (bf16[544,384]{1,0:T(8,128)(2,1)S(1)}, bf16[544,384]{1,0:T(8,128)(2,1)S(1)}, u32[]{:S(2)}, u32[]{:S(2)}) collective-permute-start(bf16[544,384]{1,0:T(8,128)(2,1)S(1)} %constant_dynamic-update-slice_fusion.refs_11_), channel_id=1, source_target_pairs={{0,3},{1,0},{2,1},{3,2},{4,7},{5,4},{6,5},{7,6},{8,11},{9,8},{10,9... | collective-permute-start | bytes 1253384 | tf_op jit(solution)/shard_map/ppermute | solution.py:149
  136.3 2.1 collective-permute-start.5
  138.5 7.1 %collective-permute-start.9 = (bf16[272,384]{1,0:T(8,128)(2,1)S(1)}, bf16[272,384]{1,0:T(8,128)(2,1)S(1)}, u32[]{:S(2)}, u32[]{:S(2)}) collective-permute-start(bf16[272,384]{1,0:T(8,128)(2,1)S(1)} %collective-permute-done.4), channel_id=1, source_target_pairs={{0,4},{1,5},{2,6},{3,7},{4,8},{5,9},{6,10},{7,11},{8,12},{9,13},{1... | collective-permute-start | bytes 626696 | tf_op jit(solution)/shard_map/ppermute | solution.py:203
  145.6 2.1 collective-permute-start.8
  147.7 16.1 %collective-permute-done.8 = bf16[256,384]{1,0:T(8,128)(2,1)S(1)} collective-permute-done((bf16[256,384]{1,0:T(8,128)(2,1)S(1)}, bf16[256,384]{1,0:T(8,128)(2,1)S(1)}, u32[]{:S(2)}, u32[]{:S(2)}) %collective-permute-start.8) | collective-permute-done | bytes 196640 | tf_op jit(solution)/shard_map/ppermute | solution.py:202
  163.9 2.3 collective-permute-start.12
  166.2 4.2 %collective-permute-start.11 = (bf16[272,384]{1,0:T(8,128)(2,1)S(1)}, bf16[272,384]{1,0:T(8,128)(2,1)S(1)}, u32[]{:S(2)}, u32[]{:S(2)}) collective-permute-start(bf16[272,384]{1,0:T(8,128)(2,1)S(1)} %collective-permute-done.9.refs_12_), channel_id=1, source_target_pairs={{0,3},{1,0},{2,1},{3,2},{4,7},{5,4},{6,5},{7,6},{8,11},{9,8},{10,9... | collective-permute-start | bytes 626696 | tf_op jit(solution)/shard_map/ppermute | solution.py:149
  170.4 3.4 %collective-permute-start.10 = (bf16[272,384]{1,0:T(8,128)(2,1)S(1)}, bf16[272,384]{1,0:T(8,128)(2,1)}, u32[]{:S(2)}, u32[]{:S(2)}) collective-permute-start(bf16[272,384]{1,0:T(8,128)(2,1)S(1)} %collective-permute-done.9.refs_12_), channel_id=1, source_target_pairs={{0,2},{1,3},{2,0},{3,1},{4,6},{5,7},{6,4},{7,5},{8,10},{9,11},{10,... | collective-permute-start | bytes 626696 | tf_op jit(solution)/shard_map/ppermute | solution.py:149
  173.8 3.8 %collective-permute-start.14 = (bf16[256,384]{1,0:T(8,128)(2,1)S(1)}, bf16[256,384]{1,0:T(8,128)(2,1)S(1)}, u32[]{:S(2)}, u32[]{:S(2)}) collective-permute-start(bf16[256,384]{1,0:T(8,128)(2,1)S(1)} %slice.14), channel_id=1, source_target_pairs={{0,4},{1,5},{2,6},{3,7},{4,8},{5,9},{6,10},{7,11},{8,12},{9,13},{1... | collective-permute-start | bytes 589832 | tf_op jit(solution)/shard_map/ppermute | solution.py:211
  177.7 5.4 %collective-permute-start.13 = (bf16[256,384]{1,0:T(8,128)(2,1)S(1)}, bf16[256,384]{1,0:T(8,128)(2,1)S(1)}, u32[]{:S(2)}, u32[]{:S(2)}) collective-permute-start(bf16[256,384]{1,0:T(8,128)(2,1)S(1)} %collective-permute-done.8), channel_id=1, source_target_pairs={{0,12},{1,13},{2,14},{3,15},{4,0},{5,1},{6,2},{7,3},{8,4},{9,5},{1... | collective-permute-start | bytes 589832 | tf_op jit(solution)/shard_map/ppermute | solution.py:210
  183.0 2.1 collective-permute-done.14
  185.1 5.4 %collective-permute-done.13 = bf16[256,384]{1,0:T(8,128)(2,1)S(1)} collective-permute-done((bf16[256,384]{1,0:T(8,128)(2,1)S(1)}, bf16[256,384]{1,0:T(8,128)(2,1)S(1)}, u32[]{:S(2)}, u32[]{:S(2)}) %collective-permute-start.13) | collective-permute-done | bytes 196640 | tf_op jit(solution)/shard_map/ppermute | solution.py:210
  190.6 0.6 copy-done.11
  191.2 0.7 copy-done.12
  192.0 1.9 collective-permute-start.17
  194.0 4.6 %collective-permute-start.16 = (bf16[768,384]{1,0:T(8,128)(2,1)S(1)}, bf16[768,384]{1,0:T(8,128)(2,1)}, u32[]{:S(2)}, u32[]{:S(2)}) collective-permute-start(bf16[768,384]{1,0:T(8,128)(2,1)S(1)} %constant_dynamic-update-slice_fusion.2.refs_8_), channel_id=1, source_target_pairs={{0,3},{1,0},{2,1},{3,2},{4,7},{5,4},{6,5},{7,6},{8,11},{9,8},{10,9... | collective-permute-start | bytes 1769480 | tf_op jit(solution)/shard_map/ppermute | solution.py:149
  198.5 5.4 %collective-permute-start.15 = (bf16[768,384]{1,0:T(8,128)(2,1)S(1)}, bf16[768,384]{1,0:T(8,128)(2,1)}, u32[]{:S(2)}, u32[]{:S(2)}) collective-permute-start(bf16[768,384]{1,0:T(8,128)(2,1)S(1)} %constant_dynamic-update-slice_fusion.2.refs_8_), channel_id=1, source_target_pairs={{0,2},{1,3},{2,0},{3,1},{4,6},{5,7},{6,4},{7,5},{8,10},{9,11},{10,... | collective-permute-start | bytes 1769480 | tf_op jit(solution)/shard_map/ppermute | solution.py:149
  203.9 0.9 copy.14.refs_12_
  204.8 0.5 fusion.1.refs_0_
  205.4 9.8 %norm_project.1 = (bf16[256,768]{1,0:T(8,128)(2,1)}, f32[1,6144]{1,0:T(1,128)}) custom-call(s32[16]{0:T(128)} %fusion.1.refs_0_, bf16[528,384]{1,0:T(8,128)(2,1)} %copy-done.4, bf16[544,384]{1,0:T(8,128)(2,1)} %copy-done.9, bf16[272,384]{1,0:T(8,128)(2,1)} %collective-permute-done.10.refs_3_, bf16[528,384]{1,0:T(8,128)(2,1)} %copy-done.3, ...), custom_call_target="tpu_custom_call" | custom-call | tf_op jit(solution)/shard_map/norm_project/pallas_call | solution.py:249
  215.2 9.3 %collective-permute-done.15.refs_2_ = bf16[768,384]{1,0:T(8,128)(2,1)} collective-permute-done((bf16[768,384]{1,0:T(8,128)(2,1)S(1)}, bf16[768,384]{1,0:T(8,128)(2,1)}, u32[]{:S(2)}, u32[]{:S(2)}) %collective-permute-start.15) | collective-permute-done | bytes 589856 | tf_op jit(solution)/shard_map/ppermute | solution.py:149
  224.5 13.3 %norm_project_attend.1 = bf16[512,256]{1,0:T(8,128)(2,1)} custom-call(s32[16]{0:T(128)} %fusion.1.refs_0_, bf16[528,384]{1,0:T(8,128)(2,1)} %copy-done.4, bf16[768,384]{1,0:T(8,128)(2,1)} %collective-permute-done.15.refs_2_, bf16[528,384]{1,0:T(8,128)(2,1)} %copy-done.3, bf16[768,384]{1,0:T(8,128)(2,1)} %collective-permute-done.16.refs_4_, ...), custom_call_target="tpu_custom_call" | custom-call | tf_op jit(solution)/shard_map/norm_project_attend/pallas_call | solution.py:260
  (63 shorter events, 0.5 us)
Async XLA Ops:
  6.5 49.6 %copy-start = (bf16[1024,384]{1,0:T(8,128)(2,1)S(1)}, bf16[1024,384]{1,0:T(8,128)(2,1)}, u32[]{:S(2)}) copy-start(bf16[1024,384]{1,0:T(8,128)(2,1)} %param.9) | copy-start | bytes 2359300
  6.5 198.3 %copy-start.15 = (s32[16]{0:T(128)S(1)}, s32[16]{0:T(128)}, u32[]{:S(2)}) copy-start(s32[16]{0:T(128)} %constant.94.clone) | copy-start | bytes 196
  6.5 198.3 %copy-start.16 = (s32[16]{0:T(128)S(1)}, s32[16]{0:T(128)}, u32[]{:S(2)}) copy-start(s32[16]{0:T(128)} %constant.93.clone) | copy-start | bytes 196
  6.5 81.9 %copy-start.14 = (bf16[384]{0:T(512)(128)(2,1)S(1)}, bf16[384]{0:T(512)(128)(2,1)}, u32[]{:S(2)}) copy-start(bf16[384]{0:T(512)(128)(2,1)} %param.10) | copy-start | bytes 2308
  6.5 48.7 %all-gather.3.cloned.1.call-start = ((), (), s32[]{:S(2)}) async-start(), calls=%async_computation.1 | async-start | bytes 1474560 | tf_op jit(solution)/shard_map/all_gather | solution.py:163
  8.4 196.9 %all-gather.5.cloned.1.call-start = ((), (), s32[]{:S(2)}) async-start(), calls=%async_computation.2 | async-start | bytes 10616832 | tf_op jit(solution)/shard_map/all_gather | solution.py:163
  57.9 28.4 %all-to-all-start = ((bf16[32,32,384]{2,1,0:T(8,128)(2,1)}), bf16[32,32,384]{2,1,0:T(8,128)(2,1)S(1)}, u32[]{:S(2)}, u32[]{:S(2)}) async-start(bf16[32,32,384]{2,1,0:T(8,128)(2,1)} %broadcast_select_fusion), calls=%async_computation | async-start | bytes 1572864 | tf_op jit(solution)/shard_map/all_to_all | solution.py:173
  64.9 150.4 %copy-start.13 = (s32[512]{0:T(512)}, s32[512]{0:T(512)S(1)}, u32[]{:S(2)}) copy-start(s32[512]{0:T(512)S(1)} %convert_reduce_fusion) | copy-start | bytes 6148
  88.5 116.8 %copy-start.1 = (bf16[528,384]{1,0:T(8,128)(2,1)}, bf16[528,384]{1,0:T(8,128)(2,1)S(1)}, u32[]{:S(2)}) copy-start(bf16[528,384]{1,0:T(8,128)(2,1)S(1)} %pad_maximum_fusion.refs_10_.refs_7_) | copy-start | bytes 1216516
  88.5 41.2 %collective-permute-start.2 = (bf16[528,384]{1,0:T(8,128)(2,1)S(1)}, bf16[528,384]{1,0:T(8,128)(2,1)S(1)}, u32[]{:S(2)}, u32[]{:S(2)}) collective-permute-start(bf16[528,384]{1,0:T(8,128)(2,1)S(1)} %pad_maximum_fusion.refs_10_.refs_7_), channel_id=1, source_target_pairs={{0,1},{1,2},{2,3},{3,0},{4,5},{5,6},{6,7},{7,4},{8,9},{9,10},{10,1... | collective-permute-start | bytes 1216520 | tf_op jit(solution)/shard_map/ppermute | solution.py:149
  91.6 38.1 %collective-permute-start.1 = (bf16[528,384]{1,0:T(8,128)(2,1)S(1)}, bf16[528,384]{1,0:T(8,128)(2,1)S(1)}, u32[]{:S(2)}, u32[]{:S(2)}) collective-permute-start(bf16[528,384]{1,0:T(8,128)(2,1)S(1)} %pad_maximum_fusion.refs_10_.refs_7_), channel_id=1, source_target_pairs={{0,3},{1,0},{2,1},{3,2},{4,7},{5,4},{6,5},{7,6},{8,11},{9,8},{10,9... | collective-permute-start | bytes 1216520 | tf_op jit(solution)/shard_map/ppermute | solution.py:149
  95.0 34.7 %collective-permute-start = (bf16[528,384]{1,0:T(8,128)(2,1)S(1)}, bf16[528,384]{1,0:T(8,128)(2,1)S(1)}, u32[]{:S(2)}, u32[]{:S(2)}) collective-permute-start(bf16[528,384]{1,0:T(8,128)(2,1)S(1)} %pad_maximum_fusion.refs_10_.refs_7_), channel_id=1, source_target_pairs={{0,2},{1,3},{2,0},{3,1},{4,6},{5,7},{6,4},{7,5},{8,10},{9,11},{10,... | collective-permute-start | bytes 1216520 | tf_op jit(solution)/shard_map/ppermute | solution.py:149
  98.5 20.1 %collective-permute-start.4 = (bf16[272,384]{1,0:T(8,128)(2,1)S(1)}, bf16[272,384]{1,0:T(8,128)(2,1)S(1)}, u32[]{:S(2)}, u32[]{:S(2)}) collective-permute-start(bf16[272,384]{1,0:T(8,128)(2,1)S(1)} %fusion), channel_id=1, source_target_pairs={{0,4},{1,5},{2,6},{3,7},{4,8},{5,9},{6,10},{7,11},{8,12},{9,13},{1... | collective-permute-start | bytes 626696 | tf_op jit(solution)/shard_map/ppermute | solution.py:194
  105.9 23.8 %collective-permute-start.3 = (bf16[272,384]{1,0:T(8,128)(2,1)S(1)}, bf16[272,384]{1,0:T(8,128)(2,1)S(1)}, u32[]{:S(2)}, u32[]{:S(2)}) collective-permute-start(bf16[272,384]{1,0:T(8,128)(2,1)S(1)} %fusion), channel_id=1, source_target_pairs={{0,12},{1,13},{2,14},{3,15},{4,0},{5,1},{6,2},{7,3},{8,4},{9,5},{1... | collective-permute-start | bytes 626696 | tf_op jit(solution)/shard_map/ppermute | solution.py:193
  129.7 75.7 %copy-start.2 = (bf16[528,384]{1,0:T(8,128)(2,1)}, bf16[528,384]{1,0:T(8,128)(2,1)S(1)}, u32[]{:S(2)}) copy-start(bf16[528,384]{1,0:T(8,128)(2,1)S(1)} %collective-permute-done.2.refs_7_.refs_5_) | copy-start | bytes 1216516
  129.7 75.7 %copy-start.3 = (bf16[528,384]{1,0:T(8,128)(2,1)}, bf16[528,384]{1,0:T(8,128)(2,1)S(1)}, u32[]{:S(2)}) copy-start(bf16[528,384]{1,0:T(8,128)(2,1)S(1)} %collective-permute-done.1.refs_4_.refs_3_) | copy-start | bytes 1216516
  129.7 75.6 %copy-start.4 = (bf16[528,384]{1,0:T(8,128)(2,1)}, bf16[528,384]{1,0:T(8,128)(2,1)S(1)}, u32[]{:S(2)}) copy-start(bf16[528,384]{1,0:T(8,128)(2,1)S(1)} %collective-permute-done.refs_1_) | copy-start | bytes 1216516
  129.8 75.6 %copy-start.6 = (bf16[544,384]{1,0:T(8,128)(2,1)}, bf16[544,384]{1,0:T(8,128)(2,1)S(1)}, u32[]{:S(2)}) copy-start(bf16[544,384]{1,0:T(8,128)(2,1)S(1)} %constant_dynamic-update-slice_fusion.refs_11_) | copy-start | bytes 1253380
  129.8 34.0 %collective-permute-start.7 = (bf16[544,384]{1,0:T(8,128)(2,1)S(1)}, bf16[544,384]{1,0:T(8,128)(2,1)S(1)}, u32[]{:S(2)}, u32[]{:S(2)}) collective-permute-start(bf16[544,384]{1,0:T(8,128)(2,1)S(1)} %constant_dynamic-update-slice_fusion.refs_11_), channel_id=1, source_target_pairs={{0,1},{1,2},{2,3},{3,0},{4,5},{5,6},{6,7},{7,4},{8,9},{9,10},{10,1... | collective-permute-start | bytes 1253384 | tf_op jit(solution)/shard_map/ppermute | solution.py:149
  132.0 31.8 %collective-permute-start.6 = (bf16[544,384]{1,0:T(8,128)(2,1)S(1)}, bf16[544,384]{1,0:T(8,128)(2,1)S(1)}, u32[]{:S(2)}, u32[]{:S(2)}) collective-permute-start(bf16[544,384]{1,0:T(8,128)(2,1)S(1)} %constant_dynamic-update-slice_fusion.refs_11_), channel_id=1, source_target_pairs={{0,3},{1,0},{2,1},{3,2},{4,7},{5,4},{6,5},{7,6},{8,11},{9,8},{10,9... | collective-permute-start | bytes 1253384 | tf_op jit(solution)/shard_map/ppermute | solution.py:149
  136.3 27.5 %collective-permute-start.5 = (bf16[544,384]{1,0:T(8,128)(2,1)S(1)}, bf16[544,384]{1,0:T(8,128)(2,1)S(1)}, u32[]{:S(2)}, u32[]{:S(2)}) collective-permute-start(bf16[544,384]{1,0:T(8,128)(2,1)S(1)} %constant_dynamic-update-slice_fusion.refs_11_), channel_id=1, source_target_pairs={{0,2},{1,3},{2,0},{3,1},{4,6},{5,7},{6,4},{7,5},{8,10},{9,11},{10,... | collective-permute-start | bytes 1253384 | tf_op jit(solution)/shard_map/ppermute | solution.py:149
  138.5 25.4 %collective-permute-start.9 = (bf16[272,384]{1,0:T(8,128)(2,1)S(1)}, bf16[272,384]{1,0:T(8,128)(2,1)S(1)}, u32[]{:S(2)}, u32[]{:S(2)}) collective-permute-start(bf16[272,384]{1,0:T(8,128)(2,1)S(1)} %collective-permute-done.4), channel_id=1, source_target_pairs={{0,4},{1,5},{2,6},{3,7},{4,8},{5,9},{6,10},{7,11},{8,12},{9,13},{1... | collective-permute-start | bytes 626696 | tf_op jit(solution)/shard_map/ppermute | solution.py:203
  145.6 18.3 %collective-permute-start.8 = (bf16[256,384]{1,0:T(8,128)(2,1)S(1)}, bf16[256,384]{1,0:T(8,128)(2,1)S(1)}, u32[]{:S(2)}, u32[]{:S(2)}) collective-permute-start(bf16[256,384]{1,0:T(8,128)(2,1)S(1)} %slice.14), channel_id=1, source_target_pairs={{0,12},{1,13},{2,14},{3,15},{4,0},{5,1},{6,2},{7,3},{8,4},{9,5},{1... | collective-permute-start | bytes 589832 | tf_op jit(solution)/shard_map/ppermute | solution.py:202
  163.8 26.7 %copy-start.10 = (bf16[272,384]{1,0:T(8,128)(2,1)}, bf16[272,384]{1,0:T(8,128)(2,1)S(1)}, u32[]{:S(2)}) copy-start(bf16[272,384]{1,0:T(8,128)(2,1)S(1)} %collective-permute-done.9.refs_12_) | copy-start | bytes 626692
  163.8 26.7 %copy-start.7 = (bf16[544,384]{1,0:T(8,128)(2,1)}, bf16[544,384]{1,0:T(8,128)(2,1)S(1)}, u32[]{:S(2)}) copy-start(bf16[544,384]{1,0:T(8,128)(2,1)S(1)} %collective-permute-done.7.refs_8_) | copy-start | bytes 1253380
  163.8 26.7 %copy-start.8 = (bf16[544,384]{1,0:T(8,128)(2,1)}, bf16[544,384]{1,0:T(8,128)(2,1)S(1)}, u32[]{:S(2)}) copy-start(bf16[544,384]{1,0:T(8,128)(2,1)S(1)} %collective-permute-done.6.refs_5_) | copy-start | bytes 1253380
  163.9 26.7 %copy-start.9 = (bf16[544,384]{1,0:T(8,128)(2,1)}, bf16[544,384]{1,0:T(8,128)(2,1)S(1)}, u32[]{:S(2)}) copy-start(bf16[544,384]{1,0:T(8,128)(2,1)S(1)} %collective-permute-done.5.refs_2_) | copy-start | bytes 1253380
  163.9 26.7 %collective-permute-start.12 = (bf16[272,384]{1,0:T(8,128)(2,1)S(1)}, bf16[272,384]{1,0:T(8,128)(2,1)S(1)}, u32[]{:S(2)}, u32[]{:S(2)}) collective-permute-start(bf16[272,384]{1,0:T(8,128)(2,1)S(1)} %collective-permute-done.9.refs_12_), channel_id=1, source_target_pairs={{0,1},{1,2},{2,3},{3,0},{4,5},{5,6},{6,7},{7,4},{8,9},{9,10},{10,1... | collective-permute-start | bytes 626696 | tf_op jit(solution)/shard_map/ppermute | solution.py:149
  166.2 24.4 %collective-permute-start.11 = (bf16[272,384]{1,0:T(8,128)(2,1)S(1)}, bf16[272,384]{1,0:T(8,128)(2,1)S(1)}, u32[]{:S(2)}, u32[]{:S(2)}) collective-permute-start(bf16[272,384]{1,0:T(8,128)(2,1)S(1)} %collective-permute-done.9.refs_12_), channel_id=1, source_target_pairs={{0,3},{1,0},{2,1},{3,2},{4,7},{5,4},{6,5},{7,6},{8,11},{9,8},{10,9... | collective-permute-start | bytes 626696 | tf_op jit(solution)/shard_map/ppermute | solution.py:149
  170.4 21.5 %collective-permute-start.10 = (bf16[272,384]{1,0:T(8,128)(2,1)S(1)}, bf16[272,384]{1,0:T(8,128)(2,1)}, u32[]{:S(2)}, u32[]{:S(2)}) collective-permute-start(bf16[272,384]{1,0:T(8,128)(2,1)S(1)} %collective-permute-done.9.refs_12_), channel_id=1, source_target_pairs={{0,2},{1,3},{2,0},{3,1},{4,6},{5,7},{6,4},{7,5},{8,10},{9,11},{10,... | collective-permute-start | bytes 626696 | tf_op jit(solution)/shard_map/ppermute | solution.py:149
  173.8 11.3 %collective-permute-start.14 = (bf16[256,384]{1,0:T(8,128)(2,1)S(1)}, bf16[256,384]{1,0:T(8,128)(2,1)S(1)}, u32[]{:S(2)}, u32[]{:S(2)}) collective-permute-start(bf16[256,384]{1,0:T(8,128)(2,1)S(1)} %slice.14), channel_id=1, source_target_pairs={{0,4},{1,5},{2,6},{3,7},{4,8},{5,9},{6,10},{7,11},{8,12},{9,13},{1... | collective-permute-start | bytes 589832 | tf_op jit(solution)/shard_map/ppermute | solution.py:211
  177.7 12.9 %collective-permute-start.13 = (bf16[256,384]{1,0:T(8,128)(2,1)S(1)}, bf16[256,384]{1,0:T(8,128)(2,1)S(1)}, u32[]{:S(2)}, u32[]{:S(2)}) collective-permute-start(bf16[256,384]{1,0:T(8,128)(2,1)S(1)} %collective-permute-done.8), channel_id=1, source_target_pairs={{0,12},{1,13},{2,14},{3,15},{4,0},{5,1},{6,2},{7,3},{8,4},{9,5},{1... | collective-permute-start | bytes 589832 | tf_op jit(solution)/shard_map/ppermute | solution.py:210
  190.5 0.7 copy-start.11
  191.2 0.7 copy-start.12
  192.0 32.5 %copy-start.5 = (bf16[768,384]{1,0:T(8,128)(2,1)}, bf16[768,384]{1,0:T(8,128)(2,1)S(1)}, u32[]{:S(2)}) copy-start(bf16[768,384]{1,0:T(8,128)(2,1)S(1)} %constant_dynamic-update-slice_fusion.2.refs_8_) | copy-start | bytes 1769476
  192.0 23.2 %collective-permute-start.17 = (bf16[768,384]{1,0:T(8,128)(2,1)S(1)}, bf16[768,384]{1,0:T(8,128)(2,1)}, u32[]{:S(2)}, u32[]{:S(2)}) collective-permute-start(bf16[768,384]{1,0:T(8,128)(2,1)S(1)} %constant_dynamic-update-slice_fusion.2.refs_8_), channel_id=1, source_target_pairs={{0,1},{1,2},{2,3},{3,0},{4,5},{5,6},{6,7},{7,4},{8,9},{9,10},{10,1... | collective-permute-start | bytes 1769480 | tf_op jit(solution)/shard_map/ppermute | solution.py:149
  194.0 21.3 %collective-permute-start.16 = (bf16[768,384]{1,0:T(8,128)(2,1)S(1)}, bf16[768,384]{1,0:T(8,128)(2,1)}, u32[]{:S(2)}, u32[]{:S(2)}) collective-permute-start(bf16[768,384]{1,0:T(8,128)(2,1)S(1)} %constant_dynamic-update-slice_fusion.2.refs_8_), channel_id=1, source_target_pairs={{0,3},{1,0},{2,1},{3,2},{4,7},{5,4},{6,5},{7,6},{8,11},{9,8},{10,9... | collective-permute-start | bytes 1769480 | tf_op jit(solution)/shard_map/ppermute | solution.py:149
  198.5 26.0 %collective-permute-start.15 = (bf16[768,384]{1,0:T(8,128)(2,1)S(1)}, bf16[768,384]{1,0:T(8,128)(2,1)}, u32[]{:S(2)}, u32[]{:S(2)}) collective-permute-start(bf16[768,384]{1,0:T(8,128)(2,1)S(1)} %constant_dynamic-update-slice_fusion.2.refs_8_), channel_id=1, source_target_pairs={{0,2},{1,3},{2,0},{3,1},{4,6},{5,7},{6,4},{7,5},{8,10},{9,11},{10,... | collective-permute-start | bytes 1769480 | tf_op jit(solution)/shard_map/ppermute | solution.py:149
Sparse Core Ops, SparseCore 0:
  9.5 45.7 all-gather.2
  57.4 63.5 all-gather.4

commit v4 on v3

v4 whole, which is shorter than its diff:
```python
import math

import jax
import jax.numpy as jnp
from jax import lax
from jax.experimental import pallas as pl
from jax.experimental.pallas import tpu as pltpu
from jax.sharding import PartitionSpec as P

HEAD_DIM = 128
NORM_EPSILON = 1e-06
Z_PARTS, Y_PARTS = 4, 4
GAIN_ROWS = 16
ROW_TILE = 16


def z_shift(step):
    return [
        (z * Y_PARTS + y, (z + step) % Z_PARTS * Y_PARTS + y)
        for z in range(Z_PARTS)
        for y in range(Y_PARTS)
    ]


def y_shift(step):
    return [
        (z * Y_PARTS + y, z * Y_PARTS + (y + step) % Y_PARTS)
        for z in range(Z_PARTS)
        for y in range(Y_PARTS)
    ]


def dp_groups(varying):
    groups = {}
    for x in range(4):
        for z in range(4):
            for core in range(2):
                key = tuple(v for name, v in (("x", x), ("z", z), ("c", core)) if name not in varying)
                groups.setdefault(key, []).append(x * 8 + z * 2 + core)
    return list(groups.values())


def load_weights(source_ref, weight_ref, sem, strip):
    copies = []
    for x in range(4):
        for z in range(4):
            for core in range(2):
                held, wanted = (x * 2 + core) * 4 + z, x * 8 + z * 2 + core
                copies.append(
                    pltpu.make_async_copy(
                        source_ref.at[pl.ds(held * strip, strip), :],
                        weight_ref.at[pl.ds(wanted * strip, strip), :],
                        sem,
                    )
                )
    for copy in copies:
        copy.start()
    return copies


def slot_columns(places_ref, count, width):
    return [pl.ds(pl.multiple_of(places_ref[j] * width, 128), width) for j in range(count)]


def normalize(sources, gains, columns, first, last, normed_ref):
    features = normed_ref.shape[1]

    def step(i, carry):
        at = pl.multiple_of(first + i * ROW_TILE, ROW_TILE)

        def load(j):
            ref, shift = sources[j]
            return ref[pl.ds(at + shift, ROW_TILE), :].astype(jnp.float32)

        total = load(0)
        for j in range(1, len(sources)):
            total = total + load(j)
        mean = jnp.sum(total, axis=1, keepdims=True) * (1.0 / features)
        square = jnp.square(load(0) - mean)
        for j in range(1, len(sources)):
            square = square + jnp.square(load(j) - mean)
        var = jnp.sum(square, axis=1, keepdims=True) * (1.0 / features)
        scale = lax.rsqrt(var + NORM_EPSILON)
        for j in range(len(sources)):
            normed_ref[pl.ds(at, ROW_TILE), columns[j]] = (
                (load(j) - mean) * scale * gains[j]
            ).astype(jnp.bfloat16)
        return carry

    lax.fori_loop(0, (last - first) // ROW_TILE, step, 0)


def project_attend_kernel(slots, count, rows, cut, strip, *refs):
    places_ref, blocks = refs[0], refs[1 : 1 + count]
    source_ref, seg_col_ref, seg_row_ref, out_ref = refs[1 + count : 5 + count]
    normed_ref, weight_ref, sums_ref, sem = refs[5 + count :]
    copies = load_weights(source_ref, weight_ref, sem, strip)
    columns = slot_columns(places_ref, len(slots), blocks[0].shape[1])

    def part(pieces, row):
        for ref, start, first, last in pieces:
            if first <= row < last:
                return blocks[ref], start - first

    gains = []
    for pieces in slots:
        ref, shift = part(pieces, rows)
        gains.append(ref[pl.ds(rows + shift, GAIN_ROWS), :][:1].astype(jnp.float32))
    for first, last in ((0, cut), (cut, rows)):
        sources = [part(pieces, first) for pieces in slots]
        normalize(sources, gains, columns, first, last, normed_ref)
    for copy in copies:
        copy.wait()
    sums_ref[...] = jnp.dot(
        normed_ref[...], weight_ref[...], preferred_element_type=jnp.float32
    ).astype(jnp.bfloat16)
    local = out_ref.shape[1]
    span, window = 128, 256
    for row in range(0, rows, span):
        low = min(max(row - (window - span) // 2, 0), rows - window)
        same = seg_col_ref[row : row + span, :1] == seg_row_ref[:1, low : low + window]
        for col in range(0, local, HEAD_DIM):
            query = sums_ref[row : row + span, col : col + HEAD_DIM]
            key = sums_ref[low : low + window, local + col : local + col + HEAD_DIM]
            value = sums_ref[low : low + window, 2 * local + col : 2 * local + col + HEAD_DIM]
            scores = lax.dot_general(
                query, key, (((1,), (1,)), ((), ())), preferred_element_type=jnp.float32
            ) * (1.0 / math.sqrt(HEAD_DIM))
            scores = jnp.where(same, scores, -jnp.inf)
            expo = jnp.exp(scores - jnp.max(scores, axis=1, keepdims=True))
            probs = (expo / jnp.sum(expo, axis=1, keepdims=True)).astype(jnp.bfloat16)
            out_ref[row : row + span, col : col + HEAD_DIM] = jnp.dot(
                probs, value, preferred_element_type=jnp.float32
            ).astype(jnp.bfloat16)


def shards(page_patches, gain, q_weight, k_weight, v_weight, pack_lengths, line_order):
    groups = lax.axis_size("dp")
    page_index = lax.axis_index("dp")
    width = page_patches.shape[1]
    slot_rows = page_patches.shape[0] // groups
    rows = slot_rows * groups // 2
    local = q_weight.shape[1]
    strip = q_weight.shape[0]
    weight = jnp.concatenate([q_weight, k_weight, v_weight], axis=1)
    weight = lax.all_gather(weight, "dp", axis=0, tiled=True, axis_index_groups=dp_groups("z"))
    targets = jnp.arange(groups, dtype=jnp.int32)
    my_order = lax.dynamic_index_in_dim(line_order, page_index, 0, keepdims=False)
    slot_for = jnp.sum(
        jnp.where(my_order[None, :] == targets[:, None], targets[None, :], 0), axis=1
    )
    slots = page_patches.reshape(groups, slot_rows, width)
    outgoing = jnp.take(slots, slot_for, axis=0)
    incoming = lax.all_to_all(outgoing, "dp", split_axis=0, concat_axis=0, tiled=True)
    my_lengths = lax.dynamic_index_in_dim(pack_lengths, page_index, 0, keepdims=False)
    line_ends = jnp.cumsum(my_lengths)
    line_starts = line_ends - my_lengths
    row_ids = jnp.arange(rows, dtype=jnp.int32)
    segment = jnp.sum((line_ends[None, :] <= row_ids[:, None]).astype(jnp.int32), axis=1)
    start_of_row = jnp.sum(
        jnp.where(segment[:, None] == targets[None, :], line_starts[None, :], 0), axis=1
    )
    source_rows = segment * slot_rows + row_ids - start_of_row
    packed = jnp.take(incoming.reshape(groups * slot_rows, width), source_rows, axis=0)

    own = jnp.concatenate([packed, jnp.broadcast_to(gain[None, :], (GAIN_ROWS, width))], axis=0)
    all_rows = rows + GAIN_ROWS
    cut = rows // 2 + GAIN_ROWS

    def along_y(block, step):
        return lax.ppermute(block, "tensor", y_shift(step))

    def along_z(block, step):
        return lax.ppermute(block, "tensor", z_shift(step))

    own_far, own_down, own_up, z_down, z_up, weight = lax.optimization_barrier(
        (
            along_y(own, 2),
            along_y(own, -1),
            along_y(own, 1),
            along_z(own, -1),
            along_z(own, 1),
            weight,
        )
    )
    weight = lax.all_gather(weight, "dp", axis=0, tiled=True, axis_index_groups=dp_groups("xc"))
    pair = jnp.concatenate([z_up, z_down], axis=0)
    pair_down, pair_up, far_rest, far_top = lax.optimization_barrier(
        (along_y(pair, -1), along_y(pair, 1), along_z(z_down[cut:], -1), along_z(z_up[:cut], 1))
    )
    far = jnp.concatenate([far_top, far_rest], axis=0)
    far_far, far_down, far_up = along_y(far, 2), along_y(far, -1), along_y(far, 1)
    pair_far_up = along_y(pair_up[:all_rows], 1)
    pair_far_down = along_y(pair_down[all_rows:], -1)

    blocks, slots_at, shifts = [], [], []

    def add(array, dy, *dzs):
        blocks.append(array)
        for k, dz in enumerate(dzs):
            slots_at.append(((len(blocks) - 1, k * all_rows, 0, all_rows),))
            shifts.append((dz, dy))

    add(own, 0, 0)
    add(own_up, -1, 0)
    add(own_down, 1, 0)
    add(own_far, 2, 0)
    add(pair, 0, -1, 1)
    add(pair_up, -1, -1, 1)
    add(pair_down, 1, -1, 1)
    add(pair_far_up, 2, -1)
    add(pair_far_down, 2, 1)
    add(far, 0, 2)
    add(far_up, -1, 2)
    add(far_down, 1, 2)
    add(far_far, 2, 2)
    tensor = lax.axis_index("tensor")
    my_z, my_y = tensor // Y_PARTS, tensor % Y_PARTS
    step_z = jnp.array([dz for dz, _ in shifts], jnp.int32)
    step_y = jnp.array([dy for _, dy in shifts], jnp.int32)
    places = (my_z + step_z + Z_PARTS) % Z_PARTS * Y_PARTS + (my_y + step_y + Y_PARTS) % Y_PARTS

    def kernel(*refs):
        project_attend_kernel(slots_at, len(blocks), rows, cut, strip, *refs)

    features = width * len(slots_at)
    vmem = pl.BlockSpec(memory_space=pltpu.VMEM)
    smem, hbm = pl.BlockSpec(memory_space=pltpu.SMEM), pl.BlockSpec(memory_space=pl.ANY)
    return pl.pallas_call(
        kernel,
        out_shape=jax.ShapeDtypeStruct((rows, local), jnp.bfloat16),
        in_specs=[smem] + [vmem] * len(blocks) + [hbm, vmem, vmem],
        out_specs=vmem,
        scratch_shapes=[
            pltpu.VMEM((rows, features), jnp.bfloat16),
            pltpu.VMEM((features, 3 * local), jnp.bfloat16),
            pltpu.VMEM((rows, 3 * local), jnp.bfloat16),
            pltpu.SemaphoreType.DMA,
        ],
        name="norm_project_attend",
    )(places, *blocks, weight, segment[:, None], segment[None, :])


def solution(mesh):
    return jax.shard_map(
        shards,
        mesh=mesh,
        in_specs=(
            P("dp", "tensor"),
            P("tensor"),
            P("dp", "tensor"),
            P("dp", "tensor"),
            P("dp", "tensor"),
            P(),
            P(),
        ),
        out_specs=P("dp", "tensor"),
        check_vma=False,
    )
```

time: 248 us -> 203 us (0.82)
  the two profiles are of different devices: /device:TPU:1 before, /device:TPU:36 now
where the time goes in v4:
time: 203 us
  waiting for transfers between devices  88.3 us (43%)
  starting transfers between devices  63.5 us (31%)
  Pallas kernels  20.9 us (10%)
  between operations  13.8 us (7%)
  local copies, waits for them, and re-layouts  11.4 us (6%)
  other arithmetic  4.71 us (2%)
    ppermute x10, starting transfers between devices, along_y(): return lax.ppermute(block, 'tensor', y_shift(step))  33.2 us
    ppermute x4, waiting for transfers between devices, along_z(): return lax.ppermute(block, 'tensor', z_shift(step))  30.3 us
    all_gather x2, waiting for transfers between devices, shards(): lax.all_gather(weight, 'dp', axis=0, tiled=True, axis_index_groups=dp_gro...  25.6 us
    ppermute x4, starting transfers between devices, along_z(): return lax.ppermute(block, 'tensor', z_shift(step))  21.1 us
    pallas_call x1, Pallas kernels, shards(): pl.pallas_call(kernel, out_shape=jax.ShapeDtypeStruct((rows, local), jnp....  20.9 us
    ppermute x10, waiting for transfers between devices, along_y(): return lax.ppermute(block, 'tensor', y_shift(step))  17.1 us
    all_to_all x1, waiting for transfers between devices, shards(): lax.all_to_all(outgoing, 'dp', split_axis=0, concat_axis=0, tiled=True)  15.3 us
    all_to_all x1, starting transfers between devices, shards(): lax.all_to_all(outgoing, 'dp', split_axis=0, concat_axis=0, tiled=True)  9.1 us
  transfers between devices with their start and end apart: 17, of which 8 were waited for; matrix products, arithmetic and copies ran while one was open for 6% of the time, Pallas kernels for 0%

profile of v4, /device:TPU:36, one launch (start us, length us, event | category | flops | bytes accessed | tf_op | source)
XLA Modules:
  0.0 202.7 jit_solution(2554823750875824685)
XLA Ops:
  6.5 0.8 dynamic-slice_bitcast_fusion
  7.3 0.1 select_reduce_fusion.1
  7.5 0.2 copy-done
  7.7 0.7 gather_fusion
  8.4 1.0 broadcast_select_fusion
  9.5 9.1 %all-to-all-start = ((bf16[32,32,384]{2,1,0:T(8,128)(2,1)}), bf16[32,32,384]{2,1,0:T(8,128)(2,1)S(1)}, u32[]{:S(2)}, u32[]{:S(2)}) async-start(bf16[32,32,384]{2,1,0:T(8,128)(2,1)} %broadcast_select_fusion), calls=%async_computation | async-start | bytes 1572864 | tf_op jit(solution)/shard_map/all_to_all | solution.py:154
  18.6 1.7 pad_maximum_fusion.1
  20.4 0.7 fusion.6
  21.1 0.1 copy.13
  21.3 0.1 reduce
  21.4 0.1 convert_reduce_fusion
  21.5 0.7 fusion.5
  22.2 0.1 select_reduce_fusion
  22.3 15.3 %all-to-all-done = bf16[32,32,384]{2,1,0:T(8,128)(2,1)S(1)} async-done(((bf16[32,32,384]{2,1,0:T(8,128)(2,1)}), bf16[32,32,384]{2,1,0:T(8,128)(2,1)S(1)}, u32[]{:S(2)}, u32[]{:S(2)}) %all-to-all-start) | async-done | bytes 786464 | tf_op jit(solution)/shard_map/all_to_all | solution.py:154
  37.7 1.9 gather_fusion.1
  39.6 0.1 broadcast_select_fusion.1
  39.8 8.6 %collective-permute-start.4 = (bf16[528,384]{1,0:T(8,128)(2,1)S(1)}, bf16[528,384]{1,0:T(8,128)(2,1)S(1)}, u32[]{:S(2)}, u32[]{:S(2)}) collective-permute-start(bf16[528,384]{1,0:T(8,128)(2,1)S(1)} %pad_maximum_fusion.refs_1_), channel_id=1, source_target_pairs={{0,4},{1,5},{2,6},{3,7},{4,8},{5,9},{6,10},{7,11},{8,12},{9,13},{1... | collective-permute-start | bytes 1216520 | tf_op jit(solution)/shard_map/ppermute | solution.py:174
  48.4 2.9 %collective-permute-start.3 = (bf16[528,384]{1,0:T(8,128)(2,1)S(1)}, bf16[528,384]{1,0:T(8,128)(2,1)S(1)}, u32[]{:S(2)}, u32[]{:S(2)}) collective-permute-start(bf16[528,384]{1,0:T(8,128)(2,1)S(1)} %pad_maximum_fusion.refs_1_), channel_id=1, source_target_pairs={{0,12},{1,13},{2,14},{3,15},{4,0},{5,1},{6,2},{7,3},{8,4},{9,5},{1... | collective-permute-start | bytes 1216520 | tf_op jit(solution)/shard_map/ppermute | solution.py:174
  51.3 3.5 %collective-permute-start.2 = (bf16[528,384]{1,0:T(8,128)(2,1)S(1)}, bf16[528,384]{1,0:T(8,128)(2,1)S(1)}, u32[]{:S(2)}, u32[]{:S(2)}) collective-permute-start(bf16[528,384]{1,0:T(8,128)(2,1)S(1)} %pad_maximum_fusion.refs_1_), channel_id=1, source_target_pairs={{0,1},{1,2},{2,3},{3,0},{4,5},{5,6},{6,7},{7,4},{8,9},{9,10},{10,1... | collective-permute-start | bytes 1216520 | tf_op jit(solution)/shard_map/ppermute | solution.py:171
  54.8 3.6 %collective-permute-start.1 = (bf16[528,384]{1,0:T(8,128)(2,1)S(1)}, bf16[528,384]{1,0:T(8,128)(2,1)S(1)}, u32[]{:S(2)}, u32[]{:S(2)}) collective-permute-start(bf16[528,384]{1,0:T(8,128)(2,1)S(1)} %pad_maximum_fusion.refs_1_), channel_id=1, source_target_pairs={{0,3},{1,0},{2,1},{3,2},{4,7},{5,4},{6,5},{7,6},{8,11},{9,8},{10,9... | collective-permute-start | bytes 1216520 | tf_op jit(solution)/shard_map/ppermute | solution.py:171
  58.3 3.9 %collective-permute-start = (bf16[528,384]{1,0:T(8,128)(2,1)S(1)}, bf16[528,384]{1,0:T(8,128)(2,1)S(1)}, u32[]{:S(2)}, u32[]{:S(2)}) collective-permute-start(bf16[528,384]{1,0:T(8,128)(2,1)S(1)} %pad_maximum_fusion.refs_1_), channel_id=1, source_target_pairs={{0,2},{1,3},{2,0},{3,1},{4,6},{5,7},{6,4},{7,5},{8,10},{9,11},{10,... | collective-permute-start | bytes 1216520 | tf_op jit(solution)/shard_map/ppermute | solution.py:171
  62.2 25.6 %all-gather.3.cloned.1.call-done = bf16[768,768]{1,0:T(8,128)(2,1)} async-done(((bf16[192,768]{1,0:T(8,128)(2,1)}), bf16[768,768]{1,0:T(8,128)(2,1)}) %all-gather.3.cloned.1.call-update) | async-done | bytes 1179664 | tf_op jit(solution)/shard_map/all_gather | solution.py:146
  87.9 10.1 %collective-permute-done.4 = bf16[528,384]{1,0:T(8,128)(2,1)S(1)} collective-permute-done((bf16[528,384]{1,0:T(8,128)(2,1)S(1)}, bf16[528,384]{1,0:T(8,128)(2,1)S(1)}, u32[]{:S(2)}, u32[]{:S(2)}) %collective-permute-start.4) | collective-permute-done | bytes 405536 | tf_op jit(solution)/shard_map/ppermute | solution.py:174
  98.0 2.9 %collective-permute-done.3 = bf16[528,384]{1,0:T(8,128)(2,1)S(1)} collective-permute-done((bf16[528,384]{1,0:T(8,128)(2,1)S(1)}, bf16[528,384]{1,0:T(8,128)(2,1)S(1)}, u32[]{:S(2)}, u32[]{:S(2)}) %collective-permute-start.3) | collective-permute-done | bytes 405536 | tf_op jit(solution)/shard_map/ppermute | solution.py:174
  100.9 0.7 copy-done.7
  101.7 0.1 copy-done.8
  102.1 3.4 %collective-permute-start.6 = (bf16[1056,384]{1,0:T(8,128)(2,1)S(1)}, bf16[1056,384]{1,0:T(8,128)(2,1)S(1)}, u32[]{:S(2)}, u32[]{:S(2)}) collective-permute-start(bf16[1056,384]{1,0:T(8,128)(2,1)S(1)} %constant_dynamic-update-slice_fusion.refs_5_), channel_id=1, source_target_pairs={{0,1},{1,2},{2,3},{3,0},{4,5},{5,6},{6,7},{7,4},{8,9},{9,10},{10,1... | collective-permute-start | bytes 2433032 | tf_op jit(solution)/shard_map/ppermute | solution.py:171
  105.4 3.7 %collective-permute-start.5 = (bf16[1056,384]{1,0:T(8,128)(2,1)S(1)}, bf16[1056,384]{1,0:T(8,128)(2,1)S(1)}, u32[]{:S(2)}, u32[]{:S(2)}) collective-permute-start(bf16[1056,384]{1,0:T(8,128)(2,1)S(1)} %constant_dynamic-update-slice_fusion.refs_5_), channel_id=1, source_target_pairs={{0,3},{1,0},{2,1},{3,2},{4,7},{5,4},{6,5},{7,6},{8,11},{9,8},{10,9... | collective-permute-start | bytes 2433032 | tf_op jit(solution)/shard_map/ppermute | solution.py:171
  109.1 1.0 slice.13
  110.1 6.7 %collective-permute-start.8 = (bf16[272,384]{1,0:T(8,128)(2,1)S(1)}, bf16[272,384]{1,0:T(8,128)(2,1)S(1)}, u32[]{:S(2)}, u32[]{:S(2)}) collective-permute-start(bf16[272,384]{1,0:T(8,128)(2,1)S(1)} %slice.13), channel_id=1, source_target_pairs={{0,4},{1,5},{2,6},{3,7},{4,8},{5,9},{6,10},{7,11},{8,12},{9,13},{1... | collective-permute-start | bytes 626696 | tf_op jit(solution)/shard_map/ppermute | solution.py:174
  116.8 1.0 slice.12
  117.8 3.0 %collective-permute-start.7 = (bf16[256,384]{1,0:T(8,128)(2,1)S(1)}, bf16[256,384]{1,0:T(8,128)(2,1)S(1)}, u32[]{:S(2)}, u32[]{:S(2)}) collective-permute-start(bf16[256,384]{1,0:T(8,128)(2,1)S(1)} %slice.12), channel_id=1, source_target_pairs={{0,12},{1,13},{2,14},{3,15},{4,0},{5,1},{6,2},{7,3},{8,4},{9,5},{1... | collective-permute-start | bytes 589832 | tf_op jit(solution)/shard_map/ppermute | solution.py:174
  120.8 17.2 %collective-permute-done.7 = bf16[256,384]{1,0:T(8,128)(2,1)S(1)} collective-permute-done((bf16[256,384]{1,0:T(8,128)(2,1)S(1)}, bf16[256,384]{1,0:T(8,128)(2,1)S(1)}, u32[]{:S(2)}, u32[]{:S(2)}) %collective-permute-start.7) | collective-permute-done | bytes 196640 | tf_op jit(solution)/shard_map/ppermute | solution.py:174
  138.1 0.9 slice.14
  138.9 0.8 slice.15
  139.7 3.4 %collective-permute-start.10 = (bf16[528,384]{1,0:T(8,128)(2,1)}, bf16[528,384]{1,0:T(8,128)(2,1)}, u32[]{:S(2)}, u32[]{:S(2)}) collective-permute-start(bf16[528,384]{1,0:T(8,128)(2,1)} %slice.15), channel_id=1, source_target_pairs={{0,3},{1,0},{2,1},{3,2},{4,7},{5,4},{6,5},{7,6},{8,11},{9,8},{10,9... | collective-permute-start | bytes 1216520 | tf_op jit(solution)/shard_map/ppermute | solution.py:171
  143.1 2.5 %collective-permute-start.9 = (bf16[528,384]{1,0:T(8,128)(2,1)}, bf16[528,384]{1,0:T(8,128)(2,1)}, u32[]{:S(2)}, u32[]{:S(2)}) collective-permute-start(bf16[528,384]{1,0:T(8,128)(2,1)} %slice.14), channel_id=1, source_target_pairs={{0,1},{1,2},{2,3},{3,0},{4,5},{5,6},{6,7},{7,4},{8,9},{9,10},{10,1... | collective-permute-start | bytes 1216520 | tf_op jit(solution)/shard_map/ppermute | solution.py:171
  145.6 0.7 constant_dynamic-update-slice_fusion.3
  146.3 0.7 constant_dynamic-update-slice_fusion.2.refs_10_
  147.0 3.6 %collective-permute-start.13 = (bf16[528,384]{1,0:T(8,128)(2,1)}, bf16[528,384]{1,0:T(8,128)(2,1)}, u32[]{:S(2)}, u32[]{:S(2)}) collective-permute-start(bf16[528,384]{1,0:T(8,128)(2,1)} %constant_dynamic-update-slice_fusion.2.refs_10_), channel_id=1, source_target_pairs={{0,2},{1,3},{2,0},{3,1},{4,6},{5,7},{6,4},{7,5},{8,10},{9,11},{10,... | collective-permute-start | bytes 1216520 | tf_op jit(solution)/shard_map/ppermute | solution.py:171
  150.6 3.2 %collective-permute-start.12 = (bf16[528,384]{1,0:T(8,128)(2,1)}, bf16[528,384]{1,0:T(8,128)(2,1)}, u32[]{:S(2)}, u32[]{:S(2)}) collective-permute-start(bf16[528,384]{1,0:T(8,128)(2,1)} %constant_dynamic-update-slice_fusion.2.refs_10_), channel_id=1, source_target_pairs={{0,3},{1,0},{2,1},{3,2},{4,7},{5,4},{6,5},{7,6},{8,11},{9,8},{10,9... | collective-permute-start | bytes 1216520 | tf_op jit(solution)/shard_map/ppermute | solution.py:171
  153.7 2.7 %collective-permute-start.11 = (bf16[528,384]{1,0:T(8,128)(2,1)}, bf16[528,384]{1,0:T(8,128)(2,1)}, u32[]{:S(2)}, u32[]{:S(2)}) collective-permute-start(bf16[528,384]{1,0:T(8,128)(2,1)} %constant_dynamic-update-slice_fusion.2.refs_10_), channel_id=1, source_target_pairs={{0,1},{1,2},{2,3},{3,0},{4,5},{5,6},{6,7},{7,4},{8,9},{9,10},{10,1... | collective-permute-start | bytes 1216520 | tf_op jit(solution)/shard_map/ppermute | solution.py:171
  156.4 0.9 copy.14.refs_15_
  157.3 0.5 fusion.refs_0_
  157.8 9.2 %collective-permute-done.9.refs_8_ = bf16[528,384]{1,0:T(8,128)(2,1)} collective-permute-done((bf16[528,384]{1,0:T(8,128)(2,1)}, bf16[528,384]{1,0:T(8,128)(2,1)}, u32[]{:S(2)}, u32[]{:S(2)}) %collective-permute-start.9) | collective-permute-done | bytes 405536 | tf_op jit(solution)/shard_map/ppermute | solution.py:171
  167.1 3.6 %collective-permute-done.12.refs_12_ = bf16[528,384]{1,0:T(8,128)(2,1)} collective-permute-done((bf16[528,384]{1,0:T(8,128)(2,1)}, bf16[528,384]{1,0:T(8,128)(2,1)}, u32[]{:S(2)}, u32[]{:S(2)}) %collective-permute-start.12) | collective-permute-done | bytes 405536 | tf_op jit(solution)/shard_map/ppermute | solution.py:171
  170.6 4.3 %collective-permute-done.11.refs_11_ = bf16[528,384]{1,0:T(8,128)(2,1)} collective-permute-done((bf16[528,384]{1,0:T(8,128)(2,1)}, bf16[528,384]{1,0:T(8,128)(2,1)}, u32[]{:S(2)}, u32[]{:S(2)}) %collective-permute-start.11) | collective-permute-done | bytes 405536 | tf_op jit(solution)/shard_map/ppermute | solution.py:171
  174.9 20.9 %norm_project_attend.1 = bf16[512,256]{1,0:T(8,128)(2,1)} custom-call(s32[16]{0:T(128)} %fusion.refs_0_, bf16[528,384]{1,0:T(8,128)(2,1)} %copy-done.4, bf16[528,384]{1,0:T(8,128)(2,1)} %copy-done.7, bf16[528,384]{1,0:T(8,128)(2,1)} %copy-done.8, bf16[528,384]{1,0:T(8,128)(2,1)} %copy-done.9, bf16[1056,384]{1,0:T(8,128)(2,1)} %copy-done.3, ...), custom_call_target="tpu_custom_call" | custom-call | tf_op jit(solution)/shard_map/norm_project_attend/pallas_call | solution.py:229
  (49 shorter events, 0.5 us)
Async XLA Ops:
  6.5 1.2 copy-start
  6.5 150.8 %copy-start.12 = (s32[16]{0:T(128)S(1)}, s32[16]{0:T(128)}, u32[]{:S(2)}) copy-start(s32[16]{0:T(128)} %constant.94.clone) | copy-start | bytes 196
  6.5 150.8 %copy-start.13 = (s32[16]{0:T(128)S(1)}, s32[16]{0:T(128)}, u32[]{:S(2)}) copy-start(s32[16]{0:T(128)} %constant.93.clone) | copy-start | bytes 196
  6.5 33.2 %copy-start.11 = (bf16[384]{0:T(512)(128)(2,1)S(1)}, bf16[384]{0:T(512)(128)(2,1)}, u32[]{:S(2)}) copy-start(bf16[384]{0:T(512)(128)(2,1)} %param.10) | copy-start | bytes 2308
  9.5 28.2 %all-to-all-start = ((bf16[32,32,384]{2,1,0:T(8,128)(2,1)}), bf16[32,32,384]{2,1,0:T(8,128)(2,1)S(1)}, u32[]{:S(2)}, u32[]{:S(2)}) async-start(bf16[32,32,384]{2,1,0:T(8,128)(2,1)} %broadcast_select_fusion), calls=%async_computation | async-start | bytes 1572864 | tf_op jit(solution)/shard_map/all_to_all | solution.py:154
  18.6 69.3 %all-gather.3.cloned.1.call-start = ((), (), s32[]{:S(2)}) async-start(), calls=%async_computation.1 | async-start | bytes 1474560 | tf_op jit(solution)/shard_map/all_gather | solution.py:146
  20.4 154.5 %all-gather.5.cloned.1.call-start = ((), (), s32[]{:S(2)}) async-start(), calls=%async_computation.2 | async-start | bytes 10616832 | tf_op jit(solution)/shard_map/all_gather | solution.py:186
  21.5 153.4 %copy-start.10 = (s32[512]{0:T(512)}, s32[512]{0:T(512)S(1)}, u32[]{:S(2)}) copy-start(s32[512]{0:T(512)S(1)} %convert_reduce_fusion) | copy-start | bytes 6148
  39.8 62.1 %copy-start.4 = (bf16[528,384]{1,0:T(8,128)(2,1)}, bf16[528,384]{1,0:T(8,128)(2,1)S(1)}, u32[]{:S(2)}) copy-start(bf16[528,384]{1,0:T(8,128)(2,1)S(1)} %pad_maximum_fusion.refs_1_) | copy-start | bytes 1216516
  39.8 58.1 %collective-permute-start.4 = (bf16[528,384]{1,0:T(8,128)(2,1)S(1)}, bf16[528,384]{1,0:T(8,128)(2,1)S(1)}, u32[]{:S(2)}, u32[]{:S(2)}) collective-permute-start(bf16[528,384]{1,0:T(8,128)(2,1)S(1)} %pad_maximum_fusion.refs_1_), channel_id=1, source_target_pairs={{0,4},{1,5},{2,6},{3,7},{4,8},{5,9},{6,10},{7,11},{8,12},{9,13},{1... | collective-permute-start | bytes 1216520 | tf_op jit(solution)/shard_map/ppermute | solution.py:174
  48.4 52.5 %collective-permute-start.3 = (bf16[528,384]{1,0:T(8,128)(2,1)S(1)}, bf16[528,384]{1,0:T(8,128)(2,1)S(1)}, u32[]{:S(2)}, u32[]{:S(2)}) collective-permute-start(bf16[528,384]{1,0:T(8,128)(2,1)S(1)} %pad_maximum_fusion.refs_1_), channel_id=1, source_target_pairs={{0,12},{1,13},{2,14},{3,15},{4,0},{5,1},{6,2},{7,3},{8,4},{9,5},{1... | collective-permute-start | bytes 1216520 | tf_op jit(solution)/shard_map/ppermute | solution.py:174
  51.3 49.6 %collective-permute-start.2 = (bf16[528,384]{1,0:T(8,128)(2,1)S(1)}, bf16[528,384]{1,0:T(8,128)(2,1)S(1)}, u32[]{:S(2)}, u32[]{:S(2)}) collective-permute-start(bf16[528,384]{1,0:T(8,128)(2,1)S(1)} %pad_maximum_fusion.refs_1_), channel_id=1, source_target_pairs={{0,1},{1,2},{2,3},{3,0},{4,5},{5,6},{6,7},{7,4},{8,9},{9,10},{10,1... | collective-permute-start | bytes 1216520 | tf_op jit(solution)/shard_map/ppermute | solution.py:171
  54.8 46.1 %collective-permute-start.1 = (bf16[528,384]{1,0:T(8,128)(2,1)S(1)}, bf16[528,384]{1,0:T(8,128)(2,1)S(1)}, u32[]{:S(2)}, u32[]{:S(2)}) collective-permute-start(bf16[528,384]{1,0:T(8,128)(2,1)S(1)} %pad_maximum_fusion.refs_1_), channel_id=1, source_target_pairs={{0,3},{1,0},{2,1},{3,2},{4,7},{5,4},{6,5},{7,6},{8,11},{9,8},{10,9... | collective-permute-start | bytes 1216520 | tf_op jit(solution)/shard_map/ppermute | solution.py:171
  58.3 42.6 %collective-permute-start = (bf16[528,384]{1,0:T(8,128)(2,1)S(1)}, bf16[528,384]{1,0:T(8,128)(2,1)S(1)}, u32[]{:S(2)}, u32[]{:S(2)}) collective-permute-start(bf16[528,384]{1,0:T(8,128)(2,1)S(1)} %pad_maximum_fusion.refs_1_), channel_id=1, source_target_pairs={{0,2},{1,3},{2,0},{3,1},{4,6},{5,7},{6,4},{7,5},{8,10},{9,11},{10,... | collective-permute-start | bytes 1216520 | tf_op jit(solution)/shard_map/ppermute | solution.py:171
  98.0 3.9 %copy-start.5 = (bf16[528,384]{1,0:T(8,128)(2,1)}, bf16[528,384]{1,0:T(8,128)(2,1)S(1)}, u32[]{:S(2)}) copy-start(bf16[528,384]{1,0:T(8,128)(2,1)S(1)} %collective-permute-done.4) | copy-start | bytes 1216516
  100.9 1.1 copy-start.6
  100.9 0.8 copy-start.7
  100.9 0.9 copy-start.8
  100.9 1.1 copy-start.9
  102.0 72.9 %copy-start.3 = (bf16[1056,384]{1,0:T(8,128)(2,1)}, bf16[1056,384]{1,0:T(8,128)(2,1)S(1)}, u32[]{:S(2)}) copy-start(bf16[1056,384]{1,0:T(8,128)(2,1)S(1)} %constant_dynamic-update-slice_fusion.refs_5_) | copy-start | bytes 2433028
  102.1 36.0 %collective-permute-start.6 = (bf16[1056,384]{1,0:T(8,128)(2,1)S(1)}, bf16[1056,384]{1,0:T(8,128)(2,1)S(1)}, u32[]{:S(2)}, u32[]{:S(2)}) collective-permute-start(bf16[1056,384]{1,0:T(8,128)(2,1)S(1)} %constant_dynamic-update-slice_fusion.refs_5_), channel_id=1, source_target_pairs={{0,1},{1,2},{2,3},{3,0},{4,5},{5,6},{6,7},{7,4},{8,9},{9,10},{10,1... | collective-permute-start | bytes 2433032 | tf_op jit(solution)/shard_map/ppermute | solution.py:171
  105.4 32.6 %collective-permute-start.5 = (bf16[1056,384]{1,0:T(8,128)(2,1)S(1)}, bf16[1056,384]{1,0:T(8,128)(2,1)S(1)}, u32[]{:S(2)}, u32[]{:S(2)}) collective-permute-start(bf16[1056,384]{1,0:T(8,128)(2,1)S(1)} %constant_dynamic-update-slice_fusion.refs_5_), channel_id=1, source_target_pairs={{0,3},{1,0},{2,1},{3,2},{4,7},{5,4},{6,5},{7,6},{8,11},{9,8},{10,9... | collective-permute-start | bytes 2433032 | tf_op jit(solution)/shard_map/ppermute | solution.py:171
  110.1 28.0 %collective-permute-start.8 = (bf16[272,384]{1,0:T(8,128)(2,1)S(1)}, bf16[272,384]{1,0:T(8,128)(2,1)S(1)}, u32[]{:S(2)}, u32[]{:S(2)}) collective-permute-start(bf16[272,384]{1,0:T(8,128)(2,1)S(1)} %slice.13), channel_id=1, source_target_pairs={{0,4},{1,5},{2,6},{3,7},{4,8},{5,9},{6,10},{7,11},{8,12},{9,13},{1... | collective-permute-start | bytes 626696 | tf_op jit(solution)/shard_map/ppermute | solution.py:174
  117.8 20.2 %collective-permute-start.7 = (bf16[256,384]{1,0:T(8,128)(2,1)S(1)}, bf16[256,384]{1,0:T(8,128)(2,1)S(1)}, u32[]{:S(2)}, u32[]{:S(2)}) collective-permute-start(bf16[256,384]{1,0:T(8,128)(2,1)S(1)} %slice.12), channel_id=1, source_target_pairs={{0,12},{1,13},{2,14},{3,15},{4,0},{5,1},{6,2},{7,3},{8,4},{9,5},{1... | collective-permute-start | bytes 589832 | tf_op jit(solution)/shard_map/ppermute | solution.py:174
  138.0 36.9 %copy-start.1 = (bf16[1056,384]{1,0:T(8,128)(2,1)}, bf16[1056,384]{1,0:T(8,128)(2,1)S(1)}, u32[]{:S(2)}) copy-start(bf16[1056,384]{1,0:T(8,128)(2,1)S(1)} %collective-permute-done.6.refs_6_) | copy-start | bytes 2433028
  138.1 36.9 %copy-start.2 = (bf16[1056,384]{1,0:T(8,128)(2,1)}, bf16[1056,384]{1,0:T(8,128)(2,1)S(1)}, u32[]{:S(2)}) copy-start(bf16[1056,384]{1,0:T(8,128)(2,1)S(1)} %collective-permute-done.5.refs_7_) | copy-start | bytes 2433028
  139.7 18.1 %collective-permute-start.10 = (bf16[528,384]{1,0:T(8,128)(2,1)}, bf16[528,384]{1,0:T(8,128)(2,1)}, u32[]{:S(2)}, u32[]{:S(2)}) collective-permute-start(bf16[528,384]{1,0:T(8,128)(2,1)} %slice.15), channel_id=1, source_target_pairs={{0,3},{1,0},{2,1},{3,2},{4,7},{5,4},{6,5},{7,6},{8,11},{9,8},{10,9... | collective-permute-start | bytes 1216520 | tf_op jit(solution)/shard_map/ppermute | solution.py:171
  143.1 24.0 %collective-permute-start.9 = (bf16[528,384]{1,0:T(8,128)(2,1)}, bf16[528,384]{1,0:T(8,128)(2,1)}, u32[]{:S(2)}, u32[]{:S(2)}) collective-permute-start(bf16[528,384]{1,0:T(8,128)(2,1)} %slice.14), channel_id=1, source_target_pairs={{0,1},{1,2},{2,3},{3,0},{4,5},{5,6},{6,7},{7,4},{8,9},{9,10},{10,1... | collective-permute-start | bytes 1216520 | tf_op jit(solution)/shard_map/ppermute | solution.py:171
  147.0 20.1 %collective-permute-start.13 = (bf16[528,384]{1,0:T(8,128)(2,1)}, bf16[528,384]{1,0:T(8,128)(2,1)}, u32[]{:S(2)}, u32[]{:S(2)}) collective-permute-start(bf16[528,384]{1,0:T(8,128)(2,1)} %constant_dynamic-update-slice_fusion.2.refs_10_), channel_id=1, source_target_pairs={{0,2},{1,3},{2,0},{3,1},{4,6},{5,7},{6,4},{7,5},{8,10},{9,11},{10,... | collective-permute-start | bytes 1216520 | tf_op jit(solution)/shard_map/ppermute | solution.py:171
  150.6 20.1 %collective-permute-start.12 = (bf16[528,384]{1,0:T(8,128)(2,1)}, bf16[528,384]{1,0:T(8,128)(2,1)}, u32[]{:S(2)}, u32[]{:S(2)}) collective-permute-start(bf16[528,384]{1,0:T(8,128)(2,1)} %constant_dynamic-update-slice_fusion.2.refs_10_), channel_id=1, source_target_pairs={{0,3},{1,0},{2,1},{3,2},{4,7},{5,4},{6,5},{7,6},{8,11},{9,8},{10,9... | collective-permute-start | bytes 1216520 | tf_op jit(solution)/shard_map/ppermute | solution.py:171
  153.7 21.2 %collective-permute-start.11 = (bf16[528,384]{1,0:T(8,128)(2,1)}, bf16[528,384]{1,0:T(8,128)(2,1)}, u32[]{:S(2)}, u32[]{:S(2)}) collective-permute-start(bf16[528,384]{1,0:T(8,128)(2,1)} %constant_dynamic-update-slice_fusion.2.refs_10_), channel_id=1, source_target_pairs={{0,1},{1,2},{2,3},{3,0},{4,5},{5,6},{6,7},{7,4},{8,9},{9,10},{10,1... | collective-permute-start | bytes 1216520 | tf_op jit(solution)/shard_map/ppermute | solution.py:171
Sparse Core Ops, SparseCore 0:
  21.5 66.3 all-gather.2
  101.9 58.1 all-gather.4

commit v5 on v4

v5 whole, which is shorter than its diff:
```python
import functools
import math

import jax
import jax.numpy as jnp
from jax import lax
from jax.experimental import pallas as pl
from jax.experimental.pallas import tpu as pltpu
from jax.sharding import PartitionSpec as P

HEAD_DIM = 128
NORM_EPSILON = 1e-06
Z_PARTS, Y_PARTS = 4, 4
GAIN_ROWS = 16
ROW_TILE = 16


def z_shift(step):
    return [
        (z * Y_PARTS + y, (z + step) % Z_PARTS * Y_PARTS + y)
        for z in range(Z_PARTS)
        for y in range(Y_PARTS)
    ]


def y_shift(step):
    return [
        (z * Y_PARTS + y, z * Y_PARTS + (y + step) % Y_PARTS)
        for z in range(Z_PARTS)
        for y in range(Y_PARTS)
    ]


def slot_columns(places_ref, count, width):
    return [pl.ds(pl.multiple_of(places_ref[j] * width, 128), width) for j in range(count)]


def moments(loads, width):
    count = width * len(loads)
    total = loads[0]()
    for load in loads[1:]:
        total = total + load()
    mean = jnp.sum(total, axis=1, keepdims=True) * (1.0 / count)
    square = jnp.square(loads[0]() - mean)
    for load in loads[1:]:
        square = square + jnp.square(load() - mean)
    return mean, jnp.sum(square, axis=1, keepdims=True)


def row_loads(blocks, slots, at):
    def load(ref, shift):
        return blocks[ref][pl.ds(at + shift, ROW_TILE), :].astype(jnp.float32)

    return [functools.partial(load, ref, shift) for ref, shift in slots]


def moments_kernel(slots, count, *refs):
    blocks, (mean_ref, square_ref) = refs[:count], refs[count:]
    width, lanes = blocks[0].shape[1], mean_ref.shape[1]

    def step(i, carry):
        at = pl.multiple_of(i * ROW_TILE, ROW_TILE)
        mean, square = moments(row_loads(blocks, slots, at), width)
        mean_ref[pl.ds(at, ROW_TILE), :] = jnp.broadcast_to(mean, (ROW_TILE, lanes))
        square_ref[pl.ds(at, ROW_TILE), :] = jnp.broadcast_to(square, (ROW_TILE, lanes))
        return carry

    lax.fori_loop(0, mean_ref.shape[0] // ROW_TILE, step, 0)


def project_attend_kernel(slots, known, count, rows, *refs):
    places_ref, blocks = refs[0], refs[1 : 1 + count]
    mean_ref, square_ref, source_ref, seg_col_ref, seg_row_ref, out_ref = refs[1 + count : 7 + count]
    normed_ref, weight_ref, sums_ref, sem = refs[7 + count :]
    copies = [pltpu.make_async_copy(source_ref, weight_ref, sem)]
    for copy in copies:
        copy.start()
    width, features = blocks[0].shape[1], normed_ref.shape[1]
    columns = slot_columns(places_ref, len(slots), width)
    gains = [
        blocks[ref][pl.ds(rows + shift, GAIN_ROWS), :][:1].astype(jnp.float32)
        for ref, shift in slots
    ]
    known_share = known * width / features
    last_share = 1.0 - known_share

    def step(i, carry):
        at = pl.multiple_of(i * ROW_TILE, ROW_TILE)
        loads = row_loads(blocks, slots, at)
        known_mean = mean_ref[pl.ds(at, ROW_TILE), :1]
        known_square = square_ref[pl.ds(at, ROW_TILE), :1]
        last_mean, last_square = moments(loads[known:], width)
        gap = last_mean - known_mean
        mean = known_mean + gap * last_share
        var = (known_square + last_square) * (1.0 / features) + jnp.square(gap) * (
            known_share * last_share
        )
        scale = lax.rsqrt(var + NORM_EPSILON)
        for j, load in enumerate(loads):
            normed_ref[pl.ds(at, ROW_TILE), columns[j]] = (
                (load() - mean) * scale * gains[j]
            ).astype(jnp.bfloat16)
        return carry

    lax.fori_loop(0, rows // ROW_TILE, step, 0)
    for copy in copies:
        copy.wait()
    sums_ref[...] = jnp.dot(
        normed_ref[...], weight_ref[...], preferred_element_type=jnp.float32
    ).astype(jnp.bfloat16)
    local = out_ref.shape[1]
    span, window = 128, 256
    for row in range(0, rows, span):
        low = min(max(row - (window - span) // 2, 0), rows - window)
        same = seg_col_ref[row : row + span, :1] == seg_row_ref[:1, low : low + window]
        for col in range(0, local, HEAD_DIM):
            query = sums_ref[row : row + span, col : col + HEAD_DIM]
            key = sums_ref[low : low + window, local + col : local + col + HEAD_DIM]
            value = sums_ref[low : low + window, 2 * local + col : 2 * local + col + HEAD_DIM]
            scores = lax.dot_general(
                query, key, (((1,), (1,)), ((), ())), preferred_element_type=jnp.float32
            ) * (1.0 / math.sqrt(HEAD_DIM))
            scores = jnp.where(same, scores, -jnp.inf)
            expo = jnp.exp(scores - jnp.max(scores, axis=1, keepdims=True))
            probs = (expo / jnp.sum(expo, axis=1, keepdims=True)).astype(jnp.bfloat16)
            out_ref[row : row + span, col : col + HEAD_DIM] = jnp.dot(
                probs, value, preferred_element_type=jnp.float32
            ).astype(jnp.bfloat16)


def shards(page_patches, gain, q_weight, k_weight, v_weight, pack_lengths, line_order):
    groups = lax.axis_size("dp")
    page_index = lax.axis_index("dp")
    width = page_patches.shape[1]
    slot_rows = page_patches.shape[0] // groups
    rows = slot_rows * groups // 2
    local = q_weight.shape[1]
    weight = jnp.concatenate([q_weight, k_weight, v_weight], axis=1)
    targets = jnp.arange(groups, dtype=jnp.int32)
    my_order = lax.dynamic_index_in_dim(line_order, page_index, 0, keepdims=False)
    slot_for = jnp.sum(
        jnp.where(my_order[None, :] == targets[:, None], targets[None, :], 0), axis=1
    )
    slots = page_patches.reshape(groups, slot_rows, width)
    outgoing = jnp.take(slots, slot_for, axis=0)
    outgoing, weight = lax.optimization_barrier((outgoing, weight))
    weight = lax.all_gather(weight, "dp", axis=0, tiled=True)
    incoming = lax.all_to_all(outgoing, "dp", split_axis=0, concat_axis=0, tiled=True)
    my_lengths = lax.dynamic_index_in_dim(pack_lengths, page_index, 0, keepdims=False)
    line_ends = jnp.cumsum(my_lengths)
    line_starts = line_ends - my_lengths
    row_ids = jnp.arange(rows, dtype=jnp.int32)
    segment = jnp.sum((line_ends[None, :] <= row_ids[:, None]).astype(jnp.int32), axis=1)
    start_of_row = jnp.sum(
        jnp.where(segment[:, None] == targets[None, :], line_starts[None, :], 0), axis=1
    )
    source_rows = segment * slot_rows + row_ids - start_of_row
    packed = jnp.take(incoming.reshape(groups * slot_rows, width), source_rows, axis=0)

    own = jnp.concatenate([packed, jnp.broadcast_to(gain[None, :], (GAIN_ROWS, width))], axis=0)
    all_rows = rows + GAIN_ROWS
    cut = rows // 2 + GAIN_ROWS

    def along_y(block, step):
        return lax.ppermute(block, "tensor", y_shift(step))

    def along_z(block, step):
        return lax.ppermute(block, "tensor", z_shift(step))

    own_far, own_down, own_up, z_down, z_up = lax.optimization_barrier(
        (
            along_y(own, 2),
            along_y(own, -1),
            along_y(own, 1),
            along_z(own, -1),
            along_z(own, 1),
        )
    )
    pair = jnp.concatenate([z_up, z_down], axis=0)
    pair_up, pair_down = along_y(pair, 1), along_y(pair, -1)
    pair_far_up = along_y(pair_up[:all_rows], 1)
    pair_far_down = along_y(pair_down[all_rows:], -1)
    far_top, far_rest = along_z(z_up[:cut], 1), along_z(z_down[cut:], -1)
    far = jnp.concatenate([far_top, far_rest], axis=0)
    far_far, far_down, far_up = along_y(far, 2), along_y(far, -1), along_y(far, 1)

    blocks, slots_at, shifts = [], [], []

    def add(array, dy, *dzs):
        blocks.append(array)
        for k, dz in enumerate(dzs):
            slots_at.append((len(blocks) - 1, k * all_rows))
            shifts.append((dz, dy))

    add(own, 0, 0)
    add(own_up, -1, 0)
    add(own_down, 1, 0)
    add(own_far, 2, 0)
    add(pair, 0, -1, 1)
    add(pair_up, -1, -1, 1)
    add(pair_down, 1, -1, 1)
    add(pair_far_up, 2, -1)
    add(pair_far_down, 2, 1)
    known, known_blocks = len(slots_at), list(blocks)
    add(far, 0, 2)
    add(far_up, -1, 2)
    add(far_down, 1, 2)
    add(far_far, 2, 2)
    tensor = lax.axis_index("tensor")
    my_z, my_y = tensor // Y_PARTS, tensor % Y_PARTS
    step_z = jnp.array([dz for dz, _ in shifts], jnp.int32)
    step_y = jnp.array([dy for _, dy in shifts], jnp.int32)
    places = (my_z + step_z + Z_PARTS) % Z_PARTS * Y_PARTS + (my_y + step_y + Y_PARTS) % Y_PARTS

    def first_kernel(*refs):
        moments_kernel(slots_at[:known], len(known_blocks), *refs)

    def last_kernel(*refs):
        project_attend_kernel(slots_at, known, len(blocks), rows, *refs)

    features = width * len(slots_at)
    vmem = pl.BlockSpec(memory_space=pltpu.VMEM)
    smem, hbm = pl.BlockSpec(memory_space=pltpu.SMEM), pl.BlockSpec(memory_space=pl.ANY)
    row_figure = jax.ShapeDtypeStruct((rows, 128), jnp.float32)
    known_mean, known_square = pl.pallas_call(
        first_kernel,
        out_shape=(row_figure, row_figure),
        in_specs=[vmem] * len(known_blocks),
        out_specs=(vmem, vmem),
        name="row_moments",
    )(*known_blocks)
    return pl.pallas_call(
        last_kernel,
        out_shape=jax.ShapeDtypeStruct((rows, local), jnp.bfloat16),
        in_specs=[smem] + [vmem] * (len(blocks) + 2) + [hbm, vmem, vmem],
        out_specs=vmem,
        scratch_shapes=[
            pltpu.VMEM((rows, features), jnp.bfloat16),
            pltpu.VMEM((features, 3 * local), jnp.bfloat16),
            pltpu.VMEM((rows, 3 * local), jnp.bfloat16),
            pltpu.SemaphoreType.DMA,
        ],
        name="norm_project_attend",
    )(
        places,
        *blocks,
        known_mean,
        known_square,
        weight,
        segment[:, None],
        segment[None, :],
    )


def solution(mesh):
    return jax.shard_map(
        shards,
        mesh=mesh,
        in_specs=(
            P("dp", "tensor"),
            P("tensor"),
            P("dp", "tensor"),
            P("dp", "tensor"),
            P("dp", "tensor"),
            P(),
            P(),
        ),
        out_specs=P("dp", "tensor"),
        check_vma=False,
    )
```

time: 203 us -> 207 us (1.020)
  the two profiles are of different devices: /device:TPU:36 before, /device:TPU:1 now
where the time goes in v5:
time: 207 us; the launch traced here: 204 us
  waiting for transfers between devices  78.3 us (38%)
  starting transfers between devices  66.5 us (32%)
  Pallas kernels  31.7 us (15%)
  between operations  13.7 us (7%)
  local copies, waits for them, and re-layouts  9.21 us (4%)
  other arithmetic  4.68 us (2%)
    ppermute x4, waiting for transfers between devices, along_z(): return lax.ppermute(block, 'tensor', z_shift(step))  44.8 us
    ppermute x10, starting transfers between devices, along_y(): return lax.ppermute(block, 'tensor', y_shift(step))  34.2 us
    all_to_all x1, waiting for transfers between devices, shards(): lax.all_to_all(outgoing, 'dp', split_axis=0, concat_axis=0, tiled=True)  25.2 us
    pallas_call x1, Pallas kernels, shards(): pl.pallas_call(last_kernel, out_shape=jax.ShapeDtypeStruct((rows, local),...  22.1 us
    ppermute x4, starting transfers between devices, along_z(): return lax.ppermute(block, 'tensor', z_shift(step))  21.8 us
    all_to_all x1, starting transfers between devices, shards(): lax.all_to_all(outgoing, 'dp', split_axis=0, concat_axis=0, tiled=True)  10.4 us
    pallas_call x1, Pallas kernels, shards(): pl.pallas_call(first_kernel, out_shape=(row_figure, row_figure), in_specs...  9.63 us
    ppermute x10, waiting for transfers between devices, along_y(): return lax.ppermute(block, 'tensor', y_shift(step))  8.25 us
  transfers between devices with their start and end apart: 16, of which 6 were waited for; matrix products, arithmetic and copies ran while one was open for 3% of the time, Pallas kernels for 5%

profile of v5, /device:TPU:1, one launch (start us, length us, event | category | flops | bytes accessed | tf_op | source)
XLA Modules:
  0.0 204.1 jit_solution(15091240501709819044)
XLA Ops:
  6.5 0.0 all-gather.2.cloned.1.call-start
  6.6 0.8 fusion.6
  7.3 0.1 copy.13
  7.4 0.1 reduce-window.4
  7.5 0.1 reduce
  7.6 0.7 fusion.5
  8.3 0.1 select_reduce_fusion.1
  8.5 0.7 gather_fusion
  9.2 1.1 broadcast_select_fusion
  10.3 1.7 pad_maximum_fusion.1
  12.0 0.0 all-gather.2.cloned.1.call-update
  12.0 10.4 %all-to-all-start = ((bf16[32,32,384]{2,1,0:T(8,128)(2,1)}), bf16[32,32,384]{2,1,0:T(8,128)(2,1)S(1)}, u32[]{:S(2)}, u32[]{:S(2)}) async-start(bf16[32,32,384]{2,1,0:T(8,128)(2,1)} %broadcast_select_fusion), calls=%async_computation | async-start | bytes 1572864 | tf_op jit(solution)/shard_map/all_to_all | solution.py:148
  22.5 0.1 convert_reduce_fusion
  22.6 0.1 select_reduce_fusion
  22.7 25.2 %all-to-all-done = bf16[32,32,384]{2,1,0:T(8,128)(2,1)S(1)} async-done(((bf16[32,32,384]{2,1,0:T(8,128)(2,1)}), bf16[32,32,384]{2,1,0:T(8,128)(2,1)S(1)}, u32[]{:S(2)}, u32[]{:S(2)}) %all-to-all-start) | async-done | bytes 786464 | tf_op jit(solution)/shard_map/all_to_all | solution.py:148
  47.8 1.9 gather_fusion.1
  49.8 0.1 broadcast_select_fusion.1
  50.0 8.5 %collective-permute-start.4 = (bf16[528,384]{1,0:T(8,128)(2,1)S(1)}, bf16[528,384]{1,0:T(8,128)(2,1)S(1)}, u32[]{:S(2)}, u32[]{:S(2)}) collective-permute-start(bf16[528,384]{1,0:T(8,128)(2,1)S(1)} %pad_maximum_fusion.refs_0_.refs_1_), channel_id=1, source_target_pairs={{0,4},{1,5},{2,6},{3,7},{4,8},{5,9},{6,10},{7,11},{8,12},{9,13},{1... | collective-permute-start | bytes 1216520 | tf_op jit(solution)/shard_map/ppermute | solution.py:168
  58.6 3.6 %collective-permute-start.3 = (bf16[528,384]{1,0:T(8,128)(2,1)S(1)}, bf16[528,384]{1,0:T(8,128)(2,1)S(1)}, u32[]{:S(2)}, u32[]{:S(2)}) collective-permute-start(bf16[528,384]{1,0:T(8,128)(2,1)S(1)} %pad_maximum_fusion.refs_0_.refs_1_), channel_id=1, source_target_pairs={{0,12},{1,13},{2,14},{3,15},{4,0},{5,1},{6,2},{7,3},{8,4},{9,5},{1... | collective-permute-start | bytes 1216520 | tf_op jit(solution)/shard_map/ppermute | solution.py:168
  62.1 3.2 %collective-permute-start.2 = (bf16[528,384]{1,0:T(8,128)(2,1)S(1)}, bf16[528,384]{1,0:T(8,128)(2,1)S(1)}, u32[]{:S(2)}, u32[]{:S(2)}) collective-permute-start(bf16[528,384]{1,0:T(8,128)(2,1)S(1)} %pad_maximum_fusion.refs_0_.refs_1_), channel_id=1, source_target_pairs={{0,1},{1,2},{2,3},{3,0},{4,5},{5,6},{6,7},{7,4},{8,9},{9,10},{10,1... | collective-permute-start | bytes 1216520 | tf_op jit(solution)/shard_map/ppermute | solution.py:165
  65.4 3.4 %collective-permute-start.1 = (bf16[528,384]{1,0:T(8,128)(2,1)S(1)}, bf16[528,384]{1,0:T(8,128)(2,1)S(1)}, u32[]{:S(2)}, u32[]{:S(2)}) collective-permute-start(bf16[528,384]{1,0:T(8,128)(2,1)S(1)} %pad_maximum_fusion.refs_0_.refs_1_), channel_id=1, source_target_pairs={{0,3},{1,0},{2,1},{3,2},{4,7},{5,4},{6,5},{7,6},{8,11},{9,8},{10,9... | collective-permute-start | bytes 1216520 | tf_op jit(solution)/shard_map/ppermute | solution.py:165
  68.8 3.5 %collective-permute-start = (bf16[528,384]{1,0:T(8,128)(2,1)S(1)}, bf16[528,384]{1,0:T(8,128)(2,1)}, u32[]{:S(2)}, u32[]{:S(2)}) collective-permute-start(bf16[528,384]{1,0:T(8,128)(2,1)S(1)} %pad_maximum_fusion.refs_0_.refs_1_), channel_id=1, source_target_pairs={{0,2},{1,3},{2,0},{3,1},{4,6},{5,7},{6,4},{7,5},{8,10},{9,11},{10,... | collective-permute-start | bytes 1216520 | tf_op jit(solution)/shard_map/ppermute | solution.py:165
  72.3 28.6 %collective-permute-done.4 = bf16[528,384]{1,0:T(8,128)(2,1)S(1)} collective-permute-done((bf16[528,384]{1,0:T(8,128)(2,1)S(1)}, bf16[528,384]{1,0:T(8,128)(2,1)S(1)}, u32[]{:S(2)}, u32[]{:S(2)}) %collective-permute-start.4) | collective-permute-done | bytes 405536 | tf_op jit(solution)/shard_map/ppermute | solution.py:168
  100.9 0.0 collective-permute-done.3
  101.0 0.8 copy-done.5
  101.7 0.8 copy-done.6
  102.6 0.1 constant_dynamic-update-slice_fusion.refs_4_.refs_5_
  102.6 7.3 %collective-permute-start.6 = (bf16[1056,384]{1,0:T(8,128)(2,1)S(1)}, bf16[1056,384]{1,0:T(8,128)(2,1)S(1)}, u32[]{:S(2)}, u32[]{:S(2)}) collective-permute-start(bf16[1056,384]{1,0:T(8,128)(2,1)S(1)} %constant_dynamic-update-slice_fusion.refs_4_.refs_5_), channel_id=1, source_target_pairs={{0,3},{1,0},{2,1},{3,2},{4,7},{5,4},{6,5},{7,6},{8,11},{9,8},{10,9... | collective-permute-start | bytes 2433032 | tf_op jit(solution)/shard_map/ppermute | solution.py:165
  110.0 1.9 collective-permute-start.5
  111.9 7.7 %collective-permute-start.9 = (bf16[272,384]{1,0:T(8,128)(2,1)S(1)}, bf16[272,384]{1,0:T(8,128)(2,1)S(1)}, u32[]{:S(2)}, u32[]{:S(2)}) collective-permute-start(bf16[272,384]{1,0:T(8,128)(2,1)S(1)} %slice.14), channel_id=1, source_target_pairs={{0,4},{1,5},{2,6},{3,7},{4,8},{5,9},{6,10},{7,11},{8,12},{9,13},{1... | collective-permute-start | bytes 626696 | tf_op jit(solution)/shard_map/ppermute | solution.py:168
  119.7 1.9 collective-permute-start.10
  121.6 16.2 %collective-permute-done.9 = bf16[272,384]{1,0:T(8,128)(2,1)S(1)} collective-permute-done((bf16[272,384]{1,0:T(8,128)(2,1)S(1)}, bf16[272,384]{1,0:T(8,128)(2,1)S(1)}, u32[]{:S(2)}, u32[]{:S(2)}) %collective-permute-start.9) | collective-permute-done | bytes 208928 | tf_op jit(solution)/shard_map/ppermute | solution.py:168
  137.9 0.7 constant_dynamic-update-slice_fusion.3
  138.6 0.9 slice.21
  139.4 3.9 %collective-permute-start.8 = (bf16[528,384]{1,0:T(8,128)(2,1)}, bf16[528,384]{1,0:T(8,128)(2,1)}, u32[]{:S(2)}, u32[]{:S(2)}) collective-permute-start(bf16[528,384]{1,0:T(8,128)(2,1)} %slice.21), channel_id=1, source_target_pairs={{0,3},{1,0},{2,1},{3,2},{4,7},{5,4},{6,5},{7,6},{8,11},{9,8},{10,9... | collective-permute-start | bytes 1216520 | tf_op jit(solution)/shard_map/ppermute | solution.py:165
  143.4 0.8 slice.20
  144.3 1.9 collective-permute-start.7
  146.2 0.7 constant_dynamic-update-slice_fusion.2.refs_10_
  146.9 3.1 %collective-permute-start.13 = (bf16[528,384]{1,0:T(8,128)(2,1)}, bf16[528,384]{1,0:T(8,128)(2,1)}, u32[]{:S(2)}, u32[]{:S(2)}) collective-permute-start(bf16[528,384]{1,0:T(8,128)(2,1)} %constant_dynamic-update-slice_fusion.2.refs_10_), channel_id=1, source_target_pairs={{0,2},{1,3},{2,0},{3,1},{4,6},{5,7},{6,4},{7,5},{8,10},{9,11},{10,... | collective-permute-start | bytes 1216520 | tf_op jit(solution)/shard_map/ppermute | solution.py:165
  150.0 3.4 %collective-permute-start.12 = (bf16[528,384]{1,0:T(8,128)(2,1)}, bf16[528,384]{1,0:T(8,128)(2,1)}, u32[]{:S(2)}, u32[]{:S(2)}) collective-permute-start(bf16[528,384]{1,0:T(8,128)(2,1)} %constant_dynamic-update-slice_fusion.2.refs_10_), channel_id=1, source_target_pairs={{0,3},{1,0},{2,1},{3,2},{4,7},{5,4},{6,5},{7,6},{8,11},{9,8},{10,9... | collective-permute-start | bytes 1216520 | tf_op jit(solution)/shard_map/ppermute | solution.py:165
  153.4 2.5 %collective-permute-start.11 = (bf16[528,384]{1,0:T(8,128)(2,1)}, bf16[528,384]{1,0:T(8,128)(2,1)}, u32[]{:S(2)}, u32[]{:S(2)}) collective-permute-start(bf16[528,384]{1,0:T(8,128)(2,1)} %constant_dynamic-update-slice_fusion.2.refs_10_), channel_id=1, source_target_pairs={{0,1},{1,2},{2,3},{3,0},{4,5},{5,6},{6,7},{7,4},{8,9},{9,10},{10,1... | collective-permute-start | bytes 1216520 | tf_op jit(solution)/shard_map/ppermute | solution.py:165
  155.9 0.9 copy.14.refs_17_
  156.7 0.5 fusion.refs_0_
  157.2 1.2 collective-permute-done.7.refs_7_.refs_8_
  158.5 9.6 %row_moments.1 = (f32[512,128]{1,0:T(8,128)}, f32[512,128]{1,0:T(8,128)}) custom-call(bf16[528,384]{1,0:T(8,128)(2,1)} %copy-done.4, bf16[528,384]{1,0:T(8,128)(2,1)} %copy-done.5, bf16[528,384]{1,0:T(8,128)(2,1)} %copy-done.6, bf16[528,384]{1,0:T(8,128)(2,1)} %collective-permute-done.refs_3_.refs_4_, bf16[1056,384]{1,0:T(8,128)(2,1)} %copy-done.3, ...), custom_call_target="tpu_custom_call" | custom-call | tf_op jit(solution)/shard_map/row_moments/pallas_call | solution.py:225
  168.1 2.0 collective-permute-done.12.refs_12_
  170.1 5.0 %collective-permute-done.11.refs_11_ = bf16[528,384]{1,0:T(8,128)(2,1)} collective-permute-done((bf16[528,384]{1,0:T(8,128)(2,1)}, bf16[528,384]{1,0:T(8,128)(2,1)}, u32[]{:S(2)}, u32[]{:S(2)}) %collective-permute-start.11) | collective-permute-done | bytes 405536 | tf_op jit(solution)/shard_map/ppermute | solution.py:165
  175.1 22.1 %norm_project_attend.1 = bf16[512,256]{1,0:T(8,128)(2,1)} custom-call(s32[16]{0:T(128)} %fusion.refs_0_, bf16[528,384]{1,0:T(8,128)(2,1)} %copy-done.4, bf16[528,384]{1,0:T(8,128)(2,1)} %copy-done.5, bf16[528,384]{1,0:T(8,128)(2,1)} %copy-done.6, bf16[528,384]{1,0:T(8,128)(2,1)} %collective-permute-done.refs_3_.refs_4_, bf16[1056,384]{1,0:T(8,128)(2,1)} %copy-done.3, ...), custom_call_target="tpu_custom_call" | custom-call | tf_op jit(solution)/shard_map/norm_project_attend/pallas_call | solution.py:232
  (40 shorter events, 0.2 us)
Async XLA Ops:
  6.5 1.9 copy-start
  6.5 150.2 %copy-start.9 = (s32[16]{0:T(128)S(1)}, s32[16]{0:T(128)}, u32[]{:S(2)}) copy-start(s32[16]{0:T(128)} %constant.94.clone) | copy-start | bytes 196
  6.5 150.2 %copy-start.10 = (s32[16]{0:T(128)S(1)}, s32[16]{0:T(128)}, u32[]{:S(2)}) copy-start(s32[16]{0:T(128)} %constant.93.clone) | copy-start | bytes 196
  6.5 43.4 %copy-start.8 = (bf16[384]{0:T(512)(128)(2,1)S(1)}, bf16[384]{0:T(512)(128)(2,1)}, u32[]{:S(2)}) copy-start(bf16[384]{0:T(512)(128)(2,1)} %param.10) | copy-start | bytes 2308
  6.5 168.6 %all-gather.2.cloned.1.call-start = ((), (), s32[]{:S(2)}) async-start(), calls=%async_computation.1 | async-start | bytes 9732096 | tf_op jit(solution)/shard_map/all_gather | solution.py:147
  12.0 35.8 %all-to-all-start = ((bf16[32,32,384]{2,1,0:T(8,128)(2,1)}), bf16[32,32,384]{2,1,0:T(8,128)(2,1)S(1)}, u32[]{:S(2)}, u32[]{:S(2)}) async-start(bf16[32,32,384]{2,1,0:T(8,128)(2,1)} %broadcast_select_fusion), calls=%async_computation | async-start | bytes 1572864 | tf_op jit(solution)/shard_map/all_to_all | solution.py:148
  22.5 152.6 %copy-start.7 = (s32[512]{0:T(512)}, s32[512]{0:T(512)S(1)}, u32[]{:S(2)}) copy-start(s32[512]{0:T(512)S(1)} %convert_reduce_fusion) | copy-start | bytes 6148
  50.0 93.4 %copy-start.4 = (bf16[528,384]{1,0:T(8,128)(2,1)}, bf16[528,384]{1,0:T(8,128)(2,1)S(1)}, u32[]{:S(2)}) copy-start(bf16[528,384]{1,0:T(8,128)(2,1)S(1)} %pad_maximum_fusion.refs_0_.refs_1_) | copy-start | bytes 1216516
  50.0 50.9 %collective-permute-start.4 = (bf16[528,384]{1,0:T(8,128)(2,1)S(1)}, bf16[528,384]{1,0:T(8,128)(2,1)S(1)}, u32[]{:S(2)}, u32[]{:S(2)}) collective-permute-start(bf16[528,384]{1,0:T(8,128)(2,1)S(1)} %pad_maximum_fusion.refs_0_.refs_1_), channel_id=1, source_target_pairs={{0,4},{1,5},{2,6},{3,7},{4,8},{5,9},{6,10},{7,11},{8,12},{9,13},{1... | collective-permute-start | bytes 1216520 | tf_op jit(solution)/shard_map/ppermute | solution.py:168
  58.6 42.4 %collective-permute-start.3 = (bf16[528,384]{1,0:T(8,128)(2,1)S(1)}, bf16[528,384]{1,0:T(8,128)(2,1)S(1)}, u32[]{:S(2)}, u32[]{:S(2)}) collective-permute-start(bf16[528,384]{1,0:T(8,128)(2,1)S(1)} %pad_maximum_fusion.refs_0_.refs_1_), channel_id=1, source_target_pairs={{0,12},{1,13},{2,14},{3,15},{4,0},{5,1},{6,2},{7,3},{8,4},{9,5},{1... | collective-permute-start | bytes 1216520 | tf_op jit(solution)/shard_map/ppermute | solution.py:168
  62.1 38.8 %collective-permute-start.2 = (bf16[528,384]{1,0:T(8,128)(2,1)S(1)}, bf16[528,384]{1,0:T(8,128)(2,1)S(1)}, u32[]{:S(2)}, u32[]{:S(2)}) collective-permute-start(bf16[528,384]{1,0:T(8,128)(2,1)S(1)} %pad_maximum_fusion.refs_0_.refs_1_), channel_id=1, source_target_pairs={{0,1},{1,2},{2,3},{3,0},{4,5},{5,6},{6,7},{7,4},{8,9},{9,10},{10,1... | collective-permute-start | bytes 1216520 | tf_op jit(solution)/shard_map/ppermute | solution.py:165
  65.4 35.6 %collective-permute-start.1 = (bf16[528,384]{1,0:T(8,128)(2,1)S(1)}, bf16[528,384]{1,0:T(8,128)(2,1)S(1)}, u32[]{:S(2)}, u32[]{:S(2)}) collective-permute-start(bf16[528,384]{1,0:T(8,128)(2,1)S(1)} %pad_maximum_fusion.refs_0_.refs_1_), channel_id=1, source_target_pairs={{0,3},{1,0},{2,1},{3,2},{4,7},{5,4},{6,5},{7,6},{8,11},{9,8},{10,9... | collective-permute-start | bytes 1216520 | tf_op jit(solution)/shard_map/ppermute | solution.py:165
  68.8 33.7 %collective-permute-start = (bf16[528,384]{1,0:T(8,128)(2,1)S(1)}, bf16[528,384]{1,0:T(8,128)(2,1)}, u32[]{:S(2)}, u32[]{:S(2)}) collective-permute-start(bf16[528,384]{1,0:T(8,128)(2,1)S(1)} %pad_maximum_fusion.refs_0_.refs_1_), channel_id=1, source_target_pairs={{0,2},{1,3},{2,0},{3,1},{4,6},{5,7},{6,4},{7,5},{8,10},{9,11},{10,... | collective-permute-start | bytes 1216520 | tf_op jit(solution)/shard_map/ppermute | solution.py:165
  101.0 0.8 copy-start.5
  101.7 0.8 copy-start.6
  102.6 55.8 %copy-start.3 = (bf16[1056,384]{1,0:T(8,128)(2,1)}, bf16[1056,384]{1,0:T(8,128)(2,1)S(1)}, u32[]{:S(2)}) copy-start(bf16[1056,384]{1,0:T(8,128)(2,1)S(1)} %constant_dynamic-update-slice_fusion.refs_4_.refs_5_) | copy-start | bytes 2433028
  102.6 35.9 %collective-permute-start.6 = (bf16[1056,384]{1,0:T(8,128)(2,1)S(1)}, bf16[1056,384]{1,0:T(8,128)(2,1)S(1)}, u32[]{:S(2)}, u32[]{:S(2)}) collective-permute-start(bf16[1056,384]{1,0:T(8,128)(2,1)S(1)} %constant_dynamic-update-slice_fusion.refs_4_.refs_5_), channel_id=1, source_target_pairs={{0,3},{1,0},{2,1},{3,2},{4,7},{5,4},{6,5},{7,6},{8,11},{9,8},{10,9... | collective-permute-start | bytes 2433032 | tf_op jit(solution)/shard_map/ppermute | solution.py:165
  110.0 33.4 %collective-permute-start.5 = (bf16[1056,384]{1,0:T(8,128)(2,1)S(1)}, bf16[1056,384]{1,0:T(8,128)(2,1)S(1)}, u32[]{:S(2)}, u32[]{:S(2)}) collective-permute-start(bf16[1056,384]{1,0:T(8,128)(2,1)S(1)} %constant_dynamic-update-slice_fusion.refs_4_.refs_5_), channel_id=1, source_target_pairs={{0,1},{1,2},{2,3},{3,0},{4,5},{5,6},{6,7},{7,4},{8,9},{9,10},{10,1... | collective-permute-start | bytes 2433032 | tf_op jit(solution)/shard_map/ppermute | solution.py:165
  111.9 25.9 %collective-permute-start.9 = (bf16[272,384]{1,0:T(8,128)(2,1)S(1)}, bf16[272,384]{1,0:T(8,128)(2,1)S(1)}, u32[]{:S(2)}, u32[]{:S(2)}) collective-permute-start(bf16[272,384]{1,0:T(8,128)(2,1)S(1)} %slice.14), channel_id=1, source_target_pairs={{0,4},{1,5},{2,6},{3,7},{4,8},{5,9},{6,10},{7,11},{8,12},{9,13},{1... | collective-permute-start | bytes 626696 | tf_op jit(solution)/shard_map/ppermute | solution.py:168
  119.7 26.5 %collective-permute-start.10 = (bf16[256,384]{1,0:T(8,128)(2,1)S(1)}, bf16[256,384]{1,0:T(8,128)(2,1)S(1)}, u32[]{:S(2)}, u32[]{:S(2)}) collective-permute-start(bf16[256,384]{1,0:T(8,128)(2,1)S(1)} %slice.15), channel_id=1, source_target_pairs={{0,12},{1,13},{2,14},{3,15},{4,0},{5,1},{6,2},{7,3},{8,4},{9,5},{1... | collective-permute-start | bytes 589832 | tf_op jit(solution)/shard_map/ppermute | solution.py:168
  138.6 19.9 %copy-start.1 = (bf16[1056,384]{1,0:T(8,128)(2,1)}, bf16[1056,384]{1,0:T(8,128)(2,1)S(1)}, u32[]{:S(2)}) copy-start(bf16[1056,384]{1,0:T(8,128)(2,1)S(1)} %collective-permute-done.6.refs_6_.refs_7_) | copy-start | bytes 2433028
  139.4 17.8 %collective-permute-start.8 = (bf16[528,384]{1,0:T(8,128)(2,1)}, bf16[528,384]{1,0:T(8,128)(2,1)}, u32[]{:S(2)}, u32[]{:S(2)}) collective-permute-start(bf16[528,384]{1,0:T(8,128)(2,1)} %slice.21), channel_id=1, source_target_pairs={{0,3},{1,0},{2,1},{3,2},{4,7},{5,4},{6,5},{7,6},{8,11},{9,8},{10,9... | collective-permute-start | bytes 1216520 | tf_op jit(solution)/shard_map/ppermute | solution.py:165
  143.4 15.1 %copy-start.2 = (bf16[1056,384]{1,0:T(8,128)(2,1)}, bf16[1056,384]{1,0:T(8,128)(2,1)S(1)}, u32[]{:S(2)}) copy-start(bf16[1056,384]{1,0:T(8,128)(2,1)S(1)} %collective-permute-done.5.refs_5_.refs_6_) | copy-start | bytes 2433028
  144.3 14.2 %collective-permute-start.7 = (bf16[528,384]{1,0:T(8,128)(2,1)}, bf16[528,384]{1,0:T(8,128)(2,1)}, u32[]{:S(2)}, u32[]{:S(2)}) collective-permute-start(bf16[528,384]{1,0:T(8,128)(2,1)} %slice.20), channel_id=1, source_target_pairs={{0,1},{1,2},{2,3},{3,0},{4,5},{5,6},{6,7},{7,4},{8,9},{9,10},{10,1... | collective-permute-start | bytes 1216520 | tf_op jit(solution)/shard_map/ppermute | solution.py:165
  146.9 21.2 %collective-permute-start.13 = (bf16[528,384]{1,0:T(8,128)(2,1)}, bf16[528,384]{1,0:T(8,128)(2,1)}, u32[]{:S(2)}, u32[]{:S(2)}) collective-permute-start(bf16[528,384]{1,0:T(8,128)(2,1)} %constant_dynamic-update-slice_fusion.2.refs_10_), channel_id=1, source_target_pairs={{0,2},{1,3},{2,0},{3,1},{4,6},{5,7},{6,4},{7,5},{8,10},{9,11},{10,... | collective-permute-start | bytes 1216520 | tf_op jit(solution)/shard_map/ppermute | solution.py:165
  150.0 20.1 %collective-permute-start.12 = (bf16[528,384]{1,0:T(8,128)(2,1)}, bf16[528,384]{1,0:T(8,128)(2,1)}, u32[]{:S(2)}, u32[]{:S(2)}) collective-permute-start(bf16[528,384]{1,0:T(8,128)(2,1)} %constant_dynamic-update-slice_fusion.2.refs_10_), channel_id=1, source_target_pairs={{0,3},{1,0},{2,1},{3,2},{4,7},{5,4},{6,5},{7,6},{8,11},{9,8},{10,9... | collective-permute-start | bytes 1216520 | tf_op jit(solution)/shard_map/ppermute | solution.py:165
  153.4 21.7 %collective-permute-start.11 = (bf16[528,384]{1,0:T(8,128)(2,1)}, bf16[528,384]{1,0:T(8,128)(2,1)}, u32[]{:S(2)}, u32[]{:S(2)}) collective-permute-start(bf16[528,384]{1,0:T(8,128)(2,1)} %constant_dynamic-update-slice_fusion.2.refs_10_), channel_id=1, source_target_pairs={{0,1},{1,2},{2,3},{3,0},{4,5},{5,6},{6,7},{7,4},{8,9},{9,10},{10,1... | collective-permute-start | bytes 1216520 | tf_op jit(solution)/shard_map/ppermute | solution.py:165
Sparse Core Ops, SparseCore 0:
  12.1 135.0 all-gather.1

commit v6 on v5

--- a/solution.py
+++ b/solution.py
@@ -29,6 +29,34 @@
         for z in range(Z_PARTS)
         for y in range(Y_PARTS)
     ]
+
+
+def dp_groups(varying):
+    groups = {}
+    for x in range(4):
+        for z in range(4):
+            for core in range(2):
+                key = tuple(v for name, v in (("x", x), ("z", z), ("c", core)) if name not in varying)
+                groups.setdefault(key, []).append(x * 8 + z * 2 + core)
+    return list(groups.values())
+
+
+def load_weights(source_ref, weight_ref, sem, strip):
+    copies = []
+    for x in range(4):
+        for z in range(4):
+            for core in range(2):
+                held, wanted = (x * 2 + core) * 4 + z, x * 8 + z * 2 + core
+                copies.append(
+                    pltpu.make_async_copy(
+                        source_ref.at[pl.ds(held * strip, strip), :],
+                        weight_ref.at[pl.ds(wanted * strip, strip), :],
+                        sem,
+                    )
+                )
+    for copy in copies:
+        copy.start()
+    return copies
 
 
 def slot_columns(places_ref, count, width):
@@ -68,13 +96,11 @@
     lax.fori_loop(0, mean_ref.shape[0] // ROW_TILE, step, 0)
 
 
-def project_attend_kernel(slots, known, count, rows, *refs):
+def project_attend_kernel(slots, known, count, rows, strip, *refs):
     places_ref, blocks = refs[0], refs[1 : 1 + count]
     mean_ref, square_ref, source_ref, seg_col_ref, seg_row_ref, out_ref = refs[1 + count : 7 + count]
     normed_ref, weight_ref, sums_ref, sem = refs[7 + count :]
-    copies = [pltpu.make_async_copy(source_ref, weight_ref, sem)]
-    for copy in copies:
-        copy.start()
+    copies = load_weights(source_ref, weight_ref, sem, strip)
     width, features = blocks[0].shape[1], normed_ref.shape[1]
     columns = slot_columns(places_ref, len(slots), width)
     gains = [
@@ -144,7 +170,7 @@
     slots = page_patches.reshape(groups, slot_rows, width)
     outgoing = jnp.take(slots, slot_for, axis=0)
     outgoing, weight = lax.optimization_barrier((outgoing, weight))
-    weight = lax.all_gather(weight, "dp", axis=0, tiled=True)
+    weight = lax.all_gather(weight, "dp", axis=0, tiled=True, axis_index_groups=dp_groups("z"))
     incoming = lax.all_to_all(outgoing, "dp", split_axis=0, concat_axis=0, tiled=True)
     my_lengths = lax.dynamic_index_in_dim(pack_lengths, page_index, 0, keepdims=False)
     line_ends = jnp.cumsum(my_lengths)
@@ -167,20 +193,25 @@
     def along_z(block, step):
         return lax.ppermute(block, "tensor", z_shift(step))
 
-    own_far, own_down, own_up, z_down, z_up = lax.optimization_barrier(
+    own_far, own_down, own_up, z_down, z_up, weight = lax.optimization_barrier(
         (
             along_y(own, 2),
             along_y(own, -1),
             along_y(own, 1),
             along_z(own, -1),
             along_z(own, 1),
+            weight,
         )
     )
+    weight = lax.all_gather(weight, "dp", axis=0, tiled=True, axis_index_groups=dp_groups("xc"))
     pair = jnp.concatenate([z_up, z_down], axis=0)
     pair_up, pair_down = along_y(pair, 1), along_y(pair, -1)
     pair_far_up = along_y(pair_up[:all_rows], 1)
     pair_far_down = along_y(pair_down[all_rows:], -1)
     far_top, far_rest = along_z(z_up[:cut], 1), along_z(z_down[cut:], -1)
+    far_top, far_rest, pair_up, pair_down = lax.optimization_barrier(
+        (far_top, far_rest, pair_up, pair_down)
+    )
     far = jnp.concatenate([far_top, far_rest], axis=0)
     far_far, far_down, far_up = along_y(far, 2), along_y(far, -1), along_y(far, 1)
 
@@ -199,9 +230,9 @@
     add(pair, 0, -1, 1)
     add(pair_up, -1, -1, 1)
     add(pair_down, 1, -1, 1)
+    known, known_blocks = len(slots_at), list(blocks)
     add(pair_far_up, 2, -1)
     add(pair_far_down, 2, 1)
-    known, known_blocks = len(slots_at), list(blocks)
     add(far, 0, 2)
     add(far_up, -1, 2)
     add(far_down, 1, 2)
@@ -216,7 +247,7 @@
         moments_kernel(slots_at[:known], len(known_blocks), *refs)
 
     def last_kernel(*refs):
-        project_attend_kernel(slots_at, known, len(blocks), rows, *refs)
+        project_attend_kernel(slots_at, known, len(blocks), rows, q_weight.shape[0], *refs)
 
     features = width * len(slots_at)
     vmem = pl.BlockSpec(memory_space=pltpu.VMEM)

time: 207 us -> 205 us (level)
  the two profiles are of different devices: /device:TPU:1 before, /device:TPU:39 now
where the time goes in v6:
time: 205 us
  waiting for transfers between devices  78.3 us (38%)
  starting transfers between devices  64.3 us (31%)
  Pallas kernels  31.1 us (15%)
  between operations  13.8 us (7%)
  local copies, waits for them, and re-layouts  12.3 us (6%)
  other arithmetic  4.8 us (2%)
    ppermute x10, starting transfers between devices, along_y(): return lax.ppermute(block, 'tensor', y_shift(step))  34.4 us
    all_gather x2, waiting for transfers between devices, shards(): lax.all_gather(weight, 'dp', axis=0, tiled=True, axis_index_groups=dp_gro...  26 us
    ppermute x4, waiting for transfers between devices, along_z(): return lax.ppermute(block, 'tensor', z_shift(step))  22.1 us
    pallas_call x1, Pallas kernels, shards(): pl.pallas_call(last_kernel, out_shape=jax.ShapeDtypeStruct((rows, local),...  22 us
    ppermute x4, starting transfers between devices, along_z(): return lax.ppermute(block, 'tensor', z_shift(step))  20.4 us
    all_to_all x1, waiting for transfers between devices, shards(): lax.all_to_all(outgoing, 'dp', split_axis=0, concat_axis=0, tiled=True)  17.6 us
    ppermute x10, waiting for transfers between devices, along_y(): return lax.ppermute(block, 'tensor', y_shift(step))  11.9 us
    all_to_all x1, starting transfers between devices, shards(): lax.all_to_all(outgoing, 'dp', split_axis=0, concat_axis=0, tiled=True)  9.44 us
  transfers between devices with their start and end apart: 17, of which 8 were waited for; matrix products, arithmetic and copies ran while one was open for 5% of the time, Pallas kernels for 4%

profile of v6, /device:TPU:39, one launch (start us, length us, event | category | flops | bytes accessed | tf_op | source)
XLA Modules:
  0.0 204.6 jit_solution(13587676799086196151)
XLA Ops:
  6.5 0.8 fusion.6
  7.3 0.1 copy.13
  7.5 0.1 reduce
  7.6 0.7 fusion.5
  8.3 0.1 select_reduce_fusion.1
  8.5 0.7 gather_fusion
  9.2 1.0 broadcast_select_fusion
  10.2 1.7 pad_maximum_fusion.1
  12.0 9.4 %all-to-all-start = ((bf16[32,32,384]{2,1,0:T(8,128)(2,1)}), bf16[32,32,384]{2,1,0:T(8,128)(2,1)S(1)}, u32[]{:S(2)}, u32[]{:S(2)}) async-start(bf16[32,32,384]{2,1,0:T(8,128)(2,1)} %broadcast_select_fusion), calls=%async_computation | async-start | bytes 1572864 | tf_op jit(solution)/shard_map/all_to_all | solution.py:174
  21.5 0.7 all-gather.3.cloned.1.call-update
  22.2 0.1 convert_reduce_fusion
  22.4 17.6 %all-to-all-done = bf16[32,32,384]{2,1,0:T(8,128)(2,1)S(1)} async-done(((bf16[32,32,384]{2,1,0:T(8,128)(2,1)}), bf16[32,32,384]{2,1,0:T(8,128)(2,1)S(1)}, u32[]{:S(2)}, u32[]{:S(2)}) %all-to-all-start) | async-done | bytes 786464 | tf_op jit(solution)/shard_map/all_to_all | solution.py:174
  40.1 1.9 gather_fusion.1
  42.0 0.1 broadcast_select_fusion.1
  42.2 8.3 %collective-permute-start.4 = (bf16[528,384]{1,0:T(8,128)(2,1)S(1)}, bf16[528,384]{1,0:T(8,128)(2,1)S(1)}, u32[]{:S(2)}, u32[]{:S(2)}) collective-permute-start(bf16[528,384]{1,0:T(8,128)(2,1)S(1)} %pad_maximum_fusion.refs_0_.refs_1_), channel_id=1, source_target_pairs={{0,4},{1,5},{2,6},{3,7},{4,8},{5,9},{6,10},{7,11},{8,12},{9,13},{1... | collective-permute-start | bytes 1216520 | tf_op jit(solution)/shard_map/ppermute | solution.py:194
  50.6 2.9 %collective-permute-start.3 = (bf16[528,384]{1,0:T(8,128)(2,1)S(1)}, bf16[528,384]{1,0:T(8,128)(2,1)S(1)}, u32[]{:S(2)}, u32[]{:S(2)}) collective-permute-start(bf16[528,384]{1,0:T(8,128)(2,1)S(1)} %pad_maximum_fusion.refs_0_.refs_1_), channel_id=1, source_target_pairs={{0,12},{1,13},{2,14},{3,15},{4,0},{5,1},{6,2},{7,3},{8,4},{9,5},{1... | collective-permute-start | bytes 1216520 | tf_op jit(solution)/shard_map/ppermute | solution.py:194
  53.4 3.2 %collective-permute-start.2 = (bf16[528,384]{1,0:T(8,128)(2,1)S(1)}, bf16[528,384]{1,0:T(8,128)(2,1)S(1)}, u32[]{:S(2)}, u32[]{:S(2)}) collective-permute-start(bf16[528,384]{1,0:T(8,128)(2,1)S(1)} %pad_maximum_fusion.refs_0_.refs_1_), channel_id=1, source_target_pairs={{0,1},{1,2},{2,3},{3,0},{4,5},{5,6},{6,7},{7,4},{8,9},{9,10},{10,1... | collective-permute-start | bytes 1216520 | tf_op jit(solution)/shard_map/ppermute | solution.py:191
  56.7 3.4 %collective-permute-start.1 = (bf16[528,384]{1,0:T(8,128)(2,1)S(1)}, bf16[528,384]{1,0:T(8,128)(2,1)S(1)}, u32[]{:S(2)}, u32[]{:S(2)}) collective-permute-start(bf16[528,384]{1,0:T(8,128)(2,1)S(1)} %pad_maximum_fusion.refs_0_.refs_1_), channel_id=1, source_target_pairs={{0,3},{1,0},{2,1},{3,2},{4,7},{5,4},{6,5},{7,6},{8,11},{9,8},{10,9... | collective-permute-start | bytes 1216520 | tf_op jit(solution)/shard_map/ppermute | solution.py:191
  60.0 3.5 %collective-permute-start = (bf16[528,384]{1,0:T(8,128)(2,1)S(1)}, bf16[528,384]{1,0:T(8,128)(2,1)S(1)}, u32[]{:S(2)}, u32[]{:S(2)}) collective-permute-start(bf16[528,384]{1,0:T(8,128)(2,1)S(1)} %pad_maximum_fusion.refs_0_.refs_1_), channel_id=1, source_target_pairs={{0,2},{1,3},{2,0},{3,1},{4,6},{5,7},{6,4},{7,5},{8,10},{9,11},{10,... | collective-permute-start | bytes 1216520 | tf_op jit(solution)/shard_map/ppermute | solution.py:191
  63.6 26.0 %all-gather.3.cloned.1.call-done = bf16[768,768]{1,0:T(8,128)(2,1)} async-done(((bf16[192,768]{1,0:T(8,128)(2,1)}), bf16[768,768]{1,0:T(8,128)(2,1)}) %all-gather.3.cloned.1.call-update) | async-done | bytes 1179664 | tf_op jit(solution)/shard_map/all_gather | solution.py:173
  89.5 11.1 %collective-permute-done.4 = bf16[528,384]{1,0:T(8,128)(2,1)S(1)} collective-permute-done((bf16[528,384]{1,0:T(8,128)(2,1)S(1)}, bf16[528,384]{1,0:T(8,128)(2,1)S(1)}, u32[]{:S(2)}, u32[]{:S(2)}) %collective-permute-start.4) | collective-permute-done | bytes 405536 | tf_op jit(solution)/shard_map/ppermute | solution.py:194
  100.6 2.7 %collective-permute-done.3 = bf16[528,384]{1,0:T(8,128)(2,1)S(1)} collective-permute-done((bf16[528,384]{1,0:T(8,128)(2,1)S(1)}, bf16[528,384]{1,0:T(8,128)(2,1)S(1)}, u32[]{:S(2)}, u32[]{:S(2)}) %collective-permute-start.3) | collective-permute-done | bytes 405536 | tf_op jit(solution)/shard_map/ppermute | solution.py:194
  103.4 0.7 copy-done.9
  104.2 1.0 constant_dynamic-update-slice_fusion.1
  105.2 1.1 constant_dynamic-update-slice_fusion.refs_4_.refs_5_
  106.3 4.5 %collective-permute-start.8 = (bf16[1056,384]{1,0:T(8,128)(2,1)S(1)}, bf16[1056,384]{1,0:T(8,128)(2,1)S(1)}, u32[]{:S(2)}, u32[]{:S(2)}) collective-permute-start(bf16[1056,384]{1,0:T(8,128)(2,1)S(1)} %constant_dynamic-update-slice_fusion.refs_4_.refs_5_), channel_id=1, source_target_pairs={{0,3},{1,0},{2,1},{3,2},{4,7},{5,4},{6,5},{7,6},{8,11},{9,8},{10,9... | collective-permute-start | bytes 2433032 | tf_op jit(solution)/shard_map/ppermute | solution.py:191
  110.8 1.9 collective-permute-start.7
  112.7 1.0 slice.12
  113.7 6.5 %collective-permute-start.5 = (bf16[272,384]{1,0:T(8,128)(2,1)S(1)}, bf16[272,384]{1,0:T(8,128)(2,1)S(1)}, u32[]{:S(2)}, u32[]{:S(2)}) collective-permute-start(bf16[272,384]{1,0:T(8,128)(2,1)S(1)} %slice.12), channel_id=1, source_target_pairs={{0,4},{1,5},{2,6},{3,7},{4,8},{5,9},{6,10},{7,11},{8,12},{9,13},{1... | collective-permute-start | bytes 626696 | tf_op jit(solution)/shard_map/ppermute | solution.py:194
  120.2 1.0 slice.13
  121.1 2.7 %collective-permute-start.6 = (bf16[256,384]{1,0:T(8,128)(2,1)S(1)}, bf16[256,384]{1,0:T(8,128)(2,1)S(1)}, u32[]{:S(2)}, u32[]{:S(2)}) collective-permute-start(bf16[256,384]{1,0:T(8,128)(2,1)S(1)} %slice.13), channel_id=1, source_target_pairs={{0,12},{1,13},{2,14},{3,15},{4,0},{5,1},{6,2},{7,3},{8,4},{9,5},{1... | collective-permute-start | bytes 589832 | tf_op jit(solution)/shard_map/ppermute | solution.py:194
  123.8 3.8 %collective-permute-done.8.refs_6_.refs_7_ = bf16[1056,384]{1,0:T(8,128)(2,1)S(1)} collective-permute-done((bf16[1056,384]{1,0:T(8,128)(2,1)S(1)}, bf16[1056,384]{1,0:T(8,128)(2,1)S(1)}, u32[]{:S(2)}, u32[]{:S(2)}) %collective-permute-start.8) | collective-permute-done | bytes 811040 | tf_op jit(solution)/shard_map/ppermute | solution.py:191
  127.7 0.9 slice.21
  128.5 5.4 %collective-permute-start.10 = (bf16[528,384]{1,0:T(8,128)(2,1)}, bf16[528,384]{1,0:T(8,128)(2,1)}, u32[]{:S(2)}, u32[]{:S(2)}) collective-permute-start(bf16[528,384]{1,0:T(8,128)(2,1)} %slice.21), channel_id=1, source_target_pairs={{0,3},{1,0},{2,1},{3,2},{4,7},{5,4},{6,5},{7,6},{8,11},{9,8},{10,9... | collective-permute-start | bytes 1216520 | tf_op jit(solution)/shard_map/ppermute | solution.py:191
  134.0 8.3 %collective-permute-done.6 = bf16[256,384]{1,0:T(8,128)(2,1)S(1)} collective-permute-done((bf16[256,384]{1,0:T(8,128)(2,1)S(1)}, bf16[256,384]{1,0:T(8,128)(2,1)S(1)}, u32[]{:S(2)}, u32[]{:S(2)}) %collective-permute-start.6) | collective-permute-done | bytes 196640 | tf_op jit(solution)/shard_map/ppermute | solution.py:194
  142.2 0.8 slice.20
  143.1 1.9 collective-permute-start.9
  145.0 0.7 constant_dynamic-update-slice_fusion.3
  145.7 0.7 constant_dynamic-update-slice_fusion.2.refs_10_
  146.4 5.3 %collective-permute-start.13 = (bf16[528,384]{1,0:T(8,128)(2,1)}, bf16[528,384]{1,0:T(8,128)(2,1)}, u32[]{:S(2)}, u32[]{:S(2)}) collective-permute-start(bf16[528,384]{1,0:T(8,128)(2,1)} %constant_dynamic-update-slice_fusion.2.refs_10_), channel_id=1, source_target_pairs={{0,2},{1,3},{2,0},{3,1},{4,6},{5,7},{6,4},{7,5},{8,10},{9,11},{10,... | collective-permute-start | bytes 1216520 | tf_op jit(solution)/shard_map/ppermute | solution.py:191
  151.7 1.9 collective-permute-start.12
  153.7 3.4 %collective-permute-start.11 = (bf16[528,384]{1,0:T(8,128)(2,1)}, bf16[528,384]{1,0:T(8,128)(2,1)}, u32[]{:S(2)}, u32[]{:S(2)}) collective-permute-start(bf16[528,384]{1,0:T(8,128)(2,1)} %constant_dynamic-update-slice_fusion.2.refs_10_), channel_id=1, source_target_pairs={{0,1},{1,2},{2,3},{3,0},{4,5},{5,6},{6,7},{7,4},{8,9},{9,10},{10,1... | collective-permute-start | bytes 1216520 | tf_op jit(solution)/shard_map/ppermute | solution.py:191
  157.1 0.9 copy.14.refs_17_
  157.9 0.6 fusion.refs_0_
  158.6 9.1 %row_moments.1 = (f32[512,128]{1,0:T(8,128)}, f32[512,128]{1,0:T(8,128)}) custom-call(bf16[528,384]{1,0:T(8,128)(2,1)} %copy-done.4, bf16[528,384]{1,0:T(8,128)(2,1)} %copy-done.5, bf16[528,384]{1,0:T(8,128)(2,1)} %copy-done.6, bf16[528,384]{1,0:T(8,128)(2,1)} %copy-done.7, bf16[1056,384]{1,0:T(8,128)(2,1)} %copy-done.3, bf16[1056,384]{1,0:T(8,128)(2,1)} %copy-done.2, ...), custom_call_target="tpu_custom_call" | custom-call | tf_op jit(solution)/shard_map/row_moments/pallas_call | solution.py:256
  167.7 1.6 collective-permute-done.12.refs_12_
  169.3 6.4 %collective-permute-done.11.refs_11_ = bf16[528,384]{1,0:T(8,128)(2,1)} collective-permute-done((bf16[528,384]{1,0:T(8,128)(2,1)}, bf16[528,384]{1,0:T(8,128)(2,1)}, u32[]{:S(2)}, u32[]{:S(2)}) %collective-permute-start.11) | collective-permute-done | bytes 405536 | tf_op jit(solution)/shard_map/ppermute | solution.py:191
  175.8 22.0 %norm_project_attend.1 = bf16[512,256]{1,0:T(8,128)(2,1)} custom-call(s32[16]{0:T(128)} %fusion.refs_0_, bf16[528,384]{1,0:T(8,128)(2,1)} %copy-done.4, bf16[528,384]{1,0:T(8,128)(2,1)} %copy-done.5, bf16[528,384]{1,0:T(8,128)(2,1)} %copy-done.6, bf16[528,384]{1,0:T(8,128)(2,1)} %copy-done.7, bf16[1056,384]{1,0:T(8,128)(2,1)} %copy-done.3, ...), custom_call_target="tpu_custom_call" | custom-call | tf_op jit(solution)/shard_map/norm_project_attend/pallas_call | solution.py:263
  (49 shorter events, 0.4 us)
Async XLA Ops:
  6.5 1.9 copy-start
  6.5 151.4 %copy-start.12 = (s32[16]{0:T(128)S(1)}, s32[16]{0:T(128)}, u32[]{:S(2)}) copy-start(s32[16]{0:T(128)} %constant.94.clone) | copy-start | bytes 196
  6.5 151.4 %copy-start.13 = (s32[16]{0:T(128)S(1)}, s32[16]{0:T(128)}, u32[]{:S(2)}) copy-start(s32[16]{0:T(128)} %constant.93.clone) | copy-start | bytes 196
  6.5 35.6 %copy-start.11 = (bf16[384]{0:T(512)(128)(2,1)S(1)}, bf16[384]{0:T(512)(128)(2,1)}, u32[]{:S(2)}) copy-start(bf16[384]{0:T(512)(128)(2,1)} %param.10) | copy-start | bytes 2308
  12.0 28.1 %all-to-all-start = ((bf16[32,32,384]{2,1,0:T(8,128)(2,1)}), bf16[32,32,384]{2,1,0:T(8,128)(2,1)S(1)}, u32[]{:S(2)}, u32[]{:S(2)}) async-start(bf16[32,32,384]{2,1,0:T(8,128)(2,1)} %broadcast_select_fusion), calls=%async_computation | async-start | bytes 1572864 | tf_op jit(solution)/shard_map/all_to_all | solution.py:174
  21.4 68.1 %all-gather.3.cloned.1.call-start = ((), (), s32[]{:S(2)}) async-start(), calls=%async_computation.1 | async-start | bytes 1474560 | tf_op jit(solution)/shard_map/all_gather | solution.py:173
  22.2 153.6 %all-gather.5.cloned.1.call-start = ((), (), s32[]{:S(2)}) async-start(), calls=%async_computation.2 | async-start | bytes 10616832 | tf_op jit(solution)/shard_map/all_gather | solution.py:206
  22.3 153.5 %copy-start.10 = (s32[512]{0:T(512)}, s32[512]{0:T(512)S(1)}, u32[]{:S(2)}) copy-start(s32[512]{0:T(512)S(1)} %convert_reduce_fusion) | copy-start | bytes 6148
  42.2 63.0 %copy-start.4 = (bf16[528,384]{1,0:T(8,128)(2,1)}, bf16[528,384]{1,0:T(8,128)(2,1)S(1)}, u32[]{:S(2)}) copy-start(bf16[528,384]{1,0:T(8,128)(2,1)S(1)} %pad_maximum_fusion.refs_0_.refs_1_) | copy-start | bytes 1216516
  42.2 58.4 %collective-permute-start.4 = (bf16[528,384]{1,0:T(8,128)(2,1)S(1)}, bf16[528,384]{1,0:T(8,128)(2,1)S(1)}, u32[]{:S(2)}, u32[]{:S(2)}) collective-permute-start(bf16[528,384]{1,0:T(8,128)(2,1)S(1)} %pad_maximum_fusion.refs_0_.refs_1_), channel_id=1, source_target_pairs={{0,4},{1,5},{2,6},{3,7},{4,8},{5,9},{6,10},{7,11},{8,12},{9,13},{1... | collective-permute-start | bytes 1216520 | tf_op jit(solution)/shard_map/ppermute | solution.py:194
  50.6 52.8 %collective-permute-start.3 = (bf16[528,384]{1,0:T(8,128)(2,1)S(1)}, bf16[528,384]{1,0:T(8,128)(2,1)S(1)}, u32[]{:S(2)}, u32[]{:S(2)}) collective-permute-start(bf16[528,384]{1,0:T(8,128)(2,1)S(1)} %pad_maximum_fusion.refs_0_.refs_1_), channel_id=1, source_target_pairs={{0,12},{1,13},{2,14},{3,15},{4,0},{5,1},{6,2},{7,3},{8,4},{9,5},{1... | collective-permute-start | bytes 1216520 | tf_op jit(solution)/shard_map/ppermute | solution.py:194
  53.4 49.9 %collective-permute-start.2 = (bf16[528,384]{1,0:T(8,128)(2,1)S(1)}, bf16[528,384]{1,0:T(8,128)(2,1)S(1)}, u32[]{:S(2)}, u32[]{:S(2)}) collective-permute-start(bf16[528,384]{1,0:T(8,128)(2,1)S(1)} %pad_maximum_fusion.refs_0_.refs_1_), channel_id=1, source_target_pairs={{0,1},{1,2},{2,3},{3,0},{4,5},{5,6},{6,7},{7,4},{8,9},{9,10},{10,1... | collective-permute-start | bytes 1216520 | tf_op jit(solution)/shard_map/ppermute | solution.py:191
  56.7 46.7 %collective-permute-start.1 = (bf16[528,384]{1,0:T(8,128)(2,1)S(1)}, bf16[528,384]{1,0:T(8,128)(2,1)S(1)}, u32[]{:S(2)}, u32[]{:S(2)}) collective-permute-start(bf16[528,384]{1,0:T(8,128)(2,1)S(1)} %pad_maximum_fusion.refs_0_.refs_1_), channel_id=1, source_target_pairs={{0,3},{1,0},{2,1},{3,2},{4,7},{5,4},{6,5},{7,6},{8,11},{9,8},{10,9... | collective-permute-start | bytes 1216520 | tf_op jit(solution)/shard_map/ppermute | solution.py:191
  60.0 43.4 %collective-permute-start = (bf16[528,384]{1,0:T(8,128)(2,1)S(1)}, bf16[528,384]{1,0:T(8,128)(2,1)S(1)}, u32[]{:S(2)}, u32[]{:S(2)}) collective-permute-start(bf16[528,384]{1,0:T(8,128)(2,1)S(1)} %pad_maximum_fusion.refs_0_.refs_1_), channel_id=1, source_target_pairs={{0,2},{1,3},{2,0},{3,1},{4,6},{5,7},{6,4},{7,5},{8,10},{9,11},{10,... | collective-permute-start | bytes 1216520 | tf_op jit(solution)/shard_map/ppermute | solution.py:191
  100.6 2.8 %copy-start.8 = (bf16[528,384]{1,0:T(8,128)(2,1)}, bf16[528,384]{1,0:T(8,128)(2,1)S(1)}, u32[]{:S(2)}) copy-start(bf16[528,384]{1,0:T(8,128)(2,1)S(1)} %collective-permute-done.4) | copy-start | bytes 1216516
  103.4 0.8 copy-start.9
  103.4 1.8 copy-start.5
  103.4 2.9 %copy-start.6 = (bf16[528,384]{1,0:T(8,128)(2,1)}, bf16[528,384]{1,0:T(8,128)(2,1)S(1)}, u32[]{:S(2)}) copy-start(bf16[528,384]{1,0:T(8,128)(2,1)S(1)} %collective-permute-done.1.refs_2_.refs_3_) | copy-start | bytes 1216516
  103.4 2.9 %copy-start.7 = (bf16[528,384]{1,0:T(8,128)(2,1)}, bf16[528,384]{1,0:T(8,128)(2,1)S(1)}, u32[]{:S(2)}) copy-start(bf16[528,384]{1,0:T(8,128)(2,1)S(1)} %collective-permute-done.refs_3_.refs_4_) | copy-start | bytes 1216516
  106.3 52.2 %copy-start.3 = (bf16[1056,384]{1,0:T(8,128)(2,1)}, bf16[1056,384]{1,0:T(8,128)(2,1)S(1)}, u32[]{:S(2)}) copy-start(bf16[1056,384]{1,0:T(8,128)(2,1)S(1)} %constant_dynamic-update-slice_fusion.refs_4_.refs_5_) | copy-start | bytes 2433028
  106.3 21.3 %collective-permute-start.8 = (bf16[1056,384]{1,0:T(8,128)(2,1)S(1)}, bf16[1056,384]{1,0:T(8,128)(2,1)S(1)}, u32[]{:S(2)}, u32[]{:S(2)}) collective-permute-start(bf16[1056,384]{1,0:T(8,128)(2,1)S(1)} %constant_dynamic-update-slice_fusion.refs_4_.refs_5_), channel_id=1, source_target_pairs={{0,3},{1,0},{2,1},{3,2},{4,7},{5,4},{6,5},{7,6},{8,11},{9,8},{10,9... | collective-permute-start | bytes 2433032 | tf_op jit(solution)/shard_map/ppermute | solution.py:191
  110.8 31.5 %collective-permute-start.7 = (bf16[1056,384]{1,0:T(8,128)(2,1)S(1)}, bf16[1056,384]{1,0:T(8,128)(2,1)S(1)}, u32[]{:S(2)}, u32[]{:S(2)}) collective-permute-start(bf16[1056,384]{1,0:T(8,128)(2,1)S(1)} %constant_dynamic-update-slice_fusion.refs_4_.refs_5_), channel_id=1, source_target_pairs={{0,1},{1,2},{2,3},{3,0},{4,5},{5,6},{6,7},{7,4},{8,9},{9,10},{10,1... | collective-permute-start | bytes 2433032 | tf_op jit(solution)/shard_map/ppermute | solution.py:191
  113.7 28.6 %collective-permute-start.5 = (bf16[272,384]{1,0:T(8,128)(2,1)S(1)}, bf16[272,384]{1,0:T(8,128)(2,1)S(1)}, u32[]{:S(2)}, u32[]{:S(2)}) collective-permute-start(bf16[272,384]{1,0:T(8,128)(2,1)S(1)} %slice.12), channel_id=1, source_target_pairs={{0,4},{1,5},{2,6},{3,7},{4,8},{5,9},{6,10},{7,11},{8,12},{9,13},{1... | collective-permute-start | bytes 626696 | tf_op jit(solution)/shard_map/ppermute | solution.py:194
  121.1 21.1 %collective-permute-start.6 = (bf16[256,384]{1,0:T(8,128)(2,1)S(1)}, bf16[256,384]{1,0:T(8,128)(2,1)S(1)}, u32[]{:S(2)}, u32[]{:S(2)}) collective-permute-start(bf16[256,384]{1,0:T(8,128)(2,1)S(1)} %slice.13), channel_id=1, source_target_pairs={{0,12},{1,13},{2,14},{3,15},{4,0},{5,1},{6,2},{7,3},{8,4},{9,5},{1... | collective-permute-start | bytes 589832 | tf_op jit(solution)/shard_map/ppermute | solution.py:194
  127.7 30.9 %copy-start.1 = (bf16[1056,384]{1,0:T(8,128)(2,1)}, bf16[1056,384]{1,0:T(8,128)(2,1)S(1)}, u32[]{:S(2)}) copy-start(bf16[1056,384]{1,0:T(8,128)(2,1)S(1)} %collective-permute-done.8.refs_6_.refs_7_) | copy-start | bytes 2433028
  128.5 39.1 %collective-permute-start.10 = (bf16[528,384]{1,0:T(8,128)(2,1)}, bf16[528,384]{1,0:T(8,128)(2,1)}, u32[]{:S(2)}, u32[]{:S(2)}) collective-permute-start(bf16[528,384]{1,0:T(8,128)(2,1)} %slice.21), channel_id=1, source_target_pairs={{0,3},{1,0},{2,1},{3,2},{4,7},{5,4},{6,5},{7,6},{8,11},{9,8},{10,9... | collective-permute-start | bytes 1216520 | tf_op jit(solution)/shard_map/ppermute | solution.py:191
  142.2 16.3 %copy-start.2 = (bf16[1056,384]{1,0:T(8,128)(2,1)}, bf16[1056,384]{1,0:T(8,128)(2,1)S(1)}, u32[]{:S(2)}) copy-start(bf16[1056,384]{1,0:T(8,128)(2,1)S(1)} %collective-permute-done.7.refs_5_.refs_6_) | copy-start | bytes 2433028
  143.1 24.6 %collective-permute-start.9 = (bf16[528,384]{1,0:T(8,128)(2,1)}, bf16[528,384]{1,0:T(8,128)(2,1)}, u32[]{:S(2)}, u32[]{:S(2)}) collective-permute-start(bf16[528,384]{1,0:T(8,128)(2,1)} %slice.20), channel_id=1, source_target_pairs={{0,1},{1,2},{2,3},{3,0},{4,5},{5,6},{6,7},{7,4},{8,9},{9,10},{10,1... | collective-permute-start | bytes 1216520 | tf_op jit(solution)/shard_map/ppermute | solution.py:191
  146.4 21.3 %collective-permute-start.13 = (bf16[528,384]{1,0:T(8,128)(2,1)}, bf16[528,384]{1,0:T(8,128)(2,1)}, u32[]{:S(2)}, u32[]{:S(2)}) collective-permute-start(bf16[528,384]{1,0:T(8,128)(2,1)} %constant_dynamic-update-slice_fusion.2.refs_10_), channel_id=1, source_target_pairs={{0,2},{1,3},{2,0},{3,1},{4,6},{5,7},{6,4},{7,5},{8,10},{9,11},{10,... | collective-permute-start | bytes 1216520 | tf_op jit(solution)/shard_map/ppermute | solution.py:191
  151.7 17.6 %collective-permute-start.12 = (bf16[528,384]{1,0:T(8,128)(2,1)}, bf16[528,384]{1,0:T(8,128)(2,1)}, u32[]{:S(2)}, u32[]{:S(2)}) collective-permute-start(bf16[528,384]{1,0:T(8,128)(2,1)} %constant_dynamic-update-slice_fusion.2.refs_10_), channel_id=1, source_target_pairs={{0,3},{1,0},{2,1},{3,2},{4,7},{5,4},{6,5},{7,6},{8,11},{9,8},{10,9... | collective-permute-start | bytes 1216520 | tf_op jit(solution)/shard_map/ppermute | solution.py:191
  153.7 22.1 %collective-permute-start.11 = (bf16[528,384]{1,0:T(8,128)(2,1)}, bf16[528,384]{1,0:T(8,128)(2,1)}, u32[]{:S(2)}, u32[]{:S(2)}) collective-permute-start(bf16[528,384]{1,0:T(8,128)(2,1)} %constant_dynamic-update-slice_fusion.2.refs_10_), channel_id=1, source_target_pairs={{0,1},{1,2},{2,3},{3,0},{4,5},{5,6},{6,7},{7,4},{8,9},{9,10},{10,1... | collective-permute-start | bytes 1216520 | tf_op jit(solution)/shard_map/ppermute | solution.py:191
Sparse Core Ops, SparseCore 0:
  24.4 65.1 all-gather.2
  104.3 58.0 all-gather.4

commit v7 on v4

--- a/solution.py
+++ b/solution.py
@@ -28,6 +28,16 @@
         for z in range(Z_PARTS)
         for y in range(Y_PARTS)
     ]
+
+
+def dp_move(x_step, z_step, core_step):
+    pairs = []
+    for x in range(4):
+        for z in range(4):
+            for core in range(2):
+                to = (x + x_step) % 4 * 8 + (z + z_step) % 4 * 2 + (core + core_step) % 2
+                pairs.append((x * 8 + z * 2 + core, to))
+    return pairs
 
 
 def dp_groups(varying):
@@ -40,16 +50,18 @@
     return list(groups.values())
 
 
-def load_weights(source_ref, weight_ref, sem, strip):
+def load_weights(source_ref, weight_ref, sem, strip, my_lo):
     copies = []
     for x in range(4):
         for z in range(4):
             for core in range(2):
-                held, wanted = (x * 2 + core) * 4 + z, x * 8 + z * 2 + core
+                held = (x * 2 + core) * 4 + z
+                wanted = x * 8 + (my_lo - z + 4) % 4 * 2 + core
+                at = pl.multiple_of(wanted * strip, strip)
                 copies.append(
                     pltpu.make_async_copy(
                         source_ref.at[pl.ds(held * strip, strip), :],
-                        weight_ref.at[pl.ds(wanted * strip, strip), :],
+                        weight_ref.at[pl.ds(at, strip), :],
                         sem,
                     )
                 )
@@ -94,7 +106,7 @@
     places_ref, blocks = refs[0], refs[1 : 1 + count]
     source_ref, seg_col_ref, seg_row_ref, out_ref = refs[1 + count : 5 + count]
     normed_ref, weight_ref, sums_ref, sem = refs[5 + count :]
-    copies = load_weights(source_ref, weight_ref, sem, strip)
+    copies = load_weights(source_ref, weight_ref, sem, strip, places_ref[len(slots)])
     columns = slot_columns(places_ref, len(slots), blocks[0].shape[1])
 
     def part(pieces, row):
@@ -143,7 +155,7 @@
     local = q_weight.shape[1]
     strip = q_weight.shape[0]
     weight = jnp.concatenate([q_weight, k_weight, v_weight], axis=1)
-    weight = lax.all_gather(weight, "dp", axis=0, tiled=True, axis_index_groups=dp_groups("z"))
+    column = [lax.ppermute(weight, "dp", dp_move(0, k, 0)) for k in (1, 2, 3)]
     targets = jnp.arange(groups, dtype=jnp.int32)
     my_order = lax.dynamic_index_in_dim(line_order, page_index, 0, keepdims=False)
     slot_for = jnp.sum(
@@ -152,6 +164,9 @@
     slots = page_patches.reshape(groups, slot_rows, width)
     outgoing = jnp.take(slots, slot_for, axis=0)
     incoming = lax.all_to_all(outgoing, "dp", split_axis=0, concat_axis=0, tiled=True)
+    incoming, *column = lax.optimization_barrier((incoming, *column))
+    weight = jnp.concatenate([weight] + column, axis=0)
+    weight = lax.all_gather(weight, "dp", axis=0, tiled=True, axis_index_groups=dp_groups("xc"))
     my_lengths = lax.dynamic_index_in_dim(pack_lengths, page_index, 0, keepdims=False)
     line_ends = jnp.cumsum(my_lengths)
     line_starts = line_ends - my_lengths
@@ -173,25 +188,25 @@
     def along_z(block, step):
         return lax.ppermute(block, "tensor", z_shift(step))
 
-    own_far, own_down, own_up, z_down, z_up, weight = lax.optimization_barrier(
+    z_up, z_down, own_up, own_down, own_far = lax.optimization_barrier(
         (
+            along_z(own, 1),
+            along_z(own, -1),
+            along_y(own, 1),
+            along_y(own, -1),
             along_y(own, 2),
-            along_y(own, -1),
-            along_y(own, 1),
-            along_z(own, -1),
-            along_z(own, 1),
-            weight,
         )
     )
-    weight = lax.all_gather(weight, "dp", axis=0, tiled=True, axis_index_groups=dp_groups("xc"))
     pair = jnp.concatenate([z_up, z_down], axis=0)
-    pair_down, pair_up, far_rest, far_top = lax.optimization_barrier(
-        (along_y(pair, -1), along_y(pair, 1), along_z(z_down[cut:], -1), along_z(z_up[:cut], 1))
+    pair_up, pair_down = along_y(pair, 1), along_y(pair, -1)
+    pair_far_up = along_y(pair_up[:all_rows], 1)
+    pair_far_down = along_y(pair_down[all_rows:], -1)
+    far_top, far_rest = along_z(z_up[:cut], 1), along_z(z_down[cut:], -1)
+    far_top, far_rest, pair_up, pair_down = lax.optimization_barrier(
+        (far_top, far_rest, pair_up, pair_down)
     )
     far = jnp.concatenate([far_top, far_rest], axis=0)
     far_far, far_down, far_up = along_y(far, 2), along_y(far, -1), along_y(far, 1)
-    pair_far_up = along_y(pair_up[:all_rows], 1)
-    pair_far_down = along_y(pair_down[all_rows:], -1)
 
     blocks, slots_at, shifts = [], [], []
 
@@ -220,6 +235,8 @@
     step_y = jnp.array([dy for _, dy in shifts], jnp.int32)
     places = (my_z + step_z + Z_PARTS) % Z_PARTS * Y_PARTS + (my_y + step_y + Y_PARTS) % Y_PARTS
 
+    places = jnp.concatenate([places, page_index[None] // 2 % 4])
+
     def kernel(*refs):
         project_attend_kernel(slots_at, len(blocks), rows, cut, strip, *refs)
 

time: 203 us -> 206 us (1.015)
  the two profiles are of different devices: /device:TPU:36 before, /device:TPU:56 now
where the time goes in v7:
time: 206 us
  waiting for transfers between devices  87.1 us (42%)
  starting transfers between devices  70.2 us (34%)
  Pallas kernels  20.9 us (10%)
  between operations  13.9 us (7%)
  local copies, waits for them, and re-layouts  9.17 us (4%)
  other arithmetic  4.19 us (2%)
    ppermute x4, waiting for transfers between devices, along_z(): return lax.ppermute(block, 'tensor', z_shift(step))  37.1 us
    ppermute x3, waiting for transfers between devices, shards(): column = [lax.ppermute(weight, 'dp', dp_move(0, k, 0)) for k in (1, 2, 3)]  34.4 us
    ppermute x10, starting transfers between devices, along_y(): return lax.ppermute(block, 'tensor', y_shift(step))  29.7 us
    ppermute x4, starting transfers between devices, along_z(): return lax.ppermute(block, 'tensor', z_shift(step))  21.7 us
    pallas_call x1, Pallas kernels, shards(): pl.pallas_call(kernel, out_shape=jax.ShapeDtypeStruct((rows, local), jnp....  20.9 us
    ppermute x10, waiting for transfers between devices, along_y(): return lax.ppermute(block, 'tensor', y_shift(step))  15.6 us
    ppermute x3, starting transfers between devices, shards(): column = [lax.ppermute(weight, 'dp', dp_move(0, k, 0)) for k in (1, 2, 3)]  10.1 us
    all_to_all x1, starting transfers between devices, shards(): lax.all_to_all(outgoing, 'dp', split_axis=0, concat_axis=0, tiled=True)  8.62 us
  transfers between devices with their start and end apart: 19, of which 11 were waited for; matrix products, arithmetic and copies ran while one was open for 3% of the time, Pallas kernels for 0%

profile of v7, /device:TPU:56, one launch (start us, length us, event | category | flops | bytes accessed | tf_op | source)
XLA Modules:
  0.0 205.5 jit_solution(7205378746611287014)
XLA Ops:
  6.5 0.8 fusion.6
  7.3 0.1 copy.13
  7.4 0.1 reduce
  7.6 0.7 fusion.5
  8.4 0.7 dynamic-slice_bitcast_fusion
  9.1 0.1 select_reduce_fusion.1
  9.4 0.7 gather_fusion
  10.1 1.1 broadcast_select_fusion
  11.1 8.6 %all-to-all-start = ((bf16[32,32,384]{2,1,0:T(8,128)(2,1)}), bf16[32,32,384]{2,1,0:T(8,128)(2,1)S(1)}, u32[]{:S(2)}, u32[]{:S(2)}) async-start(bf16[32,32,384]{2,1,0:T(8,128)(2,1)} %broadcast_select_fusion), calls=%async_computation | async-start | bytes 1572864 | tf_op jit(solution)/shard_map/all_to_all | solution.py:166
  19.9 3.4 %collective-permute-start = (bf16[192,768]{1,0:T(8,128)(2,1)S(1)}, bf16[192,768]{1,0:T(8,128)(2,1)S(1)}, u32[]{:S(2)}, u32[]{:S(2)}) collective-permute-start(bf16[192,768]{1,0:T(8,128)(2,1)S(1)} %constant_dynamic-update-slice_fusion), channel_id=1, source_target_pairs={{0,32},{16,48},{32,64},{48,80},{64,96},{80,112},{96,0},{112,16},{1... | collective-permute-start | bytes 884744 | tf_op jit(solution)/shard_map/ppermute | solution.py:158
  23.3 3.0 %collective-permute-start.1 = (bf16[192,768]{1,0:T(8,128)(2,1)S(1)}, bf16[192,768]{1,0:T(8,128)(2,1)S(1)}, u32[]{:S(2)}, u32[]{:S(2)}) collective-permute-start(bf16[192,768]{1,0:T(8,128)(2,1)S(1)} %constant_dynamic-update-slice_fusion), channel_id=1, source_target_pairs={{0,64},{16,80},{32,96},{48,112},{64,0},{80,16},{96,32},{112,48},{1... | collective-permute-start | bytes 884744 | tf_op jit(solution)/shard_map/ppermute | solution.py:158
  26.3 3.7 %collective-permute-start.2 = (bf16[192,768]{1,0:T(8,128)(2,1)S(1)}, bf16[192,768]{1,0:T(8,128)(2,1)S(1)}, u32[]{:S(2)}, u32[]{:S(2)}) collective-permute-start(bf16[192,768]{1,0:T(8,128)(2,1)S(1)} %constant_dynamic-update-slice_fusion), channel_id=1, source_target_pairs={{0,96},{16,112},{32,0},{48,16},{64,32},{80,48},{96,64},{112,80},{1... | collective-permute-start | bytes 884744 | tf_op jit(solution)/shard_map/ppermute | solution.py:158
  30.0 26.0 %collective-permute-done = bf16[192,768]{1,0:T(8,128)(2,1)S(1)} collective-permute-done((bf16[192,768]{1,0:T(8,128)(2,1)S(1)}, bf16[192,768]{1,0:T(8,128)(2,1)S(1)}, u32[]{:S(2)}, u32[]{:S(2)}) %collective-permute-start) | collective-permute-done | bytes 294944 | tf_op jit(solution)/shard_map/ppermute | solution.py:158
  56.1 6.3 %collective-permute-done.1 = bf16[192,768]{1,0:T(8,128)(2,1)S(1)} collective-permute-done((bf16[192,768]{1,0:T(8,128)(2,1)S(1)}, bf16[192,768]{1,0:T(8,128)(2,1)S(1)}, u32[]{:S(2)}, u32[]{:S(2)}) %collective-permute-start.1) | collective-permute-done | bytes 294944 | tf_op jit(solution)/shard_map/ppermute | solution.py:158
  62.3 2.1 %collective-permute-done.2 = bf16[192,768]{1,0:T(8,128)(2,1)S(1)} collective-permute-done((bf16[192,768]{1,0:T(8,128)(2,1)S(1)}, bf16[192,768]{1,0:T(8,128)(2,1)S(1)}, u32[]{:S(2)}, u32[]{:S(2)}) %collective-permute-start.2) | collective-permute-done | bytes 294944 | tf_op jit(solution)/shard_map/ppermute | solution.py:158
  64.5 1.1 pad_maximum_fusion
  65.6 1.9 gather_fusion.1
  67.6 0.1 broadcast_select_fusion.1
  67.8 9.1 %collective-permute-start.3 = (bf16[528,384]{1,0:T(8,128)(2,1)S(1)}, bf16[528,384]{1,0:T(8,128)(2,1)S(1)}, u32[]{:S(2)}, u32[]{:S(2)}) collective-permute-start(bf16[528,384]{1,0:T(8,128)(2,1)S(1)} %pad_maximum_fusion.1.refs_1_), channel_id=1, source_target_pairs={{0,4},{1,5},{2,6},{3,7},{4,8},{5,9},{6,10},{7,11},{8,12},{9,13},{1... | collective-permute-start | bytes 1216520 | tf_op jit(solution)/shard_map/ppermute | solution.py:189
  76.9 2.9 %collective-permute-start.4 = (bf16[528,384]{1,0:T(8,128)(2,1)S(1)}, bf16[528,384]{1,0:T(8,128)(2,1)S(1)}, u32[]{:S(2)}, u32[]{:S(2)}) collective-permute-start(bf16[528,384]{1,0:T(8,128)(2,1)S(1)} %pad_maximum_fusion.1.refs_1_), channel_id=1, source_target_pairs={{0,12},{1,13},{2,14},{3,15},{4,0},{5,1},{6,2},{7,3},{8,4},{9,5},{1... | collective-permute-start | bytes 1216520 | tf_op jit(solution)/shard_map/ppermute | solution.py:189
  79.8 2.1 %collective-permute-start.5 = (bf16[528,384]{1,0:T(8,128)(2,1)S(1)}, bf16[528,384]{1,0:T(8,128)(2,1)S(1)}, u32[]{:S(2)}, u32[]{:S(2)}) collective-permute-start(bf16[528,384]{1,0:T(8,128)(2,1)S(1)} %pad_maximum_fusion.1.refs_1_), channel_id=1, source_target_pairs={{0,1},{1,2},{2,3},{3,0},{4,5},{5,6},{6,7},{7,4},{8,9},{9,10},{10,1... | collective-permute-start | bytes 1216520 | tf_op jit(solution)/shard_map/ppermute | solution.py:186
  81.9 3.7 %collective-permute-start.6 = (bf16[528,384]{1,0:T(8,128)(2,1)S(1)}, bf16[528,384]{1,0:T(8,128)(2,1)S(1)}, u32[]{:S(2)}, u32[]{:S(2)}) collective-permute-start(bf16[528,384]{1,0:T(8,128)(2,1)S(1)} %pad_maximum_fusion.1.refs_1_), channel_id=1, source_target_pairs={{0,3},{1,0},{2,1},{3,2},{4,7},{5,4},{6,5},{7,6},{8,11},{9,8},{10,9... | collective-permute-start | bytes 1216520 | tf_op jit(solution)/shard_map/ppermute | solution.py:186
  85.6 3.1 %collective-permute-start.7 = (bf16[528,384]{1,0:T(8,128)(2,1)S(1)}, bf16[528,384]{1,0:T(8,128)(2,1)}, u32[]{:S(2)}, u32[]{:S(2)}) collective-permute-start(bf16[528,384]{1,0:T(8,128)(2,1)S(1)} %pad_maximum_fusion.1.refs_1_), channel_id=1, source_target_pairs={{0,2},{1,3},{2,0},{3,1},{4,6},{5,7},{6,4},{7,5},{8,10},{9,11},{10,... | collective-permute-start | bytes 1216520 | tf_op jit(solution)/shard_map/ppermute | solution.py:186
  88.8 1.8 collective-permute-done.3
  90.6 26.5 %collective-permute-done.4 = bf16[528,384]{1,0:T(8,128)(2,1)S(1)} collective-permute-done((bf16[528,384]{1,0:T(8,128)(2,1)S(1)}, bf16[528,384]{1,0:T(8,128)(2,1)S(1)}, u32[]{:S(2)}, u32[]{:S(2)}) %collective-permute-start.4) | collective-permute-done | bytes 405536 | tf_op jit(solution)/shard_map/ppermute | solution.py:189
  117.2 0.8 copy-done.6
  118.1 2.1 %collective-permute-start.10 = (bf16[1056,384]{1,0:T(8,128)(2,1)S(1)}, bf16[1056,384]{1,0:T(8,128)(2,1)S(1)}, u32[]{:S(2)}, u32[]{:S(2)}) collective-permute-start(bf16[1056,384]{1,0:T(8,128)(2,1)S(1)} %constant_dynamic-update-slice_fusion.3.refs_5_), channel_id=1, source_target_pairs={{0,1},{1,2},{2,3},{3,0},{4,5},{5,6},{6,7},{7,4},{8,9},{9,10},{10,1... | collective-permute-start | bytes 2433032 | tf_op jit(solution)/shard_map/ppermute | solution.py:186
  120.1 3.8 %collective-permute-start.11 = (bf16[1056,384]{1,0:T(8,128)(2,1)S(1)}, bf16[1056,384]{1,0:T(8,128)(2,1)S(1)}, u32[]{:S(2)}, u32[]{:S(2)}) collective-permute-start(bf16[1056,384]{1,0:T(8,128)(2,1)S(1)} %constant_dynamic-update-slice_fusion.3.refs_5_), channel_id=1, source_target_pairs={{0,3},{1,0},{2,1},{3,2},{4,7},{5,4},{6,5},{7,6},{8,11},{9,8},{10,9... | collective-permute-start | bytes 2433032 | tf_op jit(solution)/shard_map/ppermute | solution.py:186
  124.0 4.0 %collective-permute-start.8 = (bf16[272,384]{1,0:T(8,128)(2,1)S(1)}, bf16[272,384]{1,0:T(8,128)(2,1)S(1)}, u32[]{:S(2)}, u32[]{:S(2)}) collective-permute-start(bf16[272,384]{1,0:T(8,128)(2,1)S(1)} %slice.12), channel_id=1, source_target_pairs={{0,4},{1,5},{2,6},{3,7},{4,8},{5,9},{6,10},{7,11},{8,12},{9,13},{1... | collective-permute-start | bytes 626696 | tf_op jit(solution)/shard_map/ppermute | solution.py:189
  128.0 5.8 %collective-permute-start.9 = (bf16[256,384]{1,0:T(8,128)(2,1)S(1)}, bf16[256,384]{1,0:T(8,128)(2,1)S(1)}, u32[]{:S(2)}, u32[]{:S(2)}) collective-permute-start(bf16[256,384]{1,0:T(8,128)(2,1)S(1)} %slice.13), channel_id=1, source_target_pairs={{0,12},{1,13},{2,14},{3,15},{4,0},{5,1},{6,2},{7,3},{8,4},{9,5},{1... | collective-permute-start | bytes 589832 | tf_op jit(solution)/shard_map/ppermute | solution.py:189
  133.8 8.7 %collective-permute-done.9 = bf16[256,384]{1,0:T(8,128)(2,1)S(1)} collective-permute-done((bf16[256,384]{1,0:T(8,128)(2,1)S(1)}, bf16[256,384]{1,0:T(8,128)(2,1)S(1)}, u32[]{:S(2)}, u32[]{:S(2)}) %collective-permute-start.9) | collective-permute-done | bytes 196640 | tf_op jit(solution)/shard_map/ppermute | solution.py:189
  142.5 0.5 collective-permute-done.11.refs_7_
  143.0 0.8 constant_dynamic-update-slice_fusion.6
  143.8 0.7 constant_dynamic-update-slice_fusion.5.refs_10_
  144.5 2.7 %collective-permute-start.14 = (bf16[528,384]{1,0:T(8,128)(2,1)}, bf16[528,384]{1,0:T(8,128)(2,1)}, u32[]{:S(2)}, u32[]{:S(2)}) collective-permute-start(bf16[528,384]{1,0:T(8,128)(2,1)} %constant_dynamic-update-slice_fusion.5.refs_10_), channel_id=1, source_target_pairs={{0,1},{1,2},{2,3},{3,0},{4,5},{5,6},{6,7},{7,4},{8,9},{9,10},{10,1... | collective-permute-start | bytes 1216520 | tf_op jit(solution)/shard_map/ppermute | solution.py:186
  147.2 3.1 %collective-permute-start.15 = (bf16[528,384]{1,0:T(8,128)(2,1)}, bf16[528,384]{1,0:T(8,128)(2,1)}, u32[]{:S(2)}, u32[]{:S(2)}) collective-permute-start(bf16[528,384]{1,0:T(8,128)(2,1)} %constant_dynamic-update-slice_fusion.5.refs_10_), channel_id=1, source_target_pairs={{0,3},{1,0},{2,1},{3,2},{4,7},{5,4},{6,5},{7,6},{8,11},{9,8},{10,9... | collective-permute-start | bytes 1216520 | tf_op jit(solution)/shard_map/ppermute | solution.py:186
  150.3 3.2 %collective-permute-start.16 = (bf16[528,384]{1,0:T(8,128)(2,1)}, bf16[528,384]{1,0:T(8,128)(2,1)}, u32[]{:S(2)}, u32[]{:S(2)}) collective-permute-start(bf16[528,384]{1,0:T(8,128)(2,1)} %constant_dynamic-update-slice_fusion.5.refs_10_), channel_id=1, source_target_pairs={{0,2},{1,3},{2,0},{3,1},{4,6},{5,7},{6,4},{7,5},{8,10},{9,11},{10,... | collective-permute-start | bytes 1216520 | tf_op jit(solution)/shard_map/ppermute | solution.py:186
  153.6 0.8 slice.20
  154.4 3.8 %collective-permute-start.12 = (bf16[528,384]{1,0:T(8,128)(2,1)}, bf16[528,384]{1,0:T(8,128)(2,1)}, u32[]{:S(2)}, u32[]{:S(2)}) collective-permute-start(bf16[528,384]{1,0:T(8,128)(2,1)} %slice.20), channel_id=1, source_target_pairs={{0,1},{1,2},{2,3},{3,0},{4,5},{5,6},{6,7},{7,4},{8,9},{9,10},{10,1... | collective-permute-start | bytes 1216520 | tf_op jit(solution)/shard_map/ppermute | solution.py:186
  158.2 0.8 slice.21
  159.0 2.1 %collective-permute-start.13 = (bf16[528,384]{1,0:T(8,128)(2,1)}, bf16[528,384]{1,0:T(8,128)(2,1)}, u32[]{:S(2)}, u32[]{:S(2)}) collective-permute-start(bf16[528,384]{1,0:T(8,128)(2,1)} %slice.21), channel_id=1, source_target_pairs={{0,3},{1,0},{2,1},{3,2},{4,7},{5,4},{6,5},{7,6},{8,11},{9,8},{10,9... | collective-permute-start | bytes 1216520 | tf_op jit(solution)/shard_map/ppermute | solution.py:186
  161.1 0.9 copy.14.refs_15_
  162.0 0.6 pad_add_fusion.refs_0_
  162.6 5.2 %collective-permute-done.15.refs_12_ = bf16[528,384]{1,0:T(8,128)(2,1)} collective-permute-done((bf16[528,384]{1,0:T(8,128)(2,1)}, bf16[528,384]{1,0:T(8,128)(2,1)}, u32[]{:S(2)}, u32[]{:S(2)}) %collective-permute-start.15) | collective-permute-done | bytes 405536 | tf_op jit(solution)/shard_map/ppermute | solution.py:186
  167.8 3.2 %collective-permute-done.16.refs_13_ = bf16[528,384]{1,0:T(8,128)(2,1)} collective-permute-done((bf16[528,384]{1,0:T(8,128)(2,1)}, bf16[528,384]{1,0:T(8,128)(2,1)}, u32[]{:S(2)}, u32[]{:S(2)}) %collective-permute-start.16) | collective-permute-done | bytes 405536 | tf_op jit(solution)/shard_map/ppermute | solution.py:186
  171.0 3.3 %collective-permute-done.12.refs_8_ = bf16[528,384]{1,0:T(8,128)(2,1)} collective-permute-done((bf16[528,384]{1,0:T(8,128)(2,1)}, bf16[528,384]{1,0:T(8,128)(2,1)}, u32[]{:S(2)}, u32[]{:S(2)}) %collective-permute-start.12) | collective-permute-done | bytes 405536 | tf_op jit(solution)/shard_map/ppermute | solution.py:186
  174.3 3.4 %collective-permute-done.13.refs_9_ = bf16[528,384]{1,0:T(8,128)(2,1)} collective-permute-done((bf16[528,384]{1,0:T(8,128)(2,1)}, bf16[528,384]{1,0:T(8,128)(2,1)}, u32[]{:S(2)}, u32[]{:S(2)}) %collective-permute-start.13) | collective-permute-done | bytes 405536 | tf_op jit(solution)/shard_map/ppermute | solution.py:186
  177.7 20.9 %norm_project_attend.1 = bf16[512,256]{1,0:T(8,128)(2,1)} custom-call(s32[17]{0:T(128)} %pad_add_fusion.refs_0_, bf16[528,384]{1,0:T(8,128)(2,1)} %copy-done.4, bf16[528,384]{1,0:T(8,128)(2,1)} %copy-done.5, bf16[528,384]{1,0:T(8,128)(2,1)} %copy-done.6, bf16[528,384]{1,0:T(8,128)(2,1)} %collective-permute-done.7.refs_4_, bf16[1056,384]{1,0:T(8,128)(2,1)} %copy-done.3, ...), custom_call_target="tpu_custom_call" | custom-call | tf_op jit(solution)/shard_map/norm_project_attend/pallas_call | solution.py:246
  (55 shorter events, 0.7 us)
Async XLA Ops:
  6.5 2.8 %copy-start = (bf16[1024,384]{1,0:T(8,128)(2,1)S(1)}, bf16[1024,384]{1,0:T(8,128)(2,1)}, u32[]{:S(2)}) copy-start(bf16[1024,384]{1,0:T(8,128)(2,1)} %param.9) | copy-start | bytes 2359300
  8.4 152.7 %copy-start.10 = (s32[512]{0:T(512)}, s32[512]{0:T(512)S(1)}, u32[]{:S(2)}) copy-start(s32[512]{0:T(512)S(1)} %convert_reduce_fusion) | copy-start | bytes 6148
  9.3 10.5 %copy-start.7 = (bf16[192,256]{1,0:T(8,128)(2,1)S(1)}, bf16[192,256]{1,0:T(8,128)(2,1)}, u32[]{:S(2)}) copy-start(bf16[192,256]{1,0:T(8,128)(2,1)} %param.11) | copy-start | bytes 294916
  9.3 10.5 %copy-start.8 = (bf16[192,256]{1,0:T(8,128)(2,1)S(1)}, bf16[192,256]{1,0:T(8,128)(2,1)}, u32[]{:S(2)}) copy-start(bf16[192,256]{1,0:T(8,128)(2,1)} %param.12) | copy-start | bytes 294916
  9.3 10.5 %copy-start.9 = (bf16[192,256]{1,0:T(8,128)(2,1)S(1)}, bf16[192,256]{1,0:T(8,128)(2,1)}, u32[]{:S(2)}) copy-start(bf16[192,256]{1,0:T(8,128)(2,1)} %param.13) | copy-start | bytes 294916
  11.1 53.3 %all-to-all-start = ((bf16[32,32,384]{2,1,0:T(8,128)(2,1)}), bf16[32,32,384]{2,1,0:T(8,128)(2,1)S(1)}, u32[]{:S(2)}, u32[]{:S(2)}) async-start(bf16[32,32,384]{2,1,0:T(8,128)(2,1)} %broadcast_select_fusion), calls=%async_computation | async-start | bytes 1572864 | tf_op jit(solution)/shard_map/all_to_all | solution.py:166
  19.8 157.9 %all-gather.2.cloned.1.call-start = ((), (), s32[]{:S(2)}) async-start(), calls=%async_computation.1 | async-start | bytes 10616832 | tf_op jit(solution)/shard_map/all_gather | solution.py:169
  19.9 36.2 %collective-permute-start = (bf16[192,768]{1,0:T(8,128)(2,1)S(1)}, bf16[192,768]{1,0:T(8,128)(2,1)S(1)}, u32[]{:S(2)}, u32[]{:S(2)}) collective-permute-start(bf16[192,768]{1,0:T(8,128)(2,1)S(1)} %constant_dynamic-update-slice_fusion), channel_id=1, source_target_pairs={{0,32},{16,48},{32,64},{48,80},{64,96},{80,112},{96,0},{112,16},{1... | collective-permute-start | bytes 884744 | tf_op jit(solution)/shard_map/ppermute | solution.py:158
  23.3 39.1 %collective-permute-start.1 = (bf16[192,768]{1,0:T(8,128)(2,1)S(1)}, bf16[192,768]{1,0:T(8,128)(2,1)S(1)}, u32[]{:S(2)}, u32[]{:S(2)}) collective-permute-start(bf16[192,768]{1,0:T(8,128)(2,1)S(1)} %constant_dynamic-update-slice_fusion), channel_id=1, source_target_pairs={{0,64},{16,80},{32,96},{48,112},{64,0},{80,16},{96,32},{112,48},{1... | collective-permute-start | bytes 884744 | tf_op jit(solution)/shard_map/ppermute | solution.py:158
  26.3 38.1 %collective-permute-start.2 = (bf16[192,768]{1,0:T(8,128)(2,1)S(1)}, bf16[192,768]{1,0:T(8,128)(2,1)S(1)}, u32[]{:S(2)}, u32[]{:S(2)}) collective-permute-start(bf16[192,768]{1,0:T(8,128)(2,1)S(1)} %constant_dynamic-update-slice_fusion), channel_id=1, source_target_pairs={{0,96},{16,112},{32,0},{48,16},{64,32},{80,48},{96,64},{112,80},{1... | collective-permute-start | bytes 884744 | tf_op jit(solution)/shard_map/ppermute | solution.py:158
  65.6 2.1 %copy-start.11 = (bf16[384]{0:T(512)(128)(2,1)S(1)}, bf16[384]{0:T(512)(128)(2,1)}, u32[]{:S(2)}) copy-start(bf16[384]{0:T(512)(128)(2,1)} %param.10) | copy-start | bytes 2308
  67.8 91.2 %copy-start.4 = (bf16[528,384]{1,0:T(8,128)(2,1)}, bf16[528,384]{1,0:T(8,128)(2,1)S(1)}, u32[]{:S(2)}) copy-start(bf16[528,384]{1,0:T(8,128)(2,1)S(1)} %pad_maximum_fusion.1.refs_1_) | copy-start | bytes 1216516
  67.8 22.8 %collective-permute-start.3 = (bf16[528,384]{1,0:T(8,128)(2,1)S(1)}, bf16[528,384]{1,0:T(8,128)(2,1)S(1)}, u32[]{:S(2)}, u32[]{:S(2)}) collective-permute-start(bf16[528,384]{1,0:T(8,128)(2,1)S(1)} %pad_maximum_fusion.1.refs_1_), channel_id=1, source_target_pairs={{0,4},{1,5},{2,6},{3,7},{4,8},{5,9},{6,10},{7,11},{8,12},{9,13},{1... | collective-permute-start | bytes 1216520 | tf_op jit(solution)/shard_map/ppermute | solution.py:189
  76.9 40.2 %collective-permute-start.4 = (bf16[528,384]{1,0:T(8,128)(2,1)S(1)}, bf16[528,384]{1,0:T(8,128)(2,1)S(1)}, u32[]{:S(2)}, u32[]{:S(2)}) collective-permute-start(bf16[528,384]{1,0:T(8,128)(2,1)S(1)} %pad_maximum_fusion.1.refs_1_), channel_id=1, source_target_pairs={{0,12},{1,13},{2,14},{3,15},{4,0},{5,1},{6,2},{7,3},{8,4},{9,5},{1... | collective-permute-start | bytes 1216520 | tf_op jit(solution)/shard_map/ppermute | solution.py:189
  79.8 37.4 %collective-permute-start.5 = (bf16[528,384]{1,0:T(8,128)(2,1)S(1)}, bf16[528,384]{1,0:T(8,128)(2,1)S(1)}, u32[]{:S(2)}, u32[]{:S(2)}) collective-permute-start(bf16[528,384]{1,0:T(8,128)(2,1)S(1)} %pad_maximum_fusion.1.refs_1_), channel_id=1, source_target_pairs={{0,1},{1,2},{2,3},{3,0},{4,5},{5,6},{6,7},{7,4},{8,9},{9,10},{10,1... | collective-permute-start | bytes 1216520 | tf_op jit(solution)/shard_map/ppermute | solution.py:186
  81.9 35.2 %collective-permute-start.6 = (bf16[528,384]{1,0:T(8,128)(2,1)S(1)}, bf16[528,384]{1,0:T(8,128)(2,1)S(1)}, u32[]{:S(2)}, u32[]{:S(2)}) collective-permute-start(bf16[528,384]{1,0:T(8,128)(2,1)S(1)} %pad_maximum_fusion.1.refs_1_), channel_id=1, source_target_pairs={{0,3},{1,0},{2,1},{3,2},{4,7},{5,4},{6,5},{7,6},{8,11},{9,8},{10,9... | collective-permute-start | bytes 1216520 | tf_op jit(solution)/shard_map/ppermute | solution.py:186
  85.6 32.3 %collective-permute-start.7 = (bf16[528,384]{1,0:T(8,128)(2,1)S(1)}, bf16[528,384]{1,0:T(8,128)(2,1)}, u32[]{:S(2)}, u32[]{:S(2)}) collective-permute-start(bf16[528,384]{1,0:T(8,128)(2,1)S(1)} %pad_maximum_fusion.1.refs_1_), channel_id=1, source_target_pairs={{0,2},{1,3},{2,0},{3,1},{4,6},{5,7},{6,4},{7,5},{8,10},{9,11},{10,... | collective-permute-start | bytes 1216520 | tf_op jit(solution)/shard_map/ppermute | solution.py:186
  117.1 41.8 %copy-start.5 = (bf16[528,384]{1,0:T(8,128)(2,1)}, bf16[528,384]{1,0:T(8,128)(2,1)S(1)}, u32[]{:S(2)}) copy-start(bf16[528,384]{1,0:T(8,128)(2,1)S(1)} %collective-permute-done.5.refs_2_) | copy-start | bytes 1216516
  117.1 0.8 copy-start.6
  118.0 44.0 %copy-start.12 = (s32[16]{0:T(128)S(1)}, s32[16]{0:T(128)}, u32[]{:S(2)}) copy-start(s32[16]{0:T(128)} %constant.127.clone) | copy-start | bytes 196
  118.0 44.0 %copy-start.13 = (s32[16]{0:T(128)S(1)}, s32[16]{0:T(128)}, u32[]{:S(2)}) copy-start(s32[16]{0:T(128)} %constant.128.clone) | copy-start | bytes 196
  118.1 59.6 %copy-start.3 = (bf16[1056,384]{1,0:T(8,128)(2,1)}, bf16[1056,384]{1,0:T(8,128)(2,1)S(1)}, u32[]{:S(2)}) copy-start(bf16[1056,384]{1,0:T(8,128)(2,1)S(1)} %constant_dynamic-update-slice_fusion.3.refs_5_) | copy-start | bytes 2433028
  118.1 24.4 %collective-permute-start.10 = (bf16[1056,384]{1,0:T(8,128)(2,1)S(1)}, bf16[1056,384]{1,0:T(8,128)(2,1)S(1)}, u32[]{:S(2)}, u32[]{:S(2)}) collective-permute-start(bf16[1056,384]{1,0:T(8,128)(2,1)S(1)} %constant_dynamic-update-slice_fusion.3.refs_5_), channel_id=1, source_target_pairs={{0,1},{1,2},{2,3},{3,0},{4,5},{5,6},{6,7},{7,4},{8,9},{9,10},{10,1... | collective-permute-start | bytes 2433032 | tf_op jit(solution)/shard_map/ppermute | solution.py:186
  120.1 22.9 %collective-permute-start.11 = (bf16[1056,384]{1,0:T(8,128)(2,1)S(1)}, bf16[1056,384]{1,0:T(8,128)(2,1)S(1)}, u32[]{:S(2)}, u32[]{:S(2)}) collective-permute-start(bf16[1056,384]{1,0:T(8,128)(2,1)S(1)} %constant_dynamic-update-slice_fusion.3.refs_5_), channel_id=1, source_target_pairs={{0,3},{1,0},{2,1},{3,2},{4,7},{5,4},{6,5},{7,6},{8,11},{9,8},{10,9... | collective-permute-start | bytes 2433032 | tf_op jit(solution)/shard_map/ppermute | solution.py:186
  124.0 18.5 %collective-permute-start.8 = (bf16[272,384]{1,0:T(8,128)(2,1)S(1)}, bf16[272,384]{1,0:T(8,128)(2,1)S(1)}, u32[]{:S(2)}, u32[]{:S(2)}) collective-permute-start(bf16[272,384]{1,0:T(8,128)(2,1)S(1)} %slice.12), channel_id=1, source_target_pairs={{0,4},{1,5},{2,6},{3,7},{4,8},{5,9},{6,10},{7,11},{8,12},{9,13},{1... | collective-permute-start | bytes 626696 | tf_op jit(solution)/shard_map/ppermute | solution.py:189
  128.0 14.5 %collective-permute-start.9 = (bf16[256,384]{1,0:T(8,128)(2,1)S(1)}, bf16[256,384]{1,0:T(8,128)(2,1)S(1)}, u32[]{:S(2)}, u32[]{:S(2)}) collective-permute-start(bf16[256,384]{1,0:T(8,128)(2,1)S(1)} %slice.13), channel_id=1, source_target_pairs={{0,12},{1,13},{2,14},{3,15},{4,0},{5,1},{6,2},{7,3},{8,4},{9,5},{1... | collective-permute-start | bytes 589832 | tf_op jit(solution)/shard_map/ppermute | solution.py:189
  142.5 35.2 %copy-start.1 = (bf16[1056,384]{1,0:T(8,128)(2,1)}, bf16[1056,384]{1,0:T(8,128)(2,1)S(1)}, u32[]{:S(2)}) copy-start(bf16[1056,384]{1,0:T(8,128)(2,1)S(1)} %collective-permute-done.10.refs_6_) | copy-start | bytes 2433028
  143.0 34.7 %copy-start.2 = (bf16[1056,384]{1,0:T(8,128)(2,1)}, bf16[1056,384]{1,0:T(8,128)(2,1)S(1)}, u32[]{:S(2)}) copy-start(bf16[1056,384]{1,0:T(8,128)(2,1)S(1)} %collective-permute-done.11.refs_7_) | copy-start | bytes 2433028
  144.5 18.1 %collective-permute-start.14 = (bf16[528,384]{1,0:T(8,128)(2,1)}, bf16[528,384]{1,0:T(8,128)(2,1)}, u32[]{:S(2)}, u32[]{:S(2)}) collective-permute-start(bf16[528,384]{1,0:T(8,128)(2,1)} %constant_dynamic-update-slice_fusion.5.refs_10_), channel_id=1, source_target_pairs={{0,1},{1,2},{2,3},{3,0},{4,5},{5,6},{6,7},{7,4},{8,9},{9,10},{10,1... | collective-permute-start | bytes 1216520 | tf_op jit(solution)/shard_map/ppermute | solution.py:186
  147.2 20.5 %collective-permute-start.15 = (bf16[528,384]{1,0:T(8,128)(2,1)}, bf16[528,384]{1,0:T(8,128)(2,1)}, u32[]{:S(2)}, u32[]{:S(2)}) collective-permute-start(bf16[528,384]{1,0:T(8,128)(2,1)} %constant_dynamic-update-slice_fusion.5.refs_10_), channel_id=1, source_target_pairs={{0,3},{1,0},{2,1},{3,2},{4,7},{5,4},{6,5},{7,6},{8,11},{9,8},{10,9... | collective-permute-start | bytes 1216520 | tf_op jit(solution)/shard_map/ppermute | solution.py:186
  150.3 20.7 %collective-permute-start.16 = (bf16[528,384]{1,0:T(8,128)(2,1)}, bf16[528,384]{1,0:T(8,128)(2,1)}, u32[]{:S(2)}, u32[]{:S(2)}) collective-permute-start(bf16[528,384]{1,0:T(8,128)(2,1)} %constant_dynamic-update-slice_fusion.5.refs_10_), channel_id=1, source_target_pairs={{0,2},{1,3},{2,0},{3,1},{4,6},{5,7},{6,4},{7,5},{8,10},{9,11},{10,... | collective-permute-start | bytes 1216520 | tf_op jit(solution)/shard_map/ppermute | solution.py:186
  154.4 19.9 %collective-permute-start.12 = (bf16[528,384]{1,0:T(8,128)(2,1)}, bf16[528,384]{1,0:T(8,128)(2,1)}, u32[]{:S(2)}, u32[]{:S(2)}) collective-permute-start(bf16[528,384]{1,0:T(8,128)(2,1)} %slice.20), channel_id=1, source_target_pairs={{0,1},{1,2},{2,3},{3,0},{4,5},{5,6},{6,7},{7,4},{8,9},{9,10},{10,1... | collective-permute-start | bytes 1216520 | tf_op jit(solution)/shard_map/ppermute | solution.py:186
  159.0 18.7 %collective-permute-start.13 = (bf16[528,384]{1,0:T(8,128)(2,1)}, bf16[528,384]{1,0:T(8,128)(2,1)}, u32[]{:S(2)}, u32[]{:S(2)}) collective-permute-start(bf16[528,384]{1,0:T(8,128)(2,1)} %slice.21), channel_id=1, source_target_pairs={{0,3},{1,0},{2,1},{3,2},{4,7},{5,4},{6,5},{7,6},{8,11},{9,8},{10,9... | collective-permute-start | bytes 1216520 | tf_op jit(solution)/shard_map/ppermute | solution.py:186
Sparse Core Ops, SparseCore 0:
  65.7 63.3 all-gather.1

commit v8 on v4

--- a/solution.py
+++ b/solution.py
@@ -62,57 +62,88 @@
     return [pl.ds(pl.multiple_of(places_ref[j] * width, 128), width) for j in range(count)]
 
 
-def normalize(sources, gains, columns, first, last, normed_ref):
+def normalize(block_ref, gains, columns, row, normed_ref):
     features = normed_ref.shape[1]
-
-    def step(i, carry):
-        at = pl.multiple_of(first + i * ROW_TILE, ROW_TILE)
-
-        def load(j):
-            ref, shift = sources[j]
-            return ref[pl.ds(at + shift, ROW_TILE), :].astype(jnp.float32)
-
-        total = load(0)
-        for j in range(1, len(sources)):
-            total = total + load(j)
-        mean = jnp.sum(total, axis=1, keepdims=True) * (1.0 / features)
-        square = jnp.square(load(0) - mean)
-        for j in range(1, len(sources)):
-            square = square + jnp.square(load(j) - mean)
-        var = jnp.sum(square, axis=1, keepdims=True) * (1.0 / features)
-        scale = lax.rsqrt(var + NORM_EPSILON)
-        for j in range(len(sources)):
-            normed_ref[pl.ds(at, ROW_TILE), columns[j]] = (
-                (load(j) - mean) * scale * gains[j]
-            ).astype(jnp.bfloat16)
-        return carry
-
-    lax.fori_loop(0, (last - first) // ROW_TILE, step, 0)
-
-
-def project_attend_kernel(slots, count, rows, cut, strip, *refs):
+    at = pl.multiple_of(row, ROW_TILE)
+
+    def load(j):
+        return block_ref[j, pl.ds(at, ROW_TILE), :].astype(jnp.float32)
+
+    total = load(0)
+    for j in range(1, len(gains)):
+        total = total + load(j)
+    mean = jnp.sum(total, axis=1, keepdims=True) * (1.0 / features)
+    square = jnp.square(load(0) - mean)
+    for j in range(1, len(gains)):
+        square = square + jnp.square(load(j) - mean)
+    var = jnp.sum(square, axis=1, keepdims=True) * (1.0 / features)
+    scale = lax.rsqrt(var + NORM_EPSILON)
+    for j in range(len(gains)):
+        normed_ref[pl.ds(at, ROW_TILE), columns[j]] = (
+            (load(j) - mean) * scale * gains[j]
+        ).astype(jnp.bfloat16)
+
+
+def project_attend_kernel(slots, count, rows, strip, *refs):
     places_ref, blocks = refs[0], refs[1 : 1 + count]
     source_ref, seg_col_ref, seg_row_ref, out_ref = refs[1 + count : 5 + count]
-    normed_ref, weight_ref, sums_ref, sem = refs[5 + count :]
-    copies = load_weights(source_ref, weight_ref, sem, strip)
-    columns = slot_columns(places_ref, len(slots), blocks[0].shape[1])
-
-    def part(pieces, row):
-        for ref, start, first, last in pieces:
-            if first <= row < last:
-                return blocks[ref], start - first
-
-    gains = []
-    for pieces in slots:
-        ref, shift = part(pieces, rows)
-        gains.append(ref[pl.ds(rows + shift, GAIN_ROWS), :][:1].astype(jnp.float32))
-    for first, last in ((0, cut), (cut, rows)):
-        sources = [part(pieces, first) for pieces in slots]
-        normalize(sources, gains, columns, first, last, normed_ref)
-    for copy in copies:
+    block_ref, normed_ref, weight_ref, total_ref, sums_ref, sem, block_sem = refs[5 + count :]
+    width, features = block_ref.shape[2], normed_ref.shape[1]
+    half = rows // 2
+    parts = [(rows, GAIN_ROWS)] + [(row, rows // 4) for row in range(0, rows, rows // 4)]
+    block_copies = []
+    for k, (row, size) in enumerate(parts):
+        block_copies.append(
+            [
+                pltpu.make_async_copy(
+                    blocks[ref].at[pl.ds(start + row, size), :],
+                    block_ref.at[j, pl.ds(row, size), :],
+                    block_sem.at[k],
+                )
+                for j, (ref, start) in enumerate(slots)
+            ]
+        )
+    for copies in block_copies:
+        for copy in copies:
+            copy.start()
+    weight_copies = load_weights(source_ref, weight_ref, sem, strip)
+    columns = slot_columns(places_ref, len(slots), width)
+    for copy in block_copies[0]:
         copy.wait()
-    sums_ref[...] = jnp.dot(
-        normed_ref[...], weight_ref[...], preferred_element_type=jnp.float32
+    gains = [
+        block_ref[j, pl.ds(rows, GAIN_ROWS), :][:1].astype(jnp.float32) for j in range(len(slots))
+    ]
+
+    for k in range(2):
+        for copy in block_copies[1 + k]:
+            copy.wait()
+
+        def first_step(i, carry):
+            normalize(block_ref, gains, columns, k * rows // 4 + i * ROW_TILE, normed_ref)
+            return carry
+
+        lax.fori_loop(0, rows // 4 // ROW_TILE, first_step, 0)
+
+    for copies in (block_copies[3], block_copies[4], weight_copies):
+        for copy in copies:
+            copy.wait()
+    steps = half // (2 * ROW_TILE)
+    depth = features // steps
+    total_ref[...] = jnp.zeros_like(total_ref)
+
+    def second_step(i, carry):
+        at = pl.ds(pl.multiple_of(i * depth, depth), depth)
+        total_ref[...] += jnp.dot(
+            normed_ref[:half, at], weight_ref[at, :], preferred_element_type=jnp.float32
+        )
+        for k in range(2):
+            normalize(block_ref, gains, columns, half + (2 * i + k) * ROW_TILE, normed_ref)
+        return carry
+
+    lax.fori_loop(0, steps, second_step, 0)
+    sums_ref[:half] = total_ref[...].astype(jnp.bfloat16)
+    sums_ref[half:] = jnp.dot(
+        normed_ref[half:], weight_ref[...], preferred_element_type=jnp.float32
     ).astype(jnp.bfloat16)
     local = out_ref.shape[1]
     span, window = 128, 256
@@ -128,7 +159,8 @@
             ) * (1.0 / math.sqrt(HEAD_DIM))
             scores = jnp.where(same, scores, -jnp.inf)
             expo = jnp.exp(scores - jnp.max(scores, axis=1, keepdims=True))
-            probs = (expo / jnp.sum(expo, axis=1, keepdims=True)).astype(jnp.bfloat16)
+            share = 1.0 / jnp.sum(expo, axis=1, keepdims=True)
+            probs = (expo * share).astype(jnp.bfloat16)
             out_ref[row : row + span, col : col + HEAD_DIM] = jnp.dot(
                 probs, value, preferred_element_type=jnp.float32
             ).astype(jnp.bfloat16)
@@ -150,7 +182,8 @@
         jnp.where(my_order[None, :] == targets[:, None], targets[None, :], 0), axis=1
     )
     slots = page_patches.reshape(groups, slot_rows, width)
-    outgoing = jnp.take(slots, slot_for, axis=0)
+    outgoing = slots.at[slot_for].get(mode="promise_in_bounds")
+    outgoing, pack_lengths = lax.optimization_barrier((outgoing, pack_lengths))
     incoming = lax.all_to_all(outgoing, "dp", split_axis=0, concat_axis=0, tiled=True)
     my_lengths = lax.dynamic_index_in_dim(pack_lengths, page_index, 0, keepdims=False)
     line_ends = jnp.cumsum(my_lengths)
@@ -161,7 +194,9 @@
         jnp.where(segment[:, None] == targets[None, :], line_starts[None, :], 0), axis=1
     )
     source_rows = segment * slot_rows + row_ids - start_of_row
-    packed = jnp.take(incoming.reshape(groups * slot_rows, width), source_rows, axis=0)
+    packed = incoming.reshape(groups * slot_rows, width).at[source_rows].get(
+        mode="promise_in_bounds"
+    )
 
     own = jnp.concatenate([packed, jnp.broadcast_to(gain[None, :], (GAIN_ROWS, width))], axis=0)
     all_rows = rows + GAIN_ROWS
@@ -185,20 +220,22 @@
     )
     weight = lax.all_gather(weight, "dp", axis=0, tiled=True, axis_index_groups=dp_groups("xc"))
     pair = jnp.concatenate([z_up, z_down], axis=0)
-    pair_down, pair_up, far_rest, far_top = lax.optimization_barrier(
-        (along_y(pair, -1), along_y(pair, 1), along_z(z_down[cut:], -1), along_z(z_up[:cut], 1))
+    pair_up, pair_down = along_y(pair, 1), along_y(pair, -1)
+    pair_far_up = along_y(pair_up[:all_rows], 1)
+    pair_far_down = along_y(pair_down[all_rows:], -1)
+    far_top, far_rest = along_z(z_up[:cut], 1), along_z(z_down[cut:], -1)
+    far_top, far_rest, pair_up, pair_down = lax.optimization_barrier(
+        (far_top, far_rest, pair_up, pair_down)
     )
     far = jnp.concatenate([far_top, far_rest], axis=0)
     far_far, far_down, far_up = along_y(far, 2), along_y(far, -1), along_y(far, 1)
-    pair_far_up = along_y(pair_up[:all_rows], 1)
-    pair_far_down = along_y(pair_down[all_rows:], -1)
 
     blocks, slots_at, shifts = [], [], []
 
     def add(array, dy, *dzs):
         blocks.append(array)
         for k, dz in enumerate(dzs):
-            slots_at.append(((len(blocks) - 1, k * all_rows, 0, all_rows),))
+            slots_at.append((len(blocks) - 1, k * all_rows))
             shifts.append((dz, dy))
 
     add(own, 0, 0)
@@ -221,7 +258,7 @@
     places = (my_z + step_z + Z_PARTS) % Z_PARTS * Y_PARTS + (my_y + step_y + Y_PARTS) % Y_PARTS
 
     def kernel(*refs):
-        project_attend_kernel(slots_at, len(blocks), rows, cut, strip, *refs)
+        project_attend_kernel(slots_at, len(blocks), rows, strip, *refs)
 
     features = width * len(slots_at)
     vmem = pl.BlockSpec(memory_space=pltpu.VMEM)
@@ -229,13 +266,16 @@
     return pl.pallas_call(
         kernel,
         out_shape=jax.ShapeDtypeStruct((rows, local), jnp.bfloat16),
-        in_specs=[smem] + [vmem] * len(blocks) + [hbm, vmem, vmem],
+        in_specs=[smem] + [hbm] * (len(blocks) + 1) + [vmem, vmem],
         out_specs=vmem,
         scratch_shapes=[
+            pltpu.VMEM((len(slots_at), all_rows, width), jnp.bfloat16),
             pltpu.VMEM((rows, features), jnp.bfloat16),
             pltpu.VMEM((features, 3 * local), jnp.bfloat16),
+            pltpu.VMEM((rows // 2, 3 * local), jnp.float32),
             pltpu.VMEM((rows, 3 * local), jnp.bfloat16),
             pltpu.SemaphoreType.DMA,
+            pltpu.SemaphoreType.DMA((5,)),
         ],
         name="norm_project_attend",
     )(places, *blocks, weight, segment[:, None], segment[None, :])

time: 203 us -> 197 us (0.970)
  the two profiles are of different devices: /device:TPU:36 before, /device:TPU:39 now
where the time goes in v8:
time: 197 us; the launch traced here: 196 us
  waiting for transfers between devices  83.5 us (42%)
  starting transfers between devices  64.7 us (33%)
  Pallas kernels  17.4 us (9%)
  between operations  13.7 us (7%)
  local copies, waits for them, and re-layouts  13 us (7%)
  other arithmetic  3.58 us (2%)
    ppermute x10, starting transfers between devices, along_y(): return lax.ppermute(block, 'tensor', y_shift(step))  34.8 us
    all_gather x2, waiting for transfers between devices, shards(): lax.all_gather(weight, 'dp', axis=0, tiled=True, axis_index_groups=dp_gro...  24.9 us
    ppermute x4, waiting for transfers between devices, along_z(): return lax.ppermute(block, 'tensor', z_shift(step))  22.4 us
    ppermute x10, waiting for transfers between devices, along_y(): return lax.ppermute(block, 'tensor', y_shift(step))  21.3 us
    ppermute x4, starting transfers between devices, along_z(): return lax.ppermute(block, 'tensor', z_shift(step))  20.3 us
    pallas_call x1, Pallas kernels, shards(): pl.pallas_call(kernel, out_shape=jax.ShapeDtypeStruct((rows, local), jnp....  17.4 us
    all_to_all x1, waiting for transfers between devices, shards(): lax.all_to_all(outgoing, 'dp', split_axis=0, concat_axis=0, tiled=True)  14.9 us
    all_to_all x1, starting transfers between devices, shards(): lax.all_to_all(outgoing, 'dp', split_axis=0, concat_axis=0, tiled=True)  9.44 us
  transfers between devices with their start and end apart: 17, of which 9 were waited for; matrix products, arithmetic and copies ran while one was open for 7% of the time, Pallas kernels for 0%

profile of v8, /device:TPU:39, one launch (start us, length us, event | category | flops | bytes accessed | tf_op | source)
XLA Modules:
  0.0 195.9 jit_solution(4289684986440625517)
XLA Ops:
  6.5 0.8 dynamic-slice_bitcast_fusion
  7.3 0.1 select_reduce_fusion.1
  7.4 0.2 copy-done
  7.7 1.5 gather_fusion
  9.2 9.4 %all-to-all-start = ((bf16[32,32,384]{2,1,0:T(8,128)(2,1)}), bf16[32,32,384]{2,1,0:T(8,128)(2,1)S(1)}, u32[]{:S(2)}, u32[]{:S(2)}) async-start(bf16[32,32,384]{2,1,0:T(8,128)(2,1)} %gather_fusion), calls=%async_computation | async-start | bytes 1572864 | tf_op jit(solution)/shard_map/all_to_all | solution.py:187
  18.7 1.7 pad_maximum_fusion.1
  20.5 0.7 fusion.6
  21.2 0.1 copy.13
  21.4 0.1 reduce
  21.5 0.1 convert_reduce_fusion
  21.6 0.7 fusion.5
  22.3 0.1 select_reduce_fusion
  22.4 14.9 %all-to-all-done = bf16[32,32,384]{2,1,0:T(8,128)(2,1)S(1)} async-done(((bf16[32,32,384]{2,1,0:T(8,128)(2,1)}), bf16[32,32,384]{2,1,0:T(8,128)(2,1)S(1)}, u32[]{:S(2)}, u32[]{:S(2)}) %all-to-all-start) | async-done | bytes 786464 | tf_op jit(solution)/shard_map/all_to_all | solution.py:187
  37.3 1.9 gather_fusion.1
  39.3 0.7 broadcast_in_dim.51
  40.0 8.3 %collective-permute-start.4 = (bf16[528,384]{1,0:T(8,128)(2,1)S(1)}, bf16[528,384]{1,0:T(8,128)(2,1)S(1)}, u32[]{:S(2)}, u32[]{:S(2)}) collective-permute-start(bf16[528,384]{1,0:T(8,128)(2,1)S(1)} %pad_maximum_fusion.refs_1_), channel_id=1, source_target_pairs={{0,4},{1,5},{2,6},{3,7},{4,8},{5,9},{6,10},{7,11},{8,12},{9,13},{1... | collective-permute-start | bytes 1216520 | tf_op jit(solution)/shard_map/ppermute | solution.py:209
  48.3 2.9 %collective-permute-start.3 = (bf16[528,384]{1,0:T(8,128)(2,1)S(1)}, bf16[528,384]{1,0:T(8,128)(2,1)S(1)}, u32[]{:S(2)}, u32[]{:S(2)}) collective-permute-start(bf16[528,384]{1,0:T(8,128)(2,1)S(1)} %pad_maximum_fusion.refs_1_), channel_id=1, source_target_pairs={{0,12},{1,13},{2,14},{3,15},{4,0},{5,1},{6,2},{7,3},{8,4},{9,5},{1... | collective-permute-start | bytes 1216520 | tf_op jit(solution)/shard_map/ppermute | solution.py:209
  51.2 3.2 %collective-permute-start.2 = (bf16[528,384]{1,0:T(8,128)(2,1)S(1)}, bf16[528,384]{1,0:T(8,128)(2,1)S(1)}, u32[]{:S(2)}, u32[]{:S(2)}) collective-permute-start(bf16[528,384]{1,0:T(8,128)(2,1)S(1)} %pad_maximum_fusion.refs_1_), channel_id=1, source_target_pairs={{0,1},{1,2},{2,3},{3,0},{4,5},{5,6},{6,7},{7,4},{8,9},{9,10},{10,1... | collective-permute-start | bytes 1216520 | tf_op jit(solution)/shard_map/ppermute | solution.py:206
  54.4 3.4 %collective-permute-start.1 = (bf16[528,384]{1,0:T(8,128)(2,1)S(1)}, bf16[528,384]{1,0:T(8,128)(2,1)S(1)}, u32[]{:S(2)}, u32[]{:S(2)}) collective-permute-start(bf16[528,384]{1,0:T(8,128)(2,1)S(1)} %pad_maximum_fusion.refs_1_), channel_id=1, source_target_pairs={{0,3},{1,0},{2,1},{3,2},{4,7},{5,4},{6,5},{7,6},{8,11},{9,8},{10,9... | collective-permute-start | bytes 1216520 | tf_op jit(solution)/shard_map/ppermute | solution.py:206
  57.8 3.5 %collective-permute-start = (bf16[528,384]{1,0:T(8,128)(2,1)S(1)}, bf16[528,384]{1,0:T(8,128)(2,1)S(1)}, u32[]{:S(2)}, u32[]{:S(2)}) collective-permute-start(bf16[528,384]{1,0:T(8,128)(2,1)S(1)} %pad_maximum_fusion.refs_1_), channel_id=1, source_target_pairs={{0,2},{1,3},{2,0},{3,1},{4,6},{5,7},{6,4},{7,5},{8,10},{9,11},{10,... | collective-permute-start | bytes 1216520 | tf_op jit(solution)/shard_map/ppermute | solution.py:206
  61.3 24.9 %all-gather.3.cloned.1.call-done = bf16[768,768]{1,0:T(8,128)(2,1)} async-done(((bf16[192,768]{1,0:T(8,128)(2,1)}), bf16[768,768]{1,0:T(8,128)(2,1)}) %all-gather.3.cloned.1.call-update) | async-done | bytes 1179664 | tf_op jit(solution)/shard_map/all_gather | solution.py:178
  86.2 11.7 %collective-permute-done.4 = bf16[528,384]{1,0:T(8,128)(2,1)S(1)} collective-permute-done((bf16[528,384]{1,0:T(8,128)(2,1)S(1)}, bf16[528,384]{1,0:T(8,128)(2,1)S(1)}, u32[]{:S(2)}, u32[]{:S(2)}) %collective-permute-start.4) | collective-permute-done | bytes 405536 | tf_op jit(solution)/shard_map/ppermute | solution.py:209
  97.9 2.9 %collective-permute-done.3 = bf16[528,384]{1,0:T(8,128)(2,1)S(1)} collective-permute-done((bf16[528,384]{1,0:T(8,128)(2,1)S(1)}, bf16[528,384]{1,0:T(8,128)(2,1)S(1)}, u32[]{:S(2)}, u32[]{:S(2)}) %collective-permute-start.3) | collective-permute-done | bytes 405536 | tf_op jit(solution)/shard_map/ppermute | solution.py:209
  100.8 0.7 copy-done.7
  101.6 0.2 copy-done.8
  102.0 4.4 %collective-permute-start.8 = (bf16[1056,384]{1,0:T(8,128)(2,1)S(1)}, bf16[1056,384]{1,0:T(8,128)(2,1)S(1)}, u32[]{:S(2)}, u32[]{:S(2)}) collective-permute-start(bf16[1056,384]{1,0:T(8,128)(2,1)S(1)} %constant_dynamic-update-slice_fusion.refs_5_), channel_id=1, source_target_pairs={{0,3},{1,0},{2,1},{3,2},{4,7},{5,4},{6,5},{7,6},{8,11},{9,8},{10,9... | collective-permute-start | bytes 2433032 | tf_op jit(solution)/shard_map/ppermute | solution.py:206
  106.4 1.9 collective-permute-start.7
  108.3 1.0 slice.12
  109.3 6.4 %collective-permute-start.5 = (bf16[272,384]{1,0:T(8,128)(2,1)S(1)}, bf16[272,384]{1,0:T(8,128)(2,1)S(1)}, u32[]{:S(2)}, u32[]{:S(2)}) collective-permute-start(bf16[272,384]{1,0:T(8,128)(2,1)S(1)} %slice.12), channel_id=1, source_target_pairs={{0,4},{1,5},{2,6},{3,7},{4,8},{5,9},{6,10},{7,11},{8,12},{9,13},{1... | collective-permute-start | bytes 626696 | tf_op jit(solution)/shard_map/ppermute | solution.py:209
  115.7 1.0 slice.13
  116.7 2.8 %collective-permute-start.6 = (bf16[256,384]{1,0:T(8,128)(2,1)S(1)}, bf16[256,384]{1,0:T(8,128)(2,1)S(1)}, u32[]{:S(2)}, u32[]{:S(2)}) collective-permute-start(bf16[256,384]{1,0:T(8,128)(2,1)S(1)} %slice.13), channel_id=1, source_target_pairs={{0,12},{1,13},{2,14},{3,15},{4,0},{5,1},{6,2},{7,3},{8,4},{9,5},{1... | collective-permute-start | bytes 589832 | tf_op jit(solution)/shard_map/ppermute | solution.py:209
  119.4 3.9 %collective-permute-done.8.refs_7_ = bf16[1056,384]{1,0:T(8,128)(2,1)S(1)} collective-permute-done((bf16[1056,384]{1,0:T(8,128)(2,1)S(1)}, bf16[1056,384]{1,0:T(8,128)(2,1)S(1)}, u32[]{:S(2)}, u32[]{:S(2)}) %collective-permute-start.8) | collective-permute-done | bytes 811040 | tf_op jit(solution)/shard_map/ppermute | solution.py:206
  123.4 0.9 slice.21
  124.2 5.4 %collective-permute-start.10 = (bf16[528,384]{1,0:T(8,128)(2,1)}, bf16[528,384]{1,0:T(8,128)(2,1)}, u32[]{:S(2)}, u32[]{:S(2)}) collective-permute-start(bf16[528,384]{1,0:T(8,128)(2,1)} %slice.21), channel_id=1, source_target_pairs={{0,3},{1,0},{2,1},{3,2},{4,7},{5,4},{6,5},{7,6},{8,11},{9,8},{10,9... | collective-permute-start | bytes 1216520 | tf_op jit(solution)/shard_map/ppermute | solution.py:206
  129.7 7.8 %collective-permute-done.6 = bf16[256,384]{1,0:T(8,128)(2,1)S(1)} collective-permute-done((bf16[256,384]{1,0:T(8,128)(2,1)S(1)}, bf16[256,384]{1,0:T(8,128)(2,1)S(1)}, u32[]{:S(2)}, u32[]{:S(2)}) %collective-permute-start.6) | collective-permute-done | bytes 196640 | tf_op jit(solution)/shard_map/ppermute | solution.py:209
  137.5 0.8 slice.20
  138.3 2.3 %collective-permute-start.9 = (bf16[528,384]{1,0:T(8,128)(2,1)}, bf16[528,384]{1,0:T(8,128)(2,1)}, u32[]{:S(2)}, u32[]{:S(2)}) collective-permute-start(bf16[528,384]{1,0:T(8,128)(2,1)} %slice.20), channel_id=1, source_target_pairs={{0,1},{1,2},{2,3},{3,0},{4,5},{5,6},{6,7},{7,4},{8,9},{9,10},{10,1... | collective-permute-start | bytes 1216520 | tf_op jit(solution)/shard_map/ppermute | solution.py:206
  140.6 0.7 constant_dynamic-update-slice_fusion.3
  141.3 0.7 constant_dynamic-update-slice_fusion.2.refs_10_
  142.0 5.4 %collective-permute-start.13 = (bf16[528,384]{1,0:T(8,128)(2,1)}, bf16[528,384]{1,0:T(8,128)(2,1)}, u32[]{:S(2)}, u32[]{:S(2)}) collective-permute-start(bf16[528,384]{1,0:T(8,128)(2,1)} %constant_dynamic-update-slice_fusion.2.refs_10_), channel_id=1, source_target_pairs={{0,2},{1,3},{2,0},{3,1},{4,6},{5,7},{6,4},{7,5},{8,10},{9,11},{10,... | collective-permute-start | bytes 1216520 | tf_op jit(solution)/shard_map/ppermute | solution.py:206
  147.4 1.9 collective-permute-start.12
  149.3 3.4 %collective-permute-start.11 = (bf16[528,384]{1,0:T(8,128)(2,1)}, bf16[528,384]{1,0:T(8,128)(2,1)}, u32[]{:S(2)}, u32[]{:S(2)}) collective-permute-start(bf16[528,384]{1,0:T(8,128)(2,1)} %constant_dynamic-update-slice_fusion.2.refs_10_), channel_id=1, source_target_pairs={{0,1},{1,2},{2,3},{3,0},{4,5},{5,6},{6,7},{7,4},{8,9},{9,10},{10,1... | collective-permute-start | bytes 1216520 | tf_op jit(solution)/shard_map/ppermute | solution.py:206
  152.7 0.9 copy.14.refs_15_
  153.6 0.6 fusion.refs_0_
  154.2 7.9 %collective-permute-done.13.refs_13_ = bf16[528,384]{1,0:T(8,128)(2,1)} collective-permute-done((bf16[528,384]{1,0:T(8,128)(2,1)}, bf16[528,384]{1,0:T(8,128)(2,1)}, u32[]{:S(2)}, u32[]{:S(2)}) %collective-permute-start.13) | collective-permute-done | bytes 405536 | tf_op jit(solution)/shard_map/ppermute | solution.py:206
  162.1 2.5 %collective-permute-done.12.refs_12_ = bf16[528,384]{1,0:T(8,128)(2,1)} collective-permute-done((bf16[528,384]{1,0:T(8,128)(2,1)}, bf16[528,384]{1,0:T(8,128)(2,1)}, u32[]{:S(2)}, u32[]{:S(2)}) %collective-permute-start.12) | collective-permute-done | bytes 405536 | tf_op jit(solution)/shard_map/ppermute | solution.py:206
  164.6 7.0 %collective-permute-done.11.refs_11_ = bf16[528,384]{1,0:T(8,128)(2,1)} collective-permute-done((bf16[528,384]{1,0:T(8,128)(2,1)}, bf16[528,384]{1,0:T(8,128)(2,1)}, u32[]{:S(2)}, u32[]{:S(2)}) %collective-permute-start.11) | collective-permute-done | bytes 405536 | tf_op jit(solution)/shard_map/ppermute | solution.py:206
  171.6 17.4 %norm_project_attend.1 = bf16[512,256]{1,0:T(8,128)(2,1)} custom-call(s32[16]{0:T(128)} %fusion.refs_0_, bf16[528,384]{1,0:T(8,128)(2,1)} %copy-done.4, bf16[528,384]{1,0:T(8,128)(2,1)} %copy-done.7, bf16[528,384]{1,0:T(8,128)(2,1)} %copy-done.8, bf16[528,384]{1,0:T(8,128)(2,1)} %copy-done.9, bf16[1056,384]{1,0:T(8,128)(2,1)} %copy-done.3, ...), custom_call_target="tpu_custom_call" | custom-call | tf_op jit(solution)/shard_map/norm_project_attend/pallas_call | solution.py:266
  (43 shorter events, 0.5 us)
Async XLA Ops:
  6.5 1.1 copy-start
  6.5 147.1 %copy-start.11 = (s32[16]{0:T(128)S(1)}, s32[16]{0:T(128)}, u32[]{:S(2)}) copy-start(s32[16]{0:T(128)} %constant.71.clone) | copy-start | bytes 196
  6.5 147.1 %copy-start.12 = (s32[16]{0:T(128)S(1)}, s32[16]{0:T(128)}, u32[]{:S(2)}) copy-start(s32[16]{0:T(128)} %constant.70.clone) | copy-start | bytes 196
  9.2 28.1 %all-to-all-start = ((bf16[32,32,384]{2,1,0:T(8,128)(2,1)}), bf16[32,32,384]{2,1,0:T(8,128)(2,1)S(1)}, u32[]{:S(2)}, u32[]{:S(2)}) async-start(bf16[32,32,384]{2,1,0:T(8,128)(2,1)} %gather_fusion), calls=%async_computation | async-start | bytes 1572864 | tf_op jit(solution)/shard_map/all_to_all | solution.py:187
  18.7 67.5 %all-gather.3.cloned.1.call-start = ((), (), s32[]{:S(2)}) async-start(), calls=%async_computation.1 | async-start | bytes 1474560 | tf_op jit(solution)/shard_map/all_gather | solution.py:178
  20.5 151.1 %all-gather.5.cloned.1.call-start = ((), (), s32[]{:S(2)}) async-start(), calls=%async_computation.2 | async-start | bytes 10616832 | tf_op jit(solution)/shard_map/all_gather | solution.py:221
  21.6 150.0 %copy-start.10 = (s32[512]{0:T(512)}, s32[512]{0:T(512)S(1)}, u32[]{:S(2)}) copy-start(s32[512]{0:T(512)S(1)} %convert_reduce_fusion) | copy-start | bytes 6148
  40.0 61.8 %copy-start.4 = (bf16[528,384]{1,0:T(8,128)(2,1)}, bf16[528,384]{1,0:T(8,128)(2,1)S(1)}, u32[]{:S(2)}) copy-start(bf16[528,384]{1,0:T(8,128)(2,1)S(1)} %pad_maximum_fusion.refs_1_) | copy-start | bytes 1216516
  40.0 57.9 %collective-permute-start.4 = (bf16[528,384]{1,0:T(8,128)(2,1)S(1)}, bf16[528,384]{1,0:T(8,128)(2,1)S(1)}, u32[]{:S(2)}, u32[]{:S(2)}) collective-permute-start(bf16[528,384]{1,0:T(8,128)(2,1)S(1)} %pad_maximum_fusion.refs_1_), channel_id=1, source_target_pairs={{0,4},{1,5},{2,6},{3,7},{4,8},{5,9},{6,10},{7,11},{8,12},{9,13},{1... | collective-permute-start | bytes 1216520 | tf_op jit(solution)/shard_map/ppermute | solution.py:209
  48.3 52.5 %collective-permute-start.3 = (bf16[528,384]{1,0:T(8,128)(2,1)S(1)}, bf16[528,384]{1,0:T(8,128)(2,1)S(1)}, u32[]{:S(2)}, u32[]{:S(2)}) collective-permute-start(bf16[528,384]{1,0:T(8,128)(2,1)S(1)} %pad_maximum_fusion.refs_1_), channel_id=1, source_target_pairs={{0,12},{1,13},{2,14},{3,15},{4,0},{5,1},{6,2},{7,3},{8,4},{9,5},{1... | collective-permute-start | bytes 1216520 | tf_op jit(solution)/shard_map/ppermute | solution.py:209
  51.2 49.6 %collective-permute-start.2 = (bf16[528,384]{1,0:T(8,128)(2,1)S(1)}, bf16[528,384]{1,0:T(8,128)(2,1)S(1)}, u32[]{:S(2)}, u32[]{:S(2)}) collective-permute-start(bf16[528,384]{1,0:T(8,128)(2,1)S(1)} %pad_maximum_fusion.refs_1_), channel_id=1, source_target_pairs={{0,1},{1,2},{2,3},{3,0},{4,5},{5,6},{6,7},{7,4},{8,9},{9,10},{10,1... | collective-permute-start | bytes 1216520 | tf_op jit(solution)/shard_map/ppermute | solution.py:206
  54.4 46.4 %collective-permute-start.1 = (bf16[528,384]{1,0:T(8,128)(2,1)S(1)}, bf16[528,384]{1,0:T(8,128)(2,1)S(1)}, u32[]{:S(2)}, u32[]{:S(2)}) collective-permute-start(bf16[528,384]{1,0:T(8,128)(2,1)S(1)} %pad_maximum_fusion.refs_1_), channel_id=1, source_target_pairs={{0,3},{1,0},{2,1},{3,2},{4,7},{5,4},{6,5},{7,6},{8,11},{9,8},{10,9... | collective-permute-start | bytes 1216520 | tf_op jit(solution)/shard_map/ppermute | solution.py:206
  57.8 43.0 %collective-permute-start = (bf16[528,384]{1,0:T(8,128)(2,1)S(1)}, bf16[528,384]{1,0:T(8,128)(2,1)S(1)}, u32[]{:S(2)}, u32[]{:S(2)}) collective-permute-start(bf16[528,384]{1,0:T(8,128)(2,1)S(1)} %pad_maximum_fusion.refs_1_), channel_id=1, source_target_pairs={{0,2},{1,3},{2,0},{3,1},{4,6},{5,7},{6,4},{7,5},{8,10},{9,11},{10,... | collective-permute-start | bytes 1216520 | tf_op jit(solution)/shard_map/ppermute | solution.py:206
  97.9 3.9 %copy-start.5 = (bf16[528,384]{1,0:T(8,128)(2,1)}, bf16[528,384]{1,0:T(8,128)(2,1)S(1)}, u32[]{:S(2)}) copy-start(bf16[528,384]{1,0:T(8,128)(2,1)S(1)} %collective-permute-done.4) | copy-start | bytes 1216516
  100.8 1.1 copy-start.6
  100.8 0.8 copy-start.7
  100.8 0.9 copy-start.8
  100.8 1.1 copy-start.9
  102.0 69.6 %copy-start.3 = (bf16[1056,384]{1,0:T(8,128)(2,1)}, bf16[1056,384]{1,0:T(8,128)(2,1)S(1)}, u32[]{:S(2)}) copy-start(bf16[1056,384]{1,0:T(8,128)(2,1)S(1)} %constant_dynamic-update-slice_fusion.refs_5_) | copy-start | bytes 2433028
  102.0 21.4 %collective-permute-start.8 = (bf16[1056,384]{1,0:T(8,128)(2,1)S(1)}, bf16[1056,384]{1,0:T(8,128)(2,1)S(1)}, u32[]{:S(2)}, u32[]{:S(2)}) collective-permute-start(bf16[1056,384]{1,0:T(8,128)(2,1)S(1)} %constant_dynamic-update-slice_fusion.refs_5_), channel_id=1, source_target_pairs={{0,3},{1,0},{2,1},{3,2},{4,7},{5,4},{6,5},{7,6},{8,11},{9,8},{10,9... | collective-permute-start | bytes 2433032 | tf_op jit(solution)/shard_map/ppermute | solution.py:206
  106.4 31.0 %collective-permute-start.7 = (bf16[1056,384]{1,0:T(8,128)(2,1)S(1)}, bf16[1056,384]{1,0:T(8,128)(2,1)S(1)}, u32[]{:S(2)}, u32[]{:S(2)}) collective-permute-start(bf16[1056,384]{1,0:T(8,128)(2,1)S(1)} %constant_dynamic-update-slice_fusion.refs_5_), channel_id=1, source_target_pairs={{0,1},{1,2},{2,3},{3,0},{4,5},{5,6},{6,7},{7,4},{8,9},{9,10},{10,1... | collective-permute-start | bytes 2433032 | tf_op jit(solution)/shard_map/ppermute | solution.py:206
  109.3 28.2 %collective-permute-start.5 = (bf16[272,384]{1,0:T(8,128)(2,1)S(1)}, bf16[272,384]{1,0:T(8,128)(2,1)S(1)}, u32[]{:S(2)}, u32[]{:S(2)}) collective-permute-start(bf16[272,384]{1,0:T(8,128)(2,1)S(1)} %slice.12), channel_id=1, source_target_pairs={{0,4},{1,5},{2,6},{3,7},{4,8},{5,9},{6,10},{7,11},{8,12},{9,13},{1... | collective-permute-start | bytes 626696 | tf_op jit(solution)/shard_map/ppermute | solution.py:209
  116.7 20.8 %collective-permute-start.6 = (bf16[256,384]{1,0:T(8,128)(2,1)S(1)}, bf16[256,384]{1,0:T(8,128)(2,1)S(1)}, u32[]{:S(2)}, u32[]{:S(2)}) collective-permute-start(bf16[256,384]{1,0:T(8,128)(2,1)S(1)} %slice.13), channel_id=1, source_target_pairs={{0,12},{1,13},{2,14},{3,15},{4,0},{5,1},{6,2},{7,3},{8,4},{9,5},{1... | collective-permute-start | bytes 589832 | tf_op jit(solution)/shard_map/ppermute | solution.py:209
  123.4 48.2 %copy-start.1 = (bf16[1056,384]{1,0:T(8,128)(2,1)}, bf16[1056,384]{1,0:T(8,128)(2,1)S(1)}, u32[]{:S(2)}) copy-start(bf16[1056,384]{1,0:T(8,128)(2,1)S(1)} %collective-permute-done.8.refs_7_) | copy-start | bytes 2433028
  124.2 30.0 %collective-permute-start.10 = (bf16[528,384]{1,0:T(8,128)(2,1)}, bf16[528,384]{1,0:T(8,128)(2,1)}, u32[]{:S(2)}, u32[]{:S(2)}) collective-permute-start(bf16[528,384]{1,0:T(8,128)(2,1)} %slice.21), channel_id=1, source_target_pairs={{0,3},{1,0},{2,1},{3,2},{4,7},{5,4},{6,5},{7,6},{8,11},{9,8},{10,9... | collective-permute-start | bytes 1216520 | tf_op jit(solution)/shard_map/ppermute | solution.py:206
  137.5 34.2 %copy-start.2 = (bf16[1056,384]{1,0:T(8,128)(2,1)}, bf16[1056,384]{1,0:T(8,128)(2,1)S(1)}, u32[]{:S(2)}) copy-start(bf16[1056,384]{1,0:T(8,128)(2,1)S(1)} %collective-permute-done.7.refs_6_) | copy-start | bytes 2433028
  138.3 15.9 %collective-permute-start.9 = (bf16[528,384]{1,0:T(8,128)(2,1)}, bf16[528,384]{1,0:T(8,128)(2,1)}, u32[]{:S(2)}, u32[]{:S(2)}) collective-permute-start(bf16[528,384]{1,0:T(8,128)(2,1)} %slice.20), channel_id=1, source_target_pairs={{0,1},{1,2},{2,3},{3,0},{4,5},{5,6},{6,7},{7,4},{8,9},{9,10},{10,1... | collective-permute-start | bytes 1216520 | tf_op jit(solution)/shard_map/ppermute | solution.py:206
  142.0 20.1 %collective-permute-start.13 = (bf16[528,384]{1,0:T(8,128)(2,1)}, bf16[528,384]{1,0:T(8,128)(2,1)}, u32[]{:S(2)}, u32[]{:S(2)}) collective-permute-start(bf16[528,384]{1,0:T(8,128)(2,1)} %constant_dynamic-update-slice_fusion.2.refs_10_), channel_id=1, source_target_pairs={{0,2},{1,3},{2,0},{3,1},{4,6},{5,7},{6,4},{7,5},{8,10},{9,11},{10,... | collective-permute-start | bytes 1216520 | tf_op jit(solution)/shard_map/ppermute | solution.py:206
  147.4 17.2 %collective-permute-start.12 = (bf16[528,384]{1,0:T(8,128)(2,1)}, bf16[528,384]{1,0:T(8,128)(2,1)}, u32[]{:S(2)}, u32[]{:S(2)}) collective-permute-start(bf16[528,384]{1,0:T(8,128)(2,1)} %constant_dynamic-update-slice_fusion.2.refs_10_), channel_id=1, source_target_pairs={{0,3},{1,0},{2,1},{3,2},{4,7},{5,4},{6,5},{7,6},{8,11},{9,8},{10,9... | collective-permute-start | bytes 1216520 | tf_op jit(solution)/shard_map/ppermute | solution.py:206
  149.3 22.3 %collective-permute-start.11 = (bf16[528,384]{1,0:T(8,128)(2,1)}, bf16[528,384]{1,0:T(8,128)(2,1)}, u32[]{:S(2)}, u32[]{:S(2)}) collective-permute-start(bf16[528,384]{1,0:T(8,128)(2,1)} %constant_dynamic-update-slice_fusion.2.refs_10_), channel_id=1, source_target_pairs={{0,1},{1,2},{2,3},{3,0},{4,5},{5,6},{6,7},{7,4},{8,9},{9,10},{10,1... | collective-permute-start | bytes 1216520 | tf_op jit(solution)/shard_map/ppermute | solution.py:206
Sparse Core Ops, SparseCore 0:
  21.6 64.5 all-gather.2
  101.9 57.7 all-gather.4

commit v9 on v8

--- a/solution.py
+++ b/solution.py
@@ -208,13 +208,13 @@
     def along_z(block, step):
         return lax.ppermute(block, "tensor", z_shift(step))
 
-    own_far, own_down, own_up, z_down, z_up, weight = lax.optimization_barrier(
+    z_up, z_down, own_up, own_down, own_far, weight = lax.optimization_barrier(
         (
+            along_z(own, 1),
+            along_z(own, -1),
+            along_y(own, 1),
+            along_y(own, -1),
             along_y(own, 2),
-            along_y(own, -1),
-            along_y(own, 1),
-            along_z(own, -1),
-            along_z(own, 1),
             weight,
         )
     )
@@ -224,11 +224,15 @@
     pair_far_up = along_y(pair_up[:all_rows], 1)
     pair_far_down = along_y(pair_down[all_rows:], -1)
     far_top, far_rest = along_z(z_up[:cut], 1), along_z(z_down[cut:], -1)
-    far_top, far_rest, pair_up, pair_down = lax.optimization_barrier(
-        (far_top, far_rest, pair_up, pair_down)
-    )
     far = jnp.concatenate([far_top, far_rest], axis=0)
-    far_far, far_down, far_up = along_y(far, 2), along_y(far, -1), along_y(far, 1)
+    far_all = lax.all_to_all(
+        jnp.broadcast_to(far[None], (Y_PARTS, *far.shape)),
+        "tensor",
+        split_axis=0,
+        concat_axis=0,
+        tiled=True,
+        axis_index_groups=[[z * Y_PARTS + y for y in range(Y_PARTS)] for z in range(Z_PARTS)],
+    )
 
     blocks, slots_at, shifts = [], [], []
 
@@ -247,14 +251,14 @@
     add(pair_down, 1, -1, 1)
     add(pair_far_up, 2, -1)
     add(pair_far_down, 2, 1)
-    add(far, 0, 2)
-    add(far_up, -1, 2)
-    add(far_down, 1, 2)
-    add(far_far, 2, 2)
+    blocks.append(far_all.reshape(Y_PARTS * all_rows, width))
+    for y in range(Y_PARTS):
+        slots_at.append((len(blocks) - 1, y * all_rows))
     tensor = lax.axis_index("tensor")
     my_z, my_y = tensor // Y_PARTS, tensor % Y_PARTS
-    step_z = jnp.array([dz for dz, _ in shifts], jnp.int32)
+    step_z = jnp.array([dz for dz, _ in shifts] + [2] * Y_PARTS, jnp.int32)
     step_y = jnp.array([dy for _, dy in shifts], jnp.int32)
+    step_y = jnp.concatenate([step_y, jnp.arange(Y_PARTS, dtype=jnp.int32) - my_y])
     places = (my_z + step_z + Z_PARTS) % Z_PARTS * Y_PARTS + (my_y + step_y + Y_PARTS) % Y_PARTS
 
     def kernel(*refs):

time: 197 us -> 189 us (0.959)
  the two profiles are of different devices: /device:TPU:39 before, /device:TPU:1 now
where the time goes in v9:
time: 189 us; the launch traced here: 187 us
  waiting for transfers between devices  80.6 us (43%)
  starting transfers between devices  60.6 us (32%)
  Pallas kernels  17.4 us (9%)
  between operations  13.7 us (7%)
  local copies, waits for them, and re-layouts  11.8 us (6%)
  other arithmetic  2.72 us (1%)
    all_gather x2, waiting for transfers between devices, shards(): lax.all_gather(weight, 'dp', axis=0, tiled=True, axis_index_groups=dp_gro...  36.8 us
    ppermute x4, starting transfers between devices, along_z(): return lax.ppermute(block, 'tensor', z_shift(step))  23.1 us
    ppermute x7, starting transfers between devices, along_y(): return lax.ppermute(block, 'tensor', y_shift(step))  23.1 us
    ppermute x7, waiting for transfers between devices, along_y(): return lax.ppermute(block, 'tensor', y_shift(step))  19.9 us
    all_to_all x1, waiting for transfers between devices, shards(): lax.all_to_all(outgoing, 'dp', split_axis=0, concat_axis=0, tiled=True)  19.7 us
    pallas_call x1, Pallas kernels, shards(): pl.pallas_call(kernel, out_shape=jax.ShapeDtypeStruct((rows, local), jnp....  17.4 us
    all_to_all x1, starting transfers between devices, shards(): lax.all_to_all(outgoing, 'dp', split_axis=0, concat_axis=0, tiled=True)  10.4 us
    ppermute x4, waiting for transfers between devices, along_z(): return lax.ppermute(block, 'tensor', z_shift(step))  4.21 us
  transfers between devices with their start and end apart: 15, of which 8 were waited for; matrix products, arithmetic and copies ran while one was open for 6% of the time, Pallas kernels for 0%

profile of v9, /device:TPU:1, one launch (start us, length us, event | category | flops | bytes accessed | tf_op | source)
XLA Modules:
  0.0 186.8 jit_solution(15105138245199301194)
XLA Ops:
  6.5 0.8 dynamic-slice_bitcast_fusion
  7.3 0.1 select_reduce_fusion.1
  7.5 0.2 copy-done
  7.7 1.5 gather_fusion
  9.2 10.4 %all-to-all-start = ((bf16[32,32,384]{2,1,0:T(8,128)(2,1)}), bf16[32,32,384]{2,1,0:T(8,128)(2,1)S(1)}, u32[]{:S(2)}, u32[]{:S(2)}) async-start(bf16[32,32,384]{2,1,0:T(8,128)(2,1)} %gather_fusion), calls=%async_computation | async-start | bytes 1572864 | tf_op jit(solution)/shard_map/all_to_all | solution.py:187
  19.7 0.0 all-gather.3.cloned.1.call-start
  19.7 0.7 pad_maximum_fusion.2
  20.5 0.0 all-gather.3.cloned.1.call-update
  20.5 0.0 all-gather.5.cloned.1.call-start
  20.6 0.7 fusion.7
  21.3 0.1 copy.13
  21.4 0.1 reduce-window.4
  21.4 0.1 reduce
  21.5 0.1 convert_reduce_fusion
  21.6 0.7 fusion.6
  22.3 0.1 select_reduce_fusion
  22.4 19.7 %all-to-all-done = bf16[32,32,384]{2,1,0:T(8,128)(2,1)S(1)} async-done(((bf16[32,32,384]{2,1,0:T(8,128)(2,1)}), bf16[32,32,384]{2,1,0:T(8,128)(2,1)S(1)}, u32[]{:S(2)}, u32[]{:S(2)}) %all-to-all-start) | async-done | bytes 786464 | tf_op jit(solution)/shard_map/all_to_all | solution.py:187
  42.1 1.9 %gather_fusion.1 = bf16[512,384]{1,0:T(8,128)(2,1)S(1)} fusion(bf16[1024,384]{1,0:T(8,128)(2,1)S(1)} %bitcast.22, s32[1024]{0:T(1024)S(1)} %pad_clamp_fusion), kind=kCustom, calls=%fused_computation.1 | custom fusion | bytes 788480 | tf_op jit(solution)/shard_map/gather | solution.py:197
  44.1 8.3 %collective-permute-start = (bf16[528,384]{1,0:T(8,128)(2,1)S(1)}, bf16[528,384]{1,0:T(8,128)(2,1)S(1)}, u32[]{:S(2)}, u32[]{:S(2)}) collective-permute-start(bf16[528,384]{1,0:T(8,128)(2,1)S(1)} %pad_maximum_fusion.refs_1_), channel_id=1, source_target_pairs={{0,4},{1,5},{2,6},{3,7},{4,8},{5,9},{6,10},{7,11},{8,12},{9,13},{1... | collective-permute-start | bytes 1216520 | tf_op jit(solution)/shard_map/ppermute | solution.py:209
  52.4 2.9 %collective-permute-start.1 = (bf16[528,384]{1,0:T(8,128)(2,1)S(1)}, bf16[528,384]{1,0:T(8,128)(2,1)S(1)}, u32[]{:S(2)}, u32[]{:S(2)}) collective-permute-start(bf16[528,384]{1,0:T(8,128)(2,1)S(1)} %pad_maximum_fusion.refs_1_), channel_id=1, source_target_pairs={{0,12},{1,13},{2,14},{3,15},{4,0},{5,1},{6,2},{7,3},{8,4},{9,5},{1... | collective-permute-start | bytes 1216520 | tf_op jit(solution)/shard_map/ppermute | solution.py:209
  55.3 3.2 %collective-permute-start.2 = (bf16[528,384]{1,0:T(8,128)(2,1)S(1)}, bf16[528,384]{1,0:T(8,128)(2,1)S(1)}, u32[]{:S(2)}, u32[]{:S(2)}) collective-permute-start(bf16[528,384]{1,0:T(8,128)(2,1)S(1)} %pad_maximum_fusion.refs_1_), channel_id=1, source_target_pairs={{0,1},{1,2},{2,3},{3,0},{4,5},{5,6},{6,7},{7,4},{8,9},{9,10},{10,1... | collective-permute-start | bytes 1216520 | tf_op jit(solution)/shard_map/ppermute | solution.py:206
  58.5 3.4 %collective-permute-start.3 = (bf16[528,384]{1,0:T(8,128)(2,1)S(1)}, bf16[528,384]{1,0:T(8,128)(2,1)S(1)}, u32[]{:S(2)}, u32[]{:S(2)}) collective-permute-start(bf16[528,384]{1,0:T(8,128)(2,1)S(1)} %pad_maximum_fusion.refs_1_), channel_id=1, source_target_pairs={{0,3},{1,0},{2,1},{3,2},{4,7},{5,4},{6,5},{7,6},{8,11},{9,8},{10,9... | collective-permute-start | bytes 1216520 | tf_op jit(solution)/shard_map/ppermute | solution.py:206
  61.9 3.5 %collective-permute-start.4 = (bf16[528,384]{1,0:T(8,128)(2,1)S(1)}, bf16[528,384]{1,0:T(8,128)(2,1)S(1)}, u32[]{:S(2)}, u32[]{:S(2)}) collective-permute-start(bf16[528,384]{1,0:T(8,128)(2,1)S(1)} %pad_maximum_fusion.refs_1_), channel_id=1, source_target_pairs={{0,2},{1,3},{2,0},{3,1},{4,6},{5,7},{6,4},{7,5},{8,10},{9,11},{10,... | collective-permute-start | bytes 1216520 | tf_op jit(solution)/shard_map/ppermute | solution.py:206
  65.4 20.8 %all-gather.3.cloned.1.call-done = bf16[768,768]{1,0:T(8,128)(2,1)} async-done(((bf16[192,768]{1,0:T(8,128)(2,1)}), bf16[768,768]{1,0:T(8,128)(2,1)}) %all-gather.3.cloned.1.call-update) | async-done | bytes 1179664 | tf_op jit(solution)/shard_map/all_gather | solution.py:178
  86.2 1.8 collective-permute-done
  88.0 0.0 collective-permute-done.1
  88.0 0.0 collective-permute-done.2.refs_2_
  88.1 0.0 all-gather.5.cloned.1.call-update
  88.1 10.1 %collective-permute-start.10 = (bf16[256,384]{1,0:T(8,128)(2,1)S(1)}, bf16[256,384]{1,0:T(8,128)(2,1)S(1)}, u32[]{:S(2)}, u32[]{:S(2)}) collective-permute-start(bf16[256,384]{1,0:T(8,128)(2,1)S(1)} %slice.15), channel_id=1, source_target_pairs={{0,12},{1,13},{2,14},{3,15},{4,0},{5,1},{6,2},{7,3},{8,4},{9,5},{1... | collective-permute-start | bytes 589832 | tf_op jit(solution)/shard_map/ppermute | solution.py:209
  98.2 1.9 %collective-permute-start.9 = (bf16[272,384]{1,0:T(8,128)(2,1)S(1)}, bf16[272,384]{1,0:T(8,128)(2,1)S(1)}, u32[]{:S(2)}, u32[]{:S(2)}) collective-permute-start(bf16[272,384]{1,0:T(8,128)(2,1)S(1)} %slice.14), channel_id=1, source_target_pairs={{0,4},{1,5},{2,6},{3,7},{4,8},{5,9},{6,10},{7,11},{8,12},{9,13},{1... | collective-permute-start | bytes 626696 | tf_op jit(solution)/shard_map/ppermute | solution.py:209
  100.2 0.8 constant_dynamic-update-slice_fusion.1
  101.0 0.8 constant_dynamic-update-slice_fusion.refs_5_
  101.8 3.1 %collective-permute-start.5 = (bf16[1056,384]{1,0:T(8,128)(2,1)}, bf16[1056,384]{1,0:T(8,128)(2,1)S(1)}, u32[]{:S(2)}, u32[]{:S(2)}) collective-permute-start(bf16[1056,384]{1,0:T(8,128)(2,1)} %constant_dynamic-update-slice_fusion.refs_5_), channel_id=1, source_target_pairs={{0,1},{1,2},{2,3},{3,0},{4,5},{5,6},{6,7},{7,4},{8,9},{9,10},{10,1... | collective-permute-start | bytes 2433032 | tf_op jit(solution)/shard_map/ppermute | solution.py:206
  104.9 3.4 %collective-permute-start.6 = (bf16[1056,384]{1,0:T(8,128)(2,1)}, bf16[1056,384]{1,0:T(8,128)(2,1)}, u32[]{:S(2)}, u32[]{:S(2)}) collective-permute-start(bf16[1056,384]{1,0:T(8,128)(2,1)} %constant_dynamic-update-slice_fusion.refs_5_), channel_id=1, source_target_pairs={{0,3},{1,0},{2,1},{3,2},{4,7},{5,4},{6,5},{7,6},{8,11},{9,8},{10,9... | collective-permute-start | bytes 2433032 | tf_op jit(solution)/shard_map/ppermute | solution.py:206
  108.3 2.4 %collective-permute-done.9 = bf16[272,384]{1,0:T(8,128)(2,1)S(1)} collective-permute-done((bf16[272,384]{1,0:T(8,128)(2,1)S(1)}, bf16[272,384]{1,0:T(8,128)(2,1)S(1)}, u32[]{:S(2)}, u32[]{:S(2)}) %collective-permute-start.9) | collective-permute-done | bytes 208928 | tf_op jit(solution)/shard_map/ppermute | solution.py:209
  110.7 1.3 broadcast_in_dim.58
  112.0 3.9 %all-to-all-start.1 = ((bf16[4,528,384]{2,1,0:T(8,128)(2,1)}), bf16[4,528,384]{2,1,0:T(8,128)(2,1)S(1)}, u32[]{:S(2)}, u32[]{:S(2)}) async-start(bf16[4,528,384]{2,1,0:T(8,128)(2,1)} %broadcast_in_dim.58), calls=%async_computation.1 | async-start | bytes 3244032 | tf_op jit(solution)/shard_map/all_to_all | solution.py:228
  115.9 2.8 %collective-permute-done.5.refs_6_ = bf16[1056,384]{1,0:T(8,128)(2,1)S(1)} collective-permute-done((bf16[1056,384]{1,0:T(8,128)(2,1)}, bf16[1056,384]{1,0:T(8,128)(2,1)S(1)}, u32[]{:S(2)}, u32[]{:S(2)}) %collective-permute-start.5) | collective-permute-done | bytes 811040 | tf_op jit(solution)/shard_map/ppermute | solution.py:206
  118.8 0.9 slice.20
  119.6 2.0 %collective-permute-start.7 = (bf16[528,384]{1,0:T(8,128)(2,1)}, bf16[528,384]{1,0:T(8,128)(2,1)}, u32[]{:S(2)}, u32[]{:S(2)}) collective-permute-start(bf16[528,384]{1,0:T(8,128)(2,1)} %slice.20), channel_id=1, source_target_pairs={{0,1},{1,2},{2,3},{3,0},{4,5},{5,6},{6,7},{7,4},{8,9},{9,10},{10,1... | collective-permute-start | bytes 1216520 | tf_op jit(solution)/shard_map/ppermute | solution.py:206
  121.7 1.8 slice.21
  123.5 4.5 %collective-permute-start.8 = (bf16[528,384]{1,0:T(8,128)(2,1)}, bf16[528,384]{1,0:T(8,128)(2,1)}, u32[]{:S(2)}, u32[]{:S(2)}) collective-permute-start(bf16[528,384]{1,0:T(8,128)(2,1)} %slice.21), channel_id=1, source_target_pairs={{0,3},{1,0},{2,1},{3,2},{4,7},{5,4},{6,5},{7,6},{8,11},{9,8},{10,9... | collective-permute-start | bytes 1216520 | tf_op jit(solution)/shard_map/ppermute | solution.py:206
  128.0 0.9 copy.14.refs_12_
  128.8 0.7 fusion.refs_0_
  129.5 16.7 %collective-permute-done.7.refs_8_ = bf16[528,384]{1,0:T(8,128)(2,1)} collective-permute-done((bf16[528,384]{1,0:T(8,128)(2,1)}, bf16[528,384]{1,0:T(8,128)(2,1)}, u32[]{:S(2)}, u32[]{:S(2)}) %collective-permute-start.7) | collective-permute-done | bytes 405536 | tf_op jit(solution)/shard_map/ppermute | solution.py:206
  146.2 0.4 collective-permute-done.8.refs_9_
  146.6 16.0 %all-gather.5.cloned.1.call-done.refs_11_ = bf16[6144,768]{1,0:T(8,128)(2,1)} async-done(((bf16[768,768]{1,0:T(8,128)(2,1)}), bf16[6144,768]{1,0:T(8,128)(2,1)}) %all-gather.5.cloned.1.call-update) | async-done | bytes 9437200 | tf_op jit(solution)/shard_map/all_gather | solution.py:221
  162.6 17.4 %norm_project_attend.1 = bf16[512,256]{1,0:T(8,128)(2,1)} custom-call(s32[16]{0:T(128)} %fusion.refs_0_, bf16[528,384]{1,0:T(8,128)(2,1)} %copy-done.3, bf16[528,384]{1,0:T(8,128)(2,1)} %copy-done.4, bf16[528,384]{1,0:T(8,128)(2,1)} %copy-done.5, bf16[528,384]{1,0:T(8,128)(2,1)} %copy-done.6, bf16[1056,384]{1,0:T(8,128)(2,1)} %constant_dynamic-update-slice_fusion.refs_5_, ...), custom_call_target="tpu_custom_call" | custom-call | tf_op jit(solution)/shard_map/norm_project_attend/pallas_call | solution.py:270
  (42 shorter events, 0.2 us)
Async XLA Ops:
  6.5 1.1 copy-start
  6.5 13.2 %copy-start.7 = (bf16[192,256]{1,0:T(8,128)(2,1)S(1)}, bf16[192,256]{1,0:T(8,128)(2,1)}, u32[]{:S(2)}) copy-start(bf16[192,256]{1,0:T(8,128)(2,1)} %param.13) | copy-start | bytes 294916
  6.5 13.2 %copy-start.8 = (bf16[192,256]{1,0:T(8,128)(2,1)S(1)}, bf16[192,256]{1,0:T(8,128)(2,1)}, u32[]{:S(2)}) copy-start(bf16[192,256]{1,0:T(8,128)(2,1)} %param.12) | copy-start | bytes 294916
  6.5 13.2 %copy-start.9 = (bf16[192,256]{1,0:T(8,128)(2,1)S(1)}, bf16[192,256]{1,0:T(8,128)(2,1)}, u32[]{:S(2)}) copy-start(bf16[192,256]{1,0:T(8,128)(2,1)} %param.11) | copy-start | bytes 294916
  9.2 32.9 %all-to-all-start = ((bf16[32,32,384]{2,1,0:T(8,128)(2,1)}), bf16[32,32,384]{2,1,0:T(8,128)(2,1)S(1)}, u32[]{:S(2)}, u32[]{:S(2)}) async-start(bf16[32,32,384]{2,1,0:T(8,128)(2,1)} %gather_fusion), calls=%async_computation | async-start | bytes 1572864 | tf_op jit(solution)/shard_map/all_to_all | solution.py:187
  19.7 66.6 %all-gather.3.cloned.1.call-start = ((), (), s32[]{:S(2)}) async-start(), calls=%async_computation.2 | async-start | bytes 1474560 | tf_op jit(solution)/shard_map/all_gather | solution.py:178
  20.5 142.1 %all-gather.5.cloned.1.call-start = ((), (), s32[]{:S(2)}) async-start(), calls=%async_computation.3 | async-start | bytes 10616832 | tf_op jit(solution)/shard_map/all_gather | solution.py:221
  21.6 106.3 %copy-start.10 = (s32[512]{0:T(512)}, s32[512]{0:T(512)S(1)}, u32[]{:S(2)}) copy-start(s32[512]{0:T(512)S(1)} %convert_reduce_fusion) | copy-start | bytes 6148
  42.1 1.9 %copy-start.11 = (bf16[384]{0:T(512)(128)(2,1)S(1)}, bf16[384]{0:T(512)(128)(2,1)}, u32[]{:S(2)}) copy-start(bf16[384]{0:T(512)(128)(2,1)} %param.10) | copy-start | bytes 2308
  44.1 57.7 %copy-start.3 = (bf16[528,384]{1,0:T(8,128)(2,1)}, bf16[528,384]{1,0:T(8,128)(2,1)S(1)}, u32[]{:S(2)}) copy-start(bf16[528,384]{1,0:T(8,128)(2,1)S(1)} %pad_maximum_fusion.refs_1_) | copy-start | bytes 1216516
  44.1 43.9 %collective-permute-start = (bf16[528,384]{1,0:T(8,128)(2,1)S(1)}, bf16[528,384]{1,0:T(8,128)(2,1)S(1)}, u32[]{:S(2)}, u32[]{:S(2)}) collective-permute-start(bf16[528,384]{1,0:T(8,128)(2,1)S(1)} %pad_maximum_fusion.refs_1_), channel_id=1, source_target_pairs={{0,4},{1,5},{2,6},{3,7},{4,8},{5,9},{6,10},{7,11},{8,12},{9,13},{1... | collective-permute-start | bytes 1216520 | tf_op jit(solution)/shard_map/ppermute | solution.py:209
  52.4 35.6 %collective-permute-start.1 = (bf16[528,384]{1,0:T(8,128)(2,1)S(1)}, bf16[528,384]{1,0:T(8,128)(2,1)S(1)}, u32[]{:S(2)}, u32[]{:S(2)}) collective-permute-start(bf16[528,384]{1,0:T(8,128)(2,1)S(1)} %pad_maximum_fusion.refs_1_), channel_id=1, source_target_pairs={{0,12},{1,13},{2,14},{3,15},{4,0},{5,1},{6,2},{7,3},{8,4},{9,5},{1... | collective-permute-start | bytes 1216520 | tf_op jit(solution)/shard_map/ppermute | solution.py:209
  55.3 32.7 %collective-permute-start.2 = (bf16[528,384]{1,0:T(8,128)(2,1)S(1)}, bf16[528,384]{1,0:T(8,128)(2,1)S(1)}, u32[]{:S(2)}, u32[]{:S(2)}) collective-permute-start(bf16[528,384]{1,0:T(8,128)(2,1)S(1)} %pad_maximum_fusion.refs_1_), channel_id=1, source_target_pairs={{0,1},{1,2},{2,3},{3,0},{4,5},{5,6},{6,7},{7,4},{8,9},{9,10},{10,1... | collective-permute-start | bytes 1216520 | tf_op jit(solution)/shard_map/ppermute | solution.py:206
  58.5 29.5 %collective-permute-start.3 = (bf16[528,384]{1,0:T(8,128)(2,1)S(1)}, bf16[528,384]{1,0:T(8,128)(2,1)S(1)}, u32[]{:S(2)}, u32[]{:S(2)}) collective-permute-start(bf16[528,384]{1,0:T(8,128)(2,1)S(1)} %pad_maximum_fusion.refs_1_), channel_id=1, source_target_pairs={{0,3},{1,0},{2,1},{3,2},{4,7},{5,4},{6,5},{7,6},{8,11},{9,8},{10,9... | collective-permute-start | bytes 1216520 | tf_op jit(solution)/shard_map/ppermute | solution.py:206
  61.9 26.2 %collective-permute-start.4 = (bf16[528,384]{1,0:T(8,128)(2,1)S(1)}, bf16[528,384]{1,0:T(8,128)(2,1)S(1)}, u32[]{:S(2)}, u32[]{:S(2)}) collective-permute-start(bf16[528,384]{1,0:T(8,128)(2,1)S(1)} %pad_maximum_fusion.refs_1_), channel_id=1, source_target_pairs={{0,2},{1,3},{2,0},{3,1},{4,6},{5,7},{6,4},{7,5},{8,10},{9,11},{10,... | collective-permute-start | bytes 1216520 | tf_op jit(solution)/shard_map/ppermute | solution.py:206
  88.0 13.7 %copy-start.4 = (bf16[528,384]{1,0:T(8,128)(2,1)}, bf16[528,384]{1,0:T(8,128)(2,1)S(1)}, u32[]{:S(2)}) copy-start(bf16[528,384]{1,0:T(8,128)(2,1)S(1)} %collective-permute-done.2.refs_2_) | copy-start | bytes 1216516
  88.1 12.9 %copy-start.5 = (bf16[528,384]{1,0:T(8,128)(2,1)}, bf16[528,384]{1,0:T(8,128)(2,1)S(1)}, u32[]{:S(2)}) copy-start(bf16[528,384]{1,0:T(8,128)(2,1)S(1)} %collective-permute-done.3.refs_3_) | copy-start | bytes 1216516
  88.1 12.9 %copy-start.6 = (bf16[528,384]{1,0:T(8,128)(2,1)}, bf16[528,384]{1,0:T(8,128)(2,1)S(1)}, u32[]{:S(2)}) copy-start(bf16[528,384]{1,0:T(8,128)(2,1)S(1)} %collective-permute-done.4.refs_4_) | copy-start | bytes 1216516
  88.1 20.1 %collective-permute-start.10 = (bf16[256,384]{1,0:T(8,128)(2,1)S(1)}, bf16[256,384]{1,0:T(8,128)(2,1)S(1)}, u32[]{:S(2)}, u32[]{:S(2)}) collective-permute-start(bf16[256,384]{1,0:T(8,128)(2,1)S(1)} %slice.15), channel_id=1, source_target_pairs={{0,12},{1,13},{2,14},{3,15},{4,0},{5,1},{6,2},{7,3},{8,4},{9,5},{1... | collective-permute-start | bytes 589832 | tf_op jit(solution)/shard_map/ppermute | solution.py:209
  98.2 12.4 %collective-permute-start.9 = (bf16[272,384]{1,0:T(8,128)(2,1)S(1)}, bf16[272,384]{1,0:T(8,128)(2,1)S(1)}, u32[]{:S(2)}, u32[]{:S(2)}) collective-permute-start(bf16[272,384]{1,0:T(8,128)(2,1)S(1)} %slice.14), channel_id=1, source_target_pairs={{0,4},{1,5},{2,6},{3,7},{4,8},{5,9},{6,10},{7,11},{8,12},{9,13},{1... | collective-permute-start | bytes 626696 | tf_op jit(solution)/shard_map/ppermute | solution.py:209
  101.8 17.0 %collective-permute-start.5 = (bf16[1056,384]{1,0:T(8,128)(2,1)}, bf16[1056,384]{1,0:T(8,128)(2,1)S(1)}, u32[]{:S(2)}, u32[]{:S(2)}) collective-permute-start(bf16[1056,384]{1,0:T(8,128)(2,1)} %constant_dynamic-update-slice_fusion.refs_5_), channel_id=1, source_target_pairs={{0,1},{1,2},{2,3},{3,0},{4,5},{5,6},{6,7},{7,4},{8,9},{9,10},{10,1... | collective-permute-start | bytes 2433032 | tf_op jit(solution)/shard_map/ppermute | solution.py:206
  104.9 16.7 %collective-permute-start.6 = (bf16[1056,384]{1,0:T(8,128)(2,1)}, bf16[1056,384]{1,0:T(8,128)(2,1)}, u32[]{:S(2)}, u32[]{:S(2)}) collective-permute-start(bf16[1056,384]{1,0:T(8,128)(2,1)} %constant_dynamic-update-slice_fusion.refs_5_), channel_id=1, source_target_pairs={{0,3},{1,0},{2,1},{3,2},{4,7},{5,4},{6,5},{7,6},{8,11},{9,8},{10,9... | collective-permute-start | bytes 2433032 | tf_op jit(solution)/shard_map/ppermute | solution.py:206
  112.0 34.6 %all-to-all-start.1 = ((bf16[4,528,384]{2,1,0:T(8,128)(2,1)}), bf16[4,528,384]{2,1,0:T(8,128)(2,1)S(1)}, u32[]{:S(2)}, u32[]{:S(2)}) async-start(bf16[4,528,384]{2,1,0:T(8,128)(2,1)} %broadcast_in_dim.58), calls=%async_computation.1 | async-start | bytes 3244032 | tf_op jit(solution)/shard_map/all_to_all | solution.py:228
  115.9 12.9 %copy-start.12 = (s32[12]{0:T(128)S(1)}, s32[12]{0:T(128)}, u32[]{:S(2)}) copy-start(s32[12]{0:T(128)} %constant.71.clone) | copy-start | bytes 148
  115.9 12.9 %copy-start.13 = (s32[16]{0:T(128)S(1)}, s32[16]{0:T(128)}, u32[]{:S(2)}) copy-start(s32[16]{0:T(128)} %constant.70.clone) | copy-start | bytes 196
  118.8 43.8 %copy-start.2 = (bf16[1056,384]{1,0:T(8,128)(2,1)}, bf16[1056,384]{1,0:T(8,128)(2,1)S(1)}, u32[]{:S(2)}) copy-start(bf16[1056,384]{1,0:T(8,128)(2,1)S(1)} %collective-permute-done.5.refs_6_) | copy-start | bytes 2433028
  119.6 26.6 %collective-permute-start.7 = (bf16[528,384]{1,0:T(8,128)(2,1)}, bf16[528,384]{1,0:T(8,128)(2,1)}, u32[]{:S(2)}, u32[]{:S(2)}) collective-permute-start(bf16[528,384]{1,0:T(8,128)(2,1)} %slice.20), channel_id=1, source_target_pairs={{0,1},{1,2},{2,3},{3,0},{4,5},{5,6},{6,7},{7,4},{8,9},{9,10},{10,1... | collective-permute-start | bytes 1216520 | tf_op jit(solution)/shard_map/ppermute | solution.py:206
  123.5 23.1 %collective-permute-start.8 = (bf16[528,384]{1,0:T(8,128)(2,1)}, bf16[528,384]{1,0:T(8,128)(2,1)}, u32[]{:S(2)}, u32[]{:S(2)}) collective-permute-start(bf16[528,384]{1,0:T(8,128)(2,1)} %slice.21), channel_id=1, source_target_pairs={{0,3},{1,0},{2,1},{3,2},{4,7},{5,4},{6,5},{7,6},{8,11},{9,8},{10,9... | collective-permute-start | bytes 1216520 | tf_op jit(solution)/shard_map/ppermute | solution.py:206
  146.6 16.0 %copy-start.1 = (bf16[4,528,384]{2,1,0:T(8,128)(2,1)}, bf16[4,528,384]{2,1,0:T(8,128)(2,1)S(1)}, u32[]{:S(2)}) copy-start(bf16[4,528,384]{2,1,0:T(8,128)(2,1)S(1)} %all-to-all-done.1) | copy-start | bytes 4866052
Sparse Core Ops, SparseCore 0:
  22.6 63.5 all-gather.2
  88.3 74.1 all-gather.4

commit v10 on v9

--- a/solution.py
+++ b/solution.py
@@ -146,7 +146,7 @@
         normed_ref[half:], weight_ref[...], preferred_element_type=jnp.float32
     ).astype(jnp.bfloat16)
     local = out_ref.shape[1]
-    span, window = 128, 256
+    span, window = 64, 128
     for row in range(0, rows, span):
         low = min(max(row - (window - span) // 2, 0), rows - window)
         same = seg_col_ref[row : row + span, :1] == seg_row_ref[:1, low : low + window]
@@ -224,6 +224,9 @@
     pair_far_up = along_y(pair_up[:all_rows], 1)
     pair_far_down = along_y(pair_down[all_rows:], -1)
     far_top, far_rest = along_z(z_up[:cut], 1), along_z(z_down[cut:], -1)
+    far_top, far_rest, pair_up, pair_down = lax.optimization_barrier(
+        (far_top, far_rest, pair_up, pair_down)
+    )
     far = jnp.concatenate([far_top, far_rest], axis=0)
     far_all = lax.all_to_all(
         jnp.broadcast_to(far[None], (Y_PARTS, *far.shape)),

time: 189 us -> 201 us (1.063)
  the two profiles are of different devices: /device:TPU:1 before, /device:TPU:36 now
where the time goes in v10:
time: 201 us; the launch traced here: 200 us
  waiting for transfers between devices  91.9 us (46%)
  starting transfers between devices  59 us (29%)
  Pallas kernels  21.4 us (11%)
  between operations  13.8 us (7%)
  local copies, waits for them, and re-layouts  11.6 us (6%)
  other arithmetic  2.64 us (1%)
    ppermute x4, waiting for transfers between devices, along_z(): return lax.ppermute(block, 'tensor', z_shift(step))  30 us
    all_gather x2, waiting for transfers between devices, shards(): lax.all_gather(weight, 'dp', axis=0, tiled=True, axis_index_groups=dp_gro...  25.8 us
    ppermute x7, starting transfers between devices, along_y(): return lax.ppermute(block, 'tensor', y_shift(step))  25 us
    pallas_call x1, Pallas kernels, shards(): pl.pallas_call(kernel, out_shape=jax.ShapeDtypeStruct((rows, local), jnp....  21.4 us
    ppermute x4, starting transfers between devices, along_z(): return lax.ppermute(block, 'tensor', z_shift(step))  21.2 us
    ppermute x7, waiting for transfers between devices, along_y(): return lax.ppermute(block, 'tensor', y_shift(step))  19.6 us
    all_to_all x1, waiting for transfers between devices, shards(): lax.all_to_all(outgoing, 'dp', split_axis=0, concat_axis=0, tiled=True)  16.3 us
    all_to_all x1, starting transfers between devices, shards(): lax.all_to_all(outgoing, 'dp', split_axis=0, concat_axis=0, tiled=True)  9.1 us
  transfers between devices with their start and end apart: 15, of which 6 were waited for; matrix products, arithmetic and copies ran while one was open for 5% of the time, Pallas kernels for 0%

profile of v10, /device:TPU:36, one launch (start us, length us, event | category | flops | bytes accessed | tf_op | source)
XLA Modules:
  0.0 200.4 jit_solution(9565674396255945920)
XLA Ops:
  6.5 0.8 dynamic-slice_bitcast_fusion
  7.3 0.1 select_reduce_fusion.1
  7.5 0.2 copy-done
  7.7 1.5 gather_fusion
  9.2 9.1 %all-to-all-start = ((bf16[32,32,384]{2,1,0:T(8,128)(2,1)}), bf16[32,32,384]{2,1,0:T(8,128)(2,1)S(1)}, u32[]{:S(2)}, u32[]{:S(2)}) async-start(bf16[32,32,384]{2,1,0:T(8,128)(2,1)} %gather_fusion), calls=%async_computation | async-start | bytes 1572864 | tf_op jit(solution)/shard_map/all_to_all | solution.py:187
  18.3 0.0 all-gather.3.cloned.1.call-start
  18.4 0.7 pad_maximum_fusion.2
  19.2 0.0 all-gather.3.cloned.1.call-update
  19.2 0.0 all-gather.5.cloned.1.call-start
  19.2 0.7 fusion.7
  19.9 0.1 copy.13
  20.0 0.1 reduce-window.4
  20.1 0.1 reduce
  20.2 0.1 convert_reduce_fusion
  20.3 0.7 fusion.6
  21.0 0.1 select_reduce_fusion
  21.1 16.3 %all-to-all-done = bf16[32,32,384]{2,1,0:T(8,128)(2,1)S(1)} async-done(((bf16[32,32,384]{2,1,0:T(8,128)(2,1)}), bf16[32,32,384]{2,1,0:T(8,128)(2,1)S(1)}, u32[]{:S(2)}, u32[]{:S(2)}) %all-to-all-start) | async-done | bytes 786464 | tf_op jit(solution)/shard_map/all_to_all | solution.py:187
  37.4 1.9 gather_fusion.1
  39.4 8.6 %collective-permute-start = (bf16[528,384]{1,0:T(8,128)(2,1)S(1)}, bf16[528,384]{1,0:T(8,128)(2,1)S(1)}, u32[]{:S(2)}, u32[]{:S(2)}) collective-permute-start(bf16[528,384]{1,0:T(8,128)(2,1)S(1)} %pad_maximum_fusion.refs_1_), channel_id=1, source_target_pairs={{0,4},{1,5},{2,6},{3,7},{4,8},{5,9},{6,10},{7,11},{8,12},{9,13},{1... | collective-permute-start | bytes 1216520 | tf_op jit(solution)/shard_map/ppermute | solution.py:209
  48.0 2.9 %collective-permute-start.1 = (bf16[528,384]{1,0:T(8,128)(2,1)S(1)}, bf16[528,384]{1,0:T(8,128)(2,1)S(1)}, u32[]{:S(2)}, u32[]{:S(2)}) collective-permute-start(bf16[528,384]{1,0:T(8,128)(2,1)S(1)} %pad_maximum_fusion.refs_1_), channel_id=1, source_target_pairs={{0,12},{1,13},{2,14},{3,15},{4,0},{5,1},{6,2},{7,3},{8,4},{9,5},{1... | collective-permute-start | bytes 1216520 | tf_op jit(solution)/shard_map/ppermute | solution.py:209
  50.9 3.5 %collective-permute-start.2 = (bf16[528,384]{1,0:T(8,128)(2,1)S(1)}, bf16[528,384]{1,0:T(8,128)(2,1)S(1)}, u32[]{:S(2)}, u32[]{:S(2)}) collective-permute-start(bf16[528,384]{1,0:T(8,128)(2,1)S(1)} %pad_maximum_fusion.refs_1_), channel_id=1, source_target_pairs={{0,1},{1,2},{2,3},{3,0},{4,5},{5,6},{6,7},{7,4},{8,9},{9,10},{10,1... | collective-permute-start | bytes 1216520 | tf_op jit(solution)/shard_map/ppermute | solution.py:206
  54.4 3.6 %collective-permute-start.3 = (bf16[528,384]{1,0:T(8,128)(2,1)S(1)}, bf16[528,384]{1,0:T(8,128)(2,1)S(1)}, u32[]{:S(2)}, u32[]{:S(2)}) collective-permute-start(bf16[528,384]{1,0:T(8,128)(2,1)S(1)} %pad_maximum_fusion.refs_1_), channel_id=1, source_target_pairs={{0,3},{1,0},{2,1},{3,2},{4,7},{5,4},{6,5},{7,6},{8,11},{9,8},{10,9... | collective-permute-start | bytes 1216520 | tf_op jit(solution)/shard_map/ppermute | solution.py:206
  57.9 3.9 %collective-permute-start.4 = (bf16[528,384]{1,0:T(8,128)(2,1)S(1)}, bf16[528,384]{1,0:T(8,128)(2,1)S(1)}, u32[]{:S(2)}, u32[]{:S(2)}) collective-permute-start(bf16[528,384]{1,0:T(8,128)(2,1)S(1)} %pad_maximum_fusion.refs_1_), channel_id=1, source_target_pairs={{0,2},{1,3},{2,0},{3,1},{4,6},{5,7},{6,4},{7,5},{8,10},{9,11},{10,... | collective-permute-start | bytes 1216520 | tf_op jit(solution)/shard_map/ppermute | solution.py:206
  61.8 25.8 %all-gather.3.cloned.1.call-done = bf16[768,768]{1,0:T(8,128)(2,1)} async-done(((bf16[192,768]{1,0:T(8,128)(2,1)}), bf16[768,768]{1,0:T(8,128)(2,1)}) %all-gather.3.cloned.1.call-update) | async-done | bytes 1179664 | tf_op jit(solution)/shard_map/all_gather | solution.py:178
  87.7 10.0 %collective-permute-done = bf16[528,384]{1,0:T(8,128)(2,1)S(1)} collective-permute-done((bf16[528,384]{1,0:T(8,128)(2,1)S(1)}, bf16[528,384]{1,0:T(8,128)(2,1)S(1)}, u32[]{:S(2)}, u32[]{:S(2)}) %collective-permute-start) | collective-permute-done | bytes 405536 | tf_op jit(solution)/shard_map/ppermute | solution.py:209
  97.7 2.9 %collective-permute-done.1 = bf16[528,384]{1,0:T(8,128)(2,1)S(1)} collective-permute-done((bf16[528,384]{1,0:T(8,128)(2,1)S(1)}, bf16[528,384]{1,0:T(8,128)(2,1)S(1)}, u32[]{:S(2)}, u32[]{:S(2)}) %collective-permute-start.1) | collective-permute-done | bytes 405536 | tf_op jit(solution)/shard_map/ppermute | solution.py:209
  100.6 0.0 all-gather.5.cloned.1.call-update
  100.7 0.7 copy-done.6
  101.4 0.2 copy-done.7
  101.6 0.1 constant_dynamic-update-slice_fusion.refs_5_
  101.7 3.4 %collective-permute-start.7 = (bf16[1056,384]{1,0:T(8,128)(2,1)S(1)}, bf16[1056,384]{1,0:T(8,128)(2,1)S(1)}, u32[]{:S(2)}, u32[]{:S(2)}) collective-permute-start(bf16[1056,384]{1,0:T(8,128)(2,1)S(1)} %constant_dynamic-update-slice_fusion.refs_5_), channel_id=1, source_target_pairs={{0,1},{1,2},{2,3},{3,0},{4,5},{5,6},{6,7},{7,4},{8,9},{9,10},{10,1... | collective-permute-start | bytes 2433032 | tf_op jit(solution)/shard_map/ppermute | solution.py:206
  105.1 3.7 %collective-permute-start.8 = (bf16[1056,384]{1,0:T(8,128)(2,1)S(1)}, bf16[1056,384]{1,0:T(8,128)(2,1)}, u32[]{:S(2)}, u32[]{:S(2)}) collective-permute-start(bf16[1056,384]{1,0:T(8,128)(2,1)S(1)} %constant_dynamic-update-slice_fusion.refs_5_), channel_id=1, source_target_pairs={{0,3},{1,0},{2,1},{3,2},{4,7},{5,4},{6,5},{7,6},{8,11},{9,8},{10,9... | collective-permute-start | bytes 2433032 | tf_op jit(solution)/shard_map/ppermute | solution.py:206
  108.8 6.7 %collective-permute-start.5 = (bf16[272,384]{1,0:T(8,128)(2,1)S(1)}, bf16[272,384]{1,0:T(8,128)(2,1)S(1)}, u32[]{:S(2)}, u32[]{:S(2)}) collective-permute-start(bf16[272,384]{1,0:T(8,128)(2,1)S(1)} %slice.12), channel_id=1, source_target_pairs={{0,4},{1,5},{2,6},{3,7},{4,8},{5,9},{6,10},{7,11},{8,12},{9,13},{1... | collective-permute-start | bytes 626696 | tf_op jit(solution)/shard_map/ppermute | solution.py:209
  115.6 3.0 %collective-permute-start.6 = (bf16[256,384]{1,0:T(8,128)(2,1)S(1)}, bf16[256,384]{1,0:T(8,128)(2,1)S(1)}, u32[]{:S(2)}, u32[]{:S(2)}) collective-permute-start(bf16[256,384]{1,0:T(8,128)(2,1)S(1)} %slice.13), channel_id=1, source_target_pairs={{0,12},{1,13},{2,14},{3,15},{4,0},{5,1},{6,2},{7,3},{8,4},{9,5},{1... | collective-permute-start | bytes 589832 | tf_op jit(solution)/shard_map/ppermute | solution.py:209
  118.6 17.1 %collective-permute-done.6 = bf16[256,384]{1,0:T(8,128)(2,1)S(1)} collective-permute-done((bf16[256,384]{1,0:T(8,128)(2,1)S(1)}, bf16[256,384]{1,0:T(8,128)(2,1)S(1)}, u32[]{:S(2)}, u32[]{:S(2)}) %collective-permute-start.6) | collective-permute-done | bytes 196640 | tf_op jit(solution)/shard_map/ppermute | solution.py:209
  135.8 1.4 broadcast_in_dim.58
  137.1 3.6 %all-to-all-start.1 = ((bf16[4,528,384]{2,1,0:T(8,128)(2,1)}), bf16[4,528,384]{2,1,0:T(8,128)(2,1)S(1)}, u32[]{:S(2)}, u32[]{:S(2)}) async-start(bf16[4,528,384]{2,1,0:T(8,128)(2,1)} %broadcast_in_dim.58), calls=%async_computation.1 | async-start | bytes 3244032 | tf_op jit(solution)/shard_map/all_to_all | solution.py:231
  140.8 0.8 slice.20
  141.6 3.9 %collective-permute-start.9 = (bf16[528,384]{1,0:T(8,128)(2,1)}, bf16[528,384]{1,0:T(8,128)(2,1)S(1)}, u32[]{:S(2)}, u32[]{:S(2)}) collective-permute-start(bf16[528,384]{1,0:T(8,128)(2,1)} %slice.20), channel_id=1, source_target_pairs={{0,1},{1,2},{2,3},{3,0},{4,5},{5,6},{6,7},{7,4},{8,9},{9,10},{10,1... | collective-permute-start | bytes 1216520 | tf_op jit(solution)/shard_map/ppermute | solution.py:206
  145.4 1.0 slice.21
  146.5 3.2 %collective-permute-start.10 = (bf16[528,384]{1,0:T(8,128)(2,1)S(1)}, bf16[528,384]{1,0:T(8,128)(2,1)}, u32[]{:S(2)}, u32[]{:S(2)}) collective-permute-start(bf16[528,384]{1,0:T(8,128)(2,1)S(1)} %slice.21), channel_id=1, source_target_pairs={{0,3},{1,0},{2,1},{3,2},{4,7},{5,4},{6,5},{7,6},{8,11},{9,8},{10,9... | collective-permute-start | bytes 1216520 | tf_op jit(solution)/shard_map/ppermute | solution.py:206
  149.7 0.9 copy.14.refs_12_
  150.6 0.6 fusion.refs_0_
  151.2 19.6 %collective-permute-done.9.refs_8_ = bf16[528,384]{1,0:T(8,128)(2,1)S(1)} collective-permute-done((bf16[528,384]{1,0:T(8,128)(2,1)}, bf16[528,384]{1,0:T(8,128)(2,1)S(1)}, u32[]{:S(2)}, u32[]{:S(2)}) %collective-permute-start.9) | collective-permute-done | bytes 405536 | tf_op jit(solution)/shard_map/ppermute | solution.py:206
  170.8 0.0 all-gather.5.cloned.1.call-done.refs_11_
  170.8 0.7 copy-done.8
  171.5 0.5 copy-done.1
  172.1 21.4 %norm_project_attend.1 = bf16[512,256]{1,0:T(8,128)(2,1)} custom-call(s32[16]{0:T(128)} %fusion.refs_0_, bf16[528,384]{1,0:T(8,128)(2,1)} %copy-done.4, bf16[528,384]{1,0:T(8,128)(2,1)} %copy-done.5, bf16[528,384]{1,0:T(8,128)(2,1)} %copy-done.6, bf16[528,384]{1,0:T(8,128)(2,1)} %copy-done.7, bf16[1056,384]{1,0:T(8,128)(2,1)} %copy-done.3, ...), custom_call_target="tpu_custom_call" | custom-call | tf_op jit(solution)/shard_map/norm_project_attend/pallas_call | solution.py:273
  (46 shorter events, 0.3 us)
Async XLA Ops:
  6.5 1.1 copy-start
  6.5 11.9 %copy-start.9 = (bf16[192,256]{1,0:T(8,128)(2,1)S(1)}, bf16[192,256]{1,0:T(8,128)(2,1)}, u32[]{:S(2)}) copy-start(bf16[192,256]{1,0:T(8,128)(2,1)} %param.13) | copy-start | bytes 294916
  6.5 11.9 %copy-start.10 = (bf16[192,256]{1,0:T(8,128)(2,1)S(1)}, bf16[192,256]{1,0:T(8,128)(2,1)}, u32[]{:S(2)}) copy-start(bf16[192,256]{1,0:T(8,128)(2,1)} %param.12) | copy-start | bytes 294916
  6.5 11.9 %copy-start.11 = (bf16[192,256]{1,0:T(8,128)(2,1)S(1)}, bf16[192,256]{1,0:T(8,128)(2,1)}, u32[]{:S(2)}) copy-start(bf16[192,256]{1,0:T(8,128)(2,1)} %param.11) | copy-start | bytes 294916
  9.2 28.2 %all-to-all-start = ((bf16[32,32,384]{2,1,0:T(8,128)(2,1)}), bf16[32,32,384]{2,1,0:T(8,128)(2,1)S(1)}, u32[]{:S(2)}, u32[]{:S(2)}) async-start(bf16[32,32,384]{2,1,0:T(8,128)(2,1)} %gather_fusion), calls=%async_computation | async-start | bytes 1572864 | tf_op jit(solution)/shard_map/all_to_all | solution.py:187
  18.3 69.3 %all-gather.3.cloned.1.call-start = ((), (), s32[]{:S(2)}) async-start(), calls=%async_computation.2 | async-start | bytes 1474560 | tf_op jit(solution)/shard_map/all_gather | solution.py:178
  19.2 151.6 %all-gather.5.cloned.1.call-start = ((), (), s32[]{:S(2)}) async-start(), calls=%async_computation.3 | async-start | bytes 10616832 | tf_op jit(solution)/shard_map/all_gather | solution.py:221
  20.3 129.4 %copy-start.12 = (s32[512]{0:T(512)}, s32[512]{0:T(512)S(1)}, u32[]{:S(2)}) copy-start(s32[512]{0:T(512)S(1)} %convert_reduce_fusion) | copy-start | bytes 6148
  37.4 1.9 copy-start.13
  39.4 76.1 %copy-start.4 = (bf16[528,384]{1,0:T(8,128)(2,1)}, bf16[528,384]{1,0:T(8,128)(2,1)S(1)}, u32[]{:S(2)}) copy-start(bf16[528,384]{1,0:T(8,128)(2,1)S(1)} %pad_maximum_fusion.refs_1_) | copy-start | bytes 1216516
  39.4 58.3 %collective-permute-start = (bf16[528,384]{1,0:T(8,128)(2,1)S(1)}, bf16[528,384]{1,0:T(8,128)(2,1)S(1)}, u32[]{:S(2)}, u32[]{:S(2)}) collective-permute-start(bf16[528,384]{1,0:T(8,128)(2,1)S(1)} %pad_maximum_fusion.refs_1_), channel_id=1, source_target_pairs={{0,4},{1,5},{2,6},{3,7},{4,8},{5,9},{6,10},{7,11},{8,12},{9,13},{1... | collective-permute-start | bytes 1216520 | tf_op jit(solution)/shard_map/ppermute | solution.py:209
  48.0 52.6 %collective-permute-start.1 = (bf16[528,384]{1,0:T(8,128)(2,1)S(1)}, bf16[528,384]{1,0:T(8,128)(2,1)S(1)}, u32[]{:S(2)}, u32[]{:S(2)}) collective-permute-start(bf16[528,384]{1,0:T(8,128)(2,1)S(1)} %pad_maximum_fusion.refs_1_), channel_id=1, source_target_pairs={{0,12},{1,13},{2,14},{3,15},{4,0},{5,1},{6,2},{7,3},{8,4},{9,5},{1... | collective-permute-start | bytes 1216520 | tf_op jit(solution)/shard_map/ppermute | solution.py:209
  50.9 49.7 %collective-permute-start.2 = (bf16[528,384]{1,0:T(8,128)(2,1)S(1)}, bf16[528,384]{1,0:T(8,128)(2,1)S(1)}, u32[]{:S(2)}, u32[]{:S(2)}) collective-permute-start(bf16[528,384]{1,0:T(8,128)(2,1)S(1)} %pad_maximum_fusion.refs_1_), channel_id=1, source_target_pairs={{0,1},{1,2},{2,3},{3,0},{4,5},{5,6},{6,7},{7,4},{8,9},{9,10},{10,1... | collective-permute-start | bytes 1216520 | tf_op jit(solution)/shard_map/ppermute | solution.py:206
  54.4 46.2 %collective-permute-start.3 = (bf16[528,384]{1,0:T(8,128)(2,1)S(1)}, bf16[528,384]{1,0:T(8,128)(2,1)S(1)}, u32[]{:S(2)}, u32[]{:S(2)}) collective-permute-start(bf16[528,384]{1,0:T(8,128)(2,1)S(1)} %pad_maximum_fusion.refs_1_), channel_id=1, source_target_pairs={{0,3},{1,0},{2,1},{3,2},{4,7},{5,4},{6,5},{7,6},{8,11},{9,8},{10,9... | collective-permute-start | bytes 1216520 | tf_op jit(solution)/shard_map/ppermute | solution.py:206
  57.9 42.7 %collective-permute-start.4 = (bf16[528,384]{1,0:T(8,128)(2,1)S(1)}, bf16[528,384]{1,0:T(8,128)(2,1)S(1)}, u32[]{:S(2)}, u32[]{:S(2)}) collective-permute-start(bf16[528,384]{1,0:T(8,128)(2,1)S(1)} %pad_maximum_fusion.refs_1_), channel_id=1, source_target_pairs={{0,2},{1,3},{2,0},{3,1},{4,6},{5,7},{6,4},{7,5},{8,10},{9,11},{10,... | collective-permute-start | bytes 1216520 | tf_op jit(solution)/shard_map/ppermute | solution.py:206
  100.6 14.9 %copy-start.5 = (bf16[528,384]{1,0:T(8,128)(2,1)}, bf16[528,384]{1,0:T(8,128)(2,1)S(1)}, u32[]{:S(2)}) copy-start(bf16[528,384]{1,0:T(8,128)(2,1)S(1)} %collective-permute-done.2.refs_2_) | copy-start | bytes 1216516
  100.6 0.8 copy-start.6
  100.6 0.9 copy-start.7
  101.7 34.1 %copy-start.3 = (bf16[1056,384]{1,0:T(8,128)(2,1)}, bf16[1056,384]{1,0:T(8,128)(2,1)S(1)}, u32[]{:S(2)}) copy-start(bf16[1056,384]{1,0:T(8,128)(2,1)S(1)} %constant_dynamic-update-slice_fusion.refs_5_) | copy-start | bytes 2433028
  101.7 34.0 %collective-permute-start.7 = (bf16[1056,384]{1,0:T(8,128)(2,1)S(1)}, bf16[1056,384]{1,0:T(8,128)(2,1)S(1)}, u32[]{:S(2)}, u32[]{:S(2)}) collective-permute-start(bf16[1056,384]{1,0:T(8,128)(2,1)S(1)} %constant_dynamic-update-slice_fusion.refs_5_), channel_id=1, source_target_pairs={{0,1},{1,2},{2,3},{3,0},{4,5},{5,6},{6,7},{7,4},{8,9},{9,10},{10,1... | collective-permute-start | bytes 2433032 | tf_op jit(solution)/shard_map/ppermute | solution.py:206
  105.1 30.7 %collective-permute-start.8 = (bf16[1056,384]{1,0:T(8,128)(2,1)S(1)}, bf16[1056,384]{1,0:T(8,128)(2,1)}, u32[]{:S(2)}, u32[]{:S(2)}) collective-permute-start(bf16[1056,384]{1,0:T(8,128)(2,1)S(1)} %constant_dynamic-update-slice_fusion.refs_5_), channel_id=1, source_target_pairs={{0,3},{1,0},{2,1},{3,2},{4,7},{5,4},{6,5},{7,6},{8,11},{9,8},{10,9... | collective-permute-start | bytes 2433032 | tf_op jit(solution)/shard_map/ppermute | solution.py:206
  108.8 26.9 %collective-permute-start.5 = (bf16[272,384]{1,0:T(8,128)(2,1)S(1)}, bf16[272,384]{1,0:T(8,128)(2,1)S(1)}, u32[]{:S(2)}, u32[]{:S(2)}) collective-permute-start(bf16[272,384]{1,0:T(8,128)(2,1)S(1)} %slice.12), channel_id=1, source_target_pairs={{0,4},{1,5},{2,6},{3,7},{4,8},{5,9},{6,10},{7,11},{8,12},{9,13},{1... | collective-permute-start | bytes 626696 | tf_op jit(solution)/shard_map/ppermute | solution.py:209
  115.6 20.1 %collective-permute-start.6 = (bf16[256,384]{1,0:T(8,128)(2,1)S(1)}, bf16[256,384]{1,0:T(8,128)(2,1)S(1)}, u32[]{:S(2)}, u32[]{:S(2)}) collective-permute-start(bf16[256,384]{1,0:T(8,128)(2,1)S(1)} %slice.13), channel_id=1, source_target_pairs={{0,12},{1,13},{2,14},{3,15},{4,0},{5,1},{6,2},{7,3},{8,4},{9,5},{1... | collective-permute-start | bytes 589832 | tf_op jit(solution)/shard_map/ppermute | solution.py:209
  135.7 5.0 %copy-start.2 = (bf16[1056,384]{1,0:T(8,128)(2,1)}, bf16[1056,384]{1,0:T(8,128)(2,1)S(1)}, u32[]{:S(2)}) copy-start(bf16[1056,384]{1,0:T(8,128)(2,1)S(1)} %collective-permute-done.7.refs_6_) | copy-start | bytes 2433028
  137.1 33.7 %all-to-all-start.1 = ((bf16[4,528,384]{2,1,0:T(8,128)(2,1)}), bf16[4,528,384]{2,1,0:T(8,128)(2,1)S(1)}, u32[]{:S(2)}, u32[]{:S(2)}) async-start(bf16[4,528,384]{2,1,0:T(8,128)(2,1)} %broadcast_in_dim.58), calls=%async_computation.1 | async-start | bytes 3244032 | tf_op jit(solution)/shard_map/all_to_all | solution.py:231
  140.7 9.8 %copy-start.14 = (s32[12]{0:T(128)S(1)}, s32[12]{0:T(128)}, u32[]{:S(2)}) copy-start(s32[12]{0:T(128)} %constant.71.clone) | copy-start | bytes 148
  140.7 9.8 %copy-start.15 = (s32[16]{0:T(128)S(1)}, s32[16]{0:T(128)}, u32[]{:S(2)}) copy-start(s32[16]{0:T(128)} %constant.70.clone) | copy-start | bytes 196
  141.6 29.2 %collective-permute-start.9 = (bf16[528,384]{1,0:T(8,128)(2,1)}, bf16[528,384]{1,0:T(8,128)(2,1)S(1)}, u32[]{:S(2)}, u32[]{:S(2)}) collective-permute-start(bf16[528,384]{1,0:T(8,128)(2,1)} %slice.20), channel_id=1, source_target_pairs={{0,1},{1,2},{2,3},{3,0},{4,5},{5,6},{6,7},{7,4},{8,9},{9,10},{10,1... | collective-permute-start | bytes 1216520 | tf_op jit(solution)/shard_map/ppermute | solution.py:206
  146.5 24.3 %collective-permute-start.10 = (bf16[528,384]{1,0:T(8,128)(2,1)S(1)}, bf16[528,384]{1,0:T(8,128)(2,1)}, u32[]{:S(2)}, u32[]{:S(2)}) collective-permute-start(bf16[528,384]{1,0:T(8,128)(2,1)S(1)} %slice.21), channel_id=1, source_target_pairs={{0,3},{1,0},{2,1},{3,2},{4,7},{5,4},{6,5},{7,6},{8,11},{9,8},{10,9... | collective-permute-start | bytes 1216520 | tf_op jit(solution)/shard_map/ppermute | solution.py:206
  170.8 0.8 copy-start.8
  170.8 1.3 copy-start.1
Sparse Core Ops, SparseCore 0:
  21.3 66.3 all-gather.2
  100.8 59.0 all-gather.4

commit v11 on v9

--- a/solution.py
+++ b/solution.py
@@ -10,7 +10,6 @@
 HEAD_DIM = 128
 NORM_EPSILON = 1e-06
 Z_PARTS, Y_PARTS = 4, 4
-GAIN_ROWS = 16
 ROW_TILE = 16
 
 
@@ -86,11 +85,11 @@
 
 def project_attend_kernel(slots, count, rows, strip, *refs):
     places_ref, blocks = refs[0], refs[1 : 1 + count]
-    source_ref, seg_col_ref, seg_row_ref, out_ref = refs[1 + count : 5 + count]
-    block_ref, normed_ref, weight_ref, total_ref, sums_ref, sem, block_sem = refs[5 + count :]
+    source_ref, gain_ref, seg_col_ref, seg_row_ref, out_ref = refs[1 + count : 6 + count]
+    block_ref, normed_ref, weight_ref, total_ref, sums_ref, sem, block_sem = refs[6 + count :]
     width, features = block_ref.shape[2], normed_ref.shape[1]
     half = rows // 2
-    parts = [(rows, GAIN_ROWS)] + [(row, rows // 4) for row in range(0, rows, rows // 4)]
+    parts = [(row, rows // 4) for row in range(0, rows, rows // 4)]
     block_copies = []
     for k, (row, size) in enumerate(parts):
         block_copies.append(
@@ -108,14 +107,10 @@
             copy.start()
     weight_copies = load_weights(source_ref, weight_ref, sem, strip)
     columns = slot_columns(places_ref, len(slots), width)
-    for copy in block_copies[0]:
-        copy.wait()
-    gains = [
-        block_ref[j, pl.ds(rows, GAIN_ROWS), :][:1].astype(jnp.float32) for j in range(len(slots))
-    ]
+    gains = [gain_ref[pl.ds(places_ref[j], 1), :] for j in range(len(slots))]
 
     for k in range(2):
-        for copy in block_copies[1 + k]:
+        for copy in block_copies[k]:
             copy.wait()
 
         def first_step(i, carry):
@@ -124,7 +119,7 @@
 
         lax.fori_loop(0, rows // 4 // ROW_TILE, first_step, 0)
 
-    for copies in (block_copies[3], block_copies[4], weight_copies):
+    for copies in (block_copies[2], block_copies[3], weight_copies):
         for copy in copies:
             copy.wait()
     steps = half // (2 * ROW_TILE)
@@ -150,19 +145,25 @@
     for row in range(0, rows, span):
         low = min(max(row - (window - span) // 2, 0), rows - window)
         same = seg_col_ref[row : row + span, :1] == seg_row_ref[:1, low : low + window]
-        for col in range(0, local, HEAD_DIM):
-            query = sums_ref[row : row + span, col : col + HEAD_DIM]
-            key = sums_ref[low : low + window, local + col : local + col + HEAD_DIM]
+        heads = range(0, local, HEAD_DIM)
+        scores = [
+            lax.dot_general(
+                sums_ref[row : row + span, col : col + HEAD_DIM],
+                sums_ref[low : low + window, local + col : local + col + HEAD_DIM],
+                (((1,), (1,)), ((), ())),
+                preferred_element_type=jnp.float32,
+            )
+            * (1.0 / math.sqrt(HEAD_DIM))
+            for col in heads
+        ]
+        scores = [jnp.where(same, one, -jnp.inf) for one in scores]
+        tops = [jnp.max(one, axis=1, keepdims=True) for one in scores]
+        expos = [jnp.exp(one - top) for one, top in zip(scores, tops)]
+        shares = [1.0 / jnp.sum(expo, axis=1, keepdims=True) for expo in expos]
+        for col, expo, share in zip(heads, expos, shares):
             value = sums_ref[low : low + window, 2 * local + col : 2 * local + col + HEAD_DIM]
-            scores = lax.dot_general(
-                query, key, (((1,), (1,)), ((), ())), preferred_element_type=jnp.float32
-            ) * (1.0 / math.sqrt(HEAD_DIM))
-            scores = jnp.where(same, scores, -jnp.inf)
-            expo = jnp.exp(scores - jnp.max(scores, axis=1, keepdims=True))
-            share = 1.0 / jnp.sum(expo, axis=1, keepdims=True)
-            probs = (expo * share).astype(jnp.bfloat16)
             out_ref[row : row + span, col : col + HEAD_DIM] = jnp.dot(
-                probs, value, preferred_element_type=jnp.float32
+                (expo * share).astype(jnp.bfloat16), value, preferred_element_type=jnp.float32
             ).astype(jnp.bfloat16)
 
 
@@ -198,9 +199,10 @@
         mode="promise_in_bounds"
     )
 
-    own = jnp.concatenate([packed, jnp.broadcast_to(gain[None, :], (GAIN_ROWS, width))], axis=0)
-    all_rows = rows + GAIN_ROWS
-    cut = rows // 2 + GAIN_ROWS
+    own, cut = packed, rows // 2
+    features = width * Y_PARTS * Z_PARTS
+    all_gain = jnp.broadcast_to(gain[None, :], (features // width, width))
+    all_gain = lax.all_to_all(all_gain, "tensor", 0, 0, tiled=True)
 
     def along_y(block, step):
         return lax.ppermute(block, "tensor", y_shift(step))
@@ -208,21 +210,22 @@
     def along_z(block, step):
         return lax.ppermute(block, "tensor", z_shift(step))
 
-    z_up, z_down, own_up, own_down, own_far, weight = lax.optimization_barrier(
+    z_up, z_down, own_up, own_down, own_far, all_gain, weight = lax.optimization_barrier(
         (
             along_z(own, 1),
             along_z(own, -1),
             along_y(own, 1),
             along_y(own, -1),
             along_y(own, 2),
+            all_gain,
             weight,
         )
     )
     weight = lax.all_gather(weight, "dp", axis=0, tiled=True, axis_index_groups=dp_groups("xc"))
     pair = jnp.concatenate([z_up, z_down], axis=0)
     pair_up, pair_down = along_y(pair, 1), along_y(pair, -1)
-    pair_far_up = along_y(pair_up[:all_rows], 1)
-    pair_far_down = along_y(pair_down[all_rows:], -1)
+    pair_far_up = along_y(pair_up[:rows], 1)
+    pair_far_down = along_y(pair_down[rows:], -1)
     far_top, far_rest = along_z(z_up[:cut], 1), along_z(z_down[cut:], -1)
     far = jnp.concatenate([far_top, far_rest], axis=0)
     far_all = lax.all_to_all(
@@ -239,7 +242,7 @@
     def add(array, dy, *dzs):
         blocks.append(array)
         for k, dz in enumerate(dzs):
-            slots_at.append((len(blocks) - 1, k * all_rows))
+            slots_at.append((len(blocks) - 1, k * rows))
             shifts.append((dz, dy))
 
     add(own, 0, 0)
@@ -251,9 +254,9 @@
     add(pair_down, 1, -1, 1)
     add(pair_far_up, 2, -1)
     add(pair_far_down, 2, 1)
-    blocks.append(far_all.reshape(Y_PARTS * all_rows, width))
+    blocks.append(far_all.reshape(Y_PARTS * rows, width))
     for y in range(Y_PARTS):
-        slots_at.append((len(blocks) - 1, y * all_rows))
+        slots_at.append((len(blocks) - 1, y * rows))
     tensor = lax.axis_index("tensor")
     my_z, my_y = tensor // Y_PARTS, tensor % Y_PARTS
     step_z = jnp.array([dz for dz, _ in shifts] + [2] * Y_PARTS, jnp.int32)
@@ -264,25 +267,24 @@
     def kernel(*refs):
         project_attend_kernel(slots_at, len(blocks), rows, strip, *refs)
 
-    features = width * len(slots_at)
     vmem = pl.BlockSpec(memory_space=pltpu.VMEM)
     smem, hbm = pl.BlockSpec(memory_space=pltpu.SMEM), pl.BlockSpec(memory_space=pl.ANY)
     return pl.pallas_call(
         kernel,
         out_shape=jax.ShapeDtypeStruct((rows, local), jnp.bfloat16),
-        in_specs=[smem] + [hbm] * (len(blocks) + 1) + [vmem, vmem],
+        in_specs=[smem] + [hbm] * (len(blocks) + 1) + [vmem] * 3,
         out_specs=vmem,
         scratch_shapes=[
-            pltpu.VMEM((len(slots_at), all_rows, width), jnp.bfloat16),
+            pltpu.VMEM((len(slots_at), rows, width), jnp.bfloat16),
             pltpu.VMEM((rows, features), jnp.bfloat16),
             pltpu.VMEM((features, 3 * local), jnp.bfloat16),
             pltpu.VMEM((rows // 2, 3 * local), jnp.float32),
             pltpu.VMEM((rows, 3 * local), jnp.bfloat16),
             pltpu.SemaphoreType.DMA,
-            pltpu.SemaphoreType.DMA((5,)),
+            pltpu.SemaphoreType.DMA((4,)),
         ],
         name="norm_project_attend",
-    )(places, *blocks, weight, segment[:, None], segment[None, :])
+    )(places, *blocks, weight, all_gain.astype(jnp.float32), segment[:, None], segment[None, :])
 
 
 def solution(mesh):

time: 189 us -> 192 us (1.016)
  the two profiles are of different devices: /device:TPU:1 before, /device:TPU:60 now
where the time goes in v11:
time: 192 us; the launch traced here: 191 us
  starting transfers between devices  57.8 us (30%)
  blocking collectives  43.9 us (23%)
  waiting for transfers between devices  42.7 us (22%)
  Pallas kernels  16 us (8%)
  between operations  13.8 us (7%)
  local copies, waits for them, and re-layouts  12.8 us (7%)
  other arithmetic  4.59 us (2%)
    all_to_all x1, blocking collectives, shards(): all_gain = lax.all_to_all(all_gain, 'tensor', 0, 0, tiled=True)  43.9 us
    ppermute x7, waiting for transfers between devices, along_y(): return lax.ppermute(block, 'tensor', y_shift(step))  25.1 us
    ppermute x7, starting transfers between devices, along_y(): return lax.ppermute(block, 'tensor', y_shift(step))  21.9 us
    ppermute x4, starting transfers between devices, along_z(): return lax.ppermute(block, 'tensor', z_shift(step))  21.7 us
    all_to_all x1, waiting for transfers between devices, shards(): lax.all_to_all(outgoing, 'dp', split_axis=0, concat_axis=0, tiled=True)  16.3 us
    pallas_call x1, Pallas kernels, shards(): pl.pallas_call(kernel, out_shape=jax.ShapeDtypeStruct((rows, local), jnp....  16 us
    all_to_all x1, starting transfers between devices, shards(): lax.all_to_all(outgoing, 'dp', split_axis=0, concat_axis=0, tiled=True)  8.57 us
    all_to_all x1, starting transfers between devices, shards(): lax.all_to_all(jnp.broadcast_to(far[None], (Y_PARTS, *far.shape)), 'tenso...  5.53 us
  transfers between devices with their start and end apart: 15, of which 6 were waited for; matrix products, arithmetic and copies ran while one was open for 7% of the time, Pallas kernels for 0%

profile of v11, /device:TPU:60, one launch (start us, length us, event | category | flops | bytes accessed | tf_op | source)
XLA Modules:
  0.0 191.5 jit_solution(6562534663131773414)
XLA Ops:
  6.5 0.8 dynamic-slice_bitcast_fusion
  7.3 0.1 select_reduce_fusion.1
  7.4 0.2 copy-done
  7.7 1.6 gather_fusion
  9.2 8.6 %all-to-all-start = ((bf16[32,32,384]{2,1,0:T(8,128)(2,1)}), bf16[32,32,384]{2,1,0:T(8,128)(2,1)S(1)}, u32[]{:S(2)}, u32[]{:S(2)}) async-start(bf16[32,32,384]{2,1,0:T(8,128)(2,1)} %gather_fusion), calls=%async_computation | async-start | bytes 1572864 | tf_op jit(solution)/shard_map/all_to_all | solution.py:188
  17.8 0.0 all-gather.3.cloned.1.call-start
  17.9 0.7 pad_maximum_fusion.1
  18.7 0.0 all-gather.5.cloned.1.call-start
  18.7 0.7 fusion.7
  19.4 0.1 copy.17
  19.5 0.1 reduce-window.4
  19.6 0.1 reduce
  19.7 0.1 convert_reduce_fusion
  19.8 0.7 fusion.6
  20.5 0.1 select_reduce_fusion
  20.6 16.3 %all-to-all-done = bf16[32,32,384]{2,1,0:T(8,128)(2,1)S(1)} async-done(((bf16[32,32,384]{2,1,0:T(8,128)(2,1)}), bf16[32,32,384]{2,1,0:T(8,128)(2,1)S(1)}, u32[]{:S(2)}, u32[]{:S(2)}) %all-to-all-start) | async-done | bytes 786464 | tf_op jit(solution)/shard_map/all_to_all | solution.py:188
  36.9 1.9 %gather_fusion.1 = bf16[512,384]{1,0:T(8,128)(2,1)S(1)} fusion(bf16[1024,384]{1,0:T(8,128)(2,1)S(1)} %bitcast.25, s32[1024]{0:T(1024)S(1)} %pad_clamp_fusion), kind=kCustom, calls=%fused_computation.1 | custom fusion | bytes 788480 | tf_op jit(solution)/shard_map/gather | solution.py:198
  38.9 9.1 %collective-permute-start = (bf16[512,384]{1,0:T(8,128)(2,1)S(1)}, bf16[512,384]{1,0:T(8,128)(2,1)S(1)}, u32[]{:S(2)}, u32[]{:S(2)}) collective-permute-start(bf16[512,384]{1,0:T(8,128)(2,1)S(1)} %gather_fusion.1), channel_id=1, source_target_pairs={{0,4},{1,5},{2,6},{3,7},{4,8},{5,9},{6,10},{7,11},{8,12},{9,13},{1... | collective-permute-start | bytes 1179656 | tf_op jit(solution)/shard_map/ppermute | solution.py:211
  48.0 2.9 %collective-permute-start.1 = (bf16[512,384]{1,0:T(8,128)(2,1)S(1)}, bf16[512,384]{1,0:T(8,128)(2,1)S(1)}, u32[]{:S(2)}, u32[]{:S(2)}) collective-permute-start(bf16[512,384]{1,0:T(8,128)(2,1)S(1)} %gather_fusion.1), channel_id=1, source_target_pairs={{0,12},{1,13},{2,14},{3,15},{4,0},{5,1},{6,2},{7,3},{8,4},{9,5},{1... | collective-permute-start | bytes 1179656 | tf_op jit(solution)/shard_map/ppermute | solution.py:211
  50.8 2.1 %collective-permute-start.2 = (bf16[512,384]{1,0:T(8,128)(2,1)S(1)}, bf16[512,384]{1,0:T(8,128)(2,1)S(1)}, u32[]{:S(2)}, u32[]{:S(2)}) collective-permute-start(bf16[512,384]{1,0:T(8,128)(2,1)S(1)} %gather_fusion.1), channel_id=1, source_target_pairs={{0,1},{1,2},{2,3},{3,0},{4,5},{5,6},{6,7},{7,4},{8,9},{9,10},{10,1... | collective-permute-start | bytes 1179656 | tf_op jit(solution)/shard_map/ppermute | solution.py:208
  53.0 3.7 %collective-permute-start.3 = (bf16[512,384]{1,0:T(8,128)(2,1)S(1)}, bf16[512,384]{1,0:T(8,128)(2,1)S(1)}, u32[]{:S(2)}, u32[]{:S(2)}) collective-permute-start(bf16[512,384]{1,0:T(8,128)(2,1)S(1)} %gather_fusion.1), channel_id=1, source_target_pairs={{0,3},{1,0},{2,1},{3,2},{4,7},{5,4},{6,5},{7,6},{8,11},{9,8},{10,9... | collective-permute-start | bytes 1179656 | tf_op jit(solution)/shard_map/ppermute | solution.py:208
  56.7 3.1 %collective-permute-start.4 = (bf16[512,384]{1,0:T(8,128)(2,1)S(1)}, bf16[512,384]{1,0:T(8,128)(2,1)S(1)}, u32[]{:S(2)}, u32[]{:S(2)}) collective-permute-start(bf16[512,384]{1,0:T(8,128)(2,1)S(1)} %gather_fusion.1), channel_id=1, source_target_pairs={{0,2},{1,3},{2,0},{3,1},{4,6},{5,7},{6,4},{7,5},{8,10},{9,11},{10,... | collective-permute-start | bytes 1179656 | tf_op jit(solution)/shard_map/ppermute | solution.py:208
  59.9 0.5 broadcast.68
  60.4 0.7 reduce.2
  61.1 0.1 reshape.93
  61.2 43.9 %all_to_all.19 = bf16[16,2,192]{2,1,0:T(2,128)(2,1)S(1)} all-to-all(bf16[16,2,192]{2,1,0:T(2,128)(2,1)S(1)} %reshape.93), channel_id=1, replica_groups=mesh['dp'=32,'tensor'=16] {'tensor'}, dimensions={0} | all-to-all | bytes 24576 | tf_op jit(solution)/shard_map/all_to_all | solution.py:205
  105.0 0.1 reshape.94
  105.3 3.0 %collective-permute-start.10 = (bf16[256,384]{1,0:T(8,128)(2,1)S(1)}, bf16[256,384]{1,0:T(8,128)(2,1)S(1)}, u32[]{:S(2)}, u32[]{:S(2)}) collective-permute-start(bf16[256,384]{1,0:T(8,128)(2,1)S(1)} %slice.15), channel_id=1, source_target_pairs={{0,12},{1,13},{2,14},{3,15},{4,0},{5,1},{6,2},{7,3},{8,4},{9,5},{1... | collective-permute-start | bytes 589832 | tf_op jit(solution)/shard_map/ppermute | solution.py:211
  108.4 6.7 %collective-permute-start.9 = (bf16[256,384]{1,0:T(8,128)(2,1)S(1)}, bf16[256,384]{1,0:T(8,128)(2,1)S(1)}, u32[]{:S(2)}, u32[]{:S(2)}) collective-permute-start(bf16[256,384]{1,0:T(8,128)(2,1)S(1)} %slice.14), channel_id=1, source_target_pairs={{0,4},{1,5},{2,6},{3,7},{4,8},{5,9},{6,10},{7,11},{8,12},{9,13},{1... | collective-permute-start | bytes 589832 | tf_op jit(solution)/shard_map/ppermute | solution.py:211
  115.1 0.8 constant_dynamic-update-slice_fusion.1
  115.9 0.8 constant_dynamic-update-slice_fusion.refs_5_
  116.7 3.9 %collective-permute-start.5 = (bf16[1024,384]{1,0:T(8,128)(2,1)}, bf16[1024,384]{1,0:T(8,128)(2,1)S(1)}, u32[]{:S(2)}, u32[]{:S(2)}) collective-permute-start(bf16[1024,384]{1,0:T(8,128)(2,1)} %constant_dynamic-update-slice_fusion.refs_5_), channel_id=1, source_target_pairs={{0,1},{1,2},{2,3},{3,0},{4,5},{5,6},{6,7},{7,4},{8,9},{9,10},{10,1... | collective-permute-start | bytes 2359304 | tf_op jit(solution)/shard_map/ppermute | solution.py:208
  120.6 1.9 %collective-permute-start.6 = (bf16[1024,384]{1,0:T(8,128)(2,1)}, bf16[1024,384]{1,0:T(8,128)(2,1)}, u32[]{:S(2)}, u32[]{:S(2)}) collective-permute-start(bf16[1024,384]{1,0:T(8,128)(2,1)} %constant_dynamic-update-slice_fusion.refs_5_), channel_id=1, source_target_pairs={{0,3},{1,0},{2,1},{3,2},{4,7},{5,4},{6,5},{7,6},{8,11},{9,8},{10,9... | collective-permute-start | bytes 2359304 | tf_op jit(solution)/shard_map/ppermute | solution.py:208
  122.6 1.3 collective-permute-done.9
  123.9 1.3 broadcast_in_dim.58
  125.2 5.5 %all-to-all-start.2 = ((bf16[4,512,384]{2,1,0:T(8,128)(2,1)}), bf16[4,512,384]{2,1,0:T(8,128)(2,1)S(1)}, u32[]{:S(2)}, u32[]{:S(2)}) async-start(bf16[4,512,384]{2,1,0:T(8,128)(2,1)} %broadcast_in_dim.58), calls=%async_computation.2 | async-start | bytes 3145728 | tf_op jit(solution)/shard_map/all_to_all | solution.py:231
  130.7 8.5 %collective-permute-done.5.refs_6_ = bf16[1024,384]{1,0:T(8,128)(2,1)S(1)} collective-permute-done((bf16[1024,384]{1,0:T(8,128)(2,1)}, bf16[1024,384]{1,0:T(8,128)(2,1)S(1)}, u32[]{:S(2)}, u32[]{:S(2)}) %collective-permute-start.5) | collective-permute-done | bytes 786464 | tf_op jit(solution)/shard_map/ppermute | solution.py:208
  139.3 5.2 %collective-permute-start.7 = (bf16[512,384]{1,0:T(8,128)(2,1)S(1)}, bf16[512,384]{1,0:T(8,128)(2,1)}, u32[]{:S(2)}, u32[]{:S(2)}) collective-permute-start(bf16[512,384]{1,0:T(8,128)(2,1)S(1)} %slice.20), channel_id=1, source_target_pairs={{0,1},{1,2},{2,3},{3,0},{4,5},{5,6},{6,7},{7,4},{8,9},{9,10},{10,1... | collective-permute-start | bytes 1179656 | tf_op jit(solution)/shard_map/ppermute | solution.py:208
  144.5 0.1 collective-permute-done.6.refs_7_
  144.5 1.8 slice.21
  146.3 1.9 collective-permute-start.8
  148.3 0.9 copy.18.refs_13_
  149.1 1.3 fusion.refs_0_
  150.4 0.6 convert_element_type.7.refs_12_
  151.0 11.6 %collective-permute-done.7.refs_8_ = bf16[512,384]{1,0:T(8,128)(2,1)} collective-permute-done((bf16[512,384]{1,0:T(8,128)(2,1)S(1)}, bf16[512,384]{1,0:T(8,128)(2,1)}, u32[]{:S(2)}, u32[]{:S(2)}) %collective-permute-start.7) | collective-permute-done | bytes 393248 | tf_op jit(solution)/shard_map/ppermute | solution.py:208
  162.6 4.9 %collective-permute-done.8.refs_9_ = bf16[512,384]{1,0:T(8,128)(2,1)} collective-permute-done((bf16[512,384]{1,0:T(8,128)(2,1)}, bf16[512,384]{1,0:T(8,128)(2,1)}, u32[]{:S(2)}, u32[]{:S(2)}) %collective-permute-start.8) | collective-permute-done | bytes 393248 | tf_op jit(solution)/shard_map/ppermute | solution.py:208
  167.5 1.1 copy-done.1
  168.6 16.0 %norm_project_attend.1 = bf16[512,256]{1,0:T(8,128)(2,1)} custom-call(s32[16]{0:T(128)} %fusion.refs_0_, bf16[512,384]{1,0:T(8,128)(2,1)} %copy-done.3, bf16[512,384]{1,0:T(8,128)(2,1)} %copy-done.4, bf16[512,384]{1,0:T(8,128)(2,1)} %copy-done.5, bf16[512,384]{1,0:T(8,128)(2,1)} %copy-done.6, bf16[1024,384]{1,0:T(8,128)(2,1)} %constant_dynamic-update-slice_fusion.refs_5_, ...), custom_call_target="tpu_custom_call" | custom-call | tf_op jit(solution)/shard_map/norm_project_attend/pallas_call | solution.py:272
  (44 shorter events, 0.3 us)
Async XLA Ops:
  6.5 1.1 copy-start
  7.7 10.2 %copy-start.7 = (bf16[192,256]{1,0:T(8,128)(2,1)S(1)}, bf16[192,256]{1,0:T(8,128)(2,1)}, u32[]{:S(2)}) copy-start(bf16[192,256]{1,0:T(8,128)(2,1)} %param.13) | copy-start | bytes 294916
  7.7 10.2 %copy-start.8 = (bf16[192,256]{1,0:T(8,128)(2,1)S(1)}, bf16[192,256]{1,0:T(8,128)(2,1)}, u32[]{:S(2)}) copy-start(bf16[192,256]{1,0:T(8,128)(2,1)} %param.12) | copy-start | bytes 294916
  7.7 10.2 %copy-start.9 = (bf16[192,256]{1,0:T(8,128)(2,1)S(1)}, bf16[192,256]{1,0:T(8,128)(2,1)}, u32[]{:S(2)}) copy-start(bf16[192,256]{1,0:T(8,128)(2,1)} %param.11) | copy-start | bytes 294916
  9.2 27.7 %all-to-all-start = ((bf16[32,32,384]{2,1,0:T(8,128)(2,1)}), bf16[32,32,384]{2,1,0:T(8,128)(2,1)S(1)}, u32[]{:S(2)}, u32[]{:S(2)}) async-start(bf16[32,32,384]{2,1,0:T(8,128)(2,1)} %gather_fusion), calls=%async_computation | async-start | bytes 1572864 | tf_op jit(solution)/shard_map/all_to_all | solution.py:188
  17.8 87.3 %all-gather.3.cloned.1.call-start = ((), (), s32[]{:S(2)}) async-start(), calls=%async_computation.3 | async-start | bytes 1474560 | tf_op jit(solution)/shard_map/all_gather | solution.py:179
  18.7 148.8 %all-gather.5.cloned.1.call-start = ((), (), s32[]{:S(2)}) async-start(), calls=%async_computation.4 | async-start | bytes 10616832 | tf_op jit(solution)/shard_map/all_gather | solution.py:224
  19.8 128.5 %copy-start.10 = (s32[512]{0:T(512)}, s32[512]{0:T(512)S(1)}, u32[]{:S(2)}) copy-start(s32[512]{0:T(512)S(1)} %convert_reduce_fusion) | copy-start | bytes 6148
  36.9 22.9 %copy-start.11 = (bf16[384]{0:T(512)(128)(2,1)S(1)}, bf16[384]{0:T(512)(128)(2,1)}, u32[]{:S(2)}) copy-start(bf16[384]{0:T(512)(128)(2,1)} %param.10) | copy-start | bytes 2308
  38.8 77.8 %copy-start.3 = (bf16[512,384]{1,0:T(8,128)(2,1)}, bf16[512,384]{1,0:T(8,128)(2,1)S(1)}, u32[]{:S(2)}) copy-start(bf16[512,384]{1,0:T(8,128)(2,1)S(1)} %gather_fusion.1) | copy-start | bytes 1179652
  38.9 66.3 %collective-permute-start = (bf16[512,384]{1,0:T(8,128)(2,1)S(1)}, bf16[512,384]{1,0:T(8,128)(2,1)S(1)}, u32[]{:S(2)}, u32[]{:S(2)}) collective-permute-start(bf16[512,384]{1,0:T(8,128)(2,1)S(1)} %gather_fusion.1), channel_id=1, source_target_pairs={{0,4},{1,5},{2,6},{3,7},{4,8},{5,9},{6,10},{7,11},{8,12},{9,13},{1... | collective-permute-start | bytes 1179656 | tf_op jit(solution)/shard_map/ppermute | solution.py:211
  48.0 57.2 %collective-permute-start.1 = (bf16[512,384]{1,0:T(8,128)(2,1)S(1)}, bf16[512,384]{1,0:T(8,128)(2,1)S(1)}, u32[]{:S(2)}, u32[]{:S(2)}) collective-permute-start(bf16[512,384]{1,0:T(8,128)(2,1)S(1)} %gather_fusion.1), channel_id=1, source_target_pairs={{0,12},{1,13},{2,14},{3,15},{4,0},{5,1},{6,2},{7,3},{8,4},{9,5},{1... | collective-permute-start | bytes 1179656 | tf_op jit(solution)/shard_map/ppermute | solution.py:211
  50.8 54.4 %collective-permute-start.2 = (bf16[512,384]{1,0:T(8,128)(2,1)S(1)}, bf16[512,384]{1,0:T(8,128)(2,1)S(1)}, u32[]{:S(2)}, u32[]{:S(2)}) collective-permute-start(bf16[512,384]{1,0:T(8,128)(2,1)S(1)} %gather_fusion.1), channel_id=1, source_target_pairs={{0,1},{1,2},{2,3},{3,0},{4,5},{5,6},{6,7},{7,4},{8,9},{9,10},{10,1... | collective-permute-start | bytes 1179656 | tf_op jit(solution)/shard_map/ppermute | solution.py:208
  53.0 52.3 %collective-permute-start.3 = (bf16[512,384]{1,0:T(8,128)(2,1)S(1)}, bf16[512,384]{1,0:T(8,128)(2,1)S(1)}, u32[]{:S(2)}, u32[]{:S(2)}) collective-permute-start(bf16[512,384]{1,0:T(8,128)(2,1)S(1)} %gather_fusion.1), channel_id=1, source_target_pairs={{0,3},{1,0},{2,1},{3,2},{4,7},{5,4},{6,5},{7,6},{8,11},{9,8},{10,9... | collective-permute-start | bytes 1179656 | tf_op jit(solution)/shard_map/ppermute | solution.py:208
  56.7 48.6 %collective-permute-start.4 = (bf16[512,384]{1,0:T(8,128)(2,1)S(1)}, bf16[512,384]{1,0:T(8,128)(2,1)S(1)}, u32[]{:S(2)}, u32[]{:S(2)}) collective-permute-start(bf16[512,384]{1,0:T(8,128)(2,1)S(1)} %gather_fusion.1), channel_id=1, source_target_pairs={{0,2},{1,3},{2,0},{3,1},{4,6},{5,7},{6,4},{7,5},{8,10},{9,11},{10,... | collective-permute-start | bytes 1179656 | tf_op jit(solution)/shard_map/ppermute | solution.py:208
  105.2 11.5 %copy-start.4 = (bf16[512,384]{1,0:T(8,128)(2,1)}, bf16[512,384]{1,0:T(8,128)(2,1)S(1)}, u32[]{:S(2)}) copy-start(bf16[512,384]{1,0:T(8,128)(2,1)S(1)} %collective-permute-done.2.refs_2_) | copy-start | bytes 1179652
  105.2 11.5 %copy-start.5 = (bf16[512,384]{1,0:T(8,128)(2,1)}, bf16[512,384]{1,0:T(8,128)(2,1)S(1)}, u32[]{:S(2)}) copy-start(bf16[512,384]{1,0:T(8,128)(2,1)S(1)} %collective-permute-done.3.refs_3_) | copy-start | bytes 1179652
  105.3 10.7 %copy-start.6 = (bf16[512,384]{1,0:T(8,128)(2,1)}, bf16[512,384]{1,0:T(8,128)(2,1)S(1)}, u32[]{:S(2)}) copy-start(bf16[512,384]{1,0:T(8,128)(2,1)S(1)} %collective-permute-done.4.refs_4_) | copy-start | bytes 1179652
  105.3 17.3 %collective-permute-start.10 = (bf16[256,384]{1,0:T(8,128)(2,1)S(1)}, bf16[256,384]{1,0:T(8,128)(2,1)S(1)}, u32[]{:S(2)}, u32[]{:S(2)}) collective-permute-start(bf16[256,384]{1,0:T(8,128)(2,1)S(1)} %slice.15), channel_id=1, source_target_pairs={{0,12},{1,13},{2,14},{3,15},{4,0},{5,1},{6,2},{7,3},{8,4},{9,5},{1... | collective-permute-start | bytes 589832 | tf_op jit(solution)/shard_map/ppermute | solution.py:211
  108.4 15.5 %collective-permute-start.9 = (bf16[256,384]{1,0:T(8,128)(2,1)S(1)}, bf16[256,384]{1,0:T(8,128)(2,1)S(1)}, u32[]{:S(2)}, u32[]{:S(2)}) collective-permute-start(bf16[256,384]{1,0:T(8,128)(2,1)S(1)} %slice.14), channel_id=1, source_target_pairs={{0,4},{1,5},{2,6},{3,7},{4,8},{5,9},{6,10},{7,11},{8,12},{9,13},{1... | collective-permute-start | bytes 589832 | tf_op jit(solution)/shard_map/ppermute | solution.py:211
  116.7 22.6 %collective-permute-start.5 = (bf16[1024,384]{1,0:T(8,128)(2,1)}, bf16[1024,384]{1,0:T(8,128)(2,1)S(1)}, u32[]{:S(2)}, u32[]{:S(2)}) collective-permute-start(bf16[1024,384]{1,0:T(8,128)(2,1)} %constant_dynamic-update-slice_fusion.refs_5_), channel_id=1, source_target_pairs={{0,1},{1,2},{2,3},{3,0},{4,5},{5,6},{6,7},{7,4},{8,9},{9,10},{10,1... | collective-permute-start | bytes 2359304 | tf_op jit(solution)/shard_map/ppermute | solution.py:208
  120.6 23.9 %collective-permute-start.6 = (bf16[1024,384]{1,0:T(8,128)(2,1)}, bf16[1024,384]{1,0:T(8,128)(2,1)}, u32[]{:S(2)}, u32[]{:S(2)}) collective-permute-start(bf16[1024,384]{1,0:T(8,128)(2,1)} %constant_dynamic-update-slice_fusion.refs_5_), channel_id=1, source_target_pairs={{0,3},{1,0},{2,1},{3,2},{4,7},{5,4},{6,5},{7,6},{8,11},{9,8},{10,9... | collective-permute-start | bytes 2359304 | tf_op jit(solution)/shard_map/ppermute | solution.py:208
  125.2 42.3 %all-to-all-start.2 = ((bf16[4,512,384]{2,1,0:T(8,128)(2,1)}), bf16[4,512,384]{2,1,0:T(8,128)(2,1)S(1)}, u32[]{:S(2)}, u32[]{:S(2)}) async-start(bf16[4,512,384]{2,1,0:T(8,128)(2,1)} %broadcast_in_dim.58), calls=%async_computation.2 | async-start | bytes 3145728 | tf_op jit(solution)/shard_map/all_to_all | solution.py:231
  139.3 28.2 %copy-start.2 = (bf16[1024,384]{1,0:T(8,128)(2,1)}, bf16[1024,384]{1,0:T(8,128)(2,1)S(1)}, u32[]{:S(2)}) copy-start(bf16[1024,384]{1,0:T(8,128)(2,1)S(1)} %collective-permute-done.5.refs_6_) | copy-start | bytes 2359300
  139.3 23.3 %collective-permute-start.7 = (bf16[512,384]{1,0:T(8,128)(2,1)S(1)}, bf16[512,384]{1,0:T(8,128)(2,1)}, u32[]{:S(2)}, u32[]{:S(2)}) collective-permute-start(bf16[512,384]{1,0:T(8,128)(2,1)S(1)} %slice.20), channel_id=1, source_target_pairs={{0,1},{1,2},{2,3},{3,0},{4,5},{5,6},{6,7},{7,4},{8,9},{9,10},{10,1... | collective-permute-start | bytes 1179656 | tf_op jit(solution)/shard_map/ppermute | solution.py:208
  146.3 21.2 %collective-permute-start.8 = (bf16[512,384]{1,0:T(8,128)(2,1)}, bf16[512,384]{1,0:T(8,128)(2,1)}, u32[]{:S(2)}, u32[]{:S(2)}) collective-permute-start(bf16[512,384]{1,0:T(8,128)(2,1)} %slice.21), channel_id=1, source_target_pairs={{0,3},{1,0},{2,1},{3,2},{4,7},{5,4},{6,5},{7,6},{8,11},{9,8},{10,9... | collective-permute-start | bytes 1179656 | tf_op jit(solution)/shard_map/ppermute | solution.py:208
  167.5 1.1 copy-start.1
Sparse Core Ops, SparseCore 0:
  20.8 66.1 all-gather.2
  105.4 53.8 all-gather.4

commit v12 on v9

--- a/solution.py
+++ b/solution.py
@@ -150,19 +150,25 @@
     for row in range(0, rows, span):
         low = min(max(row - (window - span) // 2, 0), rows - window)
         same = seg_col_ref[row : row + span, :1] == seg_row_ref[:1, low : low + window]
-        for col in range(0, local, HEAD_DIM):
-            query = sums_ref[row : row + span, col : col + HEAD_DIM]
-            key = sums_ref[low : low + window, local + col : local + col + HEAD_DIM]
+        heads = range(0, local, HEAD_DIM)
+        scores = [
+            lax.dot_general(
+                sums_ref[row : row + span, col : col + HEAD_DIM],
+                sums_ref[low : low + window, local + col : local + col + HEAD_DIM],
+                (((1,), (1,)), ((), ())),
+                preferred_element_type=jnp.float32,
+            )
+            * (1.0 / math.sqrt(HEAD_DIM))
+            for col in heads
+        ]
+        scores = [jnp.where(same, one, -jnp.inf) for one in scores]
+        tops = [jnp.max(one, axis=1, keepdims=True) for one in scores]
+        expos = [jnp.exp(one - top) for one, top in zip(scores, tops)]
+        shares = [1.0 / jnp.sum(expo, axis=1, keepdims=True) for expo in expos]
+        for col, expo, share in zip(heads, expos, shares):
             value = sums_ref[low : low + window, 2 * local + col : 2 * local + col + HEAD_DIM]
-            scores = lax.dot_general(
-                query, key, (((1,), (1,)), ((), ())), preferred_element_type=jnp.float32
-            ) * (1.0 / math.sqrt(HEAD_DIM))
-            scores = jnp.where(same, scores, -jnp.inf)
-            expo = jnp.exp(scores - jnp.max(scores, axis=1, keepdims=True))
-            share = 1.0 / jnp.sum(expo, axis=1, keepdims=True)
-            probs = (expo * share).astype(jnp.bfloat16)
             out_ref[row : row + span, col : col + HEAD_DIM] = jnp.dot(
-                probs, value, preferred_element_type=jnp.float32
+                (expo * share).astype(jnp.bfloat16), value, preferred_element_type=jnp.float32
             ).astype(jnp.bfloat16)
 
 

time: 189 us -> 188 us (level)
  no operation moved by 1% of the time
where the time goes in v12:
time: 188 us; the launch traced here: 186 us
  waiting for transfers between devices  80.6 us (43%)
  starting transfers between devices  60.6 us (32%)
  Pallas kernels  16.1 us (9%)
  between operations  13.7 us (7%)
  local copies, waits for them, and re-layouts  11.8 us (6%)
  other arithmetic  2.72 us (1%)
    all_gather x2, waiting for transfers between devices, shards(): lax.all_gather(weight, 'dp', axis=0, tiled=True, axis_index_groups=dp_gro...  36.8 us
    ppermute x4, starting transfers between devices, along_z(): return lax.ppermute(block, 'tensor', z_shift(step))  23.1 us
    ppermute x7, starting transfers between devices, along_y(): return lax.ppermute(block, 'tensor', y_shift(step))  23.1 us
    ppermute x7, waiting for transfers between devices, along_y(): return lax.ppermute(block, 'tensor', y_shift(step))  19.9 us
    all_to_all x1, waiting for transfers between devices, shards(): lax.all_to_all(outgoing, 'dp', split_axis=0, concat_axis=0, tiled=True)  19.7 us
    pallas_call x1, Pallas kernels, shards(): pl.pallas_call(kernel, out_shape=jax.ShapeDtypeStruct((rows, local), jnp....  16.1 us
    all_to_all x1, starting transfers between devices, shards(): lax.all_to_all(outgoing, 'dp', split_axis=0, concat_axis=0, tiled=True)  10.4 us
    ppermute x4, waiting for transfers between devices, along_z(): return lax.ppermute(block, 'tensor', z_shift(step))  4.2 us
  transfers between devices with their start and end apart: 15, of which 8 were waited for; matrix products, arithmetic and copies ran while one was open for 6% of the time, Pallas kernels for 0%

profile of v12, /device:TPU:1, one launch (start us, length us, event | category | flops | bytes accessed | tf_op | source)
XLA Modules:
  0.0 185.5 jit_solution(5242962873996611532)
XLA Ops:
  6.5 0.8 dynamic-slice_bitcast_fusion
  7.3 0.1 select_reduce_fusion.1
  7.5 0.2 copy-done
  7.7 1.5 gather_fusion
  9.2 10.4 %all-to-all-start = ((bf16[32,32,384]{2,1,0:T(8,128)(2,1)}), bf16[32,32,384]{2,1,0:T(8,128)(2,1)S(1)}, u32[]{:S(2)}, u32[]{:S(2)}) async-start(bf16[32,32,384]{2,1,0:T(8,128)(2,1)} %gather_fusion), calls=%async_computation | async-start | bytes 1572864 | tf_op jit(solution)/shard_map/all_to_all | solution.py:193
  19.7 0.0 all-gather.3.cloned.1.call-start
  19.7 0.7 pad_maximum_fusion.2
  20.5 0.0 all-gather.3.cloned.1.call-update
  20.5 0.0 all-gather.5.cloned.1.call-start
  20.6 0.7 fusion.7
  21.3 0.1 copy.13
  21.4 0.1 reduce-window.4
  21.4 0.1 reduce
  21.5 0.1 convert_reduce_fusion
  21.6 0.7 fusion.6
  22.3 0.1 select_reduce_fusion
  22.4 19.7 %all-to-all-done = bf16[32,32,384]{2,1,0:T(8,128)(2,1)S(1)} async-done(((bf16[32,32,384]{2,1,0:T(8,128)(2,1)}), bf16[32,32,384]{2,1,0:T(8,128)(2,1)S(1)}, u32[]{:S(2)}, u32[]{:S(2)}) %all-to-all-start) | async-done | bytes 786464 | tf_op jit(solution)/shard_map/all_to_all | solution.py:193
  42.1 1.9 %gather_fusion.1 = bf16[512,384]{1,0:T(8,128)(2,1)S(1)} fusion(bf16[1024,384]{1,0:T(8,128)(2,1)S(1)} %bitcast.22, s32[1024]{0:T(1024)S(1)} %pad_clamp_fusion), kind=kCustom, calls=%fused_computation.1 | custom fusion | bytes 788480 | tf_op jit(solution)/shard_map/gather | solution.py:203
  44.1 8.3 %collective-permute-start = (bf16[528,384]{1,0:T(8,128)(2,1)S(1)}, bf16[528,384]{1,0:T(8,128)(2,1)S(1)}, u32[]{:S(2)}, u32[]{:S(2)}) collective-permute-start(bf16[528,384]{1,0:T(8,128)(2,1)S(1)} %pad_maximum_fusion.refs_1_), channel_id=1, source_target_pairs={{0,4},{1,5},{2,6},{3,7},{4,8},{5,9},{6,10},{7,11},{8,12},{9,13},{1... | collective-permute-start | bytes 1216520 | tf_op jit(solution)/shard_map/ppermute | solution.py:215
  52.4 2.9 %collective-permute-start.1 = (bf16[528,384]{1,0:T(8,128)(2,1)S(1)}, bf16[528,384]{1,0:T(8,128)(2,1)S(1)}, u32[]{:S(2)}, u32[]{:S(2)}) collective-permute-start(bf16[528,384]{1,0:T(8,128)(2,1)S(1)} %pad_maximum_fusion.refs_1_), channel_id=1, source_target_pairs={{0,12},{1,13},{2,14},{3,15},{4,0},{5,1},{6,2},{7,3},{8,4},{9,5},{1... | collective-permute-start | bytes 1216520 | tf_op jit(solution)/shard_map/ppermute | solution.py:215
  55.3 3.2 %collective-permute-start.2 = (bf16[528,384]{1,0:T(8,128)(2,1)S(1)}, bf16[528,384]{1,0:T(8,128)(2,1)S(1)}, u32[]{:S(2)}, u32[]{:S(2)}) collective-permute-start(bf16[528,384]{1,0:T(8,128)(2,1)S(1)} %pad_maximum_fusion.refs_1_), channel_id=1, source_target_pairs={{0,1},{1,2},{2,3},{3,0},{4,5},{5,6},{6,7},{7,4},{8,9},{9,10},{10,1... | collective-permute-start | bytes 1216520 | tf_op jit(solution)/shard_map/ppermute | solution.py:212
  58.5 3.4 %collective-permute-start.3 = (bf16[528,384]{1,0:T(8,128)(2,1)S(1)}, bf16[528,384]{1,0:T(8,128)(2,1)S(1)}, u32[]{:S(2)}, u32[]{:S(2)}) collective-permute-start(bf16[528,384]{1,0:T(8,128)(2,1)S(1)} %pad_maximum_fusion.refs_1_), channel_id=1, source_target_pairs={{0,3},{1,0},{2,1},{3,2},{4,7},{5,4},{6,5},{7,6},{8,11},{9,8},{10,9... | collective-permute-start | bytes 1216520 | tf_op jit(solution)/shard_map/ppermute | solution.py:212
  61.9 3.5 %collective-permute-start.4 = (bf16[528,384]{1,0:T(8,128)(2,1)S(1)}, bf16[528,384]{1,0:T(8,128)(2,1)S(1)}, u32[]{:S(2)}, u32[]{:S(2)}) collective-permute-start(bf16[528,384]{1,0:T(8,128)(2,1)S(1)} %pad_maximum_fusion.refs_1_), channel_id=1, source_target_pairs={{0,2},{1,3},{2,0},{3,1},{4,6},{5,7},{6,4},{7,5},{8,10},{9,11},{10,... | collective-permute-start | bytes 1216520 | tf_op jit(solution)/shard_map/ppermute | solution.py:212
  65.4 20.8 %all-gather.3.cloned.1.call-done = bf16[768,768]{1,0:T(8,128)(2,1)} async-done(((bf16[192,768]{1,0:T(8,128)(2,1)}), bf16[768,768]{1,0:T(8,128)(2,1)}) %all-gather.3.cloned.1.call-update) | async-done | bytes 1179664 | tf_op jit(solution)/shard_map/all_gather | solution.py:184
  86.2 1.8 collective-permute-done
  88.0 0.0 collective-permute-done.1
  88.0 0.0 collective-permute-done.2.refs_2_
  88.1 0.0 all-gather.5.cloned.1.call-update
  88.1 10.1 %collective-permute-start.10 = (bf16[256,384]{1,0:T(8,128)(2,1)S(1)}, bf16[256,384]{1,0:T(8,128)(2,1)S(1)}, u32[]{:S(2)}, u32[]{:S(2)}) collective-permute-start(bf16[256,384]{1,0:T(8,128)(2,1)S(1)} %slice.15), channel_id=1, source_target_pairs={{0,12},{1,13},{2,14},{3,15},{4,0},{5,1},{6,2},{7,3},{8,4},{9,5},{1... | collective-permute-start | bytes 589832 | tf_op jit(solution)/shard_map/ppermute | solution.py:215
  98.3 1.9 %collective-permute-start.9 = (bf16[272,384]{1,0:T(8,128)(2,1)S(1)}, bf16[272,384]{1,0:T(8,128)(2,1)S(1)}, u32[]{:S(2)}, u32[]{:S(2)}) collective-permute-start(bf16[272,384]{1,0:T(8,128)(2,1)S(1)} %slice.14), channel_id=1, source_target_pairs={{0,4},{1,5},{2,6},{3,7},{4,8},{5,9},{6,10},{7,11},{8,12},{9,13},{1... | collective-permute-start | bytes 626696 | tf_op jit(solution)/shard_map/ppermute | solution.py:215
  100.2 0.8 constant_dynamic-update-slice_fusion.1
  101.0 0.8 constant_dynamic-update-slice_fusion.refs_5_
  101.8 3.1 %collective-permute-start.5 = (bf16[1056,384]{1,0:T(8,128)(2,1)}, bf16[1056,384]{1,0:T(8,128)(2,1)S(1)}, u32[]{:S(2)}, u32[]{:S(2)}) collective-permute-start(bf16[1056,384]{1,0:T(8,128)(2,1)} %constant_dynamic-update-slice_fusion.refs_5_), channel_id=1, source_target_pairs={{0,1},{1,2},{2,3},{3,0},{4,5},{5,6},{6,7},{7,4},{8,9},{9,10},{10,1... | collective-permute-start | bytes 2433032 | tf_op jit(solution)/shard_map/ppermute | solution.py:212
  104.9 3.4 %collective-permute-start.6 = (bf16[1056,384]{1,0:T(8,128)(2,1)}, bf16[1056,384]{1,0:T(8,128)(2,1)}, u32[]{:S(2)}, u32[]{:S(2)}) collective-permute-start(bf16[1056,384]{1,0:T(8,128)(2,1)} %constant_dynamic-update-slice_fusion.refs_5_), channel_id=1, source_target_pairs={{0,3},{1,0},{2,1},{3,2},{4,7},{5,4},{6,5},{7,6},{8,11},{9,8},{10,9... | collective-permute-start | bytes 2433032 | tf_op jit(solution)/shard_map/ppermute | solution.py:212
  108.3 2.4 %collective-permute-done.9 = bf16[272,384]{1,0:T(8,128)(2,1)S(1)} collective-permute-done((bf16[272,384]{1,0:T(8,128)(2,1)S(1)}, bf16[272,384]{1,0:T(8,128)(2,1)S(1)}, u32[]{:S(2)}, u32[]{:S(2)}) %collective-permute-start.9) | collective-permute-done | bytes 208928 | tf_op jit(solution)/shard_map/ppermute | solution.py:215
  110.7 1.3 broadcast_in_dim.58
  112.0 3.9 %all-to-all-start.1 = ((bf16[4,528,384]{2,1,0:T(8,128)(2,1)}), bf16[4,528,384]{2,1,0:T(8,128)(2,1)S(1)}, u32[]{:S(2)}, u32[]{:S(2)}) async-start(bf16[4,528,384]{2,1,0:T(8,128)(2,1)} %broadcast_in_dim.58), calls=%async_computation.1 | async-start | bytes 3244032 | tf_op jit(solution)/shard_map/all_to_all | solution.py:234
  115.9 2.9 %collective-permute-done.5.refs_6_ = bf16[1056,384]{1,0:T(8,128)(2,1)S(1)} collective-permute-done((bf16[1056,384]{1,0:T(8,128)(2,1)}, bf16[1056,384]{1,0:T(8,128)(2,1)S(1)}, u32[]{:S(2)}, u32[]{:S(2)}) %collective-permute-start.5) | collective-permute-done | bytes 811040 | tf_op jit(solution)/shard_map/ppermute | solution.py:212
  118.8 0.9 slice.20
  119.6 2.0 %collective-permute-start.7 = (bf16[528,384]{1,0:T(8,128)(2,1)}, bf16[528,384]{1,0:T(8,128)(2,1)}, u32[]{:S(2)}, u32[]{:S(2)}) collective-permute-start(bf16[528,384]{1,0:T(8,128)(2,1)} %slice.20), channel_id=1, source_target_pairs={{0,1},{1,2},{2,3},{3,0},{4,5},{5,6},{6,7},{7,4},{8,9},{9,10},{10,1... | collective-permute-start | bytes 1216520 | tf_op jit(solution)/shard_map/ppermute | solution.py:212
  121.7 1.8 slice.21
  123.5 4.5 %collective-permute-start.8 = (bf16[528,384]{1,0:T(8,128)(2,1)}, bf16[528,384]{1,0:T(8,128)(2,1)}, u32[]{:S(2)}, u32[]{:S(2)}) collective-permute-start(bf16[528,384]{1,0:T(8,128)(2,1)} %slice.21), channel_id=1, source_target_pairs={{0,3},{1,0},{2,1},{3,2},{4,7},{5,4},{6,5},{7,6},{8,11},{9,8},{10,9... | collective-permute-start | bytes 1216520 | tf_op jit(solution)/shard_map/ppermute | solution.py:212
  128.0 0.9 copy.14.refs_12_
  128.9 0.7 fusion.refs_0_
  129.5 16.6 %collective-permute-done.7.refs_8_ = bf16[528,384]{1,0:T(8,128)(2,1)} collective-permute-done((bf16[528,384]{1,0:T(8,128)(2,1)}, bf16[528,384]{1,0:T(8,128)(2,1)}, u32[]{:S(2)}, u32[]{:S(2)}) %collective-permute-start.7) | collective-permute-done | bytes 405536 | tf_op jit(solution)/shard_map/ppermute | solution.py:212
  146.2 0.4 collective-permute-done.8.refs_9_
  146.6 16.0 %all-gather.5.cloned.1.call-done.refs_11_ = bf16[6144,768]{1,0:T(8,128)(2,1)} async-done(((bf16[768,768]{1,0:T(8,128)(2,1)}), bf16[6144,768]{1,0:T(8,128)(2,1)}) %all-gather.5.cloned.1.call-update) | async-done | bytes 9437200 | tf_op jit(solution)/shard_map/all_gather | solution.py:227
  162.6 16.1 %norm_project_attend.1 = bf16[512,256]{1,0:T(8,128)(2,1)} custom-call(s32[16]{0:T(128)} %fusion.refs_0_, bf16[528,384]{1,0:T(8,128)(2,1)} %copy-done.3, bf16[528,384]{1,0:T(8,128)(2,1)} %copy-done.4, bf16[528,384]{1,0:T(8,128)(2,1)} %copy-done.5, bf16[528,384]{1,0:T(8,128)(2,1)} %copy-done.6, bf16[1056,384]{1,0:T(8,128)(2,1)} %constant_dynamic-update-slice_fusion.refs_5_, ...), custom_call_target="tpu_custom_call" | custom-call | tf_op jit(solution)/shard_map/norm_project_attend/pallas_call | solution.py:276
  (42 shorter events, 0.2 us)
Async XLA Ops:
  6.5 1.1 copy-start
  6.5 13.2 %copy-start.7 = (bf16[192,256]{1,0:T(8,128)(2,1)S(1)}, bf16[192,256]{1,0:T(8,128)(2,1)}, u32[]{:S(2)}) copy-start(bf16[192,256]{1,0:T(8,128)(2,1)} %param.13) | copy-start | bytes 294916
  6.5 13.2 %copy-start.8 = (bf16[192,256]{1,0:T(8,128)(2,1)S(1)}, bf16[192,256]{1,0:T(8,128)(2,1)}, u32[]{:S(2)}) copy-start(bf16[192,256]{1,0:T(8,128)(2,1)} %param.12) | copy-start | bytes 294916
  6.5 13.2 %copy-start.9 = (bf16[192,256]{1,0:T(8,128)(2,1)S(1)}, bf16[192,256]{1,0:T(8,128)(2,1)}, u32[]{:S(2)}) copy-start(bf16[192,256]{1,0:T(8,128)(2,1)} %param.11) | copy-start | bytes 294916
  9.2 32.9 %all-to-all-start = ((bf16[32,32,384]{2,1,0:T(8,128)(2,1)}), bf16[32,32,384]{2,1,0:T(8,128)(2,1)S(1)}, u32[]{:S(2)}, u32[]{:S(2)}) async-start(bf16[32,32,384]{2,1,0:T(8,128)(2,1)} %gather_fusion), calls=%async_computation | async-start | bytes 1572864 | tf_op jit(solution)/shard_map/all_to_all | solution.py:193
  19.7 66.6 %all-gather.3.cloned.1.call-start = ((), (), s32[]{:S(2)}) async-start(), calls=%async_computation.2 | async-start | bytes 1474560 | tf_op jit(solution)/shard_map/all_gather | solution.py:184
  20.5 142.1 %all-gather.5.cloned.1.call-start = ((), (), s32[]{:S(2)}) async-start(), calls=%async_computation.3 | async-start | bytes 10616832 | tf_op jit(solution)/shard_map/all_gather | solution.py:227
  21.6 106.4 %copy-start.10 = (s32[512]{0:T(512)}, s32[512]{0:T(512)S(1)}, u32[]{:S(2)}) copy-start(s32[512]{0:T(512)S(1)} %convert_reduce_fusion) | copy-start | bytes 6148
  42.1 1.9 %copy-start.11 = (bf16[384]{0:T(512)(128)(2,1)S(1)}, bf16[384]{0:T(512)(128)(2,1)}, u32[]{:S(2)}) copy-start(bf16[384]{0:T(512)(128)(2,1)} %param.10) | copy-start | bytes 2308
  44.1 57.7 %copy-start.3 = (bf16[528,384]{1,0:T(8,128)(2,1)}, bf16[528,384]{1,0:T(8,128)(2,1)S(1)}, u32[]{:S(2)}) copy-start(bf16[528,384]{1,0:T(8,128)(2,1)S(1)} %pad_maximum_fusion.refs_1_) | copy-start | bytes 1216516
  44.1 43.9 %collective-permute-start = (bf16[528,384]{1,0:T(8,128)(2,1)S(1)}, bf16[528,384]{1,0:T(8,128)(2,1)S(1)}, u32[]{:S(2)}, u32[]{:S(2)}) collective-permute-start(bf16[528,384]{1,0:T(8,128)(2,1)S(1)} %pad_maximum_fusion.refs_1_), channel_id=1, source_target_pairs={{0,4},{1,5},{2,6},{3,7},{4,8},{5,9},{6,10},{7,11},{8,12},{9,13},{1... | collective-permute-start | bytes 1216520 | tf_op jit(solution)/shard_map/ppermute | solution.py:215
  52.4 35.6 %collective-permute-start.1 = (bf16[528,384]{1,0:T(8,128)(2,1)S(1)}, bf16[528,384]{1,0:T(8,128)(2,1)S(1)}, u32[]{:S(2)}, u32[]{:S(2)}) collective-permute-start(bf16[528,384]{1,0:T(8,128)(2,1)S(1)} %pad_maximum_fusion.refs_1_), channel_id=1, source_target_pairs={{0,12},{1,13},{2,14},{3,15},{4,0},{5,1},{6,2},{7,3},{8,4},{9,5},{1... | collective-permute-start | bytes 1216520 | tf_op jit(solution)/shard_map/ppermute | solution.py:215
  55.3 32.7 %collective-permute-start.2 = (bf16[528,384]{1,0:T(8,128)(2,1)S(1)}, bf16[528,384]{1,0:T(8,128)(2,1)S(1)}, u32[]{:S(2)}, u32[]{:S(2)}) collective-permute-start(bf16[528,384]{1,0:T(8,128)(2,1)S(1)} %pad_maximum_fusion.refs_1_), channel_id=1, source_target_pairs={{0,1},{1,2},{2,3},{3,0},{4,5},{5,6},{6,7},{7,4},{8,9},{9,10},{10,1... | collective-permute-start | bytes 1216520 | tf_op jit(solution)/shard_map/ppermute | solution.py:212
  58.5 29.5 %collective-permute-start.3 = (bf16[528,384]{1,0:T(8,128)(2,1)S(1)}, bf16[528,384]{1,0:T(8,128)(2,1)S(1)}, u32[]{:S(2)}, u32[]{:S(2)}) collective-permute-start(bf16[528,384]{1,0:T(8,128)(2,1)S(1)} %pad_maximum_fusion.refs_1_), channel_id=1, source_target_pairs={{0,3},{1,0},{2,1},{3,2},{4,7},{5,4},{6,5},{7,6},{8,11},{9,8},{10,9... | collective-permute-start | bytes 1216520 | tf_op jit(solution)/shard_map/ppermute | solution.py:212
  61.9 26.2 %collective-permute-start.4 = (bf16[528,384]{1,0:T(8,128)(2,1)S(1)}, bf16[528,384]{1,0:T(8,128)(2,1)S(1)}, u32[]{:S(2)}, u32[]{:S(2)}) collective-permute-start(bf16[528,384]{1,0:T(8,128)(2,1)S(1)} %pad_maximum_fusion.refs_1_), channel_id=1, source_target_pairs={{0,2},{1,3},{2,0},{3,1},{4,6},{5,7},{6,4},{7,5},{8,10},{9,11},{10,... | collective-permute-start | bytes 1216520 | tf_op jit(solution)/shard_map/ppermute | solution.py:212
  88.0 13.8 %copy-start.4 = (bf16[528,384]{1,0:T(8,128)(2,1)}, bf16[528,384]{1,0:T(8,128)(2,1)S(1)}, u32[]{:S(2)}) copy-start(bf16[528,384]{1,0:T(8,128)(2,1)S(1)} %collective-permute-done.2.refs_2_) | copy-start | bytes 1216516
  88.1 12.9 %copy-start.5 = (bf16[528,384]{1,0:T(8,128)(2,1)}, bf16[528,384]{1,0:T(8,128)(2,1)S(1)}, u32[]{:S(2)}) copy-start(bf16[528,384]{1,0:T(8,128)(2,1)S(1)} %collective-permute-done.3.refs_3_) | copy-start | bytes 1216516
  88.1 12.9 %copy-start.6 = (bf16[528,384]{1,0:T(8,128)(2,1)}, bf16[528,384]{1,0:T(8,128)(2,1)S(1)}, u32[]{:S(2)}) copy-start(bf16[528,384]{1,0:T(8,128)(2,1)S(1)} %collective-permute-done.4.refs_4_) | copy-start | bytes 1216516
  88.1 20.2 %collective-permute-start.10 = (bf16[256,384]{1,0:T(8,128)(2,1)S(1)}, bf16[256,384]{1,0:T(8,128)(2,1)S(1)}, u32[]{:S(2)}, u32[]{:S(2)}) collective-permute-start(bf16[256,384]{1,0:T(8,128)(2,1)S(1)} %slice.15), channel_id=1, source_target_pairs={{0,12},{1,13},{2,14},{3,15},{4,0},{5,1},{6,2},{7,3},{8,4},{9,5},{1... | collective-permute-start | bytes 589832 | tf_op jit(solution)/shard_map/ppermute | solution.py:215
  98.3 12.4 %collective-permute-start.9 = (bf16[272,384]{1,0:T(8,128)(2,1)S(1)}, bf16[272,384]{1,0:T(8,128)(2,1)S(1)}, u32[]{:S(2)}, u32[]{:S(2)}) collective-permute-start(bf16[272,384]{1,0:T(8,128)(2,1)S(1)} %slice.14), channel_id=1, source_target_pairs={{0,4},{1,5},{2,6},{3,7},{4,8},{5,9},{6,10},{7,11},{8,12},{9,13},{1... | collective-permute-start | bytes 626696 | tf_op jit(solution)/shard_map/ppermute | solution.py:215
  101.8 17.0 %collective-permute-start.5 = (bf16[1056,384]{1,0:T(8,128)(2,1)}, bf16[1056,384]{1,0:T(8,128)(2,1)S(1)}, u32[]{:S(2)}, u32[]{:S(2)}) collective-permute-start(bf16[1056,384]{1,0:T(8,128)(2,1)} %constant_dynamic-update-slice_fusion.refs_5_), channel_id=1, source_target_pairs={{0,1},{1,2},{2,3},{3,0},{4,5},{5,6},{6,7},{7,4},{8,9},{9,10},{10,1... | collective-permute-start | bytes 2433032 | tf_op jit(solution)/shard_map/ppermute | solution.py:212
  104.9 16.7 %collective-permute-start.6 = (bf16[1056,384]{1,0:T(8,128)(2,1)}, bf16[1056,384]{1,0:T(8,128)(2,1)}, u32[]{:S(2)}, u32[]{:S(2)}) collective-permute-start(bf16[1056,384]{1,0:T(8,128)(2,1)} %constant_dynamic-update-slice_fusion.refs_5_), channel_id=1, source_target_pairs={{0,3},{1,0},{2,1},{3,2},{4,7},{5,4},{6,5},{7,6},{8,11},{9,8},{10,9... | collective-permute-start | bytes 2433032 | tf_op jit(solution)/shard_map/ppermute | solution.py:212
  112.0 34.6 %all-to-all-start.1 = ((bf16[4,528,384]{2,1,0:T(8,128)(2,1)}), bf16[4,528,384]{2,1,0:T(8,128)(2,1)S(1)}, u32[]{:S(2)}, u32[]{:S(2)}) async-start(bf16[4,528,384]{2,1,0:T(8,128)(2,1)} %broadcast_in_dim.58), calls=%async_computation.1 | async-start | bytes 3244032 | tf_op jit(solution)/shard_map/all_to_all | solution.py:234
  115.9 12.9 %copy-start.12 = (s32[12]{0:T(128)S(1)}, s32[12]{0:T(128)}, u32[]{:S(2)}) copy-start(s32[12]{0:T(128)} %constant.71.clone) | copy-start | bytes 148
  115.9 12.9 %copy-start.13 = (s32[16]{0:T(128)S(1)}, s32[16]{0:T(128)}, u32[]{:S(2)}) copy-start(s32[16]{0:T(128)} %constant.70.clone) | copy-start | bytes 196
  118.8 43.8 %copy-start.2 = (bf16[1056,384]{1,0:T(8,128)(2,1)}, bf16[1056,384]{1,0:T(8,128)(2,1)S(1)}, u32[]{:S(2)}) copy-start(bf16[1056,384]{1,0:T(8,128)(2,1)S(1)} %collective-permute-done.5.refs_6_) | copy-start | bytes 2433028
  119.6 26.5 %collective-permute-start.7 = (bf16[528,384]{1,0:T(8,128)(2,1)}, bf16[528,384]{1,0:T(8,128)(2,1)}, u32[]{:S(2)}, u32[]{:S(2)}) collective-permute-start(bf16[528,384]{1,0:T(8,128)(2,1)} %slice.20), channel_id=1, source_target_pairs={{0,1},{1,2},{2,3},{3,0},{4,5},{5,6},{6,7},{7,4},{8,9},{9,10},{10,1... | collective-permute-start | bytes 1216520 | tf_op jit(solution)/shard_map/ppermute | solution.py:212
  123.5 23.1 %collective-permute-start.8 = (bf16[528,384]{1,0:T(8,128)(2,1)}, bf16[528,384]{1,0:T(8,128)(2,1)}, u32[]{:S(2)}, u32[]{:S(2)}) collective-permute-start(bf16[528,384]{1,0:T(8,128)(2,1)} %slice.21), channel_id=1, source_target_pairs={{0,3},{1,0},{2,1},{3,2},{4,7},{5,4},{6,5},{7,6},{8,11},{9,8},{10,9... | collective-permute-start | bytes 1216520 | tf_op jit(solution)/shard_map/ppermute | solution.py:212
  146.6 16.0 %copy-start.1 = (bf16[4,528,384]{2,1,0:T(8,128)(2,1)}, bf16[4,528,384]{2,1,0:T(8,128)(2,1)S(1)}, u32[]{:S(2)}) copy-start(bf16[4,528,384]{2,1,0:T(8,128)(2,1)S(1)} %all-to-all-done.1) | copy-start | bytes 4866052
Sparse Core Ops, SparseCore 0:
  22.6 63.5 all-gather.2
  88.3 74.1 all-gather.4

commit v13 on v12

--- a/solution.py
+++ b/solution.py
@@ -147,10 +147,12 @@
     ).astype(jnp.bfloat16)
     local = out_ref.shape[1]
     span, window = 128, 256
-    for row in range(0, rows, span):
-        low = min(max(row - (window - span) // 2, 0), rows - window)
-        same = seg_col_ref[row : row + span, :1] == seg_row_ref[:1, low : low + window]
-        heads = range(0, local, HEAD_DIM)
+    for start in range(0, rows, 2 * span):
+        units = []
+        for row in (start, start + span):
+            low = min(max(row - (window - span) // 2, 0), rows - window)
+            same = seg_col_ref[row : row + span, :1] == seg_row_ref[:1, low : low + window]
+            units += [(row, low, same, col) for col in range(0, local, HEAD_DIM)]
         scores = [
             lax.dot_general(
                 sums_ref[row : row + span, col : col + HEAD_DIM],
@@ -159,13 +161,13 @@
                 preferred_element_type=jnp.float32,
             )
             * (1.0 / math.sqrt(HEAD_DIM))
-            for col in heads
+            for row, low, _, col in units
         ]
-        scores = [jnp.where(same, one, -jnp.inf) for one in scores]
+        scores = [jnp.where(unit[2], one, -jnp.inf) for unit, one in zip(units, scores)]
         tops = [jnp.max(one, axis=1, keepdims=True) for one in scores]
         expos = [jnp.exp(one - top) for one, top in zip(scores, tops)]
         shares = [1.0 / jnp.sum(expo, axis=1, keepdims=True) for expo in expos]
-        for col, expo, share in zip(heads, expos, shares):
+        for (row, low, _, col), expo, share in zip(units, expos, shares):
             value = sums_ref[low : low + window, 2 * local + col : 2 * local + col + HEAD_DIM]
             out_ref[row : row + span, col : col + HEAD_DIM] = jnp.dot(
                 (expo * share).astype(jnp.bfloat16), value, preferred_element_type=jnp.float32

time: 188 us -> 187 us (level)
  no operation moved by 1% of the time
where the time goes in v13:
time: 187 us; the launch traced here: 185 us
  waiting for transfers between devices  80.6 us (43%)
  starting transfers between devices  60.6 us (32%)
  Pallas kernels  15.9 us (9%)
  between operations  13.7 us (7%)
  local copies, waits for them, and re-layouts  11.8 us (6%)
  other arithmetic  2.72 us (1%)
    all_gather x2, waiting for transfers between devices, shards(): lax.all_gather(weight, 'dp', axis=0, tiled=True, axis_index_groups=dp_gro...  36.8 us
    ppermute x4, starting transfers between devices, along_z(): return lax.ppermute(block, 'tensor', z_shift(step))  23.1 us
    ppermute x7, starting transfers between devices, along_y(): return lax.ppermute(block, 'tensor', y_shift(step))  23.1 us
    ppermute x7, waiting for transfers between devices, along_y(): return lax.ppermute(block, 'tensor', y_shift(step))  19.9 us
    all_to_all x1, waiting for transfers between devices, shards(): lax.all_to_all(outgoing, 'dp', split_axis=0, concat_axis=0, tiled=True)  19.7 us
    pallas_call x1, Pallas kernels, shards(): pl.pallas_call(kernel, out_shape=jax.ShapeDtypeStruct((rows, local), jnp....  15.9 us
    all_to_all x1, starting transfers between devices, shards(): lax.all_to_all(outgoing, 'dp', split_axis=0, concat_axis=0, tiled=True)  10.4 us
    ppermute x4, waiting for transfers between devices, along_z(): return lax.ppermute(block, 'tensor', z_shift(step))  4.21 us
  transfers between devices with their start and end apart: 15, of which 8 were waited for; matrix products, arithmetic and copies ran while one was open for 6% of the time, Pallas kernels for 0%

profile of v13, /device:TPU:1, one launch (start us, length us, event | category | flops | bytes accessed | tf_op | source)
XLA Modules:
  0.0 185.3 jit_solution(16982974177663931844)
XLA Ops:
  6.5 0.8 dynamic-slice_bitcast_fusion
  7.3 0.1 select_reduce_fusion.1
  7.5 0.2 copy-done
  7.7 1.5 gather_fusion
  9.2 10.4 %all-to-all-start = ((bf16[32,32,384]{2,1,0:T(8,128)(2,1)}), bf16[32,32,384]{2,1,0:T(8,128)(2,1)S(1)}, u32[]{:S(2)}, u32[]{:S(2)}) async-start(bf16[32,32,384]{2,1,0:T(8,128)(2,1)} %gather_fusion), calls=%async_computation | async-start | bytes 1572864 | tf_op jit(solution)/shard_map/all_to_all | solution.py:195
  19.7 0.0 all-gather.3.cloned.1.call-start
  19.7 0.7 pad_maximum_fusion.2
  20.5 0.0 all-gather.3.cloned.1.call-update
  20.5 0.0 all-gather.5.cloned.1.call-start
  20.6 0.7 fusion.7
  21.3 0.1 copy.13
  21.4 0.1 reduce-window.4
  21.4 0.1 reduce
  21.5 0.1 convert_reduce_fusion
  21.6 0.7 fusion.6
  22.3 0.1 select_reduce_fusion
  22.4 19.7 %all-to-all-done = bf16[32,32,384]{2,1,0:T(8,128)(2,1)S(1)} async-done(((bf16[32,32,384]{2,1,0:T(8,128)(2,1)}), bf16[32,32,384]{2,1,0:T(8,128)(2,1)S(1)}, u32[]{:S(2)}, u32[]{:S(2)}) %all-to-all-start) | async-done | bytes 786464 | tf_op jit(solution)/shard_map/all_to_all | solution.py:195
  42.1 1.9 %gather_fusion.1 = bf16[512,384]{1,0:T(8,128)(2,1)S(1)} fusion(bf16[1024,384]{1,0:T(8,128)(2,1)S(1)} %bitcast.22, s32[1024]{0:T(1024)S(1)} %pad_clamp_fusion), kind=kCustom, calls=%fused_computation.1 | custom fusion | bytes 788480 | tf_op jit(solution)/shard_map/gather | solution.py:205
  44.1 8.3 %collective-permute-start = (bf16[528,384]{1,0:T(8,128)(2,1)S(1)}, bf16[528,384]{1,0:T(8,128)(2,1)S(1)}, u32[]{:S(2)}, u32[]{:S(2)}) collective-permute-start(bf16[528,384]{1,0:T(8,128)(2,1)S(1)} %pad_maximum_fusion.refs_1_), channel_id=1, source_target_pairs={{0,4},{1,5},{2,6},{3,7},{4,8},{5,9},{6,10},{7,11},{8,12},{9,13},{1... | collective-permute-start | bytes 1216520 | tf_op jit(solution)/shard_map/ppermute | solution.py:217
  52.4 2.9 %collective-permute-start.1 = (bf16[528,384]{1,0:T(8,128)(2,1)S(1)}, bf16[528,384]{1,0:T(8,128)(2,1)S(1)}, u32[]{:S(2)}, u32[]{:S(2)}) collective-permute-start(bf16[528,384]{1,0:T(8,128)(2,1)S(1)} %pad_maximum_fusion.refs_1_), channel_id=1, source_target_pairs={{0,12},{1,13},{2,14},{3,15},{4,0},{5,1},{6,2},{7,3},{8,4},{9,5},{1... | collective-permute-start | bytes 1216520 | tf_op jit(solution)/shard_map/ppermute | solution.py:217
  55.3 3.2 %collective-permute-start.2 = (bf16[528,384]{1,0:T(8,128)(2,1)S(1)}, bf16[528,384]{1,0:T(8,128)(2,1)S(1)}, u32[]{:S(2)}, u32[]{:S(2)}) collective-permute-start(bf16[528,384]{1,0:T(8,128)(2,1)S(1)} %pad_maximum_fusion.refs_1_), channel_id=1, source_target_pairs={{0,1},{1,2},{2,3},{3,0},{4,5},{5,6},{6,7},{7,4},{8,9},{9,10},{10,1... | collective-permute-start | bytes 1216520 | tf_op jit(solution)/shard_map/ppermute | solution.py:214
  58.5 3.4 %collective-permute-start.3 = (bf16[528,384]{1,0:T(8,128)(2,1)S(1)}, bf16[528,384]{1,0:T(8,128)(2,1)S(1)}, u32[]{:S(2)}, u32[]{:S(2)}) collective-permute-start(bf16[528,384]{1,0:T(8,128)(2,1)S(1)} %pad_maximum_fusion.refs_1_), channel_id=1, source_target_pairs={{0,3},{1,0},{2,1},{3,2},{4,7},{5,4},{6,5},{7,6},{8,11},{9,8},{10,9... | collective-permute-start | bytes 1216520 | tf_op jit(solution)/shard_map/ppermute | solution.py:214
  61.9 3.5 %collective-permute-start.4 = (bf16[528,384]{1,0:T(8,128)(2,1)S(1)}, bf16[528,384]{1,0:T(8,128)(2,1)S(1)}, u32[]{:S(2)}, u32[]{:S(2)}) collective-permute-start(bf16[528,384]{1,0:T(8,128)(2,1)S(1)} %pad_maximum_fusion.refs_1_), channel_id=1, source_target_pairs={{0,2},{1,3},{2,0},{3,1},{4,6},{5,7},{6,4},{7,5},{8,10},{9,11},{10,... | collective-permute-start | bytes 1216520 | tf_op jit(solution)/shard_map/ppermute | solution.py:214
  65.4 20.8 %all-gather.3.cloned.1.call-done = bf16[768,768]{1,0:T(8,128)(2,1)} async-done(((bf16[192,768]{1,0:T(8,128)(2,1)}), bf16[768,768]{1,0:T(8,128)(2,1)}) %all-gather.3.cloned.1.call-update) | async-done | bytes 1179664 | tf_op jit(solution)/shard_map/all_gather | solution.py:186
  86.2 1.8 collective-permute-done
  88.0 0.0 collective-permute-done.2.refs_2_
  88.0 0.0 collective-permute-done.3.refs_3_
  88.1 0.0 all-gather.5.cloned.1.call-update
  88.1 10.1 %collective-permute-start.10 = (bf16[256,384]{1,0:T(8,128)(2,1)S(1)}, bf16[256,384]{1,0:T(8,128)(2,1)S(1)}, u32[]{:S(2)}, u32[]{:S(2)}) collective-permute-start(bf16[256,384]{1,0:T(8,128)(2,1)S(1)} %slice.15), channel_id=1, source_target_pairs={{0,12},{1,13},{2,14},{3,15},{4,0},{5,1},{6,2},{7,3},{8,4},{9,5},{1... | collective-permute-start | bytes 589832 | tf_op jit(solution)/shard_map/ppermute | solution.py:217
  98.2 1.9 %collective-permute-start.9 = (bf16[272,384]{1,0:T(8,128)(2,1)S(1)}, bf16[272,384]{1,0:T(8,128)(2,1)S(1)}, u32[]{:S(2)}, u32[]{:S(2)}) collective-permute-start(bf16[272,384]{1,0:T(8,128)(2,1)S(1)} %slice.14), channel_id=1, source_target_pairs={{0,4},{1,5},{2,6},{3,7},{4,8},{5,9},{6,10},{7,11},{8,12},{9,13},{1... | collective-permute-start | bytes 626696 | tf_op jit(solution)/shard_map/ppermute | solution.py:217
  100.2 0.8 constant_dynamic-update-slice_fusion.1
  101.0 0.8 constant_dynamic-update-slice_fusion.refs_5_
  101.8 3.1 %collective-permute-start.5 = (bf16[1056,384]{1,0:T(8,128)(2,1)}, bf16[1056,384]{1,0:T(8,128)(2,1)S(1)}, u32[]{:S(2)}, u32[]{:S(2)}) collective-permute-start(bf16[1056,384]{1,0:T(8,128)(2,1)} %constant_dynamic-update-slice_fusion.refs_5_), channel_id=1, source_target_pairs={{0,1},{1,2},{2,3},{3,0},{4,5},{5,6},{6,7},{7,4},{8,9},{9,10},{10,1... | collective-permute-start | bytes 2433032 | tf_op jit(solution)/shard_map/ppermute | solution.py:214
  104.9 3.4 %collective-permute-start.6 = (bf16[1056,384]{1,0:T(8,128)(2,1)}, bf16[1056,384]{1,0:T(8,128)(2,1)}, u32[]{:S(2)}, u32[]{:S(2)}) collective-permute-start(bf16[1056,384]{1,0:T(8,128)(2,1)} %constant_dynamic-update-slice_fusion.refs_5_), channel_id=1, source_target_pairs={{0,3},{1,0},{2,1},{3,2},{4,7},{5,4},{6,5},{7,6},{8,11},{9,8},{10,9... | collective-permute-start | bytes 2433032 | tf_op jit(solution)/shard_map/ppermute | solution.py:214
  108.3 2.4 %collective-permute-done.9 = bf16[272,384]{1,0:T(8,128)(2,1)S(1)} collective-permute-done((bf16[272,384]{1,0:T(8,128)(2,1)S(1)}, bf16[272,384]{1,0:T(8,128)(2,1)S(1)}, u32[]{:S(2)}, u32[]{:S(2)}) %collective-permute-start.9) | collective-permute-done | bytes 208928 | tf_op jit(solution)/shard_map/ppermute | solution.py:217
  110.7 1.3 broadcast_in_dim.58
  112.0 3.9 %all-to-all-start.1 = ((bf16[4,528,384]{2,1,0:T(8,128)(2,1)}), bf16[4,528,384]{2,1,0:T(8,128)(2,1)S(1)}, u32[]{:S(2)}, u32[]{:S(2)}) async-start(bf16[4,528,384]{2,1,0:T(8,128)(2,1)} %broadcast_in_dim.58), calls=%async_computation.1 | async-start | bytes 3244032 | tf_op jit(solution)/shard_map/all_to_all | solution.py:236
  115.9 2.8 %collective-permute-done.5.refs_6_ = bf16[1056,384]{1,0:T(8,128)(2,1)S(1)} collective-permute-done((bf16[1056,384]{1,0:T(8,128)(2,1)}, bf16[1056,384]{1,0:T(8,128)(2,1)S(1)}, u32[]{:S(2)}, u32[]{:S(2)}) %collective-permute-start.5) | collective-permute-done | bytes 811040 | tf_op jit(solution)/shard_map/ppermute | solution.py:214
  118.8 0.9 slice.20
  119.6 2.0 %collective-permute-start.7 = (bf16[528,384]{1,0:T(8,128)(2,1)}, bf16[528,384]{1,0:T(8,128)(2,1)}, u32[]{:S(2)}, u32[]{:S(2)}) collective-permute-start(bf16[528,384]{1,0:T(8,128)(2,1)} %slice.20), channel_id=1, source_target_pairs={{0,1},{1,2},{2,3},{3,0},{4,5},{5,6},{6,7},{7,4},{8,9},{9,10},{10,1... | collective-permute-start | bytes 1216520 | tf_op jit(solution)/shard_map/ppermute | solution.py:214
  121.7 1.8 slice.21
  123.5 4.5 %collective-permute-start.8 = (bf16[528,384]{1,0:T(8,128)(2,1)}, bf16[528,384]{1,0:T(8,128)(2,1)}, u32[]{:S(2)}, u32[]{:S(2)}) collective-permute-start(bf16[528,384]{1,0:T(8,128)(2,1)} %slice.21), channel_id=1, source_target_pairs={{0,3},{1,0},{2,1},{3,2},{4,7},{5,4},{6,5},{7,6},{8,11},{9,8},{10,9... | collective-permute-start | bytes 1216520 | tf_op jit(solution)/shard_map/ppermute | solution.py:214
  128.0 0.9 copy.14.refs_12_
  128.8 0.7 fusion.refs_0_
  129.5 16.7 %collective-permute-done.7.refs_8_ = bf16[528,384]{1,0:T(8,128)(2,1)} collective-permute-done((bf16[528,384]{1,0:T(8,128)(2,1)}, bf16[528,384]{1,0:T(8,128)(2,1)}, u32[]{:S(2)}, u32[]{:S(2)}) %collective-permute-start.7) | collective-permute-done | bytes 405536 | tf_op jit(solution)/shard_map/ppermute | solution.py:214
  146.2 0.4 collective-permute-done.8.refs_9_
  146.6 16.0 %all-gather.5.cloned.1.call-done.refs_11_ = bf16[6144,768]{1,0:T(8,128)(2,1)} async-done(((bf16[768,768]{1,0:T(8,128)(2,1)}), bf16[6144,768]{1,0:T(8,128)(2,1)}) %all-gather.5.cloned.1.call-update) | async-done | bytes 9437200 | tf_op jit(solution)/shard_map/all_gather | solution.py:229
  162.6 15.9 %norm_project_attend.1 = bf16[512,256]{1,0:T(8,128)(2,1)} custom-call(s32[16]{0:T(128)} %fusion.refs_0_, bf16[528,384]{1,0:T(8,128)(2,1)} %copy-done.3, bf16[528,384]{1,0:T(8,128)(2,1)} %copy-done.4, bf16[528,384]{1,0:T(8,128)(2,1)} %copy-done.5, bf16[528,384]{1,0:T(8,128)(2,1)} %copy-done.6, bf16[1056,384]{1,0:T(8,128)(2,1)} %constant_dynamic-update-slice_fusion.refs_5_, ...), custom_call_target="tpu_custom_call" | custom-call | tf_op jit(solution)/shard_map/norm_project_attend/pallas_call | solution.py:278
  (42 shorter events, 0.2 us)
Async XLA Ops:
  6.5 1.1 copy-start
  6.5 13.2 %copy-start.7 = (bf16[192,256]{1,0:T(8,128)(2,1)S(1)}, bf16[192,256]{1,0:T(8,128)(2,1)}, u32[]{:S(2)}) copy-start(bf16[192,256]{1,0:T(8,128)(2,1)} %param.13) | copy-start | bytes 294916
  6.5 13.2 %copy-start.8 = (bf16[192,256]{1,0:T(8,128)(2,1)S(1)}, bf16[192,256]{1,0:T(8,128)(2,1)}, u32[]{:S(2)}) copy-start(bf16[192,256]{1,0:T(8,128)(2,1)} %param.12) | copy-start | bytes 294916
  6.5 13.2 %copy-start.9 = (bf16[192,256]{1,0:T(8,128)(2,1)S(1)}, bf16[192,256]{1,0:T(8,128)(2,1)}, u32[]{:S(2)}) copy-start(bf16[192,256]{1,0:T(8,128)(2,1)} %param.11) | copy-start | bytes 294916
  9.2 32.9 %all-to-all-start = ((bf16[32,32,384]{2,1,0:T(8,128)(2,1)}), bf16[32,32,384]{2,1,0:T(8,128)(2,1)S(1)}, u32[]{:S(2)}, u32[]{:S(2)}) async-start(bf16[32,32,384]{2,1,0:T(8,128)(2,1)} %gather_fusion), calls=%async_computation | async-start | bytes 1572864 | tf_op jit(solution)/shard_map/all_to_all | solution.py:195
  19.7 66.6 %all-gather.3.cloned.1.call-start = ((), (), s32[]{:S(2)}) async-start(), calls=%async_computation.2 | async-start | bytes 1474560 | tf_op jit(solution)/shard_map/all_gather | solution.py:186
  20.5 142.1 %all-gather.5.cloned.1.call-start = ((), (), s32[]{:S(2)}) async-start(), calls=%async_computation.3 | async-start | bytes 10616832 | tf_op jit(solution)/shard_map/all_gather | solution.py:229
  21.6 106.3 %copy-start.10 = (s32[512]{0:T(512)}, s32[512]{0:T(512)S(1)}, u32[]{:S(2)}) copy-start(s32[512]{0:T(512)S(1)} %convert_reduce_fusion) | copy-start | bytes 6148
  42.1 1.9 %copy-start.11 = (bf16[384]{0:T(512)(128)(2,1)S(1)}, bf16[384]{0:T(512)(128)(2,1)}, u32[]{:S(2)}) copy-start(bf16[384]{0:T(512)(128)(2,1)} %param.10) | copy-start | bytes 2308
  44.1 57.7 %copy-start.3 = (bf16[528,384]{1,0:T(8,128)(2,1)}, bf16[528,384]{1,0:T(8,128)(2,1)S(1)}, u32[]{:S(2)}) copy-start(bf16[528,384]{1,0:T(8,128)(2,1)S(1)} %pad_maximum_fusion.refs_1_) | copy-start | bytes 1216516
  44.1 43.9 %collective-permute-start = (bf16[528,384]{1,0:T(8,128)(2,1)S(1)}, bf16[528,384]{1,0:T(8,128)(2,1)S(1)}, u32[]{:S(2)}, u32[]{:S(2)}) collective-permute-start(bf16[528,384]{1,0:T(8,128)(2,1)S(1)} %pad_maximum_fusion.refs_1_), channel_id=1, source_target_pairs={{0,4},{1,5},{2,6},{3,7},{4,8},{5,9},{6,10},{7,11},{8,12},{9,13},{1... | collective-permute-start | bytes 1216520 | tf_op jit(solution)/shard_map/ppermute | solution.py:217
  52.4 35.6 %collective-permute-start.1 = (bf16[528,384]{1,0:T(8,128)(2,1)S(1)}, bf16[528,384]{1,0:T(8,128)(2,1)S(1)}, u32[]{:S(2)}, u32[]{:S(2)}) collective-permute-start(bf16[528,384]{1,0:T(8,128)(2,1)S(1)} %pad_maximum_fusion.refs_1_), channel_id=1, source_target_pairs={{0,12},{1,13},{2,14},{3,15},{4,0},{5,1},{6,2},{7,3},{8,4},{9,5},{1... | collective-permute-start | bytes 1216520 | tf_op jit(solution)/shard_map/ppermute | solution.py:217
  55.3 32.7 %collective-permute-start.2 = (bf16[528,384]{1,0:T(8,128)(2,1)S(1)}, bf16[528,384]{1,0:T(8,128)(2,1)S(1)}, u32[]{:S(2)}, u32[]{:S(2)}) collective-permute-start(bf16[528,384]{1,0:T(8,128)(2,1)S(1)} %pad_maximum_fusion.refs_1_), channel_id=1, source_target_pairs={{0,1},{1,2},{2,3},{3,0},{4,5},{5,6},{6,7},{7,4},{8,9},{9,10},{10,1... | collective-permute-start | bytes 1216520 | tf_op jit(solution)/shard_map/ppermute | solution.py:214
  58.5 29.5 %collective-permute-start.3 = (bf16[528,384]{1,0:T(8,128)(2,1)S(1)}, bf16[528,384]{1,0:T(8,128)(2,1)S(1)}, u32[]{:S(2)}, u32[]{:S(2)}) collective-permute-start(bf16[528,384]{1,0:T(8,128)(2,1)S(1)} %pad_maximum_fusion.refs_1_), channel_id=1, source_target_pairs={{0,3},{1,0},{2,1},{3,2},{4,7},{5,4},{6,5},{7,6},{8,11},{9,8},{10,9... | collective-permute-start | bytes 1216520 | tf_op jit(solution)/shard_map/ppermute | solution.py:214
  61.9 26.2 %collective-permute-start.4 = (bf16[528,384]{1,0:T(8,128)(2,1)S(1)}, bf16[528,384]{1,0:T(8,128)(2,1)S(1)}, u32[]{:S(2)}, u32[]{:S(2)}) collective-permute-start(bf16[528,384]{1,0:T(8,128)(2,1)S(1)} %pad_maximum_fusion.refs_1_), channel_id=1, source_target_pairs={{0,2},{1,3},{2,0},{3,1},{4,6},{5,7},{6,4},{7,5},{8,10},{9,11},{10,... | collective-permute-start | bytes 1216520 | tf_op jit(solution)/shard_map/ppermute | solution.py:214
  88.0 13.7 %copy-start.4 = (bf16[528,384]{1,0:T(8,128)(2,1)}, bf16[528,384]{1,0:T(8,128)(2,1)S(1)}, u32[]{:S(2)}) copy-start(bf16[528,384]{1,0:T(8,128)(2,1)S(1)} %collective-permute-done.2.refs_2_) | copy-start | bytes 1216516
  88.1 12.9 %copy-start.5 = (bf16[528,384]{1,0:T(8,128)(2,1)}, bf16[528,384]{1,0:T(8,128)(2,1)S(1)}, u32[]{:S(2)}) copy-start(bf16[528,384]{1,0:T(8,128)(2,1)S(1)} %collective-permute-done.3.refs_3_) | copy-start | bytes 1216516
  88.1 12.9 %copy-start.6 = (bf16[528,384]{1,0:T(8,128)(2,1)}, bf16[528,384]{1,0:T(8,128)(2,1)S(1)}, u32[]{:S(2)}) copy-start(bf16[528,384]{1,0:T(8,128)(2,1)S(1)} %collective-permute-done.4.refs_4_) | copy-start | bytes 1216516
  88.1 20.1 %collective-permute-start.10 = (bf16[256,384]{1,0:T(8,128)(2,1)S(1)}, bf16[256,384]{1,0:T(8,128)(2,1)S(1)}, u32[]{:S(2)}, u32[]{:S(2)}) collective-permute-start(bf16[256,384]{1,0:T(8,128)(2,1)S(1)} %slice.15), channel_id=1, source_target_pairs={{0,12},{1,13},{2,14},{3,15},{4,0},{5,1},{6,2},{7,3},{8,4},{9,5},{1... | collective-permute-start | bytes 589832 | tf_op jit(solution)/shard_map/ppermute | solution.py:217
  98.2 12.4 %collective-permute-start.9 = (bf16[272,384]{1,0:T(8,128)(2,1)S(1)}, bf16[272,384]{1,0:T(8,128)(2,1)S(1)}, u32[]{:S(2)}, u32[]{:S(2)}) collective-permute-start(bf16[272,384]{1,0:T(8,128)(2,1)S(1)} %slice.14), channel_id=1, source_target_pairs={{0,4},{1,5},{2,6},{3,7},{4,8},{5,9},{6,10},{7,11},{8,12},{9,13},{1... | collective-permute-start | bytes 626696 | tf_op jit(solution)/shard_map/ppermute | solution.py:217
  101.8 17.0 %collective-permute-start.5 = (bf16[1056,384]{1,0:T(8,128)(2,1)}, bf16[1056,384]{1,0:T(8,128)(2,1)S(1)}, u32[]{:S(2)}, u32[]{:S(2)}) collective-permute-start(bf16[1056,384]{1,0:T(8,128)(2,1)} %constant_dynamic-update-slice_fusion.refs_5_), channel_id=1, source_target_pairs={{0,1},{1,2},{2,3},{3,0},{4,5},{5,6},{6,7},{7,4},{8,9},{9,10},{10,1... | collective-permute-start | bytes 2433032 | tf_op jit(solution)/shard_map/ppermute | solution.py:214
  104.9 16.7 %collective-permute-start.6 = (bf16[1056,384]{1,0:T(8,128)(2,1)}, bf16[1056,384]{1,0:T(8,128)(2,1)}, u32[]{:S(2)}, u32[]{:S(2)}) collective-permute-start(bf16[1056,384]{1,0:T(8,128)(2,1)} %constant_dynamic-update-slice_fusion.refs_5_), channel_id=1, source_target_pairs={{0,3},{1,0},{2,1},{3,2},{4,7},{5,4},{6,5},{7,6},{8,11},{9,8},{10,9... | collective-permute-start | bytes 2433032 | tf_op jit(solution)/shard_map/ppermute | solution.py:214
  112.0 34.6 %all-to-all-start.1 = ((bf16[4,528,384]{2,1,0:T(8,128)(2,1)}), bf16[4,528,384]{2,1,0:T(8,128)(2,1)S(1)}, u32[]{:S(2)}, u32[]{:S(2)}) async-start(bf16[4,528,384]{2,1,0:T(8,128)(2,1)} %broadcast_in_dim.58), calls=%async_computation.1 | async-start | bytes 3244032 | tf_op jit(solution)/shard_map/all_to_all | solution.py:236
  115.9 12.9 %copy-start.12 = (s32[12]{0:T(128)S(1)}, s32[12]{0:T(128)}, u32[]{:S(2)}) copy-start(s32[12]{0:T(128)} %constant.71.clone) | copy-start | bytes 148
  115.9 12.9 %copy-start.13 = (s32[16]{0:T(128)S(1)}, s32[16]{0:T(128)}, u32[]{:S(2)}) copy-start(s32[16]{0:T(128)} %constant.70.clone) | copy-start | bytes 196
  118.8 43.8 %copy-start.2 = (bf16[1056,384]{1,0:T(8,128)(2,1)}, bf16[1056,384]{1,0:T(8,128)(2,1)S(1)}, u32[]{:S(2)}) copy-start(bf16[1056,384]{1,0:T(8,128)(2,1)S(1)} %collective-permute-done.5.refs_6_) | copy-start | bytes 2433028
  119.6 26.6 %collective-permute-start.7 = (bf16[528,384]{1,0:T(8,128)(2,1)}, bf16[528,384]{1,0:T(8,128)(2,1)}, u32[]{:S(2)}, u32[]{:S(2)}) collective-permute-start(bf16[528,384]{1,0:T(8,128)(2,1)} %slice.20), channel_id=1, source_target_pairs={{0,1},{1,2},{2,3},{3,0},{4,5},{5,6},{6,7},{7,4},{8,9},{9,10},{10,1... | collective-permute-start | bytes 1216520 | tf_op jit(solution)/shard_map/ppermute | solution.py:214
  123.5 23.1 %collective-permute-start.8 = (bf16[528,384]{1,0:T(8,128)(2,1)}, bf16[528,384]{1,0:T(8,128)(2,1)}, u32[]{:S(2)}, u32[]{:S(2)}) collective-permute-start(bf16[528,384]{1,0:T(8,128)(2,1)} %slice.21), channel_id=1, source_target_pairs={{0,3},{1,0},{2,1},{3,2},{4,7},{5,4},{6,5},{7,6},{8,11},{9,8},{10,9... | collective-permute-start | bytes 1216520 | tf_op jit(solution)/shard_map/ppermute | solution.py:214
  146.6 16.0 %copy-start.1 = (bf16[4,528,384]{2,1,0:T(8,128)(2,1)}, bf16[4,528,384]{2,1,0:T(8,128)(2,1)S(1)}, u32[]{:S(2)}) copy-start(bf16[4,528,384]{2,1,0:T(8,128)(2,1)S(1)} %all-to-all-done.1) | copy-start | bytes 4866052
Sparse Core Ops, SparseCore 0:
  22.6 63.5 all-gather.2
  88.3 74.1 all-gather.4

commit v14 on v13

--- a/solution.py
+++ b/solution.py
@@ -147,9 +147,9 @@
     ).astype(jnp.bfloat16)
     local = out_ref.shape[1]
     span, window = 128, 256
-    for start in range(0, rows, 2 * span):
+    for start in range(0, rows, 4 * span):
         units = []
-        for row in (start, start + span):
+        for row in range(start, start + 4 * span, span):
             low = min(max(row - (window - span) // 2, 0), rows - window)
             same = seg_col_ref[row : row + span, :1] == seg_row_ref[:1, low : low + window]
             units += [(row, low, same, col) for col in range(0, local, HEAD_DIM)]

time: 187 us -> 189 us (1.011)
  no operation moved by 1% of the time
where the time goes in v14:
time: 189 us; the launch traced here: 186 us
  waiting for transfers between devices  80.6 us (43%)
  starting transfers between devices  60.6 us (32%)
  Pallas kernels  17 us (9%)
  between operations  13.7 us (7%)
  local copies, waits for them, and re-layouts  11.8 us (6%)
  other arithmetic  2.72 us (1%)
    all_gather x2, waiting for transfers between devices, shards(): lax.all_gather(weight, 'dp', axis=0, tiled=True, axis_index_groups=dp_gro...  36.8 us
    ppermute x4, starting transfers between devices, along_z(): return lax.ppermute(block, 'tensor', z_shift(step))  23.1 us
    ppermute x7, starting transfers between devices, along_y(): return lax.ppermute(block, 'tensor', y_shift(step))  23.1 us
    ppermute x7, waiting for transfers between devices, along_y(): return lax.ppermute(block, 'tensor', y_shift(step))  19.9 us
    all_to_all x1, waiting for transfers between devices, shards(): lax.all_to_all(outgoing, 'dp', split_axis=0, concat_axis=0, tiled=True)  19.7 us
    pallas_call x1, Pallas kernels, shards(): pl.pallas_call(kernel, out_shape=jax.ShapeDtypeStruct((rows, local), jnp....  17 us
    all_to_all x1, starting transfers between devices, shards(): lax.all_to_all(outgoing, 'dp', split_axis=0, concat_axis=0, tiled=True)  10.4 us
    ppermute x4, waiting for transfers between devices, along_z(): return lax.ppermute(block, 'tensor', z_shift(step))  4.2 us
  transfers between devices with their start and end apart: 15, of which 8 were waited for; matrix products, arithmetic and copies ran while one was open for 6% of the time, Pallas kernels for 0%

profile of v14, /device:TPU:1, one launch (start us, length us, event | category | flops | bytes accessed | tf_op | source)
XLA Modules:
  0.0 186.4 jit_solution(10716131971621684875)
XLA Ops:
  6.5 0.8 dynamic-slice_bitcast_fusion
  7.3 0.1 select_reduce_fusion.1
  7.5 0.2 copy-done
  7.7 1.5 gather_fusion
  9.2 10.4 %all-to-all-start = ((bf16[32,32,384]{2,1,0:T(8,128)(2,1)}), bf16[32,32,384]{2,1,0:T(8,128)(2,1)S(1)}, u32[]{:S(2)}, u32[]{:S(2)}) async-start(bf16[32,32,384]{2,1,0:T(8,128)(2,1)} %gather_fusion), calls=%async_computation | async-start | bytes 1572864 | tf_op jit(solution)/shard_map/all_to_all | solution.py:195
  19.7 0.0 all-gather.3.cloned.1.call-start
  19.7 0.7 pad_maximum_fusion.2
  20.5 0.0 all-gather.3.cloned.1.call-update
  20.5 0.0 all-gather.5.cloned.1.call-start
  20.6 0.7 fusion.7
  21.3 0.1 copy.13
  21.4 0.1 reduce-window.4
  21.4 0.1 reduce
  21.5 0.1 convert_reduce_fusion
  21.6 0.7 fusion.6
  22.3 0.1 select_reduce_fusion
  22.4 19.7 %all-to-all-done = bf16[32,32,384]{2,1,0:T(8,128)(2,1)S(1)} async-done(((bf16[32,32,384]{2,1,0:T(8,128)(2,1)}), bf16[32,32,384]{2,1,0:T(8,128)(2,1)S(1)}, u32[]{:S(2)}, u32[]{:S(2)}) %all-to-all-start) | async-done | bytes 786464 | tf_op jit(solution)/shard_map/all_to_all | solution.py:195
  42.1 1.9 %gather_fusion.1 = bf16[512,384]{1,0:T(8,128)(2,1)S(1)} fusion(bf16[1024,384]{1,0:T(8,128)(2,1)S(1)} %bitcast.22, s32[1024]{0:T(1024)S(1)} %pad_clamp_fusion), kind=kCustom, calls=%fused_computation.1 | custom fusion | bytes 788480 | tf_op jit(solution)/shard_map/gather | solution.py:205
  44.1 8.3 %collective-permute-start = (bf16[528,384]{1,0:T(8,128)(2,1)S(1)}, bf16[528,384]{1,0:T(8,128)(2,1)S(1)}, u32[]{:S(2)}, u32[]{:S(2)}) collective-permute-start(bf16[528,384]{1,0:T(8,128)(2,1)S(1)} %pad_maximum_fusion.refs_1_), channel_id=1, source_target_pairs={{0,4},{1,5},{2,6},{3,7},{4,8},{5,9},{6,10},{7,11},{8,12},{9,13},{1... | collective-permute-start | bytes 1216520 | tf_op jit(solution)/shard_map/ppermute | solution.py:217
  52.4 2.9 %collective-permute-start.1 = (bf16[528,384]{1,0:T(8,128)(2,1)S(1)}, bf16[528,384]{1,0:T(8,128)(2,1)S(1)}, u32[]{:S(2)}, u32[]{:S(2)}) collective-permute-start(bf16[528,384]{1,0:T(8,128)(2,1)S(1)} %pad_maximum_fusion.refs_1_), channel_id=1, source_target_pairs={{0,12},{1,13},{2,14},{3,15},{4,0},{5,1},{6,2},{7,3},{8,4},{9,5},{1... | collective-permute-start | bytes 1216520 | tf_op jit(solution)/shard_map/ppermute | solution.py:217
  55.3 3.2 %collective-permute-start.2 = (bf16[528,384]{1,0:T(8,128)(2,1)S(1)}, bf16[528,384]{1,0:T(8,128)(2,1)S(1)}, u32[]{:S(2)}, u32[]{:S(2)}) collective-permute-start(bf16[528,384]{1,0:T(8,128)(2,1)S(1)} %pad_maximum_fusion.refs_1_), channel_id=1, source_target_pairs={{0,1},{1,2},{2,3},{3,0},{4,5},{5,6},{6,7},{7,4},{8,9},{9,10},{10,1... | collective-permute-start | bytes 1216520 | tf_op jit(solution)/shard_map/ppermute | solution.py:214
  58.5 3.4 %collective-permute-start.3 = (bf16[528,384]{1,0:T(8,128)(2,1)S(1)}, bf16[528,384]{1,0:T(8,128)(2,1)S(1)}, u32[]{:S(2)}, u32[]{:S(2)}) collective-permute-start(bf16[528,384]{1,0:T(8,128)(2,1)S(1)} %pad_maximum_fusion.refs_1_), channel_id=1, source_target_pairs={{0,3},{1,0},{2,1},{3,2},{4,7},{5,4},{6,5},{7,6},{8,11},{9,8},{10,9... | collective-permute-start | bytes 1216520 | tf_op jit(solution)/shard_map/ppermute | solution.py:214
  61.9 3.5 %collective-permute-start.4 = (bf16[528,384]{1,0:T(8,128)(2,1)S(1)}, bf16[528,384]{1,0:T(8,128)(2,1)S(1)}, u32[]{:S(2)}, u32[]{:S(2)}) collective-permute-start(bf16[528,384]{1,0:T(8,128)(2,1)S(1)} %pad_maximum_fusion.refs_1_), channel_id=1, source_target_pairs={{0,2},{1,3},{2,0},{3,1},{4,6},{5,7},{6,4},{7,5},{8,10},{9,11},{10,... | collective-permute-start | bytes 1216520 | tf_op jit(solution)/shard_map/ppermute | solution.py:214
  65.4 20.8 %all-gather.3.cloned.1.call-done = bf16[768,768]{1,0:T(8,128)(2,1)} async-done(((bf16[192,768]{1,0:T(8,128)(2,1)}), bf16[768,768]{1,0:T(8,128)(2,1)}) %all-gather.3.cloned.1.call-update) | async-done | bytes 1179664 | tf_op jit(solution)/shard_map/all_gather | solution.py:186
  86.2 1.8 collective-permute-done
  88.0 0.0 collective-permute-done.2.refs_2_
  88.0 0.0 collective-permute-done.3.refs_3_
  88.1 0.0 all-gather.5.cloned.1.call-update
  88.1 10.1 %collective-permute-start.10 = (bf16[256,384]{1,0:T(8,128)(2,1)S(1)}, bf16[256,384]{1,0:T(8,128)(2,1)S(1)}, u32[]{:S(2)}, u32[]{:S(2)}) collective-permute-start(bf16[256,384]{1,0:T(8,128)(2,1)S(1)} %slice.15), channel_id=1, source_target_pairs={{0,12},{1,13},{2,14},{3,15},{4,0},{5,1},{6,2},{7,3},{8,4},{9,5},{1... | collective-permute-start | bytes 589832 | tf_op jit(solution)/shard_map/ppermute | solution.py:217
  98.3 1.9 %collective-permute-start.9 = (bf16[272,384]{1,0:T(8,128)(2,1)S(1)}, bf16[272,384]{1,0:T(8,128)(2,1)S(1)}, u32[]{:S(2)}, u32[]{:S(2)}) collective-permute-start(bf16[272,384]{1,0:T(8,128)(2,1)S(1)} %slice.14), channel_id=1, source_target_pairs={{0,4},{1,5},{2,6},{3,7},{4,8},{5,9},{6,10},{7,11},{8,12},{9,13},{1... | collective-permute-start | bytes 626696 | tf_op jit(solution)/shard_map/ppermute | solution.py:217
  100.2 0.8 constant_dynamic-update-slice_fusion.1
  101.0 0.8 constant_dynamic-update-slice_fusion.refs_5_
  101.8 3.1 %collective-permute-start.5 = (bf16[1056,384]{1,0:T(8,128)(2,1)}, bf16[1056,384]{1,0:T(8,128)(2,1)S(1)}, u32[]{:S(2)}, u32[]{:S(2)}) collective-permute-start(bf16[1056,384]{1,0:T(8,128)(2,1)} %constant_dynamic-update-slice_fusion.refs_5_), channel_id=1, source_target_pairs={{0,1},{1,2},{2,3},{3,0},{4,5},{5,6},{6,7},{7,4},{8,9},{9,10},{10,1... | collective-permute-start | bytes 2433032 | tf_op jit(solution)/shard_map/ppermute | solution.py:214
  104.9 3.4 %collective-permute-start.6 = (bf16[1056,384]{1,0:T(8,128)(2,1)}, bf16[1056,384]{1,0:T(8,128)(2,1)}, u32[]{:S(2)}, u32[]{:S(2)}) collective-permute-start(bf16[1056,384]{1,0:T(8,128)(2,1)} %constant_dynamic-update-slice_fusion.refs_5_), channel_id=1, source_target_pairs={{0,3},{1,0},{2,1},{3,2},{4,7},{5,4},{6,5},{7,6},{8,11},{9,8},{10,9... | collective-permute-start | bytes 2433032 | tf_op jit(solution)/shard_map/ppermute | solution.py:214
  108.3 2.4 %collective-permute-done.9 = bf16[272,384]{1,0:T(8,128)(2,1)S(1)} collective-permute-done((bf16[272,384]{1,0:T(8,128)(2,1)S(1)}, bf16[272,384]{1,0:T(8,128)(2,1)S(1)}, u32[]{:S(2)}, u32[]{:S(2)}) %collective-permute-start.9) | collective-permute-done | bytes 208928 | tf_op jit(solution)/shard_map/ppermute | solution.py:217
  110.7 1.3 broadcast_in_dim.58
  112.0 3.9 %all-to-all-start.1 = ((bf16[4,528,384]{2,1,0:T(8,128)(2,1)}), bf16[4,528,384]{2,1,0:T(8,128)(2,1)S(1)}, u32[]{:S(2)}, u32[]{:S(2)}) async-start(bf16[4,528,384]{2,1,0:T(8,128)(2,1)} %broadcast_in_dim.58), calls=%async_computation.1 | async-start | bytes 3244032 | tf_op jit(solution)/shard_map/all_to_all | solution.py:236
  115.9 2.9 %collective-permute-done.5.refs_6_ = bf16[1056,384]{1,0:T(8,128)(2,1)S(1)} collective-permute-done((bf16[1056,384]{1,0:T(8,128)(2,1)}, bf16[1056,384]{1,0:T(8,128)(2,1)S(1)}, u32[]{:S(2)}, u32[]{:S(2)}) %collective-permute-start.5) | collective-permute-done | bytes 811040 | tf_op jit(solution)/shard_map/ppermute | solution.py:214
  118.8 0.9 slice.20
  119.6 2.0 %collective-permute-start.7 = (bf16[528,384]{1,0:T(8,128)(2,1)}, bf16[528,384]{1,0:T(8,128)(2,1)}, u32[]{:S(2)}, u32[]{:S(2)}) collective-permute-start(bf16[528,384]{1,0:T(8,128)(2,1)} %slice.20), channel_id=1, source_target_pairs={{0,1},{1,2},{2,3},{3,0},{4,5},{5,6},{6,7},{7,4},{8,9},{9,10},{10,1... | collective-permute-start | bytes 1216520 | tf_op jit(solution)/shard_map/ppermute | solution.py:214
  121.7 1.8 slice.21
  123.5 4.5 %collective-permute-start.8 = (bf16[528,384]{1,0:T(8,128)(2,1)}, bf16[528,384]{1,0:T(8,128)(2,1)}, u32[]{:S(2)}, u32[]{:S(2)}) collective-permute-start(bf16[528,384]{1,0:T(8,128)(2,1)} %slice.21), channel_id=1, source_target_pairs={{0,3},{1,0},{2,1},{3,2},{4,7},{5,4},{6,5},{7,6},{8,11},{9,8},{10,9... | collective-permute-start | bytes 1216520 | tf_op jit(solution)/shard_map/ppermute | solution.py:214
  128.0 0.9 copy.14.refs_12_
  128.9 0.7 fusion.refs_0_
  129.5 16.6 %collective-permute-done.7.refs_8_ = bf16[528,384]{1,0:T(8,128)(2,1)} collective-permute-done((bf16[528,384]{1,0:T(8,128)(2,1)}, bf16[528,384]{1,0:T(8,128)(2,1)}, u32[]{:S(2)}, u32[]{:S(2)}) %collective-permute-start.7) | collective-permute-done | bytes 405536 | tf_op jit(solution)/shard_map/ppermute | solution.py:214
  146.2 0.4 collective-permute-done.8.refs_9_
  146.6 16.0 %all-gather.5.cloned.1.call-done.refs_11_ = bf16[6144,768]{1,0:T(8,128)(2,1)} async-done(((bf16[768,768]{1,0:T(8,128)(2,1)}), bf16[6144,768]{1,0:T(8,128)(2,1)}) %all-gather.5.cloned.1.call-update) | async-done | bytes 9437200 | tf_op jit(solution)/shard_map/all_gather | solution.py:229
  162.6 17.0 %norm_project_attend.1 = bf16[512,256]{1,0:T(8,128)(2,1)} custom-call(s32[16]{0:T(128)} %fusion.refs_0_, bf16[528,384]{1,0:T(8,128)(2,1)} %copy-done.3, bf16[528,384]{1,0:T(8,128)(2,1)} %copy-done.4, bf16[528,384]{1,0:T(8,128)(2,1)} %copy-done.5, bf16[528,384]{1,0:T(8,128)(2,1)} %copy-done.6, bf16[1056,384]{1,0:T(8,128)(2,1)} %constant_dynamic-update-slice_fusion.refs_5_, ...), custom_call_target="tpu_custom_call" | custom-call | tf_op jit(solution)/shard_map/norm_project_attend/pallas_call | solution.py:278
  (42 shorter events, 0.2 us)
Async XLA Ops:
  6.5 1.1 copy-start
  6.5 13.2 %copy-start.7 = (bf16[192,256]{1,0:T(8,128)(2,1)S(1)}, bf16[192,256]{1,0:T(8,128)(2,1)}, u32[]{:S(2)}) copy-start(bf16[192,256]{1,0:T(8,128)(2,1)} %param.13) | copy-start | bytes 294916
  6.5 13.2 %copy-start.8 = (bf16[192,256]{1,0:T(8,128)(2,1)S(1)}, bf16[192,256]{1,0:T(8,128)(2,1)}, u32[]{:S(2)}) copy-start(bf16[192,256]{1,0:T(8,128)(2,1)} %param.12) | copy-start | bytes 294916
  6.5 13.2 %copy-start.9 = (bf16[192,256]{1,0:T(8,128)(2,1)S(1)}, bf16[192,256]{1,0:T(8,128)(2,1)}, u32[]{:S(2)}) copy-start(bf16[192,256]{1,0:T(8,128)(2,1)} %param.11) | copy-start | bytes 294916
  9.2 32.9 %all-to-all-start = ((bf16[32,32,384]{2,1,0:T(8,128)(2,1)}), bf16[32,32,384]{2,1,0:T(8,128)(2,1)S(1)}, u32[]{:S(2)}, u32[]{:S(2)}) async-start(bf16[32,32,384]{2,1,0:T(8,128)(2,1)} %gather_fusion), calls=%async_computation | async-start | bytes 1572864 | tf_op jit(solution)/shard_map/all_to_all | solution.py:195
  19.7 66.6 %all-gather.3.cloned.1.call-start = ((), (), s32[]{:S(2)}) async-start(), calls=%async_computation.2 | async-start | bytes 1474560 | tf_op jit(solution)/shard_map/all_gather | solution.py:186
  20.5 142.1 %all-gather.5.cloned.1.call-start = ((), (), s32[]{:S(2)}) async-start(), calls=%async_computation.3 | async-start | bytes 10616832 | tf_op jit(solution)/shard_map/all_gather | solution.py:229
  21.6 106.4 %copy-start.10 = (s32[512]{0:T(512)}, s32[512]{0:T(512)S(1)}, u32[]{:S(2)}) copy-start(s32[512]{0:T(512)S(1)} %convert_reduce_fusion) | copy-start | bytes 6148
  42.1 1.9 %copy-start.11 = (bf16[384]{0:T(512)(128)(2,1)S(1)}, bf16[384]{0:T(512)(128)(2,1)}, u32[]{:S(2)}) copy-start(bf16[384]{0:T(512)(128)(2,1)} %param.10) | copy-start | bytes 2308
  44.1 57.7 %copy-start.3 = (bf16[528,384]{1,0:T(8,128)(2,1)}, bf16[528,384]{1,0:T(8,128)(2,1)S(1)}, u32[]{:S(2)}) copy-start(bf16[528,384]{1,0:T(8,128)(2,1)S(1)} %pad_maximum_fusion.refs_1_) | copy-start | bytes 1216516
  44.1 43.9 %collective-permute-start = (bf16[528,384]{1,0:T(8,128)(2,1)S(1)}, bf16[528,384]{1,0:T(8,128)(2,1)S(1)}, u32[]{:S(2)}, u32[]{:S(2)}) collective-permute-start(bf16[528,384]{1,0:T(8,128)(2,1)S(1)} %pad_maximum_fusion.refs_1_), channel_id=1, source_target_pairs={{0,4},{1,5},{2,6},{3,7},{4,8},{5,9},{6,10},{7,11},{8,12},{9,13},{1... | collective-permute-start | bytes 1216520 | tf_op jit(solution)/shard_map/ppermute | solution.py:217
  52.4 35.6 %collective-permute-start.1 = (bf16[528,384]{1,0:T(8,128)(2,1)S(1)}, bf16[528,384]{1,0:T(8,128)(2,1)S(1)}, u32[]{:S(2)}, u32[]{:S(2)}) collective-permute-start(bf16[528,384]{1,0:T(8,128)(2,1)S(1)} %pad_maximum_fusion.refs_1_), channel_id=1, source_target_pairs={{0,12},{1,13},{2,14},{3,15},{4,0},{5,1},{6,2},{7,3},{8,4},{9,5},{1... | collective-permute-start | bytes 1216520 | tf_op jit(solution)/shard_map/ppermute | solution.py:217
  55.3 32.7 %collective-permute-start.2 = (bf16[528,384]{1,0:T(8,128)(2,1)S(1)}, bf16[528,384]{1,0:T(8,128)(2,1)S(1)}, u32[]{:S(2)}, u32[]{:S(2)}) collective-permute-start(bf16[528,384]{1,0:T(8,128)(2,1)S(1)} %pad_maximum_fusion.refs_1_), channel_id=1, source_target_pairs={{0,1},{1,2},{2,3},{3,0},{4,5},{5,6},{6,7},{7,4},{8,9},{9,10},{10,1... | collective-permute-start | bytes 1216520 | tf_op jit(solution)/shard_map/ppermute | solution.py:214
  58.5 29.5 %collective-permute-start.3 = (bf16[528,384]{1,0:T(8,128)(2,1)S(1)}, bf16[528,384]{1,0:T(8,128)(2,1)S(1)}, u32[]{:S(2)}, u32[]{:S(2)}) collective-permute-start(bf16[528,384]{1,0:T(8,128)(2,1)S(1)} %pad_maximum_fusion.refs_1_), channel_id=1, source_target_pairs={{0,3},{1,0},{2,1},{3,2},{4,7},{5,4},{6,5},{7,6},{8,11},{9,8},{10,9... | collective-permute-start | bytes 1216520 | tf_op jit(solution)/shard_map/ppermute | solution.py:214
  61.9 26.2 %collective-permute-start.4 = (bf16[528,384]{1,0:T(8,128)(2,1)S(1)}, bf16[528,384]{1,0:T(8,128)(2,1)S(1)}, u32[]{:S(2)}, u32[]{:S(2)}) collective-permute-start(bf16[528,384]{1,0:T(8,128)(2,1)S(1)} %pad_maximum_fusion.refs_1_), channel_id=1, source_target_pairs={{0,2},{1,3},{2,0},{3,1},{4,6},{5,7},{6,4},{7,5},{8,10},{9,11},{10,... | collective-permute-start | bytes 1216520 | tf_op jit(solution)/shard_map/ppermute | solution.py:214
  88.0 13.8 %copy-start.4 = (bf16[528,384]{1,0:T(8,128)(2,1)}, bf16[528,384]{1,0:T(8,128)(2,1)S(1)}, u32[]{:S(2)}) copy-start(bf16[528,384]{1,0:T(8,128)(2,1)S(1)} %collective-permute-done.2.refs_2_) | copy-start | bytes 1216516
  88.1 12.9 %copy-start.5 = (bf16[528,384]{1,0:T(8,128)(2,1)}, bf16[528,384]{1,0:T(8,128)(2,1)S(1)}, u32[]{:S(2)}) copy-start(bf16[528,384]{1,0:T(8,128)(2,1)S(1)} %collective-permute-done.3.refs_3_) | copy-start | bytes 1216516
  88.1 12.9 %copy-start.6 = (bf16[528,384]{1,0:T(8,128)(2,1)}, bf16[528,384]{1,0:T(8,128)(2,1)S(1)}, u32[]{:S(2)}) copy-start(bf16[528,384]{1,0:T(8,128)(2,1)S(1)} %collective-permute-done.4.refs_4_) | copy-start | bytes 1216516
  88.1 20.2 %collective-permute-start.10 = (bf16[256,384]{1,0:T(8,128)(2,1)S(1)}, bf16[256,384]{1,0:T(8,128)(2,1)S(1)}, u32[]{:S(2)}, u32[]{:S(2)}) collective-permute-start(bf16[256,384]{1,0:T(8,128)(2,1)S(1)} %slice.15), channel_id=1, source_target_pairs={{0,12},{1,13},{2,14},{3,15},{4,0},{5,1},{6,2},{7,3},{8,4},{9,5},{1... | collective-permute-start | bytes 589832 | tf_op jit(solution)/shard_map/ppermute | solution.py:217
  98.3 12.4 %collective-permute-start.9 = (bf16[272,384]{1,0:T(8,128)(2,1)S(1)}, bf16[272,384]{1,0:T(8,128)(2,1)S(1)}, u32[]{:S(2)}, u32[]{:S(2)}) collective-permute-start(bf16[272,384]{1,0:T(8,128)(2,1)S(1)} %slice.14), channel_id=1, source_target_pairs={{0,4},{1,5},{2,6},{3,7},{4,8},{5,9},{6,10},{7,11},{8,12},{9,13},{1... | collective-permute-start | bytes 626696 | tf_op jit(solution)/shard_map/ppermute | solution.py:217
  101.8 17.0 %collective-permute-start.5 = (bf16[1056,384]{1,0:T(8,128)(2,1)}, bf16[1056,384]{1,0:T(8,128)(2,1)S(1)}, u32[]{:S(2)}, u32[]{:S(2)}) collective-permute-start(bf16[1056,384]{1,0:T(8,128)(2,1)} %constant_dynamic-update-slice_fusion.refs_5_), channel_id=1, source_target_pairs={{0,1},{1,2},{2,3},{3,0},{4,5},{5,6},{6,7},{7,4},{8,9},{9,10},{10,1... | collective-permute-start | bytes 2433032 | tf_op jit(solution)/shard_map/ppermute | solution.py:214
  104.9 16.7 %collective-permute-start.6 = (bf16[1056,384]{1,0:T(8,128)(2,1)}, bf16[1056,384]{1,0:T(8,128)(2,1)}, u32[]{:S(2)}, u32[]{:S(2)}) collective-permute-start(bf16[1056,384]{1,0:T(8,128)(2,1)} %constant_dynamic-update-slice_fusion.refs_5_), channel_id=1, source_target_pairs={{0,3},{1,0},{2,1},{3,2},{4,7},{5,4},{6,5},{7,6},{8,11},{9,8},{10,9... | collective-permute-start | bytes 2433032 | tf_op jit(solution)/shard_map/ppermute | solution.py:214
  112.0 34.6 %all-to-all-start.1 = ((bf16[4,528,384]{2,1,0:T(8,128)(2,1)}), bf16[4,528,384]{2,1,0:T(8,128)(2,1)S(1)}, u32[]{:S(2)}, u32[]{:S(2)}) async-start(bf16[4,528,384]{2,1,0:T(8,128)(2,1)} %broadcast_in_dim.58), calls=%async_computation.1 | async-start | bytes 3244032 | tf_op jit(solution)/shard_map/all_to_all | solution.py:236
  115.9 12.9 %copy-start.12 = (s32[12]{0:T(128)S(1)}, s32[12]{0:T(128)}, u32[]{:S(2)}) copy-start(s32[12]{0:T(128)} %constant.71.clone) | copy-start | bytes 148
  115.9 12.9 %copy-start.13 = (s32[16]{0:T(128)S(1)}, s32[16]{0:T(128)}, u32[]{:S(2)}) copy-start(s32[16]{0:T(128)} %constant.70.clone) | copy-start | bytes 196
  118.8 43.8 %copy-start.2 = (bf16[1056,384]{1,0:T(8,128)(2,1)}, bf16[1056,384]{1,0:T(8,128)(2,1)S(1)}, u32[]{:S(2)}) copy-start(bf16[1056,384]{1,0:T(8,128)(2,1)S(1)} %collective-permute-done.5.refs_6_) | copy-start | bytes 2433028
  119.6 26.5 %collective-permute-start.7 = (bf16[528,384]{1,0:T(8,128)(2,1)}, bf16[528,384]{1,0:T(8,128)(2,1)}, u32[]{:S(2)}, u32[]{:S(2)}) collective-permute-start(bf16[528,384]{1,0:T(8,128)(2,1)} %slice.20), channel_id=1, source_target_pairs={{0,1},{1,2},{2,3},{3,0},{4,5},{5,6},{6,7},{7,4},{8,9},{9,10},{10,1... | collective-permute-start | bytes 1216520 | tf_op jit(solution)/shard_map/ppermute | solution.py:214
  123.5 23.1 %collective-permute-start.8 = (bf16[528,384]{1,0:T(8,128)(2,1)}, bf16[528,384]{1,0:T(8,128)(2,1)}, u32[]{:S(2)}, u32[]{:S(2)}) collective-permute-start(bf16[528,384]{1,0:T(8,128)(2,1)} %slice.21), channel_id=1, source_target_pairs={{0,3},{1,0},{2,1},{3,2},{4,7},{5,4},{6,5},{7,6},{8,11},{9,8},{10,9... | collective-permute-start | bytes 1216520 | tf_op jit(solution)/shard_map/ppermute | solution.py:214
  146.6 16.0 %copy-start.1 = (bf16[4,528,384]{2,1,0:T(8,128)(2,1)}, bf16[4,528,384]{2,1,0:T(8,128)(2,1)S(1)}, u32[]{:S(2)}) copy-start(bf16[4,528,384]{2,1,0:T(8,128)(2,1)S(1)} %all-to-all-done.1) | copy-start | bytes 4866052
Sparse Core Ops, SparseCore 0:
  22.6 63.5 all-gather.2
  88.3 74.1 all-gather.4
